TPU v7x, 256 devices: a whole 4x4x8 slice. The times are simulated.
256 devices in a mesh: src: 32 (over z, x), dst: 8 (over y, core).
Axes of the slice: x: 4, y: 4, z: 8, core: 2. Of those that a mesh axis runs over, the one named last changes fastest.
Arguments:
- counts: int32 [8, 8192, 8192], P(None, 'src', 'dst'), may hold values from 0 to 63
- src_factor: float32 [8192, 128], P('src'), may hold values from 0.25 to 32
- dst_factor: float32 [8192, 128], P('dst'), may hold values from 0.25 to 32
- hour_factor: float32 [8, 32], replicated, may hold values from 0.25 to 4
- core: float32 [32, 128, 128], replicated, may hold values from 1e-06 to 1e-05
Outputs:
- grad_src: float32 [8192, 128], P('src')
- grad_dst: float32 [8192, 128], P('dst')
- grad_hour: float32 [8, 32], replicated
- grad_core: float32 [32, 128, 128], P(None, 'src')
All inputs are finite; a program needn't handle non-finite values.
Results may differ from a plain program's by a relative error of at most 0.0003.
Values sent between devices are 32-bit elements; how exact they have to be, the bound alone decides.
No kernel may reach another device: no remote copies, remote signals or barrier semaphores. Data moves between devices by JAX's collectives and lax.ppermute only.
A program may use at most 64 MiB of HBM per device.

v0:
```python
import math

import jax
import jax.numpy as jnp
from jax import lax
from jax.sharding import PartitionSpec as P


def in_blocks(x, dim, length):
    shape = x.shape
    tiles = x.reshape(*shape[:dim], length, shape[dim] // length, *shape[dim + 1 :])
    return jnp.moveaxis(tiles, dim, 0)


def sent_and_summed(x, axis, dim):
    tiles = in_blocks(x, dim, lax.axis_size(axis))
    arrived = lax.all_to_all(tiles, axis, split_axis=0, concat_axis=0, tiled=True)
    return arrived.sum(axis=0)


def rows_for(lines, length):
    spare = -lines.shape[0] % length
    if not spare:
        return lines
    return jnp.concatenate([lines, jnp.zeros((spare, *lines.shape[1:]), lines.dtype)])


def sent_to_all(x, axis):
    copies = jnp.broadcast_to(x, (lax.axis_size(axis), *x.shape))
    return lax.all_to_all(copies, axis, split_axis=0, concat_axis=0, tiled=True)


def laid_out(tiles, dim):
    shape = list(tiles.shape[1:])
    shape[dim] *= tiles.shape[0]
    return jnp.moveaxis(tiles, 0, dim).reshape(shape)


def gather_directly(x, axis, dim):
    tiles = sent_to_all(x, axis)
    return laid_out(tiles, dim)


def nested_sum(x, axes):
    lines = x.reshape(-1, x.shape[-1])
    own = sent_and_summed(rows_for(lines, lax.axis_size(axes)), axes, 0)
    whole = gather_directly(own, axes, 0)
    return whole[: len(lines)].reshape(x.shape)


def over_copies(x, axis):
    return sent_to_all(x, axis).sum(axis=0)


def shards(counts, src_factor, dst_factor, hour_factor, core):
    highest = lax.Precision.HIGHEST
    src_devices = lax.axis_size("src")
    dst_devices = lax.axis_size("dst")
    hour_count = counts.shape[0]
    total_src = src_factor.shape[0] * src_devices
    total_dst = dst_factor.shape[0] * dst_devices
    core_hours = jnp.einsum("kr,rpq->kpq", hour_factor, core, precision=highest)
    partial_fit = jnp.einsum("ip,kpq->kiq", src_factor, core_hours, precision=highest)
    fitted = jnp.einsum("kiq,jq->kij", partial_fit, dst_factor, precision=highest)
    misfit = 1.0 - counts.astype(jnp.float32) / fitted
    dst_terms = jnp.einsum("kij,kiq->jq", misfit, partial_fit, precision=highest)
    through = jnp.einsum("kij,jq->kiq", misfit, dst_factor, precision=highest)
    dst_sum = nested_sum(dst_terms, "src")
    src_terms = jnp.einsum("kiq,kpq->ip", through, core_hours, precision=highest)
    src_sum = over_copies(src_terms, "dst")
    projected_terms = jnp.einsum("ip,kiq->kpq", src_factor, through, precision=highest)
    core_share = sent_and_summed(projected_terms, "src", 1)
    core_share = over_copies(core_share, "dst")
    share_rows = core_share.shape[1]
    core_rows = lax.dynamic_slice_in_dim(core, lax.axis_index("src") * share_rows, share_rows, 1)
    hour_terms = jnp.einsum("kpq,rpq->kr", core_share, core_rows, precision=highest)
    hour_sum = over_copies(hour_terms, "src")
    grad_src = src_sum / math.sqrt(total_dst * hour_count)
    grad_dst = dst_sum / math.sqrt(total_src * hour_count)
    grad_hour = hour_sum / math.sqrt(total_src * total_dst)
    grad_core = jnp.einsum("kr,kpq->rpq", hour_factor, core_share, precision=highest) / math.sqrt(
        total_src * total_dst * hour_count
    )
    return (grad_src, grad_dst, grad_hour, grad_core)


def solution(mesh):
    in_specs = (P(None, "src", "dst"), P("src", None), P("dst", None), P(), P())
    out_specs = (P("src", None), P("dst", None), P(), P(None, "src", None))
    return jax.shard_map(shards, mesh=mesh, in_specs=in_specs, out_specs=out_specs, check_vma=False)
```

profile of v0, /device:TPU:8, one launch (start us, length us, event | category | flops | bytes accessed | tf_op | source)
XLA Modules:
  0.0 159.5 jit_solution(12957600458927288346)
XLA Ops:
  0.6 3.8 %fusion.11 = f32[8,128,128]{2,0,1:T(8,128)S(1)} fusion(f32[8,32]{1,0:T(8,128)} %param.8, f32[32,128,128]{2,1,0:T(8,128)} %param.9), kind=kOutput, calls=%fused_computation.19 | convolution fusion | flops 50331648 | bytes 2622464 | tf_op jit(solution)/shard_map/kr,rpq->kpq/dot_general | solution.py:62
  4.5 1.9 %convolution_bitcast_fusion = f32[8,256,128]{1,2,0:T(8,128)S(1)} fusion(f32[8,128,128]{2,0,1:T(8,128)S(1)} %fusion.11, f32[256,128]{1,0:T(8,128)} %param.6), kind=kOutput, calls=%fused_computation.1 | convolution fusion | flops 402653184 | bytes 1703936 | tf_op jit(solution)/shard_map/ip,kpq->kiq/dot_general | solution.py:63
  6.4 10.6 %divide_subtract_fusion = f32[8,256,1024]{2,1,0:T(8,128)S(1)} fusion(s32[8,256,1024]{2,1,0:T(8,128)} %param.5, f32[8,256,128]{1,2,0:T(8,128)S(1)} %convolution_bitcast_fusion, f32[1024,128]{1,0:T(8,128)S(1)} %copy-done), kind=kOutput, calls=%fused_computation | convolution fusion | flops 3227516928 | bytes 18350080 | tf_op jit(solution)/shard_map/kiq,jq->kij/dot_general | solution.py:64
  17.1 3.2 %copy-done.1 = f32[8,256,1024]{2,1,0:T(8,128)} copy-done((f32[8,256,1024]{2,1,0:T(8,128)}, f32[8,256,1024]{2,1,0:T(8,128)S(1)}, u32[]{:S(2)}) %copy-start.1) | copy-done | bytes 8388632
  20.3 6.8 %fusion.1 = f32[8,256,128]{2,1,0:T(8,128)S(1)} fusion(f32[8,256,1024]{2,1,0:T(8,128)S(1)} %divide_subtract_fusion, f32[1024,128]{1,0:T(8,128)S(1)} %copy-done), kind=kOutput, calls=%fused_computation.6 | convolution fusion | flops 3221225472 | bytes 9961472 | tf_op jit(solution)/shard_map/kij,jq->kiq/dot_general | solution.py:67
  27.8 0.9 copy.61
  28.8 11.5 %all-to-all-start.3 = ((f32[32,8,4,128]{3,2,1,0:T(4,128)}), f32[32,8,4,128]{3,2,1,0:T(4,128)S(1)}, u32[]{:S(2)}, u32[]{:S(2)}) async-start(f32[32,8,4,128]{3,2,1,0:T(4,128)} %bitcast.41), calls=%async_computation.3 | async-start | bytes 1048576 | tf_op jit(solution)/shard_map/all_to_all | solution.py:17
  40.3 1.0 convolution_bitcast_fusion.1
  41.3 16.7 %all-to-all-done.3 = f32[32,8,4,128]{3,2,1,0:T(4,128)S(1)} async-done(((f32[32,8,4,128]{3,2,1,0:T(4,128)}), f32[32,8,4,128]{3,2,1,0:T(4,128)S(1)}, u32[]{:S(2)}, u32[]{:S(2)}) %all-to-all-start.3) | async-done | bytes 524320 | tf_op jit(solution)/shard_map/all_to_all | solution.py:17
  58.0 1.0 broadcast_in_dim.12
  59.1 4.9 %all-to-all-start = ((f32[8,256,128]{2,1,0:T(8,128)}), f32[8,256,128]{2,1,0:T(8,128)}, u32[]{:S(2)}, u32[]{:S(2)}) async-start(f32[8,256,128]{2,1,0:T(8,128)} %broadcast_in_dim.12), calls=%async_computation | async-start | bytes 2097152 | tf_op jit(solution)/shard_map/all_to_all | solution.py:30
  64.1 14.5 %all-to-all-done = f32[8,256,128]{2,1,0:T(8,128)} async-done(((f32[8,256,128]{2,1,0:T(8,128)}), f32[8,256,128]{2,1,0:T(8,128)}, u32[]{:S(2)}, u32[]{:S(2)}) %all-to-all-start) | async-done | bytes 1048608 | tf_op jit(solution)/shard_map/all_to_all | solution.py:30
  79.2 4.7 %all-to-all-start.4 = ((f32[8,8,4,128]{3,1,2,0:T(8,128)}), f32[8,8,4,128]{3,1,2,0:T(8,128)S(1)}, u32[]{:S(2)}, u32[]{:S(2)}) async-start(f32[8,8,4,128]{3,1,2,0:T(8,128)} %broadcast_in_dim.14), calls=%async_computation.4 | async-start | bytes 262144 | tf_op jit(solution)/shard_map/all_to_all | solution.py:30
  84.0 16.5 %fusion.15 = f32[1024,128,1]{1,0,2:T(8,128)} fusion(f32[8,256,1024]{2,1,0:T(8,128)} %copy-done.1, f32[8,256,128]{1,2,0:T(8,128)} %copy-done.3), kind=kOutput, calls=%fused_computation.24 | convolution fusion | flops 3221225472 | bytes 9961472 | tf_op jit(solution)/shard_map/kij,kiq->jq/dot_general | solution.py:66
  100.5 4.7 %all-to-all-start.1 = ((f32[32,32,128]{2,1,0:T(8,128)}), f32[32,32,128]{2,1,0:T(8,128)S(1)}, u32[]{:S(2)}, u32[]{:S(2)}) async-start(f32[32,32,128]{2,1,0:T(8,128)} %bitcast.6), calls=%async_computation.1 | async-start | bytes 1048576 | tf_op jit(solution)/shard_map/all_to_all | solution.py:17
  105.2 2.6 %copy.38 = f32[32,128,128]{2,0,1:T(8,128)} copy(f32[32,128,128]{2,1,0:T(8,128)S(1)} %copy-done.2) | data formatting | bytes 4194304 | tf_op args[4]
  107.8 1.0 convolution_bitcast_fusion.2
  109.6 13.8 %all-to-all-done.1 = f32[32,32,128]{2,1,0:T(8,128)S(1)} async-done(((f32[32,32,128]{2,1,0:T(8,128)}), f32[32,32,128]{2,1,0:T(8,128)S(1)}, u32[]{:S(2)}, u32[]{:S(2)}) %all-to-all-start.1) | async-done | bytes 524320 | tf_op jit(solution)/shard_map/all_to_all | solution.py:17
  123.3 4.6 %all-to-all-start.5 = ((f32[32,1,256]{2,1,0:T(1,128)}), f32[32,1,256]{2,1,0:T(1,128)S(1)}, u32[]{:S(2)}, u32[]{:S(2)}) async-start(f32[32,1,256]{2,1,0:T(1,128)} %reshape.26), calls=%async_computation.5 | async-start | bytes 65536 | tf_op jit(solution)/shard_map/all_to_all | solution.py:30
  128.0 9.7 %all-to-all-done.5 = f32[32,1,256]{2,1,0:T(1,128)S(1)} async-done(((f32[32,1,256]{2,1,0:T(1,128)}), f32[32,1,256]{2,1,0:T(1,128)S(1)}, u32[]{:S(2)}, u32[]{:S(2)}) %all-to-all-start.5) | async-done | bytes 32800 | tf_op jit(solution)/shard_map/all_to_all | solution.py:30
  137.7 0.9 broadcast_in_dim.13
  138.6 3.9 %all-to-all-start.2 = ((f32[32,32,128]{2,1,0:T(8,128)}), f32[32,32,128]{2,1,0:T(8,128)S(1)}, u32[]{:S(2)}, u32[]{:S(2)}) async-start(f32[32,32,128]{2,1,0:T(8,128)} %broadcast_in_dim.13), calls=%async_computation.2 | async-start | bytes 1048576 | tf_op jit(solution)/shard_map/all_to_all | solution.py:30
  142.5 1.3 reduce_sum.45
  147.3 11.3 %all-to-all-done.2 = f32[32,32,128]{2,1,0:T(8,128)S(1)} async-done(((f32[32,32,128]{2,1,0:T(8,128)}), f32[32,32,128]{2,1,0:T(8,128)S(1)}, u32[]{:S(2)}, u32[]{:S(2)}) %all-to-all-start.2) | async-done | bytes 524320 | tf_op jit(solution)/shard_map/all_to_all | solution.py:30
  (29 shorter events, 6.8 us)
Async XLA Ops:
  0.6 5.8 %copy-start = (f32[1024,128]{1,0:T(8,128)S(1)}, f32[1024,128]{1,0:T(8,128)}, u32[]{:S(2)}) copy-start(f32[1024,128]{1,0:T(8,128)} %param.7) | copy-start | bytes 1572868
  6.4 10.6 %copy-start.3 = (f32[8,256,128]{1,2,0:T(8,128)}, f32[8,256,128]{1,2,0:T(8,128)S(1)}, u32[]{:S(2)}) copy-start(f32[8,256,128]{1,2,0:T(8,128)S(1)} %convolution_bitcast_fusion) | copy-start | bytes 3145732
  17.1 3.2 %copy-start.1 = (f32[8,256,1024]{2,1,0:T(8,128)}, f32[8,256,1024]{2,1,0:T(8,128)S(1)}, u32[]{:S(2)}) copy-start(f32[8,256,1024]{2,1,0:T(8,128)S(1)} %divide_subtract_fusion) | copy-start | bytes 25165828
  20.3 6.8 %copy-start.4 = (f32[256,128]{1,0:T(8,128)S(1)}, f32[256,128]{1,0:T(8,128)}, u32[]{:S(2)}) copy-start(f32[256,128]{1,0:T(8,128)} %param.6) | copy-start | bytes 393220
  28.8 29.3 %all-to-all-start.3 = ((f32[32,8,4,128]{3,2,1,0:T(4,128)}), f32[32,8,4,128]{3,2,1,0:T(4,128)S(1)}, u32[]{:S(2)}, u32[]{:S(2)}) async-start(f32[32,8,4,128]{3,2,1,0:T(4,128)} %bitcast.41), calls=%async_computation.3 | async-start | bytes 1048576 | tf_op jit(solution)/shard_map/all_to_all | solution.py:17
  59.1 19.5 %all-to-all-start = ((f32[8,256,128]{2,1,0:T(8,128)}), f32[8,256,128]{2,1,0:T(8,128)}, u32[]{:S(2)}, u32[]{:S(2)}) async-start(f32[8,256,128]{2,1,0:T(8,128)} %broadcast_in_dim.12), calls=%async_computation | async-start | bytes 2097152 | tf_op jit(solution)/shard_map/all_to_all | solution.py:30
  64.0 41.3 %copy-start.2 = (f32[32,128,128]{2,1,0:T(8,128)S(1)}, f32[32,128,128]{2,1,0:T(8,128)}, u32[]{:S(2)}) copy-start(f32[32,128,128]{2,1,0:T(8,128)} %param.9) | copy-start | bytes 6291460
  79.2 21.3 %all-to-all-start.4 = ((f32[8,8,4,128]{3,1,2,0:T(8,128)}), f32[8,8,4,128]{3,1,2,0:T(8,128)S(1)}, u32[]{:S(2)}, u32[]{:S(2)}) async-start(f32[8,8,4,128]{3,1,2,0:T(8,128)} %broadcast_in_dim.14), calls=%async_computation.4 | async-start | bytes 262144 | tf_op jit(solution)/shard_map/all_to_all | solution.py:30
  84.0 60.5 %copy-start.5 = (f32[8,32]{1,0:T(8,128)S(1)}, f32[8,32]{1,0:T(8,128)}, u32[]{:S(2)}) copy-start(f32[8,32]{1,0:T(8,128)} %param.8) | copy-start | bytes 3076
  100.5 22.8 %all-to-all-start.1 = ((f32[32,32,128]{2,1,0:T(8,128)}), f32[32,32,128]{2,1,0:T(8,128)S(1)}, u32[]{:S(2)}, u32[]{:S(2)}) async-start(f32[32,32,128]{2,1,0:T(8,128)} %bitcast.6), calls=%async_computation.1 | async-start | bytes 1048576 | tf_op jit(solution)/shard_map/all_to_all | solution.py:17
  123.3 14.4 %all-to-all-start.5 = ((f32[32,1,256]{2,1,0:T(1,128)}), f32[32,1,256]{2,1,0:T(1,128)S(1)}, u32[]{:S(2)}, u32[]{:S(2)}) async-start(f32[32,1,256]{2,1,0:T(1,128)} %reshape.26), calls=%async_computation.5 | async-start | bytes 65536 | tf_op jit(solution)/shard_map/all_to_all | solution.py:30
  138.6 20.1 %all-to-all-start.2 = ((f32[32,32,128]{2,1,0:T(8,128)}), f32[32,32,128]{2,1,0:T(8,128)S(1)}, u32[]{:S(2)}, u32[]{:S(2)}) async-start(f32[32,32,128]{2,1,0:T(8,128)} %broadcast_in_dim.13), calls=%async_computation.2 | async-start | bytes 1048576 | tf_op jit(solution)/shard_map/all_to_all | solution.py:30
where the time goes:
time: 160 us; the launch traced here: 159 us
  waiting for transfers between devices  66 us (41%)
  matrix products  42.6 us (27%)
  starting transfers between devices  34.3 us (21%)
  local copies, waits for them, and re-layouts  11.3 us (7%)
  other arithmetic  4.31 us (3%)
    all_to_all x4, waiting for transfers between devices, sent_to_all(): return lax.all_to_all(copies, axis, split_axis=0, concat_axis=0, tiled=True)  35.5 us
    all_to_all x2, waiting for transfers between devices, sent_and_summed(): lax.all_to_all(tiles, axis, split_axis=0, concat_axis=0, tiled=True)  30.5 us
    all_to_all x4, starting transfers between devices, sent_to_all(): return lax.all_to_all(copies, axis, split_axis=0, concat_axis=0, tiled=True)  18.1 us
    dot_general x1, matrix products, shards(): jnp.einsum('kij,kiq->jq', misfit, partial_fit, precision=highest)  16.5 us
    all_to_all x2, starting transfers between devices, sent_and_summed(): lax.all_to_all(tiles, axis, split_axis=0, concat_axis=0, tiled=True)  16.2 us
    dot_general x1, matrix products, shards(): jnp.einsum('kiq,jq->kij', partial_fit, dst_factor, precision=highest)  10.6 us
    unnamed x16, local copies, waits for them, and re-layouts  7.29 us
    dot_general x1, matrix products, shards(): through = jnp.einsum('kij,jq->kiq', misfit, dst_factor, precision=highest)  6.77 us
  transfers between devices with their start and end apart: 6, of which 5 were waited for; matrix products, arithmetic and copies ran while one was open for 17% of the time, Pallas kernels for 0%

commit v1 on v0

v1 whole, which is shorter than its diff:
```python
import functools
import math

import jax
import jax.numpy as jnp
from jax import lax
from jax.experimental import pallas as pl
from jax.experimental.pallas import tpu as pltpu
from jax.sharding import Mesh, PartitionSpec as P

X = 4
CORES = 2
F32 = jnp.float32
BF16 = jnp.bfloat16


def split(x):
    hi = x.astype(BF16)
    return hi, (x - hi.astype(F32)).astype(BF16)


def mm(a, b):
    return jnp.dot(a, b, preferred_element_type=F32)


def halves(x, axis):
    hi, lo = split(x)
    return jnp.concatenate([hi, lo], axis=axis)


def quarters(x):
    row = halves(x, 1)
    return jnp.concatenate([row, row], axis=0)


def vmem(*shape):
    return pl.BlockSpec(shape, lambda *_: (0,) * len(shape))


def main_kernel(hour_ref, counts_ref, src_ref, dst_ref, core_ref,
                a0, a1, a2, a3, own, send,
                dst_cols, dst_rows, src_cols, src_rows, dst_sum, src_sum):
    k = pl.program_id(0)
    last = pl.num_programs(0) - 1
    hours = pl.num_programs(0)
    x, y, c = lax.axis_index("x"), lax.axis_index("y"), lax.axis_index("core")
    rank = core_ref.shape[0]
    rows, cols = counts_ref.shape[1], counts_ref.shape[2]
    p1, q1 = core_ref.shape[1], core_ref.shape[2]
    y_count = own.shape[0]

    @pl.when(k == 0)
    def _():
        dst = dst_ref[...]
        dst_rows[...] = halves(dst, 1)
        turned = dst.T
        hi, lo = split(turned)
        dst_cols[...] = jnp.concatenate([hi, hi, lo, lo], axis=0)
        src = src_ref[...]
        src_rows[...] = halves(src, 1)
        src_cols[...] = halves(src.T, 0)
        dst_sum[...] = jnp.zeros_like(dst_sum)
        src_sum[...] = jnp.zeros_like(src_sum)

    core_hour = hour_ref[k, 0] * core_ref[0]
    for r in range(1, rank):
        core_hour = core_hour + hour_ref[k, r] * core_ref[r]

    both = mm(src_rows[...], quarters(core_hour))
    fit = both[:, :q1] + both[:, q1:]
    fit_rows = halves(fit, 1)
    fit_rows = jnp.concatenate([fit_rows, fit_rows], axis=1)
    fit_cols = halves(fit.T, 0)

    through = jnp.zeros((rows, q1), F32)
    step = 256
    for j in range(0, cols, step):
        fitted = mm(fit_rows, dst_cols[:, j:j + step])
        misfit = 1.0 - counts_ref[0, :, j:j + step].astype(F32) / fitted
        hi, lo = split(misfit)
        both = mm(jnp.concatenate([hi, lo], axis=0), dst_rows[j:j + step, :])
        both = both[:rows] + both[rows:]
        through = through + (both[:, :q1] + both[:, q1:])
        first = mm(fit_cols, hi)
        second = mm(fit_cols[:q1], lo)
        dst_sum[:, j:j + step] += first[:q1] + (first[q1:] + second)

    turned = core_hour.T
    th = halves(through, 1)
    both = mm(th, quarters(turned))
    src_sum[...] += both[:, :p1] + both[:, p1:]
    both = mm(src_cols[...], th)
    both = both[:p1] + both[p1:]
    projected = both[:, :q1] + both[:, q1:]
    slot = lax.rem(k // CORES - y + y_count, y_count)

    @pl.when(lax.rem(k, CORES) == c)
    def _():
        own[slot, :p1, :] = projected

    @pl.when(lax.rem(k, CORES) != c)
    def _():
        send[slot, :p1, :] = projected

    @pl.when(k == last)
    def _():
        turned = dst_sum[...].T
        dst_rows_out = turned
        block = cols // X
        share = rows // hours
        for s, out in enumerate((a0, a1, a2, a3)):
            place = lax.rem(x + s, X)
            for b in range(X):
                @pl.when(place == b)
                def _():
                    out[...] = dst_rows_out[b * block:(b + 1) * block]
        for s in range(y_count):
            other = lax.rem(y + s, y_count) * CORES
            own[s, p1:, :] = src_sum[pl.ds(pl.multiple_of((other + c) * share, share), share), :]
            send[s, p1:, :] = src_sum[pl.ds(pl.multiple_of((other + 1 - c) * share, share), share), :]


def main_call(counts, src, dst, hour, core):
    hours, rows, cols = counts.shape
    p1, q1 = core.shape[1:]
    block = cols // X
    share = rows // hours
    ys = hours // CORES
    out = [jax.ShapeDtypeStruct((block, q1), F32)] * X + [jax.ShapeDtypeStruct((ys, p1 + share, q1), F32)] * 2
    flops = 2 * 6 * hours * rows * cols * q1
    return pl.pallas_call(
        main_kernel,
        out_shape=out,
        grid=(hours,),
        in_specs=[
            pl.BlockSpec(memory_space=pltpu.SMEM),
            pl.BlockSpec((1, rows, cols), lambda k: (k, 0, 0)),
            vmem(rows, p1), vmem(cols, q1), vmem(*core.shape),
        ],
        out_specs=[vmem(block, q1)] * X + [vmem(ys, p1 + share, q1)] * 2,
        scratch_shapes=[
            pltpu.VMEM((4 * q1, cols), BF16),
            pltpu.VMEM((cols, 2 * q1), BF16),
            pltpu.VMEM((2 * p1, rows), BF16),
            pltpu.VMEM((rows, 2 * p1), BF16),
            pltpu.VMEM((q1, cols), F32),
            pltpu.VMEM((rows, p1), F32),
        ],
        compiler_params=pltpu.CompilerParams(vmem_limit_bytes=40 << 20),
        cost_estimate=pl.CostEstimate(flops=flops, bytes_accessed=12 << 20, transcendentals=0),
        name="gradient_terms",
    )(hour, counts, src, dst, core)


def add_kernel(own, came, *outs):
    for s, out in enumerate(outs):
        out[...] = own[s] + came[s]


def add_call(own, came):
    shape = own.shape[1:]
    return pl.pallas_call(
        add_kernel,
        out_shape=[jax.ShapeDtypeStruct(shape, F32)] * own.shape[0],
        name="core_sum",
    )(own, came)


def share_kernel(t0, r1, r2, r3, core_ref, m0, m1, m2, m3, src_out):
    x = lax.axis_index("x")
    total = (t0[...] + r1[...]) + (r2[...] + r3[...])
    p1 = core_ref.shape[1]
    rank = core_ref.shape[0]
    src_out[...] = total[p1:]
    projected = total[:p1]
    lanes = lax.broadcasted_iota(jnp.int32, (8, 128), 1)
    hour = jnp.zeros((8, 128), F32)
    for r in range(rank):
        prod = projected * core_ref[r]
        part = jnp.sum(prod, axis=0, keepdims=True)
        value = jnp.sum(part, axis=1, keepdims=True)
        hour = jnp.where(lanes == r, value, hour)
    tiles = projected.reshape(p1 // 16, X, 4, 128)
    for s, out in enumerate((m0, m1, m2, m3)):
        place = lax.rem(x + s, X)
        for b in range(X):
            @pl.when(place == b)
            def _():
                for z in range(p1 // 16):
                    out[4 * z:4 * z + 4, :] = tiles[z, b]
        out[p1 // 4:, :] = hour


def share_call(t0, r1, r2, r3, core):
    rows, q1 = t0.shape
    p1 = core.shape[1]
    out = [jax.ShapeDtypeStruct((p1 // 4 + 8, q1), F32)] * X + [jax.ShapeDtypeStruct((rows - p1, q1), F32)]
    return pl.pallas_call(share_kernel, out_shape=out, name="hour_terms")(t0, r1, r2, r3, core)


def z_kernel(a_ref, m0, m1, m2, m3, out):
    zs, share, _ = a_ref.shape
    total = jnp.sum(a_ref[...], axis=0)
    m = (m0[...] + m1[...]) + (m2[...] + m3[...])
    for z in range(zs):
        out[z, :share, :] = total
        out[z, share:share + 4, :] = m[4 * z:4 * z + 4]
        out[z, share + 4:, :] = m[4 * zs:4 * zs + 4]


def z_call(a, m):
    zs, share, q1 = a.shape
    return pl.pallas_call(
        z_kernel, out_shape=jax.ShapeDtypeStruct((zs, share + 8, q1), F32), name="z_terms",
    )(a, *m)


def back_kernel(w, src_part, block, rest):
    zs, rows, _ = w.shape
    share = rows - 8
    tail = w[0, share:, :]
    block[:share, :] = w[0, :share, :]
    for z in range(1, zs):
        block[z * share:(z + 1) * share, :] = w[z, :share, :]
        tail = tail + w[z, share:, :]
    rest[:8, :] = tail
    rest[8:, :] = src_part[...]


def back_call(w, src_part):
    zs, rows, q1 = w.shape
    return pl.pallas_call(
        back_kernel,
        out_shape=[jax.ShapeDtypeStruct((zs * (rows - 8), q1), F32),
                   jax.ShapeDtypeStruct((src_part.shape[0] + 8, q1), F32)],
        name="z_sums",
    )(w, src_part)


def pair_kernel(own, other, out):
    c = lax.axis_index("core")
    out[c] = own[...]
    out[1 - c] = other[...]


def pair_call(own, other):
    return pl.pallas_call(
        pair_kernel, out_shape=jax.ShapeDtypeStruct((2, *own.shape), F32), name="core_pair",
    )(own, other)


def end_kernel(scales, hour_ref, b0, b1, b2, b3, d0, d1, d2, d3, src_out, dst_out, hour_out, core_out, shares):
    x, y = lax.axis_index("x"), lax.axis_index("y")
    src_scale, dst_scale, hour_scale, core_scale = scales
    for s, block in enumerate((b0, b1, b2, b3)):
        dst_out[lax.rem(x - s + X, X)] = block[...] * dst_scale
    for s, pair in enumerate((d0, d1, d2, d3)):
        spot = lax.rem(y - s + 4, 4)
        for c in range(CORES):
            at = spot * CORES + c
            shares[at] = pair[c, :8, :]
            src_out[at] = pair[c, 8:, :] * src_scale
    hours, rank = hour_ref.shape
    for k in range(hours):
        hour_out[k:k + 1, :] = shares[k, 4:5, :rank] * hour_scale
    tiles = [shares[k, :4, :] * core_scale for k in range(hours)]
    for r in range(rank):
        total = hour_ref[0, r] * tiles[0]
        for k in range(1, hours):
            total = total + hour_ref[k, r] * tiles[k]
        core_out[r] = total


def end_call(scales, hour, blocks, pairs):
    block, q1 = blocks[0].shape
    share = pairs[0].shape[1] - 8
    hours, rank = hour.shape
    whole = pl.BlockSpec(memory_space=pltpu.VMEM)
    return pl.pallas_call(
        functools.partial(end_kernel, scales),
        in_specs=[pl.BlockSpec(memory_space=pltpu.SMEM)] + [whole] * 8,
        out_specs=[whole] * 4,
        out_shape=[jax.ShapeDtypeStruct((hours, share, q1), F32),
                   jax.ShapeDtypeStruct((X, block, q1), F32),
                   jax.ShapeDtypeStruct((hours, rank), F32),
                   jax.ShapeDtypeStruct((rank, 4, q1), F32)],
        scratch_shapes=[pltpu.VMEM((hours, 8, q1), F32)],
        name="outputs",
    )(hour, *blocks, *pairs)


def shifted(x, axis, s):
    n = lax.axis_size(axis)
    return lax.ppermute(x, axis, [(i, (i + s) % n) for i in range(n)])


def swapped(x, axis):
    n = lax.axis_size(axis)
    return lax.all_to_all(x, axis, split_axis=0, concat_axis=0, tiled=True)


def shards(scales, counts, src_factor, dst_factor, hour_factor, core):
    z_count = lax.axis_size("z")
    a0, a1, a2, a3, own, send = main_call(counts, src_factor, dst_factor, hour_factor, core)
    came = [shifted(a, "x", s) for s, a in ((1, a1), (2, a2), (3, a3))]
    other = shifted(send, "core", 1)
    parts = add_call(own, other)
    y_came = [shifted(parts[s], "y", s) for s in (1, 2, 3)]
    a = (a0 + came[0]) + (came[1] + came[2])
    a = swapped(a.reshape(z_count, -1, a.shape[-1]), "z")
    m0, m1, m2, m3, src_part = share_call(parts[0], *y_came, core)
    m = [m0] + [shifted(v, "x", s) for s, v in ((1, m1), (2, m2), (3, m3))]
    w = swapped(z_call(a, m), "z")
    block, rest = back_call(w, src_part)
    pair = pair_call(rest, shifted(rest, "core", 1))
    blocks = [block] + [shifted(block, "x", s) for s in (1, 2, 3)]
    pairs = [pair] + [shifted(pair, "y", s) for s in (1, 2, 3)]
    grad_src, grad_dst, grad_hour, grad_core = end_call(scales, hour_factor, blocks, pairs)
    return (grad_src.reshape(src_factor.shape), grad_dst.reshape(dst_factor.shape), grad_hour, grad_core)


def solution(mesh):
    n_src, n_dst = mesh.shape["src"], mesh.shape["dst"]
    fine = Mesh(mesh.devices.reshape(n_src // X, X, n_dst // CORES, CORES), ("z", "x", "y", "core"))
    src, dst = ("z", "x"), ("y", "core")
    in_specs = (P(None, src, dst), P(src, None), P(dst, None), P(), P())
    out_specs = (P(src, None), P(dst, None), P(), P(None, src, None))

    def run(counts, src_factor, dst_factor, hour_factor, core):
        hours, total_src, total_dst = counts.shape
        scales = (1 / math.sqrt(total_dst * hours), 1 / math.sqrt(total_src * hours),
                  1 / math.sqrt(total_src * total_dst), 1 / math.sqrt(total_src * total_dst * hours))
        body = jax.shard_map(functools.partial(shards, scales), mesh=fine, in_specs=in_specs,
                             out_specs=out_specs, check_vma=False)
        return body(counts, src_factor, dst_factor, hour_factor, core)

    return run
```

time: 160 us -> 112 us (0.70)
  the two profiles are of different devices: /device:TPU:8 before, /device:TPU:2 now
where the time goes in v1:
time: 112 us; the launch traced here: 111 us
  starting transfers between devices  31.7 us (28%)
  Pallas kernels  28.3 us (25%)
  waiting for transfers between devices  20.6 us (18%)
  blocking collectives  16.7 us (15%)
  local copies, waits for them, and re-layouts  12.2 us (11%)
    ppermute x17, starting transfers between devices, shifted(): return lax.ppermute(x, axis, [(i, (i + s) % n) for i in range(n)])  23.3 us
    ppermute x17, waiting for transfers between devices, shifted(): return lax.ppermute(x, axis, [(i, (i + s) % n) for i in range(n)])  20.6 us
    pallas_call x1, Pallas kernels, main_call(): pl.pallas_call(main_kernel, out_shape=out, grid=(hours,), in_specs=[pl.Bl...  17.2 us
    all_to_all x1, blocking collectives, swapped(): return lax.all_to_all(x, axis, split_axis=0, concat_axis=0, tiled=True)  16.7 us
    unnamed x42, local copies, waits for them, and re-layouts  12.2 us
    all_to_all x1, starting transfers between devices, swapped(): return lax.all_to_all(x, axis, split_axis=0, concat_axis=0, tiled=True)  8.48 us
    pallas_call x1, Pallas kernels, share_call(): pl.pallas_call(share_kernel, out_shape=out, name='hour_terms')  2.7 us
  transfers between devices with their start and end apart: 18, of which 12 were waited for; matrix products, arithmetic and copies ran while one was open for 1% of the time, Pallas kernels for 5%

profile of v1, /device:TPU:2, one launch (start us, length us, event | category | flops | bytes accessed | tf_op | source)
XLA Modules:
  0.0 111.1 jit_solution(4504778810457267030)
XLA Ops:
  0.6 1.6 %copy-done = f32[32,128,128]{2,1,0:T(8,128)S(1)} copy-done((f32[32,128,128]{2,1,0:T(8,128)S(1)}, f32[32,128,128]{2,1,0:T(8,128)}, u32[]{:S(2)}) %copy-start) | copy-done | bytes 2097176
  2.9 3.4 %copy-done.3 = s32[8,256,1024]{2,1,0:T(8,128)S(1)} copy-done((s32[8,256,1024]{2,1,0:T(8,128)S(1)}, s32[8,256,1024]{2,1,0:T(8,128)}, u32[]{:S(2)}) %copy-start.3) | copy-done | bytes 8388632
  8.2 17.2 %gradient_terms.1 = (f32[256,128]{1,0:T(8,128)S(1)}, f32[256,128]{1,0:T(8,128)S(1)}, f32[256,128]{1,0:T(8,128)S(1)}, f32[256,128]{1,0:T(8,128)S(1)}, f32[4,160,1...) custom-call(f32[8,32]{1,0:T(8,128)S(1)} %copy-done.2, s32[8,256,1024]{2,1,0:T(8,128)S(1)} %copy-done.3, ...), custom_call_target="tpu_custom_call" | custom-call | flops 3221225472 | bytes 12582912 | tf_op jit(solution)/shard_map/gradient_terms/pallas_call | solution.py:131
  26.1 1.5 %collective-permute-start = (f32[256,128]{1,0:T(8,128)S(1)}, f32[256,128]{1,0:T(8,128)S(1)}, u32[]{:S(2)}, u32[]{:S(2)}) collective-permute-start(f32[256,128]{1,0:T(8,128)S(1)} %get-tuple-element.26), channel_id=1, source_target_pairs={{0,8},{8,16},{16,24},{24,0},{1,9},{9,17},{17,25},{25,1},{2,10},{10... | collective-permute-start | bytes 393224 | tf_op jit(solution)/shard_map/ppermute | solution.py:294
  27.6 2.8 %collective-permute-start.1 = (f32[256,128]{1,0:T(8,128)S(1)}, f32[256,128]{1,0:T(8,128)S(1)}, u32[]{:S(2)}, u32[]{:S(2)}) collective-permute-start(f32[256,128]{1,0:T(8,128)S(1)} %get-tuple-element.27), channel_id=1, source_target_pairs={{0,16},{8,24},{16,0},{24,8},{1,17},{9,25},{17,1},{25,9},{2,18},{10... | collective-permute-start | bytes 393224 | tf_op jit(solution)/shard_map/ppermute | solution.py:294
  31.7 3.8 %collective-permute-done.1 = f32[256,128]{1,0:T(8,128)S(1)} collective-permute-done((f32[256,128]{1,0:T(8,128)S(1)}, f32[256,128]{1,0:T(8,128)S(1)}, u32[]{:S(2)}, u32[]{:S(2)}) %collective-permute-start.1) | collective-permute-done | bytes 131104 | tf_op jit(solution)/shard_map/ppermute | solution.py:294
  36.9 8.5 %all-to-all-start = ((f32[8,32,128]{2,1,0:T(8,128)}), f32[8,32,128]{2,1,0:T(8,128)S(1)}, u32[]{:S(2)}, u32[]{:S(2)}) async-start(f32[8,32,128]{2,1,0:T(8,128)} %bitcast), calls=%async_computation | async-start | bytes 262144 | tf_op jit(solution)/shard_map/all_to_all | solution.py:299
  46.1 1.8 %core_sum.1 = (f32[160,128]{1,0:T(8,128)}, f32[160,128]{1,0:T(8,128)}, f32[160,128]{1,0:T(8,128)}, f32[160,128]{1,0:T(8,128)}) custom-call(f32[4,160,128]{2,1,0:T(8,128)} %copy-done.1, f32[4,160,128]{2,1,0:T(8,128)} %copy-done.7), custom_call_target="tpu_custom_call" | custom-call | tf_op jit(solution)/shard_map/core_sum/pallas_call | solution.py:162
  47.9 1.6 %collective-permute-start.4 = (f32[160,128]{1,0:T(8,128)}, f32[160,128]{1,0:T(8,128)S(1)}, u32[]{:S(2)}, u32[]{:S(2)}) collective-permute-start(f32[160,128]{1,0:T(8,128)} %get-tuple-element.32), channel_id=1, source_target_pairs={{0,2},{2,4},{4,6},{6,0},{1,3},{3,5},{5,7},{7,1},{8,10},{10,12},{12... | collective-permute-start | bytes 245768 | tf_op jit(solution)/shard_map/ppermute | solution.py:294
  49.5 2.9 %collective-permute-start.5 = (f32[160,128]{1,0:T(8,128)}, f32[160,128]{1,0:T(8,128)S(1)}, u32[]{:S(2)}, u32[]{:S(2)}) collective-permute-start(f32[160,128]{1,0:T(8,128)} %get-tuple-element.33), channel_id=1, source_target_pairs={{0,4},{2,6},{4,0},{6,2},{1,5},{3,7},{5,1},{7,3},{8,12},{10,14},{12... | collective-permute-start | bytes 245768 | tf_op jit(solution)/shard_map/ppermute | solution.py:294
  57.7 2.7 %hour_terms.1 = (f32[40,128]{1,0:T(8,128)}, f32[40,128]{1,0:T(8,128)}, f32[40,128]{1,0:T(8,128)}, f32[40,128]{1,0:T(8,128)}, f32[32,128]{1,0:T(8,128)}) custom-call(f32[160,128]{1,0:T(8,128)} %get-tuple-element.31.t0, f32[160,128]{1,0:T(8,128)} %copy-done.11, f32[160,128]{1,0:T(8,128)} %copy-done.12, f32[160,128]{1,0:T(8,128)} %copy-done.13, ...), custom_call_target="tpu_custom_call" | custom-call | tf_op jit(solution)/shard_map/hour_terms/pallas_call | solution.py:198
  61.7 1.5 %collective-permute-start.8 = (f32[40,128]{1,0:T(8,128)}, f32[40,128]{1,0:T(8,128)S(1)}, u32[]{:S(2)}, u32[]{:S(2)}) collective-permute-start(f32[40,128]{1,0:T(8,128)} %get-tuple-element.37), channel_id=1, source_target_pairs={{0,16},{8,24},{16,0},{24,8},{1,17},{9,25},{17,1},{25,9},{2,18},{10... | collective-permute-start | bytes 61448 | tf_op jit(solution)/shard_map/ppermute | solution.py:294
  63.2 1.7 %collective-permute-start.9 = (f32[40,128]{1,0:T(8,128)}, f32[40,128]{1,0:T(8,128)S(1)}, u32[]{:S(2)}, u32[]{:S(2)}) collective-permute-start(f32[40,128]{1,0:T(8,128)} %get-tuple-element.38), channel_id=1, source_target_pairs={{0,24},{8,0},{16,8},{24,16},{1,25},{9,1},{17,9},{25,17},{2,26},{10... | collective-permute-start | bytes 61448 | tf_op jit(solution)/shard_map/ppermute | solution.py:294
  64.9 2.4 %collective-permute-done.8.m2 = f32[40,128]{1,0:T(8,128)S(1)} collective-permute-done((f32[40,128]{1,0:T(8,128)}, f32[40,128]{1,0:T(8,128)S(1)}, u32[]{:S(2)}, u32[]{:S(2)}) %collective-permute-start.8) | collective-permute-done | bytes 20512 | tf_op jit(solution)/shard_map/ppermute | solution.py:294
  68.0 1.6 %z_terms.1 = f32[8,40,128]{2,1,0:T(8,128)} custom-call(f32[8,32,128]{2,1,0:T(8,128)} %copy-done.6, f32[40,128]{1,0:T(8,128)} %get-tuple-element.35.m0, f32[40,128]{1,0:T(8,128)} %copy-done.17, f32[40,128]{1,0:T(8,128)} %copy-done.18, f32[40,128]{1,0:T(8,128)} %copy-done.19), custom_call_target="tpu_custom_call" | custom-call | tf_op jit(solution)/shard_map/z_terms/pallas_call | solution.py:213
  69.6 16.7 %all_to_all.10.w = f32[8,40,128]{2,1,0:T(8,128)} all-to-all(f32[8,40,128]{2,1,0:T(8,128)} %z_terms.1), channel_id=1, replica_groups=mesh['z'=8,'x'=4,'y'=4,'core'=2] {'z'}, dimensions={0} | all-to-all | bytes 327680 | tf_op jit(solution)/shard_map/all_to_all | solution.py:299
  86.3 1.6 %z_sums.1 = (f32[256,128]{1,0:T(8,128)}, f32[40,128]{1,0:T(8,128)}) custom-call(f32[8,40,128]{2,1,0:T(8,128)} %all_to_all.10.w, f32[32,128]{1,0:T(8,128)} %get-tuple-element.39.src_part), custom_call_target="tpu_custom_call" | custom-call | tf_op jit(solution)/shard_map/z_sums/pallas_call | solution.py:232
  89.4 1.6 %collective-permute-start.11 = (f32[256,128]{1,0:T(8,128)}, f32[256,128]{1,0:T(8,128)S(1)}, u32[]{:S(2)}, u32[]{:S(2)}) collective-permute-start(f32[256,128]{1,0:T(8,128)} %get-tuple-element.40.b0), channel_id=1, source_target_pairs={{0,16},{8,24},{16,0},{24,8},{1,17},{9,25},{17,1},{25,9},{2,18},{10... | collective-permute-start | bytes 393224 | tf_op jit(solution)/shard_map/ppermute | solution.py:294
  91.0 2.6 %collective-permute-start.10 = (f32[256,128]{1,0:T(8,128)}, f32[256,128]{1,0:T(8,128)S(1)}, u32[]{:S(2)}, u32[]{:S(2)}) collective-permute-start(f32[256,128]{1,0:T(8,128)} %get-tuple-element.40.b0), channel_id=1, source_target_pairs={{0,8},{8,16},{16,24},{24,0},{1,9},{9,17},{17,25},{25,1},{2,10},{10... | collective-permute-start | bytes 393224 | tf_op jit(solution)/shard_map/ppermute | solution.py:294
  97.0 2.6 %collective-permute-start.16 = (f32[2,40,128]{2,1,0:T(8,128)}, f32[2,40,128]{2,1,0:T(8,128)S(1)}, u32[]{:S(2)}, u32[]{:S(2)}) collective-permute-start(f32[2,40,128]{2,1,0:T(8,128)} %core_pair.1.d0), channel_id=1, source_target_pairs={{0,6},{2,0},{4,2},{6,4},{1,7},{3,1},{5,3},{7,5},{8,14},{10,8},{12,... | collective-permute-start | bytes 122888 | tf_op jit(solution)/shard_map/ppermute | solution.py:294
  99.5 2.3 %collective-permute-done.16.d3 = f32[2,40,128]{2,1,0:T(8,128)S(1)} collective-permute-done((f32[2,40,128]{2,1,0:T(8,128)}, f32[2,40,128]{2,1,0:T(8,128)S(1)}, u32[]{:S(2)}, u32[]{:S(2)}) %collective-permute-start.16) | collective-permute-done | bytes 40992 | tf_op jit(solution)/shard_map/ppermute | solution.py:294
  101.8 3.4 %collective-permute-done.15.d2 = f32[2,40,128]{2,1,0:T(8,128)S(1)} collective-permute-done((f32[2,40,128]{2,1,0:T(8,128)}, f32[2,40,128]{2,1,0:T(8,128)S(1)}, u32[]{:S(2)}, u32[]{:S(2)}) %collective-permute-start.15) | collective-permute-done | bytes 40992 | tf_op jit(solution)/shard_map/ppermute | solution.py:294
  105.3 2.4 %collective-permute-done.14.d1 = f32[2,40,128]{2,1,0:T(8,128)S(1)} collective-permute-done((f32[2,40,128]{2,1,0:T(8,128)}, f32[2,40,128]{2,1,0:T(8,128)S(1)}, u32[]{:S(2)}, u32[]{:S(2)}) %collective-permute-start.14) | collective-permute-done | bytes 40992 | tf_op jit(solution)/shard_map/ppermute | solution.py:294
  109.1 2.0 %outputs.1 = (f32[8,32,128]{2,1,0:T(8,128)}, f32[4,256,128]{2,1,0:T(8,128)}, f32[8,32]{1,0:T(8,128)}, f32[32,4,128]{2,1,0:T(4,128)}) custom-call(f32[8,32]{1,0:T(8,128)} %hour_ref.3, f32[256,128]{1,0:T(8,128)} %get-tuple-element.40.b0, f32[256,128]{1,0:T(8,128)} %copy-done.10, f32[256,128]{1,0:T(8,128)} %copy-done.9, f32[256,128]{1,0:T(8,128)} %copy-done.8, ...), custom_call_target="tpu_custom_call" | custom-call | tf_op jit(solution)/shard_map/outputs/pallas_call | solution.py:279
  (63 shorter events, 20.1 us)
Async XLA Ops:
  2.9 3.4 %copy-start.3 = (s32[8,256,1024]{2,1,0:T(8,128)S(1)}, s32[8,256,1024]{2,1,0:T(8,128)}, u32[]{:S(2)}) copy-start(s32[8,256,1024]{2,1,0:T(8,128)} %counts_ref.1) | copy-start | bytes 25165828
  26.1 5.6 %collective-permute-start = (f32[256,128]{1,0:T(8,128)S(1)}, f32[256,128]{1,0:T(8,128)S(1)}, u32[]{:S(2)}, u32[]{:S(2)}) collective-permute-start(f32[256,128]{1,0:T(8,128)S(1)} %get-tuple-element.26), channel_id=1, source_target_pairs={{0,8},{8,16},{16,24},{24,0},{1,9},{9,17},{17,25},{25,1},{2,10},{10... | collective-permute-start | bytes 393224 | tf_op jit(solution)/shard_map/ppermute | solution.py:294
  27.6 7.9 %collective-permute-start.1 = (f32[256,128]{1,0:T(8,128)S(1)}, f32[256,128]{1,0:T(8,128)S(1)}, u32[]{:S(2)}, u32[]{:S(2)}) collective-permute-start(f32[256,128]{1,0:T(8,128)S(1)} %get-tuple-element.27), channel_id=1, source_target_pairs={{0,16},{8,24},{16,0},{24,8},{1,17},{9,25},{17,1},{25,9},{2,18},{10... | collective-permute-start | bytes 393224 | tf_op jit(solution)/shard_map/ppermute | solution.py:294
  30.5 5.7 %collective-permute-start.2 = (f32[256,128]{1,0:T(8,128)S(1)}, f32[256,128]{1,0:T(8,128)S(1)}, u32[]{:S(2)}, u32[]{:S(2)}) collective-permute-start(f32[256,128]{1,0:T(8,128)S(1)} %get-tuple-element.28), channel_id=1, source_target_pairs={{0,24},{8,0},{16,8},{24,16},{1,25},{9,1},{17,9},{25,17},{2,26},{10... | collective-permute-start | bytes 393224 | tf_op jit(solution)/shard_map/ppermute | solution.py:294
  30.9 14.5 %collective-permute-start.3 = (f32[4,160,128]{2,1,0:T(8,128)S(1)}, f32[4,160,128]{2,1,0:T(8,128)S(1)}, u32[]{:S(2)}, u32[]{:S(2)}) collective-permute-start(f32[4,160,128]{2,1,0:T(8,128)S(1)} %get-tuple-element.30), channel_id=1, source_target_pairs={{0,1},{1,0},{2,3},{3,2},{4,5},{5,4},{6,7},{7,6},{8,9},{9,8},{10,11... | collective-permute-start | bytes 983048 | tf_op jit(solution)/shard_map/ppermute | solution.py:294
  36.9 28.0 %all-to-all-start = ((f32[8,32,128]{2,1,0:T(8,128)}), f32[8,32,128]{2,1,0:T(8,128)S(1)}, u32[]{:S(2)}, u32[]{:S(2)}) async-start(f32[8,32,128]{2,1,0:T(8,128)} %bitcast), calls=%async_computation | async-start | bytes 262144 | tf_op jit(solution)/shard_map/all_to_all | solution.py:299
  47.9 6.7 %collective-permute-start.4 = (f32[160,128]{1,0:T(8,128)}, f32[160,128]{1,0:T(8,128)S(1)}, u32[]{:S(2)}, u32[]{:S(2)}) collective-permute-start(f32[160,128]{1,0:T(8,128)} %get-tuple-element.32), channel_id=1, source_target_pairs={{0,2},{2,4},{4,6},{6,0},{1,3},{3,5},{5,7},{7,1},{8,10},{10,12},{12... | collective-permute-start | bytes 245768 | tf_op jit(solution)/shard_map/ppermute | solution.py:294
  49.5 6.4 %collective-permute-start.5 = (f32[160,128]{1,0:T(8,128)}, f32[160,128]{1,0:T(8,128)S(1)}, u32[]{:S(2)}, u32[]{:S(2)}) collective-permute-start(f32[160,128]{1,0:T(8,128)} %get-tuple-element.33), channel_id=1, source_target_pairs={{0,4},{2,6},{4,0},{6,2},{1,5},{3,7},{5,1},{7,3},{8,12},{10,14},{12... | collective-permute-start | bytes 245768 | tf_op jit(solution)/shard_map/ppermute | solution.py:294
  52.4 4.7 %collective-permute-start.6 = (f32[160,128]{1,0:T(8,128)}, f32[160,128]{1,0:T(8,128)S(1)}, u32[]{:S(2)}, u32[]{:S(2)}) collective-permute-start(f32[160,128]{1,0:T(8,128)} %get-tuple-element.34), channel_id=1, source_target_pairs={{0,6},{2,0},{4,2},{6,4},{1,7},{3,1},{5,3},{7,5},{8,14},{10,8},{12,... | collective-permute-start | bytes 245768 | tf_op jit(solution)/shard_map/ppermute | solution.py:294
  54.6 2.5 %copy-start.11 = (f32[160,128]{1,0:T(8,128)}, f32[160,128]{1,0:T(8,128)S(1)}, u32[]{:S(2)}) copy-start(f32[160,128]{1,0:T(8,128)S(1)} %collective-permute-done.4.r1) | copy-start | bytes 245764
  60.4 4.4 %collective-permute-start.7 = (f32[40,128]{1,0:T(8,128)}, f32[40,128]{1,0:T(8,128)S(1)}, u32[]{:S(2)}, u32[]{:S(2)}) collective-permute-start(f32[40,128]{1,0:T(8,128)} %get-tuple-element.36), channel_id=1, source_target_pairs={{0,8},{8,16},{16,24},{24,0},{1,9},{9,17},{17,25},{25,1},{2,10},{10... | collective-permute-start | bytes 61448 | tf_op jit(solution)/shard_map/ppermute | solution.py:294
  61.7 5.6 %collective-permute-start.8 = (f32[40,128]{1,0:T(8,128)}, f32[40,128]{1,0:T(8,128)S(1)}, u32[]{:S(2)}, u32[]{:S(2)}) collective-permute-start(f32[40,128]{1,0:T(8,128)} %get-tuple-element.37), channel_id=1, source_target_pairs={{0,16},{8,24},{16,0},{24,8},{1,17},{9,25},{17,1},{25,9},{2,18},{10... | collective-permute-start | bytes 61448 | tf_op jit(solution)/shard_map/ppermute | solution.py:294
  63.2 4.2 %collective-permute-start.9 = (f32[40,128]{1,0:T(8,128)}, f32[40,128]{1,0:T(8,128)S(1)}, u32[]{:S(2)}, u32[]{:S(2)}) collective-permute-start(f32[40,128]{1,0:T(8,128)} %get-tuple-element.38), channel_id=1, source_target_pairs={{0,24},{8,0},{16,8},{24,16},{1,25},{9,1},{17,9},{25,17},{2,26},{10... | collective-permute-start | bytes 61448 | tf_op jit(solution)/shard_map/ppermute | solution.py:294
  64.8 2.5 %copy-start.6 = (f32[8,32,128]{2,1,0:T(8,128)}, f32[8,32,128]{2,1,0:T(8,128)S(1)}, u32[]{:S(2)}) copy-start(f32[8,32,128]{2,1,0:T(8,128)S(1)} %all-to-all-done.a_ref) | copy-start | bytes 393220
  64.8 2.5 %copy-start.17 = (f32[40,128]{1,0:T(8,128)}, f32[40,128]{1,0:T(8,128)S(1)}, u32[]{:S(2)}) copy-start(f32[40,128]{1,0:T(8,128)S(1)} %collective-permute-done.7.m1) | copy-start | bytes 61444
  87.9 19.8 %collective-permute-start.12 = (f32[256,128]{1,0:T(8,128)}, f32[256,128]{1,0:T(8,128)S(1)}, u32[]{:S(2)}, u32[]{:S(2)}) collective-permute-start(f32[256,128]{1,0:T(8,128)} %get-tuple-element.40.b0), channel_id=1, source_target_pairs={{0,24},{8,0},{16,8},{24,16},{1,25},{9,1},{17,9},{25,17},{2,26},{10... | collective-permute-start | bytes 393224 | tf_op jit(solution)/shard_map/ppermute | solution.py:294
  89.4 18.3 %collective-permute-start.11 = (f32[256,128]{1,0:T(8,128)}, f32[256,128]{1,0:T(8,128)S(1)}, u32[]{:S(2)}, u32[]{:S(2)}) collective-permute-start(f32[256,128]{1,0:T(8,128)} %get-tuple-element.40.b0), channel_id=1, source_target_pairs={{0,16},{8,24},{16,0},{24,8},{1,17},{9,25},{17,1},{25,9},{2,18},{10... | collective-permute-start | bytes 393224 | tf_op jit(solution)/shard_map/ppermute | solution.py:294
  91.0 16.7 %collective-permute-start.10 = (f32[256,128]{1,0:T(8,128)}, f32[256,128]{1,0:T(8,128)S(1)}, u32[]{:S(2)}, u32[]{:S(2)}) collective-permute-start(f32[256,128]{1,0:T(8,128)} %get-tuple-element.40.b0), channel_id=1, source_target_pairs={{0,8},{8,16},{16,24},{24,0},{1,9},{9,17},{17,25},{25,1},{2,10},{10... | collective-permute-start | bytes 393224 | tf_op jit(solution)/shard_map/ppermute | solution.py:294
  93.6 1.4 %collective-permute-start.13 = (f32[40,128]{1,0:T(8,128)}, f32[40,128]{1,0:T(8,128)S(1)}, u32[]{:S(2)}, u32[]{:S(2)}) collective-permute-start(f32[40,128]{1,0:T(8,128)} %get-tuple-element.41.own), channel_id=1, source_target_pairs={{0,1},{1,0},{2,3},{3,2},{4,5},{5,4},{6,7},{7,6},{8,9},{9,8},{10,11... | collective-permute-start | bytes 61448 | tf_op jit(solution)/shard_map/ppermute | solution.py:294
  97.0 4.8 %collective-permute-start.16 = (f32[2,40,128]{2,1,0:T(8,128)}, f32[2,40,128]{2,1,0:T(8,128)S(1)}, u32[]{:S(2)}, u32[]{:S(2)}) collective-permute-start(f32[2,40,128]{2,1,0:T(8,128)} %core_pair.1.d0), channel_id=1, source_target_pairs={{0,6},{2,0},{4,2},{6,4},{1,7},{3,1},{5,3},{7,5},{8,14},{10,8},{12,... | collective-permute-start | bytes 122888 | tf_op jit(solution)/shard_map/ppermute | solution.py:294
  99.5 5.7 %collective-permute-start.15 = (f32[2,40,128]{2,1,0:T(8,128)}, f32[2,40,128]{2,1,0:T(8,128)S(1)}, u32[]{:S(2)}, u32[]{:S(2)}) collective-permute-start(f32[2,40,128]{2,1,0:T(8,128)} %core_pair.1.d0), channel_id=1, source_target_pairs={{0,4},{2,6},{4,0},{6,2},{1,5},{3,7},{5,1},{7,3},{8,12},{10,14},{12... | collective-permute-start | bytes 122888 | tf_op jit(solution)/shard_map/ppermute | solution.py:294
  101.8 5.9 %copy-start.14 = (f32[2,40,128]{2,1,0:T(8,128)}, f32[2,40,128]{2,1,0:T(8,128)S(1)}, u32[]{:S(2)}) copy-start(f32[2,40,128]{2,1,0:T(8,128)S(1)} %collective-permute-done.16.d3) | copy-start | bytes 122884
  101.8 5.8 %collective-permute-start.14 = (f32[2,40,128]{2,1,0:T(8,128)}, f32[2,40,128]{2,1,0:T(8,128)S(1)}, u32[]{:S(2)}, u32[]{:S(2)}) collective-permute-start(f32[2,40,128]{2,1,0:T(8,128)} %core_pair.1.d0), channel_id=1, source_target_pairs={{0,2},{2,4},{4,6},{6,0},{1,3},{3,5},{5,7},{7,1},{8,10},{10,12},{12... | collective-permute-start | bytes 122888 | tf_op jit(solution)/shard_map/ppermute | solution.py:294
  105.3 2.5 %copy-start.15 = (f32[2,40,128]{2,1,0:T(8,128)}, f32[2,40,128]{2,1,0:T(8,128)S(1)}, u32[]{:S(2)}) copy-start(f32[2,40,128]{2,1,0:T(8,128)S(1)} %collective-permute-done.15.d2) | copy-start | bytes 122884
  (15 other events, 11.9 us)

commit v2 on v0

v2 whole, which is shorter than its diff:
```python
import functools
import math

import jax
import jax.numpy as jnp
from jax import lax
from jax.experimental import pallas as pl
from jax.experimental.pallas import tpu as pltpu
from jax.sharding import Mesh, PartitionSpec as P

X = 4
CORES = 2
PAIR = 2
SPAN = 1024
F32 = jnp.float32
BF16 = jnp.bfloat16
ANY = pl.BlockSpec(memory_space=pl.ANY)
VMEM = pl.BlockSpec(memory_space=pltpu.VMEM)
SMEM = pl.BlockSpec(memory_space=pltpu.SMEM)


def struct(*shape, dtype=F32):
    return jax.ShapeDtypeStruct(shape, dtype)


def params(mib):
    return pltpu.CompilerParams(vmem_limit_bytes=mib << 20)


def cost(flops, size):
    return pl.CostEstimate(flops=flops, bytes_accessed=size, transcendentals=0)


def split(x):
    hi = x.astype(BF16)
    return hi, (x - hi.astype(F32)).astype(BF16)


def mm(a, b):
    return jnp.dot(a, b, preferred_element_type=F32)


def halves(x, axis):
    return jnp.concatenate(split(x), axis=axis)


def first_kernel(hour_ref, counts_hbm, src_hbm, dst_hbm, core_hbm,
                 a0, a1, a2, a3, hours_out, hi_hbm, lo_hbm,
                 counts, src, dst, core, fit_rows, fit_cols, dst_cols, hi_all, lo_all, dst_sum, turned, sems):
    hours, rows, cols = counts.shape
    rank, p1, q1 = core.shape
    steps = hours // PAIR
    x = lax.axis_index("x")
    small = [pltpu.make_async_copy(a, b, sems.at[i])
             for i, (a, b) in enumerate(((core_hbm, core), (src_hbm, src), (dst_hbm, dst)))]
    parts = [pl.ds(s * PAIR, PAIR) for s in range(steps)]
    large = [pltpu.make_async_copy(counts_hbm.at[part], counts.at[part], sems.at[3 + s])
             for s, part in enumerate(parts)]
    for copy in small + large:
        copy.start()
    small[2].wait()
    hi, lo = split(dst[...].T)
    dst_cols[...] = jnp.concatenate([hi, hi, lo], axis=0)
    small[0].wait()
    small[1].wait()
    hi, lo = split(src[...])
    src_rows = jnp.concatenate([hi, lo, hi], axis=1)
    for k in range(hours):
        core_hour = hour_ref[k, 0] * core[0]
        for r in range(1, rank):
            core_hour = core_hour + hour_ref[k, r] * core[r]
        hours_out[k] = core_hour
        hi, lo = split(core_hour)
        fit = mm(src_rows, jnp.concatenate([hi, hi, lo], axis=0))
        hi, lo = split(fit)
        fit_rows[k * rows:(k + 1) * rows] = jnp.concatenate([hi, lo, hi], axis=1)
        fit_cols[k] = halves(fit.T, 0)
    sends = []
    for s, part in enumerate(parts):
        large[s].wait()
        block = pl.ds(s * PAIR * rows, PAIR * rows)
        for j in range(0, cols, SPAN):
            wide = pl.ds(j, SPAN)
            fitted = mm(fit_rows[block, :], dst_cols[:, wide])
            misfit = 1.0 - counts[part, :, wide].reshape(PAIR * rows, SPAN).astype(F32) / fitted
            hi, lo = split(misfit)
            hi_all[part, :, wide] = hi.reshape(PAIR, rows, SPAN)
            lo_all[part, :, wide] = lo.reshape(PAIR, rows, SPAN)
            total = None
            for k in range(PAIR):
                left = fit_cols[s * PAIR + k]
                both = mm(left, hi[k * rows:(k + 1) * rows])
                term = both[:q1] + (both[q1:] + mm(left[:q1], lo[k * rows:(k + 1) * rows]))
                total = term if total is None else total + term
            if s == 0:
                dst_sum[:, wide] = total
            else:
                dst_sum[:, wide] += total
        for i, (a, b) in enumerate(((hi_all, hi_hbm), (lo_all, lo_hbm))):
            sends.append(pltpu.make_async_copy(a.at[part], b.at[part], sems.at[3 + steps + 2 * s + i]))
            sends[-1].start()
    turned[...] = dst_sum[...].T.reshape(turned.shape)
    for s, out in enumerate((a0, a1, a2, a3)):
        out[...] = turned[lax.rem(x + s, X)]
    for copy in sends:
        copy.wait()


def first_call(hour, counts, src, dst, core):
    hours, rows, cols = counts.shape
    rank, p1, q1 = core.shape
    block = cols // X
    out = [struct(block, q1)] * X + [struct(hours, p1, q1)] + [struct(*counts.shape, dtype=BF16)] * 2
    return pl.pallas_call(
        first_kernel,
        out_shape=out,
        in_specs=[SMEM] + [ANY] * 4,
        out_specs=[VMEM] * (X + 1) + [ANY] * 2,
        scratch_shapes=[
            pltpu.VMEM(counts.shape, jnp.int32),
            pltpu.VMEM(src.shape, F32),
            pltpu.VMEM(dst.shape, F32),
            pltpu.VMEM(core.shape, F32),
            pltpu.VMEM((hours * rows, 3 * q1), BF16),
            pltpu.VMEM((hours, 2 * q1, rows), BF16),
            pltpu.VMEM((3 * q1, cols), BF16),
            pltpu.VMEM(counts.shape, BF16),
            pltpu.VMEM(counts.shape, BF16),
            pltpu.VMEM((q1, cols), F32),
            pltpu.VMEM((X, block, q1), F32),
            pltpu.SemaphoreType.DMA((3 + 3 * (hours // PAIR),)),
        ],
        compiler_params=params(60),
        cost_estimate=cost(2 * 6 * counts.size * q1, 20 << 20),
        name="misfit_and_dst",
    )(hour, counts, src, dst, core)


def second_kernel(hi_hbm, lo_hbm, src_hbm, dst_hbm, core_hbm, hours_hbm,
                  m0, m1, m2, m3, src_own, src_send,
                  hi_all, lo_all, src, dst, core, core_hours, dst_rows, src_cols, projected, rowsums, message, src_all, sems):
    hours, rows, cols = hi_all.shape
    rank, p1, q1 = core.shape
    steps = hours // PAIR
    zs = message.shape[1]
    x = lax.axis_index("x")
    small = [pltpu.make_async_copy(a, b, sems.at[i])
             for i, (a, b) in enumerate(((dst_hbm, dst), (src_hbm, src), (hours_hbm, core_hours), (core_hbm, core)))]
    parts = [pl.ds(s * PAIR, PAIR) for s in range(steps)]
    large = []
    for s, part in enumerate(parts):
        for i, (a, b) in enumerate(((hi_hbm, hi_all), (lo_hbm, lo_all))):
            large.append(pltpu.make_async_copy(a.at[part], b.at[part], sems.at[4 + 2 * s + i]))
    for copy in small[:3] + large + small[3:]:
        copy.start()
    small[0].wait()
    dst_rows[...] = halves(dst[...], 1)
    small[1].wait()
    src_cols[...] = halves(src[...].T, 0)
    small[2].wait()
    src_sum = None
    for s, part in enumerate(parts):
        large[2 * s].wait()
        large[2 * s + 1].wait()
        both = mm(hi_all[part].reshape(PAIR * rows, cols), dst_rows[...])
        through = both[:, :q1] + (both[:, q1:] + mm(lo_all[part].reshape(PAIR * rows, cols), dst_rows[:, :q1]))
        for i in range(PAIR):
            k = s * PAIR + i
            th = halves(through[i * rows:(i + 1) * rows], 1)
            right = halves(core_hours[k].T, 1)
            both = mm(th, jnp.concatenate([right, right], axis=0))
            both = both[:, :p1] + both[:, p1:]
            src_sum = both if src_sum is None else src_sum + both
            both = mm(src_cols[...], th)
            both = both[:p1] + both[p1:]
            projected[k] = both[:, :q1] + both[:, q1:]
    y, c = lax.axis_index("y"), lax.axis_index("core")
    ys, share, _ = src_own.shape
    src_all[...] = src_sum.reshape(src_all.shape)
    for s in range(ys):
        at = lax.rem(y + s, ys) * CORES
        src_own[s] = src_all[at + c]
        src_send[s] = src_all[at + 1 - c]
    small[3].wait()
    for k in range(hours):
        here = projected[k]
        for r in range(rank):
            product = (here * core[r]).reshape(p1 // 8, 8, q1)
            at = k * rank + r
            rowsums[at:at + 1, :] = jnp.sum(jnp.sum(product, axis=0), axis=0, keepdims=True)
        for z in range(zs):
            for b in range(X):
                start = (z * X + b) * 4
                message[b, z, 4 * k:4 * k + 4, :] = here[start:start + 4]
    sums = jnp.sum(rowsums[...].T, axis=0, keepdims=True)
    spare = jnp.zeros((8 - sums.shape[1] // 128, 128), F32)
    tail = jnp.concatenate([sums[:, i:i + 128] for i in range(0, sums.shape[1], 128)] + [spare], axis=0)
    for s, out in enumerate((m0, m1, m2, m3)):
        out[:zs] = message[lax.rem(x + s, X)]
        out[zs, :8, :] = tail


def second_call(hi, lo, src, dst, core, core_hours, zs, devices):
    hours, rows, cols = hi.shape
    rank, p1, q1 = core.shape
    share = hours * p1 // (zs * X)
    return pl.pallas_call(
        second_kernel,
        out_shape=[struct(zs + 1, share, q1)] * X + [struct(devices // CORES, rows // devices, p1)] * 2,
        in_specs=[ANY] * 6,
        out_specs=[VMEM] * (X + 2),
        scratch_shapes=[
            pltpu.VMEM(hi.shape, BF16),
            pltpu.VMEM(hi.shape, BF16),
            pltpu.VMEM(src.shape, F32),
            pltpu.VMEM(dst.shape, F32),
            pltpu.VMEM(core.shape, F32),
            pltpu.VMEM(core_hours.shape, F32),
            pltpu.VMEM((cols, 2 * q1), BF16),
            pltpu.VMEM((2 * p1, rows), BF16),
            pltpu.VMEM((hours, p1, q1), F32),
            pltpu.VMEM((hours * rank, q1), F32),
            pltpu.VMEM((X, zs, share, q1), F32),
            pltpu.VMEM((devices, rows // devices, p1), F32),
            pltpu.SemaphoreType.DMA((4 + 2 * (hours // PAIR),)),
        ],
        compiler_params=params(60),
        cost_estimate=cost(2 * 3 * hi.size * q1, 12 << 20),
        name="src_and_projected",
    )(hi, lo, src, dst, core, core_hours)


def z_kernel(a, m0, m1, m2, m3, out):
    zs, share, _ = a.shape
    total = jnp.sum(a[...], axis=0)
    m = (m0[...] + m1[...]) + (m2[...] + m3[...])
    for z in range(zs):
        out[z, :share, :] = total
        out[z, share:2 * share, :] = m[z]
        out[z, 2 * share:, :] = m[zs, :8]


def z_call(a, m):
    zs, share, q1 = a.shape
    return pl.pallas_call(
        z_kernel, out_shape=struct(zs, 2 * share + 8, q1), in_specs=[VMEM] * 5, out_specs=VMEM,
        compiler_params=params(8), cost_estimate=cost(1 << 20, 1 << 20), name="z_terms",
    )(a, *m)


def pair_kernel(own, came, *outs):
    for s, out in enumerate(outs):
        out[...] = own[s] + came[s]


def pair_call(own, came):
    return pl.pallas_call(
        pair_kernel, out_shape=[struct(*own.shape[1:])] * own.shape[0],
        in_specs=[VMEM] * 2, out_specs=[VMEM] * own.shape[0],
        compiler_params=params(8), cost_estimate=cost(1 << 18, 1 << 18), name="core_sums",
    )(own, came)


def back_kernel(w, t0, t1, t2, t3, block, copies):
    zs, rows, _ = w.shape
    share = (rows - 8) // 2
    tail = w[0, share:, :]
    block[:share, :] = w[0, :share, :]
    for z in range(1, zs):
        block[z * share:(z + 1) * share, :] = w[z, :share, :]
        tail = tail + w[z, share:, :]
    total = (t0[...] + t1[...]) + (t2[...] + t3[...])
    for d in range(copies.shape[0]):
        copies[d, :share + 8, :] = tail
        copies[d, share + 8:, :] = total


def back_call(w, terms, devices):
    zs, rows, q1 = w.shape
    src_share = terms[0].shape[0]
    share = (rows - 8) // 2
    return pl.pallas_call(
        back_kernel, out_shape=[struct(zs * share, q1), struct(devices, rows - share + src_share, q1)],
        in_specs=[VMEM] * 5, out_specs=[VMEM] * 2,
        compiler_params=params(8), cost_estimate=cost(1 << 20, 1 << 20), name="z_sums",
    )(w, *terms)


def end_kernel(scales, hour_ref, b0, b1, b2, b3, d, src_out, dst_out, hour_out, core_out):
    x = lax.axis_index("x")
    src_scale, dst_scale, hour_scale, core_scale = scales
    for s, block in enumerate((b0, b1, b2, b3)):
        dst_out[lax.rem(x - s + X, X)] = block[...] * dst_scale
    hours, rank = hour_ref.shape
    share = 4 * hours
    total = jnp.sum(d[:, :share + 8, :], axis=0)
    src_out[...] = d[:, share + 8:, :] * src_scale
    each = 128 // rank
    for k in range(hours):
        row = share + k // each
        hour_out[k:k + 1, :] = total[row:row + 1, k % each * rank:(k % each + 1) * rank] * hour_scale
    tiles = [total[4 * k:4 * k + 4] * core_scale for k in range(hours)]
    for r in range(rank):
        out = hour_ref[0, r] * tiles[0]
        for k in range(1, hours):
            out = out + hour_ref[k, r] * tiles[k]
        core_out[r] = out


def end_call(scales, hour, blocks, d):
    block, q1 = blocks[0].shape
    hours, rank = hour.shape
    return pl.pallas_call(
        functools.partial(end_kernel, scales),
        in_specs=[SMEM] + [VMEM] * (X + 1),
        out_specs=[VMEM] * 4,
        out_shape=[struct(d.shape[0], d.shape[1] - 4 * hours - 8, q1), struct(X, block, q1), struct(hours, rank), struct(rank, 4, q1)],
        compiler_params=params(8), cost_estimate=cost(1 << 20, 1 << 20), name="outputs",
    )(hour, *blocks, d)


def shifted(x, axis, s):
    n = lax.axis_size(axis)
    return lax.ppermute(x, axis, [(i, (i + s) % n) for i in range(n)])


def swapped(x, axis):
    return lax.all_to_all(x, axis, split_axis=0, concat_axis=0, tiled=True)


def after(x, *others):
    return lax.optimization_barrier((x, *others))[0]


def shards(scales, counts, src_factor, dst_factor, hour_factor, core):
    zs = lax.axis_size("z")
    dst_axes = ("y", "core")
    devices = lax.axis_size(dst_axes)
    q1 = dst_factor.shape[1]
    a0, a1, a2, a3, core_hours, hi, lo = first_call(hour_factor, counts, src_factor, dst_factor, core)
    came = [shifted(a, "x", s) for s, a in ((1, a1), (2, a2), (3, a3))]
    m0, m1, m2, m3, src_own, src_send = second_call(
        hi, lo, src_factor, dst_factor, core, core_hours, zs, devices)
    came = lax.optimization_barrier((*came, src_own))[:3]
    a = (a0 + came[0]) + (came[1] + came[2])
    a = swapped(a.reshape(zs, -1, q1), "z")
    m = [m0] + [shifted(v, "x", s) for s, v in ((1, m1), (2, m2), (3, m3))]
    parts = pair_call(src_own, shifted(src_send, "core", 1))
    w_out = z_call(a, m)
    w = swapped(w_out, "z")
    parts = lax.optimization_barrier((*parts, w_out))[:4]
    parts = [parts[0]] + [shifted(parts[s], "y", s) for s in (1, 2, 3)]
    block, copies = back_call(w, parts, devices)
    shares = swapped(copies, dst_axes)
    blocks = [block] + [shifted(block, "x", s) for s in (1, 2, 3)]
    grad_src, grad_dst, grad_hour, grad_core = end_call(scales, hour_factor, blocks, shares)
    return (grad_src.reshape(src_factor.shape), grad_dst.reshape(dst_factor.shape), grad_hour, grad_core)


def solution(mesh):
    n_src, n_dst = mesh.shape["src"], mesh.shape["dst"]
    fine = Mesh(mesh.devices.reshape(n_src // X, X, n_dst // CORES, CORES), ("z", "x", "y", "core"))
    src, dst = ("z", "x"), ("y", "core")
    in_specs = (P(None, src, dst), P(src, None), P(dst, None), P(), P())
    out_specs = (P(src, None), P(dst, None), P(), P(None, src, None))

    def run(counts, src_factor, dst_factor, hour_factor, core):
        hours, total_src, total_dst = counts.shape
        scales = (1 / math.sqrt(total_dst * hours), 1 / math.sqrt(total_src * hours),
                  1 / math.sqrt(total_src * total_dst), 1 / math.sqrt(total_src * total_dst * hours))
        body = jax.shard_map(functools.partial(shards, scales), mesh=fine, in_specs=in_specs,
                             out_specs=out_specs, check_vma=False)
        return body(counts, src_factor, dst_factor, hour_factor, core)

    return run
```

time: 160 us -> 84.1 us (0.53)
  waiting for transfers between devices: 66 us -> 19.7 us
  matrix products: 42.6 us -> 0 us
  Pallas kernels: 0 us -> 22.5 us
  local copies, waits for them, and re-layouts: 11.3 us -> 1.76 us
  other arithmetic: 4.31 us -> 0.68 us
  starting transfers between devices: 34.3 us -> 37.6 us
    all_to_all x6 -> x3, waiting for transfers between devices: 66 us -> 1.62 us  [swapped(): return lax.all_to_all(x, axis, split_axis=0, concat_axis=0, tiled=True)]
    dot_general x9 -> x0, matrix products: 42.6 us -> none  [the longest x1 16.5 us: shards(): jnp.einsum('kij,kiq->jq', misfit, partial_fit, precision=highest)]
    pallas_call x0 -> x6, Pallas kernels: none -> 22.5 us  [the longest x1 11.4 us: first_call(): pl.pallas_call(first_kernel, out_shape=out, in_specs=[SMEM] + [ANY] * 4,...]
    ppermute x0 -> x13, waiting for transfers between devices: none -> 18.1 us  [shifted(): return lax.ppermute(x, axis, [(i, (i + s) % n) for i in range(n)])]
    ppermute x0 -> x13, starting transfers between devices: none -> 17.3 us  [shifted(): return lax.ppermute(x, axis, [(i, (i + s) % n) for i in range(n)])]
    all_to_all x6 -> x3, starting transfers between devices: 34.3 us -> 20.3 us  [swapped(): return lax.all_to_all(x, axis, split_axis=0, concat_axis=0, tiled=True)]
    unnamed x16 -> x8, local copies, waits for them, and re-layouts: 7.29 us -> 1.76 us
    broadcast_in_dim x4 -> x0, local copies, waits for them, and re-layouts: 2.6 us -> none  [sent_to_all(): copies = jnp.broadcast_to(x, (lax.axis_size(axis), *x.shape))]
  transfers between devices with their start and end apart: 6 -> 16, of which waited for: 5 -> 8; matrix products, arithmetic and copies ran while one was open for 17% -> 0% of each run, Pallas kernels for 0% -> 10%
where the time goes in v2:
time: 84.1 us; the launch traced here: 83 us
  starting transfers between devices  37.6 us (45%)
  Pallas kernels  22.5 us (27%)
  waiting for transfers between devices  19.7 us (23%)
  local copies, waits for them, and re-layouts  1.76 us (2%)
    all_to_all x3, starting transfers between devices, swapped(): return lax.all_to_all(x, axis, split_axis=0, concat_axis=0, tiled=True)  20.3 us
    ppermute x13, waiting for transfers between devices, shifted(): return lax.ppermute(x, axis, [(i, (i + s) % n) for i in range(n)])  18.1 us
    ppermute x13, starting transfers between devices, shifted(): return lax.ppermute(x, axis, [(i, (i + s) % n) for i in range(n)])  17.3 us
    pallas_call x1, Pallas kernels, first_call(): pl.pallas_call(first_kernel, out_shape=out, in_specs=[SMEM] + [ANY] * 4,...  11.4 us
    pallas_call x1, Pallas kernels, second_call(): pl.pallas_call(second_kernel, out_shape=[struct(zs + 1, share, q1)] * X +...  8.04 us
    unnamed x8, local copies, waits for them, and re-layouts  1.76 us
  transfers between devices with their start and end apart: 16, of which 8 were waited for; matrix products, arithmetic and copies ran while one was open for 0% of the time, Pallas kernels for 10%

profile of v2, /device:TPU:8, one launch (start us, length us, event | category | flops | bytes accessed | tf_op | source)
XLA Modules:
  0.0 83.0 jit_solution(12607659341113809877)
XLA Ops:
  0.6 11.4 %misfit_and_dst.1 = (f32[256,128]{1,0:T(8,128)}, f32[256,128]{1,0:T(8,128)}, f32[256,128]{1,0:T(8,128)}, f32[256,128]{1,0:T(8,128)}, f32[8,128,128]{2,1,0:T(8,12...) custom-call(f32[8,32]{1,0:T(8,128)} %hour_ref.3, s32[8,256,1024]{2,1,0:T(8,128)} %counts_hbm.1, ...), custom_call_target="tpu_custom_call" | custom-call | flops 3221225472 | bytes 20971520 | tf_op jit(solution)/shard_map/misfit_and_dst/pallas_call | solution.py:114
  12.0 1.6 %collective-permute-start = (f32[256,128]{1,0:T(8,128)}, f32[256,128]{1,0:T(8,128)S(1)}, u32[]{:S(2)}, u32[]{:S(2)}) collective-permute-start(f32[256,128]{1,0:T(8,128)} %get-tuple-element.35), channel_id=1, source_target_pairs={{0,8},{8,16},{16,24},{24,0},{1,9},{9,17},{17,25},{25,1},{2,10},{10... | collective-permute-start | bytes 393224 | tf_op jit(solution)/shard_map/ppermute | solution.py:324
  13.6 2.7 %collective-permute-start.1 = (f32[256,128]{1,0:T(8,128)}, f32[256,128]{1,0:T(8,128)S(1)}, u32[]{:S(2)}, u32[]{:S(2)}) collective-permute-start(f32[256,128]{1,0:T(8,128)} %get-tuple-element.36), channel_id=1, source_target_pairs={{0,16},{8,24},{16,0},{24,8},{1,17},{9,25},{17,1},{25,9},{2,18},{10... | collective-permute-start | bytes 393224 | tf_op jit(solution)/shard_map/ppermute | solution.py:324
  16.3 1.4 %collective-permute-start.2 = (f32[256,128]{1,0:T(8,128)}, f32[256,128]{1,0:T(8,128)S(1)}, u32[]{:S(2)}, u32[]{:S(2)}) collective-permute-start(f32[256,128]{1,0:T(8,128)} %get-tuple-element.37), channel_id=1, source_target_pairs={{0,24},{8,0},{16,8},{24,16},{1,25},{9,1},{17,9},{25,17},{2,26},{10... | collective-permute-start | bytes 393224 | tf_op jit(solution)/shard_map/ppermute | solution.py:324
  17.8 8.0 %src_and_projected.1 = (f32[9,32,128]{2,1,0:T(8,128)}, f32[9,32,128]{2,1,0:T(8,128)}, f32[9,32,128]{2,1,0:T(8,128)}, f32[9,32,128]{2,1,0:T(8,128)}, f32[4,32,128]{2,1,0:T(8,128)}, /*index=5*/f32[4,32,128]{2,1,0:T(8,128)}) custom-call(bf16[8,256,1024]{2,1,0:T(8,128)(2,1)} %get-tuple-element.38.hi_hbm, bf16[8,256,1024]{2,1,0:T(8,128)(2,1)} %get-tuple-element.39.lo_hbm, ...), custom_call_target="tpu_custom_call" | custom-call | flops 1610612736 | bytes 12582912 | tf_op jit(solution)/shard_map/src_and_projected/pallas_call | solution.py:207
  26.6 8.5 %all-to-all-start = ((f32[8,32,128]{2,1,0:T(8,128)}), f32[8,32,128]{2,1,0:T(8,128)S(1)}, u32[]{:S(2)}, u32[]{:S(2)}) async-start(f32[8,32,128]{2,1,0:T(8,128)} %bitcast), calls=%async_computation | async-start | bytes 262144 | tf_op jit(solution)/shard_map/all_to_all | solution.py:328
  35.6 0.9 %collective-permute-start.4 = (f32[9,32,128]{2,1,0:T(8,128)}, f32[9,32,128]{2,1,0:T(8,128)S(1)}, u32[]{:S(2)}, u32[]{:S(2)}) collective-permute-start(f32[9,32,128]{2,1,0:T(8,128)} %get-tuple-element.47), channel_id=1, source_target_pairs={{0,16},{8,24},{16,0},{24,8},{1,17},{9,25},{17,1},{25,9},{2,18},{10... | collective-permute-start | bytes 442376 | tf_op jit(solution)/shard_map/ppermute | solution.py:324
  36.5 1.9 %collective-permute-start.5 = (f32[9,32,128]{2,1,0:T(8,128)}, f32[9,32,128]{2,1,0:T(8,128)S(1)}, u32[]{:S(2)}, u32[]{:S(2)}) collective-permute-start(f32[9,32,128]{2,1,0:T(8,128)} %get-tuple-element.48), channel_id=1, source_target_pairs={{0,24},{8,0},{16,8},{24,16},{1,25},{9,1},{17,9},{25,17},{2,26},{10... | collective-permute-start | bytes 442376 | tf_op jit(solution)/shard_map/ppermute | solution.py:324
  38.4 5.7 %collective-permute-done.3.m1 = f32[9,32,128]{2,1,0:T(8,128)S(1)} collective-permute-done((f32[9,32,128]{2,1,0:T(8,128)}, f32[9,32,128]{2,1,0:T(8,128)S(1)}, u32[]{:S(2)}, u32[]{:S(2)}) %collective-permute-start.3) | collective-permute-done | bytes 147488 | tf_op jit(solution)/shard_map/ppermute | solution.py:324
  44.7 0.9 %copy-done = f32[9,32,128]{2,1,0:T(8,128)S(1)} copy-done((f32[9,32,128]{2,1,0:T(8,128)S(1)}, f32[9,32,128]{2,1,0:T(8,128)}, u32[]{:S(2)}) %copy-start) | copy-done | bytes 147480
  46.4 7.0 %all-to-all-start.1 = ((f32[8,72,128]{2,1,0:T(8,128)}), f32[8,72,128]{2,1,0:T(8,128)S(1)}, u32[]{:S(2)}, u32[]{:S(2)}) async-start(f32[8,72,128]{2,1,0:T(8,128)} %z_terms.1), calls=%async_computation.1 | async-start | bytes 589824 | tf_op jit(solution)/shard_map/all_to_all | solution.py:328
  53.3 1.5 %collective-permute-done.6.came = f32[4,32,128]{2,1,0:T(8,128)S(1)} collective-permute-done((f32[4,32,128]{2,1,0:T(8,128)}, f32[4,32,128]{2,1,0:T(8,128)S(1)}, u32[]{:S(2)}, u32[]{:S(2)}) %collective-permute-start.6) | collective-permute-done | bytes 65568 | tf_op jit(solution)/shard_map/ppermute | solution.py:324
  55.7 1.7 %collective-permute-start.7 = (f32[32,128]{1,0:T(8,128)S(1)}, f32[32,128]{1,0:T(8,128)S(1)}, u32[]{:S(2)}, u32[]{:S(2)}) collective-permute-start(f32[32,128]{1,0:T(8,128)S(1)} %get-tuple-element.55), channel_id=1, source_target_pairs={{0,2},{2,4},{4,6},{6,0},{1,3},{3,5},{5,7},{7,1},{8,10},{10,12},{12... | collective-permute-start | bytes 49160 | tf_op jit(solution)/shard_map/ppermute | solution.py:324
  57.3 0.9 %collective-permute-start.8 = (f32[32,128]{1,0:T(8,128)S(1)}, f32[32,128]{1,0:T(8,128)S(1)}, u32[]{:S(2)}, u32[]{:S(2)}) collective-permute-start(f32[32,128]{1,0:T(8,128)S(1)} %get-tuple-element.56), channel_id=1, source_target_pairs={{0,4},{2,6},{4,0},{6,2},{1,5},{3,7},{5,1},{7,3},{8,12},{10,14},{12... | collective-permute-start | bytes 49160 | tf_op jit(solution)/shard_map/ppermute | solution.py:324
  58.3 2.4 %collective-permute-start.9 = (f32[32,128]{1,0:T(8,128)S(1)}, f32[32,128]{1,0:T(8,128)S(1)}, u32[]{:S(2)}, u32[]{:S(2)}) collective-permute-start(f32[32,128]{1,0:T(8,128)S(1)} %get-tuple-element.57), channel_id=1, source_target_pairs={{0,6},{2,0},{4,2},{6,4},{1,7},{3,1},{5,3},{7,5},{8,14},{10,8},{12,... | collective-permute-start | bytes 49160 | tf_op jit(solution)/shard_map/ppermute | solution.py:324
  60.7 1.9 %collective-permute-done.8.t2 = f32[32,128]{1,0:T(8,128)S(1)} collective-permute-done((f32[32,128]{1,0:T(8,128)S(1)}, f32[32,128]{1,0:T(8,128)S(1)}, u32[]{:S(2)}, u32[]{:S(2)}) %collective-permute-start.8) | collective-permute-done | bytes 16416 | tf_op jit(solution)/shard_map/ppermute | solution.py:324
  62.6 1.6 %all-to-all-done.1.w = f32[8,72,128]{2,1,0:T(8,128)S(1)} async-done(((f32[8,72,128]{2,1,0:T(8,128)}), f32[8,72,128]{2,1,0:T(8,128)S(1)}, u32[]{:S(2)}, u32[]{:S(2)}) %all-to-all-start.1) | async-done | bytes 294944 | tf_op jit(solution)/shard_map/all_to_all | solution.py:328
  64.9 4.9 %all-to-all-start.2 = ((f32[8,72,128]{2,1,0:T(8,128)}), f32[8,72,128]{2,1,0:T(8,128)S(1)}, u32[]{:S(2)}, u32[]{:S(2)}) async-start(f32[8,72,128]{2,1,0:T(8,128)} %get-tuple-element.59), calls=%async_computation.2 | async-start | bytes 589824 | tf_op jit(solution)/shard_map/all_to_all | solution.py:328
  69.8 2.3 %collective-permute-start.12 = (f32[256,128]{1,0:T(8,128)S(1)}, f32[256,128]{1,0:T(8,128)S(1)}, u32[]{:S(2)}, u32[]{:S(2)}) collective-permute-start(f32[256,128]{1,0:T(8,128)S(1)} %get-tuple-element.58.b0), channel_id=1, source_target_pairs={{0,24},{8,0},{16,8},{24,16},{1,25},{9,1},{17,9},{25,17},{2,26},{10... | collective-permute-start | bytes 393224 | tf_op jit(solution)/shard_map/ppermute | solution.py:324
  72.2 0.9 %collective-permute-start.10 = (f32[256,128]{1,0:T(8,128)S(1)}, f32[256,128]{1,0:T(8,128)S(1)}, u32[]{:S(2)}, u32[]{:S(2)}) collective-permute-start(f32[256,128]{1,0:T(8,128)S(1)} %get-tuple-element.58.b0), channel_id=1, source_target_pairs={{0,8},{8,16},{16,24},{24,0},{1,9},{9,17},{17,25},{25,1},{2,10},{10... | collective-permute-start | bytes 393224 | tf_op jit(solution)/shard_map/ppermute | solution.py:324
  73.0 5.1 %collective-permute-done.12.b3 = f32[256,128]{1,0:T(8,128)S(1)} collective-permute-done((f32[256,128]{1,0:T(8,128)S(1)}, f32[256,128]{1,0:T(8,128)S(1)}, u32[]{:S(2)}, u32[]{:S(2)}) %collective-permute-start.12) | collective-permute-done | bytes 131104 | tf_op jit(solution)/shard_map/ppermute | solution.py:324
  78.1 2.0 %collective-permute-done.11.b2 = f32[256,128]{1,0:T(8,128)S(1)} collective-permute-done((f32[256,128]{1,0:T(8,128)S(1)}, f32[256,128]{1,0:T(8,128)S(1)}, u32[]{:S(2)}, u32[]{:S(2)}) %collective-permute-start.11) | collective-permute-done | bytes 131104 | tf_op jit(solution)/shard_map/ppermute | solution.py:324
  80.0 1.4 %collective-permute-done.10.b1 = f32[256,128]{1,0:T(8,128)S(1)} collective-permute-done((f32[256,128]{1,0:T(8,128)S(1)}, f32[256,128]{1,0:T(8,128)S(1)}, u32[]{:S(2)}, u32[]{:S(2)}) %collective-permute-start.10) | collective-permute-done | bytes 131104 | tf_op jit(solution)/shard_map/ppermute | solution.py:324
  81.5 1.5 %outputs.1 = (f32[8,32,128]{2,1,0:T(8,128)}, f32[4,256,128]{2,1,0:T(8,128)}, f32[8,32]{1,0:T(8,128)}, f32[32,4,128]{2,1,0:T(4,128)}) custom-call(f32[8,32]{1,0:T(8,128)S(1)} %copy-done.2, f32[256,128]{1,0:T(8,128)S(1)} %get-tuple-element.58.b0, f32[256,128]{1,0:T(8,128)S(1)} %collective-permute-done.10.b1, f32[256,128]{1,0:T(8,128)S(1)} %collective-permute-done.11.b2, ...), custom_call_target="tpu_custom_call" | custom-call | flops 1048576 | bytes 1048576 | tf_op jit(solution)/shard_map/outputs/pallas_call | solution.py:313
  (23 shorter events, 4.3 us)
Async XLA Ops:
  12.0 13.8 %collective-permute-start = (f32[256,128]{1,0:T(8,128)}, f32[256,128]{1,0:T(8,128)S(1)}, u32[]{:S(2)}, u32[]{:S(2)}) collective-permute-start(f32[256,128]{1,0:T(8,128)} %get-tuple-element.35), channel_id=1, source_target_pairs={{0,8},{8,16},{16,24},{24,0},{1,9},{9,17},{17,25},{25,1},{2,10},{10... | collective-permute-start | bytes 393224 | tf_op jit(solution)/shard_map/ppermute | solution.py:324
  13.6 12.2 %collective-permute-start.1 = (f32[256,128]{1,0:T(8,128)}, f32[256,128]{1,0:T(8,128)S(1)}, u32[]{:S(2)}, u32[]{:S(2)}) collective-permute-start(f32[256,128]{1,0:T(8,128)} %get-tuple-element.36), channel_id=1, source_target_pairs={{0,16},{8,24},{16,0},{24,8},{1,17},{9,25},{17,1},{25,9},{2,18},{10... | collective-permute-start | bytes 393224 | tf_op jit(solution)/shard_map/ppermute | solution.py:324
  16.3 9.5 %collective-permute-start.2 = (f32[256,128]{1,0:T(8,128)}, f32[256,128]{1,0:T(8,128)S(1)}, u32[]{:S(2)}, u32[]{:S(2)}) collective-permute-start(f32[256,128]{1,0:T(8,128)} %get-tuple-element.37), channel_id=1, source_target_pairs={{0,24},{8,0},{16,8},{24,16},{1,25},{9,1},{17,9},{25,17},{2,26},{10... | collective-permute-start | bytes 393224 | tf_op jit(solution)/shard_map/ppermute | solution.py:324
  17.8 8.1 %copy-start.3 = (f32[256,128]{1,0:T(8,128)S(1)}, f32[256,128]{1,0:T(8,128)}, u32[]{:S(2)}) copy-start(f32[256,128]{1,0:T(8,128)} %get-tuple-element.34) | copy-start | bytes 393220
  17.8 63.7 %copy-start.2 = (f32[8,32]{1,0:T(8,128)S(1)}, f32[8,32]{1,0:T(8,128)}, u32[]{:S(2)}) copy-start(f32[8,32]{1,0:T(8,128)} %hour_ref.3) | copy-start | bytes 3076
  26.6 18.1 %all-to-all-start = ((f32[8,32,128]{2,1,0:T(8,128)}), f32[8,32,128]{2,1,0:T(8,128)S(1)}, u32[]{:S(2)}, u32[]{:S(2)}) async-start(f32[8,32,128]{2,1,0:T(8,128)} %bitcast), calls=%async_computation | async-start | bytes 262144 | tf_op jit(solution)/shard_map/all_to_all | solution.py:328
  35.0 9.0 %collective-permute-start.3 = (f32[9,32,128]{2,1,0:T(8,128)}, f32[9,32,128]{2,1,0:T(8,128)S(1)}, u32[]{:S(2)}, u32[]{:S(2)}) collective-permute-start(f32[9,32,128]{2,1,0:T(8,128)} %get-tuple-element.46), channel_id=1, source_target_pairs={{0,8},{8,16},{16,24},{24,0},{1,9},{9,17},{17,25},{25,1},{2,10},{10... | collective-permute-start | bytes 442376 | tf_op jit(solution)/shard_map/ppermute | solution.py:324
  35.6 8.5 %collective-permute-start.4 = (f32[9,32,128]{2,1,0:T(8,128)}, f32[9,32,128]{2,1,0:T(8,128)S(1)}, u32[]{:S(2)}, u32[]{:S(2)}) collective-permute-start(f32[9,32,128]{2,1,0:T(8,128)} %get-tuple-element.47), channel_id=1, source_target_pairs={{0,16},{8,24},{16,0},{24,8},{1,17},{9,25},{17,1},{25,9},{2,18},{10... | collective-permute-start | bytes 442376 | tf_op jit(solution)/shard_map/ppermute | solution.py:324
  36.5 8.2 %collective-permute-start.5 = (f32[9,32,128]{2,1,0:T(8,128)}, f32[9,32,128]{2,1,0:T(8,128)S(1)}, u32[]{:S(2)}, u32[]{:S(2)}) collective-permute-start(f32[9,32,128]{2,1,0:T(8,128)} %get-tuple-element.48), channel_id=1, source_target_pairs={{0,24},{8,0},{16,8},{24,16},{1,25},{9,1},{17,9},{25,17},{2,26},{10... | collective-permute-start | bytes 442376 | tf_op jit(solution)/shard_map/ppermute | solution.py:324
  44.7 0.9 %copy-start = (f32[9,32,128]{2,1,0:T(8,128)S(1)}, f32[9,32,128]{2,1,0:T(8,128)}, u32[]{:S(2)}) copy-start(f32[9,32,128]{2,1,0:T(8,128)} %get-tuple-element.45.m0) | copy-start | bytes 442372
  46.4 17.8 %all-to-all-start.1 = ((f32[8,72,128]{2,1,0:T(8,128)}), f32[8,72,128]{2,1,0:T(8,128)S(1)}, u32[]{:S(2)}, u32[]{:S(2)}) async-start(f32[8,72,128]{2,1,0:T(8,128)} %z_terms.1), calls=%async_computation.1 | async-start | bytes 589824 | tf_op jit(solution)/shard_map/all_to_all | solution.py:328
  53.3 1.5 %collective-permute-start.6 = (f32[4,32,128]{2,1,0:T(8,128)}, f32[4,32,128]{2,1,0:T(8,128)S(1)}, u32[]{:S(2)}, u32[]{:S(2)}) collective-permute-start(f32[4,32,128]{2,1,0:T(8,128)} %get-tuple-element.49), channel_id=1, source_target_pairs={{0,1},{1,0},{2,3},{3,2},{4,5},{5,4},{6,7},{7,6},{8,9},{9,8},{10,11... | collective-permute-start | bytes 196616 | tf_op jit(solution)/shard_map/ppermute | solution.py:324
  54.8 0.8 %copy-start.1 = (f32[4,32,128]{2,1,0:T(8,128)S(1)}, f32[4,32,128]{2,1,0:T(8,128)}, u32[]{:S(2)}) copy-start(f32[4,32,128]{2,1,0:T(8,128)} %get-tuple-element.41.own) | copy-start | bytes 196612
  55.7 5.0 %collective-permute-start.7 = (f32[32,128]{1,0:T(8,128)S(1)}, f32[32,128]{1,0:T(8,128)S(1)}, u32[]{:S(2)}, u32[]{:S(2)}) collective-permute-start(f32[32,128]{1,0:T(8,128)S(1)} %get-tuple-element.55), channel_id=1, source_target_pairs={{0,2},{2,4},{4,6},{6,0},{1,3},{3,5},{5,7},{7,1},{8,10},{10,12},{12... | collective-permute-start | bytes 49160 | tf_op jit(solution)/shard_map/ppermute | solution.py:324
  57.3 5.2 %collective-permute-start.8 = (f32[32,128]{1,0:T(8,128)S(1)}, f32[32,128]{1,0:T(8,128)S(1)}, u32[]{:S(2)}, u32[]{:S(2)}) collective-permute-start(f32[32,128]{1,0:T(8,128)S(1)} %get-tuple-element.56), channel_id=1, source_target_pairs={{0,4},{2,6},{4,0},{6,2},{1,5},{3,7},{5,1},{7,3},{8,12},{10,14},{12... | collective-permute-start | bytes 49160 | tf_op jit(solution)/shard_map/ppermute | solution.py:324
  58.3 4.3 %collective-permute-start.9 = (f32[32,128]{1,0:T(8,128)S(1)}, f32[32,128]{1,0:T(8,128)S(1)}, u32[]{:S(2)}, u32[]{:S(2)}) collective-permute-start(f32[32,128]{1,0:T(8,128)S(1)} %get-tuple-element.57), channel_id=1, source_target_pairs={{0,6},{2,0},{4,2},{6,4},{1,7},{3,1},{5,3},{7,5},{8,14},{10,8},{12,... | collective-permute-start | bytes 49160 | tf_op jit(solution)/shard_map/ppermute | solution.py:324
  64.9 16.5 %all-to-all-start.2 = ((f32[8,72,128]{2,1,0:T(8,128)}), f32[8,72,128]{2,1,0:T(8,128)S(1)}, u32[]{:S(2)}, u32[]{:S(2)}) async-start(f32[8,72,128]{2,1,0:T(8,128)} %get-tuple-element.59), calls=%async_computation.2 | async-start | bytes 589824 | tf_op jit(solution)/shard_map/all_to_all | solution.py:328
  69.8 8.2 %collective-permute-start.12 = (f32[256,128]{1,0:T(8,128)S(1)}, f32[256,128]{1,0:T(8,128)S(1)}, u32[]{:S(2)}, u32[]{:S(2)}) collective-permute-start(f32[256,128]{1,0:T(8,128)S(1)} %get-tuple-element.58.b0), channel_id=1, source_target_pairs={{0,24},{8,0},{16,8},{24,16},{1,25},{9,1},{17,9},{25,17},{2,26},{10... | collective-permute-start | bytes 393224 | tf_op jit(solution)/shard_map/ppermute | solution.py:324
  72.2 7.9 %collective-permute-start.11 = (f32[256,128]{1,0:T(8,128)S(1)}, f32[256,128]{1,0:T(8,128)S(1)}, u32[]{:S(2)}, u32[]{:S(2)}) collective-permute-start(f32[256,128]{1,0:T(8,128)S(1)} %get-tuple-element.58.b0), channel_id=1, source_target_pairs={{0,16},{8,24},{16,0},{24,8},{1,17},{9,25},{17,1},{25,9},{2,18},{10... | collective-permute-start | bytes 393224 | tf_op jit(solution)/shard_map/ppermute | solution.py:324
  72.2 9.3 %collective-permute-start.10 = (f32[256,128]{1,0:T(8,128)S(1)}, f32[256,128]{1,0:T(8,128)S(1)}, u32[]{:S(2)}, u32[]{:S(2)}) collective-permute-start(f32[256,128]{1,0:T(8,128)S(1)} %get-tuple-element.58.b0), channel_id=1, source_target_pairs={{0,8},{8,16},{16,24},{24,0},{1,9},{9,17},{17,25},{25,1},{2,10},{10... | collective-permute-start | bytes 393224 | tf_op jit(solution)/shard_map/ppermute | solution.py:324

commit v3 on v2

v3 whole, which is shorter than its diff:
```python
import functools
import math

import jax
import jax.numpy as jnp
from jax import lax
from jax.experimental import pallas as pl
from jax.experimental.pallas import tpu as pltpu
from jax.sharding import Mesh, PartitionSpec as P

X = 4
CORES = 2
GROUP = 4
SPAN = 512
F32 = jnp.float32
BF16 = jnp.bfloat16
HBM = pl.BlockSpec(memory_space=pltpu.HBM)
VMEM = pl.BlockSpec(memory_space=pltpu.VMEM)
SMEM = pl.BlockSpec(memory_space=pltpu.SMEM)


def struct(*shape, dtype=F32):
    return jax.ShapeDtypeStruct(shape, dtype)


def params(mib):
    return pltpu.CompilerParams(vmem_limit_bytes=mib << 20)


def cost(flops, size):
    return pl.CostEstimate(flops=flops, bytes_accessed=size, transcendentals=0)


def split(x):
    hi = x.astype(BF16)
    return hi, (x - hi.astype(F32)).astype(BF16)


def mm(a, b):
    return jnp.dot(a, b, preferred_element_type=F32)


def halves(x, axis):
    return jnp.concatenate(split(x), axis=axis)


def first_kernel(hour_ref, counts_hbm, src_hbm, dst_hbm, core_hbm,
                 a0, a1, a2, a3, hours_out, through_hbm,
                 counts, src, dst, core, fit_rows, fit_cols, dst_cols, dst_rows, hi_all, lo_all, dst_sum, turned,
                 through, sems):
    hours, rows, cols = counts.shape
    rank, p1, q1 = core.shape
    steps = hours // GROUP
    x = lax.axis_index("x")
    small = [pltpu.make_async_copy(a, b, sems.at[i])
             for i, (a, b) in enumerate(((core_hbm, core), (src_hbm, src), (dst_hbm, dst)))]
    parts = [pl.ds(s * GROUP, GROUP) for s in range(steps)]
    large = [pltpu.make_async_copy(counts_hbm.at[part], counts.at[part], sems.at[3 + s])
             for s, part in enumerate(parts)]
    for copy in small + large:
        copy.start()
    small[2].wait()
    dst_rows[...] = halves(dst[...], 1)
    hi, lo = split(dst[...].T)
    dst_cols[...] = jnp.concatenate([hi, hi, lo], axis=0)
    small[0].wait()
    small[1].wait()
    hi, lo = split(src[...])
    src_rows = jnp.concatenate([hi, lo, hi], axis=1)
    for k in range(hours):
        core_hour = hour_ref[k, 0] * core[0]
        for r in range(1, rank):
            core_hour = core_hour + hour_ref[k, r] * core[r]
        hours_out[k] = core_hour
        hi, lo = split(core_hour)
        fit = mm(src_rows, jnp.concatenate([hi, hi, lo], axis=0))
        hi, lo = split(fit)
        fit_rows[k * rows:(k + 1) * rows] = jnp.concatenate([hi, lo, hi], axis=1)
        fit_cols[k] = halves(fit.T, 0)
    sends = []
    for s, part in enumerate(parts):
        large[s].wait()
        block = pl.ds(s * GROUP * rows, GROUP * rows)
        for j in range(0, cols, SPAN):
            wide = pl.ds(j, SPAN)
            fitted = mm(fit_rows[block, :], dst_cols[:, wide])
            misfit = 1.0 - counts[part, :, wide].reshape(GROUP * rows, SPAN).astype(F32) / fitted
            hi, lo = split(misfit)
            hi_all[:, wide] = hi
            lo_all[:, wide] = lo
            total = None
            for k in range(GROUP):
                left = fit_cols[s * GROUP + k]
                both = mm(left, hi[k * rows:(k + 1) * rows])
                term = both[:q1] + (both[q1:] + mm(left[:q1], lo[k * rows:(k + 1) * rows]))
                total = term if total is None else total + term
            if s == 0:
                dst_sum[:, wide] = total
            else:
                dst_sum[:, wide] += total
        both = mm(hi_all[...], dst_rows[...])
        through[block, :] = both[:, :q1] + (both[:, q1:] + mm(lo_all[...], dst_rows[:, :q1]))
        sends.append(pltpu.make_async_copy(through.at[block], through_hbm.at[block], sems.at[3 + steps + s]))
        sends[-1].start()
    turned[...] = dst_sum[...].T.reshape(turned.shape)
    for s, out in enumerate((a0, a1, a2, a3)):
        out[...] = turned[lax.rem(x + s, X)]
    for copy in sends:
        copy.wait()


def first_call(hour, counts, src, dst, core):
    hours, rows, cols = counts.shape
    rank, p1, q1 = core.shape
    block = cols // X
    out = [struct(block, q1)] * X + [struct(hours, p1, q1), struct(hours * rows, q1)]
    return pl.pallas_call(
        first_kernel,
        out_shape=out,
        in_specs=[SMEM] + [HBM] * 4,
        out_specs=[VMEM] * (X + 1) + [HBM],
        scratch_shapes=[
            pltpu.VMEM(counts.shape, jnp.int32),
            pltpu.VMEM(src.shape, F32),
            pltpu.VMEM(dst.shape, F32),
            pltpu.VMEM(core.shape, F32),
            pltpu.VMEM((hours * rows, 3 * q1), BF16),
            pltpu.VMEM((hours, 2 * q1, rows), BF16),
            pltpu.VMEM((3 * q1, cols), BF16),
            pltpu.VMEM((cols, 2 * q1), BF16),
            pltpu.VMEM((GROUP * rows, cols), BF16),
            pltpu.VMEM((GROUP * rows, cols), BF16),
            pltpu.VMEM((q1, cols), F32),
            pltpu.VMEM((X, block, q1), F32),
            pltpu.VMEM((hours * rows, q1), F32),
            pltpu.SemaphoreType.DMA((3 + 2 * (hours // GROUP),)),
        ],
        compiler_params=params(60),
        cost_estimate=cost(2 * 9 * counts.size * q1, 14 << 20),
        name="misfit_terms",
    )(hour, counts, src, dst, core)


def second_kernel(through, src, core, core_hours,
                  m0, m1, m2, m3, src_own, src_send,
                  projected, rowsums, message):
    hours = core_hours.shape[0]
    rows = src.shape[0]
    rank, p1, q1 = core.shape
    zs = message.shape[1]
    x, c = lax.axis_index("x"), lax.axis_index("core")
    src_cols = halves(src[...].T, 0)
    src_sum = None
    for k in range(hours):
        th = halves(through[k * rows:(k + 1) * rows, :], 1)
        right = halves(core_hours[k].T, 1)
        both = mm(th, jnp.concatenate([right, right], axis=0))
        both = both[:, :p1] + both[:, p1:]
        src_sum = both if src_sum is None else src_sum + both
        both = mm(src_cols, th)
        both = both[:p1] + both[p1:]
        projected[k] = both[:, :q1] + both[:, q1:]
    half = rows // CORES

    @pl.when(c == 0)
    def _():
        src_own[...] = src_sum[:half]
        src_send[...] = src_sum[half:]

    @pl.when(c == 1)
    def _():
        src_own[...] = src_sum[half:]
        src_send[...] = src_sum[:half]

    for k in range(hours):
        here = projected[k]
        for r in range(rank):
            product = (here * core[r]).reshape(p1 // 8, 8, q1)
            at = k * rank + r
            rowsums[at:at + 1, :] = jnp.sum(jnp.sum(product, axis=0), axis=0, keepdims=True)
        for z in range(zs):
            for b in range(X):
                start = (z * X + b) * 4
                message[b, z, 4 * k:4 * k + 4, :] = here[start:start + 4]
    sums = jnp.sum(rowsums[...].T, axis=0, keepdims=True)
    spare = jnp.zeros((8 - sums.shape[1] // 128, 128), F32)
    tail = jnp.concatenate([sums[:, i:i + 128] for i in range(0, sums.shape[1], 128)] + [spare], axis=0)
    for s, out in enumerate((m0, m1, m2, m3)):
        out[:zs] = message[lax.rem(x + s, X)]
        out[zs, :8, :] = tail


def second_call(through, src, core, core_hours, zs):
    hours = core_hours.shape[0]
    rows = src.shape[0]
    rank, p1, q1 = core.shape
    share = hours * p1 // (zs * X)
    return pl.pallas_call(
        second_kernel,
        out_shape=[struct(zs + 1, share, q1)] * X + [struct(rows // CORES, p1)] * 2,
        in_specs=[VMEM] * 4,
        out_specs=[VMEM] * (X + 2),
        scratch_shapes=[
            pltpu.VMEM((hours, p1, q1), F32),
            pltpu.VMEM((hours * rank, q1), F32),
            pltpu.VMEM((X, zs, share, q1), F32),
        ],
        compiler_params=params(16),
        cost_estimate=cost(2 << 30, 12 << 20),
        name="src_and_projected",
    )(through, src, core, core_hours)


def sum_kernel(a0, a1, a2, a3, out):
    out[...] = (a0[...] + a1[...]) + (a2[...] + a3[...])


def sum_call(parts):
    return pl.pallas_call(
        sum_kernel, out_shape=struct(*parts[0].shape), in_specs=[VMEM] * 4, out_specs=VMEM,
        compiler_params=params(4), cost_estimate=cost(1 << 34, 1 << 20), name="x_sums",
    )(*parts)


def z_kernel(a, m0, m1, m2, m3, out):
    zs, share, _ = a.shape
    total = jnp.sum(a[...], axis=0)
    m = (m0[...] + m1[...]) + (m2[...] + m3[...])
    for z in range(zs):
        out[z, :share, :] = total
        out[z, share:2 * share, :] = m[z]
        out[z, 2 * share:, :] = m[zs, :8]


def z_call(a, m):
    zs, share, q1 = a.shape
    return pl.pallas_call(
        z_kernel, out_shape=struct(zs, 2 * share + 8, q1), in_specs=[VMEM] * 5, out_specs=VMEM,
        compiler_params=params(8), cost_estimate=cost(1 << 20, 1 << 20), name="z_terms",
    )(a, *m)


def back_kernel(w, src_own, src_came, block, copies):
    zs, rows, _ = w.shape
    share = (rows - 8) // 2
    tail = w[0, share:, :]
    block[:share, :] = w[0, :share, :]
    for z in range(1, zs):
        block[z * share:(z + 1) * share, :] = w[z, :share, :]
        tail = tail + w[z, share:, :]
    total = src_own[...] + src_came[...]
    for d in range(copies.shape[0]):
        copies[d, :share + 8, :] = tail
        copies[d, share + 8:, :] = total


def back_call(w, src_own, src_came, devices):
    zs, rows, q1 = w.shape
    share = (rows - 8) // 2
    return pl.pallas_call(
        back_kernel,
        out_shape=[struct(zs * share, q1), struct(devices, rows - share + src_own.shape[0], q1)],
        in_specs=[VMEM] * 3, out_specs=[VMEM] * 2,
        compiler_params=params(8), cost_estimate=cost(1 << 20, 1 << 20), name="z_sums",
    )(w, src_own, src_came)


def end_kernel(scales, hour_ref, b0, b1, b2, b3, d, src_out, dst_out, hour_out, core_out):
    x = lax.axis_index("x")
    src_scale, dst_scale, hour_scale, core_scale = scales
    for s, block in enumerate((b0, b1, b2, b3)):
        dst_out[lax.rem(x - s + X, X)] = block[...] * dst_scale
    hours, rank = hour_ref.shape
    share = 4 * hours
    total = jnp.sum(d[:, :share + 8, :], axis=0)
    for c in range(CORES):
        half = d[c, share + 8:, :]
        for at in range(c + CORES, d.shape[0], CORES):
            half = half + d[at, share + 8:, :]
        src_out[c] = half * src_scale
    each = 128 // rank
    for k in range(hours):
        row = share + k // each
        hour_out[k:k + 1, :] = total[row:row + 1, k % each * rank:(k % each + 1) * rank] * hour_scale
    tiles = [total[4 * k:4 * k + 4] * core_scale for k in range(hours)]
    for r in range(rank):
        out = hour_ref[0, r] * tiles[0]
        for k in range(1, hours):
            out = out + hour_ref[k, r] * tiles[k]
        core_out[r] = out


def end_call(scales, hour, blocks, d):
    block, q1 = blocks[0].shape
    hours, rank = hour.shape
    return pl.pallas_call(
        functools.partial(end_kernel, scales),
        in_specs=[SMEM] + [VMEM] * (X + 1),
        out_specs=[VMEM] * 4,
        out_shape=[struct(CORES, d.shape[1] - 4 * hours - 8, q1), struct(X, block, q1),
                   struct(hours, rank), struct(rank, 4, q1)],
        compiler_params=params(8), cost_estimate=cost(1 << 20, 1 << 20), name="outputs",
    )(hour, *blocks, d)


def shifted(x, axis, s):
    n = lax.axis_size(axis)
    return lax.ppermute(x, axis, [(i, (i + s) % n) for i in range(n)])


def swapped(x, axis):
    return lax.all_to_all(x, axis, split_axis=0, concat_axis=0, tiled=True)


def shards(scales, counts, src_factor, dst_factor, hour_factor, core):
    zs = lax.axis_size("z")
    dst_axes = ("y", "core")
    devices = lax.axis_size(dst_axes)
    q1 = dst_factor.shape[1]
    a0, a1, a2, a3, core_hours, through = first_call(hour_factor, counts, src_factor, dst_factor, core)
    came = [shifted(a, "x", s) for s, a in ((1, a1), (2, a2), (3, a3))]
    m0, m1, m2, m3, src_own, src_send = second_call(through, src_factor, core, core_hours, zs)
    src_came = shifted(src_send, "core", 1)
    m = [m0] + [shifted(v, "x", s) for s, v in ((1, m1), (2, m2), (3, m3))]
    came = lax.optimization_barrier((*came, src_own))[:3]
    a = sum_call([a0, *came])
    a = swapped(a.reshape(zs, -1, q1), "z")
    w = swapped(z_call(a, m), "z")
    block, copies = back_call(w, src_own, src_came, devices)
    shares = swapped(copies, dst_axes)
    blocks = [block] + [shifted(block, "x", s) for s in (1, 2, 3)]
    grad_src, grad_dst, grad_hour, grad_core = end_call(scales, hour_factor, blocks, shares)
    return (grad_src.reshape(src_factor.shape), grad_dst.reshape(dst_factor.shape), grad_hour, grad_core)


def solution(mesh):
    n_src, n_dst = mesh.shape["src"], mesh.shape["dst"]
    fine = Mesh(mesh.devices.reshape(n_src // X, X, n_dst // CORES, CORES), ("z", "x", "y", "core"))
    src, dst = ("z", "x"), ("y", "core")
    in_specs = (P(None, src, dst), P(src, None), P(dst, None), P(), P())
    out_specs = (P(src, None), P(dst, None), P(), P(None, src, None))

    def run(counts, src_factor, dst_factor, hour_factor, core):
        hours, total_src, total_dst = counts.shape
        scales = (1 / math.sqrt(total_dst * hours), 1 / math.sqrt(total_src * hours),
                  1 / math.sqrt(total_src * total_dst), 1 / math.sqrt(total_src * total_dst * hours))
        body = jax.shard_map(functools.partial(shards, scales), mesh=fine, in_specs=in_specs,
                             out_specs=out_specs, check_vma=False)
        return body(counts, src_factor, dst_factor, hour_factor, core)

    return run
```

time: 84.1 us -> 83.6 us (level)
  waiting for transfers between devices: 19.7 us -> 23.6 us
  Pallas kernels: 22.5 us -> 19.7 us
  starting transfers between devices: 37.6 us -> 35 us
  local copies, waits for them, and re-layouts: 1.76 us -> 3.18 us
    all_to_all x3, waiting for transfers between devices: 1.62 us -> 9.58 us  [swapped(): return lax.all_to_all(x, axis, split_axis=0, concat_axis=0, tiled=True)]
    pallas_call x1, Pallas kernels: 8.04 us -> 2.41 us  [second_call(): pl.pallas_call(second_kernel, out_shape=[struct(zs + 1, share, q1)] * X +...]
    ppermute x13 -> x10, waiting for transfers between devices: 18.1 us -> 14.1 us  [shifted(): return lax.ppermute(x, axis, [(i, (i + s) % n) for i in range(n)])]
    pallas_call x2, Pallas kernels: 11.4 us -> 14.1 us  [the longest x1 13.4 us: first_call(): pl.pallas_call(first_kernel, out_shape=out, in_specs=[SMEM] + [HBM] * 4,...]
    ppermute x13 -> x10, starting transfers between devices: 17.3 us -> 14.7 us  [shifted(): return lax.ppermute(x, axis, [(i, (i + s) % n) for i in range(n)])]
    unnamed x8 -> x12, local copies, waits for them, and re-layouts: 1.76 us -> 3.18 us
  transfers between devices with their start and end apart: 16 -> 13, of which waited for: 8 -> 8; matrix products, arithmetic and copies ran while one was open for 0% -> 0% of each run, Pallas kernels for 10% -> 3%
where the time goes in v3:
time: 83.6 us; the launch traced here: 82.2 us
  starting transfers between devices  35 us (42%)
  waiting for transfers between devices  23.6 us (28%)
  Pallas kernels  19.7 us (24%)
  local copies, waits for them, and re-layouts  3.18 us (4%)
    all_to_all x3, starting transfers between devices, swapped(): return lax.all_to_all(x, axis, split_axis=0, concat_axis=0, tiled=True)  20.3 us
    ppermute x10, starting transfers between devices, shifted(): return lax.ppermute(x, axis, [(i, (i + s) % n) for i in range(n)])  14.7 us
    ppermute x10, waiting for transfers between devices, shifted(): return lax.ppermute(x, axis, [(i, (i + s) % n) for i in range(n)])  14.1 us
    pallas_call x1, Pallas kernels, first_call(): pl.pallas_call(first_kernel, out_shape=out, in_specs=[SMEM] + [HBM] * 4,...  13.4 us
    all_to_all x3, waiting for transfers between devices, swapped(): return lax.all_to_all(x, axis, split_axis=0, concat_axis=0, tiled=True)  9.58 us
    unnamed x12, local copies, waits for them, and re-layouts  3.18 us
    pallas_call x1, Pallas kernels, second_call(): pl.pallas_call(second_kernel, out_shape=[struct(zs + 1, share, q1)] * X +...  2.41 us
  transfers between devices with their start and end apart: 13, of which 8 were waited for; matrix products, arithmetic and copies ran while one was open for 0% of the time, Pallas kernels for 3%

profile of v3, /device:TPU:8, one launch (start us, length us, event | category | flops | bytes accessed | tf_op | source)
XLA Modules:
  0.0 82.2 jit_solution(325021456480589558)
XLA Ops:
  0.7 13.4 %misfit_terms.1 = (f32[256,128]{1,0:T(8,128)}, f32[256,128]{1,0:T(8,128)}, f32[256,128]{1,0:T(8,128)}, f32[256,128]{1,0:T(8,128)}, f32[8,128,128]{2,1,0:T(8,128)}, /*index=5*/f32[2048,128]{1,0:T(8,128)}) custom-call(f32[8,32]{1,0:T(8,128)} %hour_ref.3, s32[8,256,1024]{2,1,0:T(8,128)} %counts_hbm.1, f32[256,128]{1,0:T(8,128)} %src.1, f32[1024,128]{1,0:T(8,128)} %dst_hbm.1, ...), custom_call_target="tpu_custom_call" | custom-call | flops 4831838208 | bytes 14680064 | tf_op jit(solution)/shard_map/misfit_terms/pallas_call | solution.py:117
  14.1 1.6 %collective-permute-start = (f32[256,128]{1,0:T(8,128)}, f32[256,128]{1,0:T(8,128)S(1)}, u32[]{:S(2)}, u32[]{:S(2)}) collective-permute-start(f32[256,128]{1,0:T(8,128)} %get-tuple-element.26), channel_id=1, source_target_pairs={{0,8},{8,16},{16,24},{24,0},{1,9},{9,17},{17,25},{25,1},{2,10},{10... | collective-permute-start | bytes 393224 | tf_op jit(solution)/shard_map/ppermute | solution.py:308
  15.7 2.7 %collective-permute-start.1 = (f32[256,128]{1,0:T(8,128)}, f32[256,128]{1,0:T(8,128)S(1)}, u32[]{:S(2)}, u32[]{:S(2)}) collective-permute-start(f32[256,128]{1,0:T(8,128)} %get-tuple-element.27), channel_id=1, source_target_pairs={{0,16},{8,24},{16,0},{24,8},{1,17},{9,25},{17,1},{25,9},{2,18},{10... | collective-permute-start | bytes 393224 | tf_op jit(solution)/shard_map/ppermute | solution.py:308
  18.4 1.4 %collective-permute-start.2 = (f32[256,128]{1,0:T(8,128)}, f32[256,128]{1,0:T(8,128)S(1)}, u32[]{:S(2)}, u32[]{:S(2)}) collective-permute-start(f32[256,128]{1,0:T(8,128)} %get-tuple-element.28), channel_id=1, source_target_pairs={{0,24},{8,0},{16,8},{24,16},{1,25},{9,1},{17,9},{25,17},{2,26},{10... | collective-permute-start | bytes 393224 | tf_op jit(solution)/shard_map/ppermute | solution.py:308
  19.8 1.2 %copy-done.3 = f32[2048,128]{1,0:T(8,128)S(1)} copy-done((f32[2048,128]{1,0:T(8,128)S(1)}, f32[2048,128]{1,0:T(8,128)}, u32[]{:S(2)}) %copy-start.3) | copy-done | bytes 1048600
  21.0 1.0 %copy-done.4 = f32[8,128,128]{2,1,0:T(8,128)S(1)} copy-done((f32[8,128,128]{2,1,0:T(8,128)S(1)}, f32[8,128,128]{2,1,0:T(8,128)}, u32[]{:S(2)}) %copy-start.4) | copy-done | bytes 524312
  22.1 2.4 %src_and_projected.1 = (f32[9,32,128]{2,1,0:T(8,128)S(1)}, f32[9,32,128]{2,1,0:T(8,128)S(1)}, f32[9,32,128]{2,1,0:T(8,128)S(1)}, f32[9,32,128]{2,1,0:T(8,128)S(1...) custom-call(f32[2048,128]{1,0:T(8,128)S(1)} %copy-done.3, f32[256,128]{1,0:T(8,128)S(1)} %copy-done.2, ...), custom_call_target="tpu_custom_call" | custom-call | flops 2147483648 | bytes 12582912 | tf_op jit(solution)/shard_map/src_and_projected/pallas_call | solution.py:198
  26.2 8.5 %all-to-all-start = ((f32[8,32,128]{2,1,0:T(8,128)}), f32[8,32,128]{2,1,0:T(8,128)S(1)}, u32[]{:S(2)}, u32[]{:S(2)}) async-start(f32[8,32,128]{2,1,0:T(8,128)} %bitcast), calls=%async_computation | async-start | bytes 262144 | tf_op jit(solution)/shard_map/all_to_all | solution.py:312
  34.7 1.3 %collective-permute-start.3 = (f32[9,32,128]{2,1,0:T(8,128)S(1)}, f32[9,32,128]{2,1,0:T(8,128)S(1)}, u32[]{:S(2)}, u32[]{:S(2)}) collective-permute-start(f32[9,32,128]{2,1,0:T(8,128)S(1)} %get-tuple-element.36), channel_id=1, source_target_pairs={{0,8},{8,16},{16,24},{24,0},{1,9},{9,17},{17,25},{25,1},{2,10},{10... | collective-permute-start | bytes 442376 | tf_op jit(solution)/shard_map/ppermute | solution.py:308
  36.0 2.4 %collective-permute-start.4 = (f32[9,32,128]{2,1,0:T(8,128)S(1)}, f32[9,32,128]{2,1,0:T(8,128)S(1)}, u32[]{:S(2)}, u32[]{:S(2)}) collective-permute-start(f32[9,32,128]{2,1,0:T(8,128)S(1)} %get-tuple-element.37), channel_id=1, source_target_pairs={{0,16},{8,24},{16,0},{24,8},{1,17},{9,25},{17,1},{25,9},{2,18},{10... | collective-permute-start | bytes 442376 | tf_op jit(solution)/shard_map/ppermute | solution.py:308
  38.4 1.6 %collective-permute-start.5 = (f32[9,32,128]{2,1,0:T(8,128)S(1)}, f32[9,32,128]{2,1,0:T(8,128)S(1)}, u32[]{:S(2)}, u32[]{:S(2)}) collective-permute-start(f32[9,32,128]{2,1,0:T(8,128)S(1)} %get-tuple-element.38), channel_id=1, source_target_pairs={{0,24},{8,0},{16,8},{24,16},{1,25},{9,1},{17,9},{25,17},{2,26},{10... | collective-permute-start | bytes 442376 | tf_op jit(solution)/shard_map/ppermute | solution.py:308
  40.0 2.6 %collective-permute-done.3.m1 = f32[9,32,128]{2,1,0:T(8,128)S(1)} collective-permute-done((f32[9,32,128]{2,1,0:T(8,128)S(1)}, f32[9,32,128]{2,1,0:T(8,128)S(1)}, u32[]{:S(2)}, u32[]{:S(2)}) %collective-permute-start.3) | collective-permute-done | bytes 147488 | tf_op jit(solution)/shard_map/ppermute | solution.py:308
  42.6 1.6 %collective-permute-done.4.m2 = f32[9,32,128]{2,1,0:T(8,128)S(1)} collective-permute-done((f32[9,32,128]{2,1,0:T(8,128)S(1)}, f32[9,32,128]{2,1,0:T(8,128)S(1)}, u32[]{:S(2)}, u32[]{:S(2)}) %collective-permute-start.4) | collective-permute-done | bytes 147488 | tf_op jit(solution)/shard_map/ppermute | solution.py:308
  44.9 6.9 %all-to-all-start.1 = ((f32[8,72,128]{2,1,0:T(8,128)}), f32[8,72,128]{2,1,0:T(8,128)S(1)}, u32[]{:S(2)}, u32[]{:S(2)}) async-start(f32[8,72,128]{2,1,0:T(8,128)} %z_terms.1), calls=%async_computation.1 | async-start | bytes 589824 | tf_op jit(solution)/shard_map/all_to_all | solution.py:312
  51.9 1.2 %collective-permute-done.6.src_came = f32[128,128]{1,0:T(8,128)S(1)} collective-permute-done((f32[128,128]{1,0:T(8,128)S(1)}, f32[128,128]{1,0:T(8,128)S(1)}, u32[]{:S(2)}, u32[]{:S(2)}) %collective-permute-start.6) | collective-permute-done | bytes 65568 | tf_op jit(solution)/shard_map/ppermute | solution.py:308
  53.1 9.6 %all-to-all-done.1.w = f32[8,72,128]{2,1,0:T(8,128)S(1)} async-done(((f32[8,72,128]{2,1,0:T(8,128)}), f32[8,72,128]{2,1,0:T(8,128)S(1)}, u32[]{:S(2)}, u32[]{:S(2)}) %all-to-all-start.1) | async-done | bytes 294944 | tf_op jit(solution)/shard_map/all_to_all | solution.py:312
  62.7 0.9 %z_sums.1 = (f32[256,128]{1,0:T(8,128)S(1)}, f32[8,168,128]{2,1,0:T(8,128)}) custom-call(f32[8,72,128]{2,1,0:T(8,128)S(1)} %all-to-all-done.1.w, f32[128,128]{1,0:T(8,128)S(1)} %get-tuple-element.31.src_own, f32[128,128]{1,0:T(8,128)S(1)} %collective-permute-done.6.src_came), custom_call_target="tpu_custom_call" | custom-call | flops 1048576 | bytes 1048576 | tf_op jit(solution)/shard_map/z_sums/pallas_call | solution.py:260
  63.6 4.9 %all-to-all-start.2 = ((f32[8,168,128]{2,1,0:T(8,128)}), f32[8,168,128]{2,1,0:T(8,128)S(1)}, u32[]{:S(2)}, u32[]{:S(2)}) async-start(f32[8,168,128]{2,1,0:T(8,128)} %get-tuple-element.41), calls=%async_computation.2 | async-start | bytes 1376256 | tf_op jit(solution)/shard_map/all_to_all | solution.py:312
  68.6 2.6 %collective-permute-start.9 = (f32[256,128]{1,0:T(8,128)S(1)}, f32[256,128]{1,0:T(8,128)S(1)}, u32[]{:S(2)}, u32[]{:S(2)}) collective-permute-start(f32[256,128]{1,0:T(8,128)S(1)} %get-tuple-element.40.b0), channel_id=1, source_target_pairs={{0,24},{8,0},{16,8},{24,16},{1,25},{9,1},{17,9},{25,17},{2,26},{10... | collective-permute-start | bytes 393224 | tf_op jit(solution)/shard_map/ppermute | solution.py:308
  71.1 1.1 %collective-permute-start.8 = (f32[256,128]{1,0:T(8,128)S(1)}, f32[256,128]{1,0:T(8,128)S(1)}, u32[]{:S(2)}, u32[]{:S(2)}) collective-permute-start(f32[256,128]{1,0:T(8,128)S(1)} %get-tuple-element.40.b0), channel_id=1, source_target_pairs={{0,16},{8,24},{16,0},{24,8},{1,17},{9,25},{17,1},{25,9},{2,18},{10... | collective-permute-start | bytes 393224 | tf_op jit(solution)/shard_map/ppermute | solution.py:308
  72.2 4.8 %collective-permute-done.9.b3 = f32[256,128]{1,0:T(8,128)S(1)} collective-permute-done((f32[256,128]{1,0:T(8,128)S(1)}, f32[256,128]{1,0:T(8,128)S(1)}, u32[]{:S(2)}, u32[]{:S(2)}) %collective-permute-start.9) | collective-permute-done | bytes 131104 | tf_op jit(solution)/shard_map/ppermute | solution.py:308
  77.0 2.0 %collective-permute-done.8.b2 = f32[256,128]{1,0:T(8,128)S(1)} collective-permute-done((f32[256,128]{1,0:T(8,128)S(1)}, f32[256,128]{1,0:T(8,128)S(1)}, u32[]{:S(2)}, u32[]{:S(2)}) %collective-permute-start.8) | collective-permute-done | bytes 131104 | tf_op jit(solution)/shard_map/ppermute | solution.py:308
  79.0 1.7 %collective-permute-done.7.b1 = f32[256,128]{1,0:T(8,128)S(1)} collective-permute-done((f32[256,128]{1,0:T(8,128)S(1)}, f32[256,128]{1,0:T(8,128)S(1)}, u32[]{:S(2)}, u32[]{:S(2)}) %collective-permute-start.7) | collective-permute-done | bytes 131104 | tf_op jit(solution)/shard_map/ppermute | solution.py:308
  80.7 1.5 %outputs.1 = (f32[2,128,128]{2,1,0:T(8,128)}, f32[4,256,128]{2,1,0:T(8,128)}, f32[8,32]{1,0:T(8,128)}, f32[32,4,128]{2,1,0:T(4,128)}) custom-call(f32[8,32]{1,0:T(8,128)S(1)} %copy-done, f32[256,128]{1,0:T(8,128)S(1)} %get-tuple-element.40.b0, f32[256,128]{1,0:T(8,128)S(1)} %collective-permute-done.7.b1, f32[256,128]{1,0:T(8,128)S(1)} %collective-permute-done.8.b2, ...), custom_call_target="tpu_custom_call" | custom-call | flops 1048576 | bytes 1048576 | tf_op jit(solution)/shard_map/outputs/pallas_call | solution.py:296
  (20 shorter events, 2.5 us)
Async XLA Ops:
  0.6 19.2 %copy-start.1 = (f32[32,128,128]{2,1,0:T(8,128)S(1)}, f32[32,128,128]{2,1,0:T(8,128)}, u32[]{:S(2)}) copy-start(f32[32,128,128]{2,1,0:T(8,128)} %core.1) | copy-start | bytes 6291460
  0.6 19.2 %copy-start.2 = (f32[256,128]{1,0:T(8,128)S(1)}, f32[256,128]{1,0:T(8,128)}, u32[]{:S(2)}) copy-start(f32[256,128]{1,0:T(8,128)} %src.1) | copy-start | bytes 393220
  14.1 10.4 %collective-permute-start = (f32[256,128]{1,0:T(8,128)}, f32[256,128]{1,0:T(8,128)S(1)}, u32[]{:S(2)}, u32[]{:S(2)}) collective-permute-start(f32[256,128]{1,0:T(8,128)} %get-tuple-element.26), channel_id=1, source_target_pairs={{0,8},{8,16},{16,24},{24,0},{1,9},{9,17},{17,25},{25,1},{2,10},{10... | collective-permute-start | bytes 393224 | tf_op jit(solution)/shard_map/ppermute | solution.py:308
  15.7 8.9 %collective-permute-start.1 = (f32[256,128]{1,0:T(8,128)}, f32[256,128]{1,0:T(8,128)S(1)}, u32[]{:S(2)}, u32[]{:S(2)}) collective-permute-start(f32[256,128]{1,0:T(8,128)} %get-tuple-element.27), channel_id=1, source_target_pairs={{0,16},{8,24},{16,0},{24,8},{1,17},{9,25},{17,1},{25,9},{2,18},{10... | collective-permute-start | bytes 393224 | tf_op jit(solution)/shard_map/ppermute | solution.py:308
  18.4 6.2 %collective-permute-start.2 = (f32[256,128]{1,0:T(8,128)}, f32[256,128]{1,0:T(8,128)S(1)}, u32[]{:S(2)}, u32[]{:S(2)}) collective-permute-start(f32[256,128]{1,0:T(8,128)} %get-tuple-element.28), channel_id=1, source_target_pairs={{0,24},{8,0},{16,8},{24,16},{1,25},{9,1},{17,9},{25,17},{2,26},{10... | collective-permute-start | bytes 393224 | tf_op jit(solution)/shard_map/ppermute | solution.py:308
  19.8 1.2 %copy-start.3 = (f32[2048,128]{1,0:T(8,128)S(1)}, f32[2048,128]{1,0:T(8,128)}, u32[]{:S(2)}) copy-start(f32[2048,128]{1,0:T(8,128)} %get-tuple-element.29.through) | copy-start | bytes 3145732
  21.0 1.0 %copy-start.4 = (f32[8,128,128]{2,1,0:T(8,128)S(1)}, f32[8,128,128]{2,1,0:T(8,128)}, u32[]{:S(2)}) copy-start(f32[8,128,128]{2,1,0:T(8,128)} %get-tuple-element.30.core_hours) | copy-start | bytes 1572868
  24.6 0.9 %copy-start.5 = (f32[256,128]{1,0:T(8,128)S(1)}, f32[256,128]{1,0:T(8,128)}, u32[]{:S(2)}) copy-start(f32[256,128]{1,0:T(8,128)} %get-tuple-element.25.a0) | copy-start | bytes 393220
  25.5 55.2 %copy-start = (f32[8,32]{1,0:T(8,128)S(1)}, f32[8,32]{1,0:T(8,128)}, u32[]{:S(2)}) copy-start(f32[8,32]{1,0:T(8,128)} %hour_ref.3) | copy-start | bytes 3076
  26.2 18.0 %all-to-all-start = ((f32[8,32,128]{2,1,0:T(8,128)}), f32[8,32,128]{2,1,0:T(8,128)S(1)}, u32[]{:S(2)}, u32[]{:S(2)}) async-start(f32[8,32,128]{2,1,0:T(8,128)} %bitcast), calls=%async_computation | async-start | bytes 262144 | tf_op jit(solution)/shard_map/all_to_all | solution.py:312
  34.7 7.9 %collective-permute-start.3 = (f32[9,32,128]{2,1,0:T(8,128)S(1)}, f32[9,32,128]{2,1,0:T(8,128)S(1)}, u32[]{:S(2)}, u32[]{:S(2)}) collective-permute-start(f32[9,32,128]{2,1,0:T(8,128)S(1)} %get-tuple-element.36), channel_id=1, source_target_pairs={{0,8},{8,16},{16,24},{24,0},{1,9},{9,17},{17,25},{25,1},{2,10},{10... | collective-permute-start | bytes 442376 | tf_op jit(solution)/shard_map/ppermute | solution.py:308
  36.0 8.2 %collective-permute-start.4 = (f32[9,32,128]{2,1,0:T(8,128)S(1)}, f32[9,32,128]{2,1,0:T(8,128)S(1)}, u32[]{:S(2)}, u32[]{:S(2)}) collective-permute-start(f32[9,32,128]{2,1,0:T(8,128)S(1)} %get-tuple-element.37), channel_id=1, source_target_pairs={{0,16},{8,24},{16,0},{24,8},{1,17},{9,25},{17,1},{25,9},{2,18},{10... | collective-permute-start | bytes 442376 | tf_op jit(solution)/shard_map/ppermute | solution.py:308
  38.4 5.8 %collective-permute-start.5 = (f32[9,32,128]{2,1,0:T(8,128)S(1)}, f32[9,32,128]{2,1,0:T(8,128)S(1)}, u32[]{:S(2)}, u32[]{:S(2)}) collective-permute-start(f32[9,32,128]{2,1,0:T(8,128)S(1)} %get-tuple-element.38), channel_id=1, source_target_pairs={{0,24},{8,0},{16,8},{24,16},{1,25},{9,1},{17,9},{25,17},{2,26},{10... | collective-permute-start | bytes 442376 | tf_op jit(solution)/shard_map/ppermute | solution.py:308
  44.9 17.8 %all-to-all-start.1 = ((f32[8,72,128]{2,1,0:T(8,128)}), f32[8,72,128]{2,1,0:T(8,128)S(1)}, u32[]{:S(2)}, u32[]{:S(2)}) async-start(f32[8,72,128]{2,1,0:T(8,128)} %z_terms.1), calls=%async_computation.1 | async-start | bytes 589824 | tf_op jit(solution)/shard_map/all_to_all | solution.py:312
  51.9 1.3 %collective-permute-start.6 = (f32[128,128]{1,0:T(8,128)S(1)}, f32[128,128]{1,0:T(8,128)S(1)}, u32[]{:S(2)}, u32[]{:S(2)}) collective-permute-start(f32[128,128]{1,0:T(8,128)S(1)} %get-tuple-element.39), channel_id=1, source_target_pairs={{0,1},{1,0},{2,3},{3,2},{4,5},{5,4},{6,7},{7,6},{8,9},{9,8},{10,11... | collective-permute-start | bytes 196616 | tf_op jit(solution)/shard_map/ppermute | solution.py:308
  63.6 17.1 %all-to-all-start.2 = ((f32[8,168,128]{2,1,0:T(8,128)}), f32[8,168,128]{2,1,0:T(8,128)S(1)}, u32[]{:S(2)}, u32[]{:S(2)}) async-start(f32[8,168,128]{2,1,0:T(8,128)} %get-tuple-element.41), calls=%async_computation.2 | async-start | bytes 1376256 | tf_op jit(solution)/shard_map/all_to_all | solution.py:312
  68.6 8.5 %collective-permute-start.9 = (f32[256,128]{1,0:T(8,128)S(1)}, f32[256,128]{1,0:T(8,128)S(1)}, u32[]{:S(2)}, u32[]{:S(2)}) collective-permute-start(f32[256,128]{1,0:T(8,128)S(1)} %get-tuple-element.40.b0), channel_id=1, source_target_pairs={{0,24},{8,0},{16,8},{24,16},{1,25},{9,1},{17,9},{25,17},{2,26},{10... | collective-permute-start | bytes 393224 | tf_op jit(solution)/shard_map/ppermute | solution.py:308
  71.1 7.9 %collective-permute-start.8 = (f32[256,128]{1,0:T(8,128)S(1)}, f32[256,128]{1,0:T(8,128)S(1)}, u32[]{:S(2)}, u32[]{:S(2)}) collective-permute-start(f32[256,128]{1,0:T(8,128)S(1)} %get-tuple-element.40.b0), channel_id=1, source_target_pairs={{0,16},{8,24},{16,0},{24,8},{1,17},{9,25},{17,1},{25,9},{2,18},{10... | collective-permute-start | bytes 393224 | tf_op jit(solution)/shard_map/ppermute | solution.py:308
  72.2 8.5 %collective-permute-start.7 = (f32[256,128]{1,0:T(8,128)S(1)}, f32[256,128]{1,0:T(8,128)S(1)}, u32[]{:S(2)}, u32[]{:S(2)}) collective-permute-start(f32[256,128]{1,0:T(8,128)S(1)} %get-tuple-element.40.b0), channel_id=1, source_target_pairs={{0,8},{8,16},{16,24},{24,0},{1,9},{9,17},{17,25},{25,1},{2,10},{10... | collective-permute-start | bytes 393224 | tf_op jit(solution)/shard_map/ppermute | solution.py:308

commit v4 on v3

v4 whole, which is shorter than its diff:
```python
import functools
import math

import jax
import jax.numpy as jnp
from jax import lax
from jax.experimental import pallas as pl
from jax.experimental.pallas import tpu as pltpu
from jax.sharding import Mesh, PartitionSpec as P

X = 4
CORES = 2
GROUP = 4
SPAN = 512
F32 = jnp.float32
BF16 = jnp.bfloat16
HBM = pl.BlockSpec(memory_space=pltpu.HBM)
VMEM = pl.BlockSpec(memory_space=pltpu.VMEM)
SMEM = pl.BlockSpec(memory_space=pltpu.SMEM)


def struct(*shape, dtype=F32):
    return jax.ShapeDtypeStruct(shape, dtype)


def params(mib):
    return pltpu.CompilerParams(vmem_limit_bytes=mib << 20)


def cost(flops, size):
    return pl.CostEstimate(flops=flops, bytes_accessed=size, transcendentals=0)


def split(x):
    hi = x.astype(BF16)
    return hi, (x - hi.astype(F32)).astype(BF16)


def mm(a, b):
    return jnp.dot(a, b, preferred_element_type=F32)


def halves(x, axis):
    return jnp.concatenate(split(x), axis=axis)


def main_kernel(zs, hour_ref, counts_hbm, src_hbm, dst_hbm, core_hbm,
                m0, m1, m2, m3, src_own, src_send,
                counts, src, dst, core, fit_rows, fit_cols, dst_cols, dst_rows, hi_all, lo_all, dst_sum, turned,
                core_hours, projected, rowsums, message, sems):
    hours, rows, cols = counts.shape
    rank, p1, q1 = core.shape
    steps = hours // GROUP
    block = turned.shape[1]
    x, c = lax.axis_index("x"), lax.axis_index("core")
    outs = (m0, m1, m2, m3)
    small = [pltpu.make_async_copy(a, b, sems.at[i])
             for i, (a, b) in enumerate(((core_hbm, core), (src_hbm, src), (dst_hbm, dst)))]
    parts = [pl.ds(s * GROUP, GROUP) for s in range(steps)]
    large = [pltpu.make_async_copy(counts_hbm.at[part], counts.at[part], sems.at[3 + s])
             for s, part in enumerate(parts)]
    for copy in small + large:
        copy.start()
    small[2].wait()
    dst_rows[...] = halves(dst[...], 1)
    hi, lo = split(dst[...].T)
    dst_cols[...] = jnp.concatenate([hi, hi, lo], axis=0)
    small[0].wait()
    small[1].wait()
    hi, lo = split(src[...])
    src_rows = jnp.concatenate([hi, lo, hi], axis=1)
    for k in range(hours):
        core_hour = hour_ref[k, 0] * core[0]
        for r in range(1, rank):
            core_hour = core_hour + hour_ref[k, r] * core[r]
        core_hours[k] = core_hour
        hi, lo = split(core_hour)
        fit = mm(src_rows, jnp.concatenate([hi, hi, lo], axis=0))
        hi, lo = split(fit)
        fit_rows[k * rows:(k + 1) * rows] = jnp.concatenate([hi, lo, hi], axis=1)
        fit_cols[k] = halves(fit.T, 0)
    src_cols = halves(src[...].T, 0)
    src_sum = None
    for s, part in enumerate(parts):
        large[s].wait()
        for j in range(0, cols, SPAN):
            wide = pl.ds(j, SPAN)
            fitted = mm(fit_rows[s * GROUP * rows:(s + 1) * GROUP * rows, :], dst_cols[:, wide])
            misfit = 1.0 - counts[part, :, wide].reshape(GROUP * rows, SPAN).astype(F32) / fitted
            hi, lo = split(misfit)
            hi_all[:, wide] = hi
            lo_all[:, wide] = lo
            total = None
            for k in range(GROUP):
                left = fit_cols[s * GROUP + k]
                both = mm(left, hi[k * rows:(k + 1) * rows])
                term = both[:q1] + (both[q1:] + mm(left[:q1], lo[k * rows:(k + 1) * rows]))
                total = term if total is None else total + term
            if s == 0:
                dst_sum[:, wide] = total
            else:
                dst_sum[:, wide] += total
        both = mm(hi_all[...], dst_rows[...])
        through = both[:, :q1] + (both[:, q1:] + mm(lo_all[...], dst_rows[:, :q1]))
        for i in range(GROUP):
            k = s * GROUP + i
            th = halves(through[i * rows:(i + 1) * rows], 1)
            right = halves(core_hours[k].T, 1)
            both = mm(th, jnp.concatenate([right, right], axis=0))
            both = both[:, :p1] + both[:, p1:]
            src_sum = both if src_sum is None else src_sum + both
            both = mm(src_cols, th)
            both = both[:p1] + both[p1:]
            projected[k] = both[:, :q1] + both[:, q1:]
    turned[...] = dst_sum[...].T.reshape(turned.shape)
    places = [lax.rem(x + s, X) for s in range(X)]
    sends = [pltpu.make_async_copy(turned.at[place], out.at[pl.ds(0, block)], sems.at[3 + steps + i])
             for i, (place, out) in enumerate(zip(places, outs))]
    for copy in sends:
        copy.start()
    half = rows // CORES

    @pl.when(c == 0)
    def _():
        src_own[...] = src_sum[:half]
        src_send[...] = src_sum[half:]

    @pl.when(c == 1)
    def _():
        src_own[...] = src_sum[half:]
        src_send[...] = src_sum[:half]

    for k in range(hours):
        here = projected[k]
        for r in range(rank):
            product = (here * core[r]).reshape(p1 // 8, 8, q1)
            at = k * rank + r
            rowsums[at:at + 1, :] = jnp.sum(jnp.sum(product, axis=0), axis=0, keepdims=True)
        for z in range(zs):
            for b in range(X):
                start = (z * X + b) * 4
                row = z * 4 * hours + 4 * k
                message[b, row:row + 4, :] = here[start:start + 4]
    sums = jnp.sum(rowsums[...].T, axis=0, keepdims=True)
    spare = jnp.zeros((8 - sums.shape[1] // 128, 128), F32)
    tail = jnp.concatenate([sums[:, i:i + 128] for i in range(0, sums.shape[1], 128)] + [spare], axis=0)
    size = message.shape[1]
    for b in range(X):
        message[b, size - 8:, :] = tail
    more = [pltpu.make_async_copy(message.at[place], out.at[pl.ds(block, size)], sems.at[3 + steps + X + i])
            for i, (place, out) in enumerate(zip(places, outs))]
    for copy in more:
        copy.start()
    for copy in sends + more:
        copy.wait()


def main_call(hour, counts, src, dst, core, zs):
    hours, rows, cols = counts.shape
    rank, p1, q1 = core.shape
    block = cols // X
    size = hours * p1 // X + 8
    return pl.pallas_call(
        functools.partial(main_kernel, zs),
        out_shape=[struct(block + size, q1)] * X + [struct(rows // CORES, p1)] * 2,
        in_specs=[SMEM] + [HBM] * 4,
        out_specs=[HBM] * X + [VMEM] * 2,
        scratch_shapes=[
            pltpu.VMEM(counts.shape, jnp.int32),
            pltpu.VMEM(src.shape, F32),
            pltpu.VMEM(dst.shape, F32),
            pltpu.VMEM(core.shape, F32),
            pltpu.VMEM((hours * rows, 3 * q1), BF16),
            pltpu.VMEM((hours, 2 * q1, rows), BF16),
            pltpu.VMEM((3 * q1, cols), BF16),
            pltpu.VMEM((cols, 2 * q1), BF16),
            pltpu.VMEM((GROUP * rows, cols), BF16),
            pltpu.VMEM((GROUP * rows, cols), BF16),
            pltpu.VMEM((q1, cols), F32),
            pltpu.VMEM((X, block, q1), F32),
            pltpu.VMEM((hours, p1, q1), F32),
            pltpu.VMEM((hours, p1, q1), F32),
            pltpu.VMEM((hours * rank, q1), F32),
            pltpu.VMEM((X, size, q1), F32),
            pltpu.SemaphoreType.DMA((3 + hours // GROUP + 2 * X,)),
        ],
        compiler_params=params(60),
        cost_estimate=cost(2 * 9 * counts.size * q1, 14 << 20),
        name="all_terms",
    )(hour, counts, src, dst, core)


def small_call(kernel, name, outs, args, flops=1 << 20):
    return pl.pallas_call(
        kernel, out_shape=outs, in_specs=[VMEM] * len(args), out_specs=jax.tree.map(lambda _: VMEM, outs),
        compiler_params=params(4), cost_estimate=cost(flops, 1 << 20), name=name,
    )(*args)


def hold_kernel(a, out):
    out[...] = a[...]


def sum_kernel(*refs):
    parts = [ref[...] for ref in refs[:-1]]
    while len(parts) > 1:
        half = len(parts) // 2
        parts = [a + b for a, b in zip(parts[:half], parts[half:])]
    refs[-1][...] = parts[0]


def summed(name, *parts):
    return small_call(sum_kernel, name, struct(*parts[0].shape), parts)


def x_kernel(m0, m1, m2, m3, out):
    zs, rows, _ = out.shape
    share = (rows - 8) // 2
    block = share * zs
    m = (m0[...] + m2[...]) + (m1[...] + m3[...])
    for z in range(zs):
        out[z, :share, :] = m[z * share:(z + 1) * share]
        out[z, share:2 * share, :] = m[block + z * share:block + (z + 1) * share]
        out[z, 2 * share:, :] = m[2 * block:]


def z_kernel(w, copies, tail):
    share = copies.shape[1]
    total = jnp.sum(w[...], axis=0)
    for z in range(copies.shape[0]):
        copies[z] = total[:share]
    tail[...] = total[share:]


def end_kernel(scales, hour_ref, b0, b1, b2, b3, t0, t1, src_own, src_other,
               src_out, dst_out, hour_out, core_out):
    x, c = lax.axis_index("x"), lax.axis_index("core")
    src_scale, dst_scale, hour_scale, core_scale = scales
    for s, block in enumerate((b0, b1, b2, b3)):
        dst_out[lax.rem(x - s + X, X)] = block[...] * dst_scale
    src_out[c] = src_own[...] * src_scale
    src_out[1 - c] = src_other[...] * src_scale
    hours, rank = hour_ref.shape
    share = 4 * hours
    total = t0[...] + t1[...]
    each = 128 // rank
    for k in range(hours):
        row = share + k // each
        hour_out[k:k + 1, :] = total[row:row + 1, k % each * rank:(k % each + 1) * rank] * hour_scale
    tiles = [total[4 * k:4 * k + 4] * core_scale for k in range(hours)]
    for r in range(rank):
        out = hour_ref[0, r] * tiles[0]
        for k in range(1, hours):
            out = out + hour_ref[k, r] * tiles[k]
        core_out[r] = out


def end_call(scales, hour, blocks, tails, src_own, src_other):
    block, q1 = blocks[0].shape
    hours, rank = hour.shape
    return pl.pallas_call(
        functools.partial(end_kernel, scales),
        in_specs=[SMEM] + [VMEM] * 8,
        out_specs=[VMEM] * 4,
        out_shape=[struct(CORES, *src_own.shape), struct(X, block, q1), struct(hours, rank), struct(rank, 4, q1)],
        compiler_params=params(8), cost_estimate=cost(1 << 20, 1 << 20), name="outputs",
    )(hour, *blocks, *tails, src_own, src_other)


def shifted(x, axis, s):
    n = lax.axis_size(axis)
    return lax.ppermute(x, axis, [(i, (i + s) % n) for i in range(n)])


def swapped(x, axis):
    return lax.all_to_all(x, axis, split_axis=0, concat_axis=0, tiled=True)


def paired(x, axis, flip):
    n = lax.axis_size(axis)
    return lax.ppermute(x, axis, [(i, flip(i, n)) for i in range(n)])


def around(x, axis):
    return [x] + [shifted(x, axis, s) for s in range(1, lax.axis_size(axis))]


def shards(scales, counts, src_factor, dst_factor, hour_factor, core):
    zs = lax.axis_size("z")
    q1 = dst_factor.shape[1]
    hours = counts.shape[0]
    *m, src_own, src_send = main_call(hour_factor, counts, src_factor, dst_factor, core, zs)
    kept = small_call(hold_kernel, "kept", struct(*m[0].shape), [m[0]])
    m = [kept] + [shifted(m[s], "x", s) for s in (1, 2, 3)]
    src_half = summed("src_core_sum", src_own, shifted(src_send, "core", 1))
    src_half = summed("src_y_sum", *around(src_half, "y"))
    src_other = shifted(src_half, "core", 1)
    m = lax.optimization_barrier((*m, src_half))[:X]
    share = dst_factor.shape[0] // X // zs
    w = small_call(x_kernel, "x_sums", struct(zs, 2 * share + 8, q1), m)
    copies, tail = small_call(z_kernel, "z_sums", [struct(zs, share, q1), struct(share + 8, q1)], [swapped(w, "z")])
    tail = summed("core_sum", tail, shifted(tail, "core", 1))
    tail = summed("near_sum", tail, paired(tail, "y", lambda i, n: i ^ 1))
    block = swapped(copies, "z").reshape(zs * share, q1)
    block = lax.optimization_barrier((block, tail))[0]
    tails = [tail, paired(tail, "y", lambda i, n: n - 1 - i)]
    blocks = around(block, "x")
    grad_src, grad_dst, grad_hour, grad_core = end_call(scales, hour_factor, blocks, tails, src_half, src_other)
    return (grad_src.reshape(src_factor.shape), grad_dst.reshape(dst_factor.shape), grad_hour, grad_core)


def solution(mesh):
    n_src, n_dst = mesh.shape["src"], mesh.shape["dst"]
    fine = Mesh(mesh.devices.reshape(n_src // X, X, n_dst // CORES, CORES), ("z", "x", "y", "core"))
    src, dst = ("z", "x"), ("y", "core")
    in_specs = (P(None, src, dst), P(src, None), P(dst, None), P(), P())
    out_specs = (P(src, None), P(dst, None), P(), P(None, src, None))

    def run(counts, src_factor, dst_factor, hour_factor, core):
        hours, total_src, total_dst = counts.shape
        scales = (1 / math.sqrt(total_dst * hours), 1 / math.sqrt(total_src * hours),
                  1 / math.sqrt(total_src * total_dst), 1 / math.sqrt(total_src * total_dst * hours))
        body = jax.shard_map(functools.partial(shards, scales), mesh=fine, in_specs=in_specs,
                             out_specs=out_specs, check_vma=False)
        return body(counts, src_factor, dst_factor, hour_factor, core)

    return run
```

time: 83.6 us -> 78 us (0.933)
  blocking collectives: 0 us -> 20.3 us
  starting transfers between devices: 35 us -> 19.6 us
  waiting for transfers between devices: 23.6 us -> 17.4 us
  Pallas kernels: 19.7 us -> 17.5 us
  local copies, waits for them, and re-layouts: 3.18 us -> 1.79 us
    all_to_all x0 -> x1, blocking collectives: none -> 20.3 us  [swapped(): return lax.all_to_all(x, axis, split_axis=0, concat_axis=0, tiled=True)]
    all_to_all x3 -> x1, starting transfers between devices: 20.3 us -> 3.37 us  [swapped(): return lax.all_to_all(x, axis, split_axis=0, concat_axis=0, tiled=True)]
    ppermute x10 -> x12, waiting for transfers between devices: 14.1 us -> 8.29 us  [shifted(): return lax.ppermute(x, axis, [(i, (i + s) % n) for i in range(n)])]
    all_to_all x3 -> x1, waiting for transfers between devices: 9.58 us -> 3.91 us  [swapped(): return lax.all_to_all(x, axis, split_axis=0, concat_axis=0, tiled=True)]
    ppermute x0 -> x2, waiting for transfers between devices: none -> 5.16 us  [paired(): return lax.ppermute(x, axis, [(i, flip(i, n)) for i in range(n)])]
    ppermute x0 -> x2, starting transfers between devices: none -> 2.4 us  [paired(): return lax.ppermute(x, axis, [(i, flip(i, n)) for i in range(n)])]
    pallas_call x5 -> x8, Pallas kernels: 18.2 us -> 16 us  [the longest x1 15.2 us: main_call(): pl.pallas_call(functools.partial(main_kernel, zs), out_shape=[struct(bloc...]
    unnamed x12 -> x6, local copies, waits for them, and re-layouts: 3.18 us -> 1.79 us
  transfers between devices with their start and end apart: 13 -> 15, of which waited for: 8 -> 10; matrix products, arithmetic and copies ran while one was open for 0% -> 0% of each run, Pallas kernels for 3% -> 0%
where the time goes in v4:
time: 78 us; the launch traced here: 77.3 us
  blocking collectives  20.3 us (26%)
  starting transfers between devices  19.6 us (25%)
  Pallas kernels  17.5 us (22%)
  waiting for transfers between devices  17.4 us (22%)
  local copies, waits for them, and re-layouts  1.79 us (2%)
    all_to_all x1, blocking collectives, swapped(): return lax.all_to_all(x, axis, split_axis=0, concat_axis=0, tiled=True)  20.3 us
    pallas_call x1, Pallas kernels, main_call(): pl.pallas_call(functools.partial(main_kernel, zs), out_shape=[struct(bloc...  15.2 us
    ppermute x12, starting transfers between devices, shifted(): return lax.ppermute(x, axis, [(i, (i + s) % n) for i in range(n)])  13.9 us
    ppermute x12, waiting for transfers between devices, shifted(): return lax.ppermute(x, axis, [(i, (i + s) % n) for i in range(n)])  8.29 us
    ppermute x2, waiting for transfers between devices, paired(): return lax.ppermute(x, axis, [(i, flip(i, n)) for i in range(n)])  5.16 us
    all_to_all x1, waiting for transfers between devices, swapped(): return lax.all_to_all(x, axis, split_axis=0, concat_axis=0, tiled=True)  3.91 us
    all_to_all x1, starting transfers between devices, swapped(): return lax.all_to_all(x, axis, split_axis=0, concat_axis=0, tiled=True)  3.37 us
    ppermute x2, starting transfers between devices, paired(): return lax.ppermute(x, axis, [(i, flip(i, n)) for i in range(n)])  2.4 us
  transfers between devices with their start and end apart: 15, of which 10 were waited for; matrix products, arithmetic and copies ran while one was open for 0% of the time, Pallas kernels for 0%

profile of v4, /device:TPU:8, one launch (start us, length us, event | category | flops | bytes accessed | tf_op | source)
XLA Modules:
  0.0 77.3 jit_solution(15583328753978463154)
XLA Ops:
  0.6 15.2 %all_terms.1 = (f32[520,128]{1,0:T(8,128)}, f32[520,128]{1,0:T(8,128)}, f32[520,128]{1,0:T(8,128)}, f32[520,128]{1,0:T(8,128)}, f32[128,128]{1,0:T(8,128)}, /*index=5*/f32[128,128]{1,0:T(8,128)}) custom-call(f32[8,32]{1,0:T(8,128)} %hour_ref.3, s32[8,256,1024]{2,1,0:T(8,128)} %counts_hbm.1, f32[256,128]{1,0:T(8,128)} %src_hbm.1, f32[1024,128]{1,0:T(8,128)} %dst_hbm.1, ...), custom_call_target="tpu_custom_call" | custom-call | flops 4831838208 | bytes 14680064 | tf_op jit(solution)/shard_map/all_terms/pallas_call | solution.py:163
  15.8 1.6 %collective-permute-start = (f32[520,128]{1,0:T(8,128)}, f32[520,128]{1,0:T(8,128)S(1)}, u32[]{:S(2)}, u32[]{:S(2)}) collective-permute-start(f32[520,128]{1,0:T(8,128)} %get-tuple-element.22), channel_id=1, source_target_pairs={{0,8},{8,16},{16,24},{24,0},{1,9},{9,17},{17,25},{25,1},{2,10},{10... | collective-permute-start | bytes 798728 | tf_op jit(solution)/shard_map/ppermute | solution.py:272
  17.4 2.7 %collective-permute-start.1 = (f32[520,128]{1,0:T(8,128)}, f32[520,128]{1,0:T(8,128)S(1)}, u32[]{:S(2)}, u32[]{:S(2)}) collective-permute-start(f32[520,128]{1,0:T(8,128)} %get-tuple-element.23), channel_id=1, source_target_pairs={{0,16},{8,24},{16,0},{24,8},{1,17},{9,25},{17,1},{25,9},{2,18},{10... | collective-permute-start | bytes 798728 | tf_op jit(solution)/shard_map/ppermute | solution.py:272
  20.1 1.4 %collective-permute-start.2 = (f32[520,128]{1,0:T(8,128)}, f32[520,128]{1,0:T(8,128)S(1)}, u32[]{:S(2)}, u32[]{:S(2)}) collective-permute-start(f32[520,128]{1,0:T(8,128)} %get-tuple-element.24), channel_id=1, source_target_pairs={{0,24},{8,0},{16,8},{24,16},{1,25},{9,1},{17,9},{25,17},{2,26},{10... | collective-permute-start | bytes 798728 | tf_op jit(solution)/shard_map/ppermute | solution.py:272
  21.6 1.5 %collective-permute-done.3.refs_1_ = f32[128,128]{1,0:T(8,128)S(1)} collective-permute-done((f32[128,128]{1,0:T(8,128)}, f32[128,128]{1,0:T(8,128)S(1)}, u32[]{:S(2)}, u32[]{:S(2)}) %collective-permute-start.3) | collective-permute-done | bytes 65568 | tf_op jit(solution)/shard_map/ppermute | solution.py:272
  23.0 0.8 %copy-done.1 = f32[128,128]{1,0:T(8,128)S(1)} copy-done((f32[128,128]{1,0:T(8,128)S(1)}, f32[128,128]{1,0:T(8,128)}, u32[]{:S(2)}) %copy-start.1) | copy-done | bytes 65560
  23.9 1.8 %collective-permute-start.4 = (f32[128,128]{1,0:T(8,128)S(1)}, f32[128,128]{1,0:T(8,128)S(1)}, u32[]{:S(2)}, u32[]{:S(2)}) collective-permute-start(f32[128,128]{1,0:T(8,128)S(1)} %src_core_sum.1.refs_0_), channel_id=1, source_target_pairs={{0,2},{2,4},{4,6},{6,0},{1,3},{3,5},{5,7},{7,1},{8,10},{10,12},{12... | collective-permute-start | bytes 196616 | tf_op jit(solution)/shard_map/ppermute | solution.py:272
  25.7 0.9 %collective-permute-start.5 = (f32[128,128]{1,0:T(8,128)S(1)}, f32[128,128]{1,0:T(8,128)S(1)}, u32[]{:S(2)}, u32[]{:S(2)}) collective-permute-start(f32[128,128]{1,0:T(8,128)S(1)} %src_core_sum.1.refs_0_), channel_id=1, source_target_pairs={{0,4},{2,6},{4,0},{6,2},{1,5},{3,7},{5,1},{7,3},{8,12},{10,14},{12... | collective-permute-start | bytes 196616 | tf_op jit(solution)/shard_map/ppermute | solution.py:272
  26.7 1.7 %collective-permute-done.4.refs_1_ = f32[128,128]{1,0:T(8,128)S(1)} collective-permute-done((f32[128,128]{1,0:T(8,128)S(1)}, f32[128,128]{1,0:T(8,128)S(1)}, u32[]{:S(2)}, u32[]{:S(2)}) %collective-permute-start.4) | collective-permute-done | bytes 65568 | tf_op jit(solution)/shard_map/ppermute | solution.py:272
  28.4 1.7 %collective-permute-start.6 = (f32[128,128]{1,0:T(8,128)S(1)}, f32[128,128]{1,0:T(8,128)S(1)}, u32[]{:S(2)}, u32[]{:S(2)}) collective-permute-start(f32[128,128]{1,0:T(8,128)S(1)} %src_core_sum.1.refs_0_), channel_id=1, source_target_pairs={{0,6},{2,0},{4,2},{6,4},{1,7},{3,1},{5,3},{7,5},{8,14},{10,8},{12,... | collective-permute-start | bytes 196616 | tf_op jit(solution)/shard_map/ppermute | solution.py:272
  30.1 0.9 %copy-done = f32[520,128]{1,0:T(8,128)S(1)} copy-done((f32[520,128]{1,0:T(8,128)S(1)}, f32[520,128]{1,0:T(8,128)}, u32[]{:S(2)}) %copy-start) | copy-done | bytes 266264
  31.7 0.9 %collective-permute-done.6.refs_3_ = f32[128,128]{1,0:T(8,128)S(1)} collective-permute-done((f32[128,128]{1,0:T(8,128)S(1)}, f32[128,128]{1,0:T(8,128)S(1)}, u32[]{:S(2)}, u32[]{:S(2)}) %collective-permute-start.6) | collective-permute-done | bytes 65568 | tf_op jit(solution)/shard_map/ppermute | solution.py:272
  32.8 20.3 %all_to_all.10.w = f32[8,72,128]{2,1,0:T(8,128)S(1)} all-to-all(f32[8,72,128]{2,1,0:T(8,128)S(1)} %x_sums.1), channel_id=1, replica_groups=mesh['z'=8,'x'=4,'y'=4,'core'=2] {'z'}, dimensions={0} | all-to-all | bytes 589824 | tf_op jit(solution)/shard_map/all_to_all | solution.py:276
  53.7 3.4 %all-to-all-start.1 = ((f32[8,32,128]{2,1,0:T(8,128)}), f32[8,32,128]{2,1,0:T(8,128)S(1)}, u32[]{:S(2)}, u32[]{:S(2)}) async-start(f32[8,32,128]{2,1,0:T(8,128)} %get-tuple-element.31), calls=%async_computation.1 | async-start | bytes 262144 | tf_op jit(solution)/shard_map/all_to_all | solution.py:276
  57.2 1.2 %collective-permute-done.7.refs_1_ = f32[40,128]{1,0:T(8,128)S(1)} collective-permute-done((f32[40,128]{1,0:T(8,128)S(1)}, f32[40,128]{1,0:T(8,128)S(1)}, u32[]{:S(2)}, u32[]{:S(2)}) %collective-permute-start.7) | collective-permute-done | bytes 20512 | tf_op jit(solution)/shard_map/ppermute | solution.py:272
  58.4 0.8 %collective-permute-start.8 = (f32[40,128]{1,0:T(8,128)S(1)}, f32[40,128]{1,0:T(8,128)S(1)}, u32[]{:S(2)}, u32[]{:S(2)}) collective-permute-start(f32[40,128]{1,0:T(8,128)S(1)} %core_sum.1.refs_0_), channel_id=1, source_target_pairs={{0,2},{2,0},{4,6},{6,4},{1,3},{3,1},{5,7},{7,5},{8,10},{10,8},{12,... | collective-permute-start | bytes 61448 | tf_op jit(solution)/shard_map/ppermute | solution.py:281
  59.2 3.0 %collective-permute-done.8.refs_1_ = f32[40,128]{1,0:T(8,128)S(1)} collective-permute-done((f32[40,128]{1,0:T(8,128)S(1)}, f32[40,128]{1,0:T(8,128)S(1)}, u32[]{:S(2)}, u32[]{:S(2)}) %collective-permute-start.8) | collective-permute-done | bytes 20512 | tf_op jit(solution)/shard_map/ppermute | solution.py:281
  62.2 3.9 %all-to-all-done.1 = f32[8,32,128]{2,1,0:T(8,128)S(1)} async-done(((f32[8,32,128]{2,1,0:T(8,128)}), f32[8,32,128]{2,1,0:T(8,128)S(1)}, u32[]{:S(2)}, u32[]{:S(2)}) %all-to-all-start.1) | async-done | bytes 131104 | tf_op jit(solution)/shard_map/all_to_all | solution.py:276
  66.1 1.6 %collective-permute-start.10 = (f32[256,128]{1,0:T(8,128)S(1)}, f32[256,128]{1,0:T(8,128)S(1)}, u32[]{:S(2)}, u32[]{:S(2)}) collective-permute-start(f32[256,128]{1,0:T(8,128)S(1)} %bitcast.3), channel_id=1, source_target_pairs={{0,16},{8,24},{16,0},{24,8},{1,17},{9,25},{17,1},{25,9},{2,18},{10... | collective-permute-start | bytes 393224 | tf_op jit(solution)/shard_map/ppermute | solution.py:272
  67.7 1.9 %collective-permute-start.11 = (f32[256,128]{1,0:T(8,128)S(1)}, f32[256,128]{1,0:T(8,128)S(1)}, u32[]{:S(2)}, u32[]{:S(2)}) collective-permute-start(f32[256,128]{1,0:T(8,128)S(1)} %bitcast.4), channel_id=1, source_target_pairs={{0,24},{8,0},{16,8},{24,16},{1,25},{9,1},{17,9},{25,17},{2,26},{10... | collective-permute-start | bytes 393224 | tf_op jit(solution)/shard_map/ppermute | solution.py:272
  69.7 1.6 %collective-permute-start.12 = (f32[40,128]{1,0:T(8,128)S(1)}, f32[40,128]{1,0:T(8,128)S(1)}, u32[]{:S(2)}, u32[]{:S(2)}) collective-permute-start(f32[40,128]{1,0:T(8,128)S(1)} %near_sum.1.t0), channel_id=1, source_target_pairs={{0,6},{2,4},{4,2},{6,0},{1,7},{3,5},{5,3},{7,1},{8,14},{10,12},{12... | collective-permute-start | bytes 61448 | tf_op jit(solution)/shard_map/ppermute | solution.py:281
  71.3 2.2 %collective-permute-done.12.t1 = f32[40,128]{1,0:T(8,128)S(1)} collective-permute-done((f32[40,128]{1,0:T(8,128)S(1)}, f32[40,128]{1,0:T(8,128)S(1)}, u32[]{:S(2)}, u32[]{:S(2)}) %collective-permute-start.12) | collective-permute-done | bytes 20512 | tf_op jit(solution)/shard_map/ppermute | solution.py:281
  73.8 2.0 %collective-permute-done.9.b1 = f32[256,128]{1,0:T(8,128)S(1)} collective-permute-done((f32[256,128]{1,0:T(8,128)S(1)}, f32[256,128]{1,0:T(8,128)S(1)}, u32[]{:S(2)}, u32[]{:S(2)}) %collective-permute-start.9) | collective-permute-done | bytes 131104 | tf_op jit(solution)/shard_map/ppermute | solution.py:272
  75.8 1.5 %outputs.1 = (f32[2,128,128]{2,1,0:T(8,128)}, f32[4,256,128]{2,1,0:T(8,128)}, f32[8,32]{1,0:T(8,128)}, f32[32,4,128]{2,1,0:T(4,128)}) custom-call(f32[8,32]{1,0:T(8,128)S(1)} %copy-done.2, f32[256,128]{1,0:T(8,128)S(1)} %bitcast.6, f32[256,128]{1,0:T(8,128)S(1)} %collective-permute-done.9.b1, f32[256,128]{1,0:T(8,128)S(1)} %collective-permute-done.10.b2, ...), custom_call_target="tpu_custom_call" | custom-call | flops 1048576 | bytes 1048576 | tf_op jit(solution)/shard_map/outputs/pallas_call | solution.py:261
  (22 shorter events, 2.0 us)
Async XLA Ops:
  0.6 75.1 %copy-start.2 = (f32[8,32]{1,0:T(8,128)S(1)}, f32[8,32]{1,0:T(8,128)}, u32[]{:S(2)}) copy-start(f32[8,32]{1,0:T(8,128)} %hour_ref.3) | copy-start | bytes 3076
  15.8 16.9 %collective-permute-start = (f32[520,128]{1,0:T(8,128)}, f32[520,128]{1,0:T(8,128)S(1)}, u32[]{:S(2)}, u32[]{:S(2)}) collective-permute-start(f32[520,128]{1,0:T(8,128)} %get-tuple-element.22), channel_id=1, source_target_pairs={{0,8},{8,16},{16,24},{24,0},{1,9},{9,17},{17,25},{25,1},{2,10},{10... | collective-permute-start | bytes 798728 | tf_op jit(solution)/shard_map/ppermute | solution.py:272
  17.4 15.3 %collective-permute-start.1 = (f32[520,128]{1,0:T(8,128)}, f32[520,128]{1,0:T(8,128)S(1)}, u32[]{:S(2)}, u32[]{:S(2)}) collective-permute-start(f32[520,128]{1,0:T(8,128)} %get-tuple-element.23), channel_id=1, source_target_pairs={{0,16},{8,24},{16,0},{24,8},{1,17},{9,25},{17,1},{25,9},{2,18},{10... | collective-permute-start | bytes 798728 | tf_op jit(solution)/shard_map/ppermute | solution.py:272
  20.1 12.6 %collective-permute-start.2 = (f32[520,128]{1,0:T(8,128)}, f32[520,128]{1,0:T(8,128)S(1)}, u32[]{:S(2)}, u32[]{:S(2)}) collective-permute-start(f32[520,128]{1,0:T(8,128)} %get-tuple-element.24), channel_id=1, source_target_pairs={{0,24},{8,0},{16,8},{24,16},{1,25},{9,1},{17,9},{25,17},{2,26},{10... | collective-permute-start | bytes 798728 | tf_op jit(solution)/shard_map/ppermute | solution.py:272
  21.6 1.5 %collective-permute-start.3 = (f32[128,128]{1,0:T(8,128)}, f32[128,128]{1,0:T(8,128)S(1)}, u32[]{:S(2)}, u32[]{:S(2)}) collective-permute-start(f32[128,128]{1,0:T(8,128)} %get-tuple-element.26), channel_id=1, source_target_pairs={{0,1},{1,0},{2,3},{3,2},{4,5},{5,4},{6,7},{7,6},{8,9},{9,8},{10,11... | collective-permute-start | bytes 196616 | tf_op jit(solution)/shard_map/ppermute | solution.py:272
  23.0 0.8 %copy-start.1 = (f32[128,128]{1,0:T(8,128)S(1)}, f32[128,128]{1,0:T(8,128)}, u32[]{:S(2)}) copy-start(f32[128,128]{1,0:T(8,128)} %get-tuple-element.25.refs_0_) | copy-start | bytes 196612
  23.9 4.5 %collective-permute-start.4 = (f32[128,128]{1,0:T(8,128)S(1)}, f32[128,128]{1,0:T(8,128)S(1)}, u32[]{:S(2)}, u32[]{:S(2)}) collective-permute-start(f32[128,128]{1,0:T(8,128)S(1)} %src_core_sum.1.refs_0_), channel_id=1, source_target_pairs={{0,2},{2,4},{4,6},{6,0},{1,3},{3,5},{5,7},{7,1},{8,10},{10,12},{12... | collective-permute-start | bytes 196616 | tf_op jit(solution)/shard_map/ppermute | solution.py:272
  25.7 6.0 %collective-permute-start.5 = (f32[128,128]{1,0:T(8,128)S(1)}, f32[128,128]{1,0:T(8,128)S(1)}, u32[]{:S(2)}, u32[]{:S(2)}) collective-permute-start(f32[128,128]{1,0:T(8,128)S(1)} %src_core_sum.1.refs_0_), channel_id=1, source_target_pairs={{0,4},{2,6},{4,0},{6,2},{1,5},{3,7},{5,1},{7,3},{8,12},{10,14},{12... | collective-permute-start | bytes 196616 | tf_op jit(solution)/shard_map/ppermute | solution.py:272
  28.4 4.3 %collective-permute-start.6 = (f32[128,128]{1,0:T(8,128)S(1)}, f32[128,128]{1,0:T(8,128)S(1)}, u32[]{:S(2)}, u32[]{:S(2)}) collective-permute-start(f32[128,128]{1,0:T(8,128)S(1)} %src_core_sum.1.refs_0_), channel_id=1, source_target_pairs={{0,6},{2,0},{4,2},{6,4},{1,7},{3,1},{5,3},{7,5},{8,14},{10,8},{12,... | collective-permute-start | bytes 196616 | tf_op jit(solution)/shard_map/ppermute | solution.py:272
  30.1 1.0 %copy-start = (f32[520,128]{1,0:T(8,128)S(1)}, f32[520,128]{1,0:T(8,128)}, u32[]{:S(2)}) copy-start(f32[520,128]{1,0:T(8,128)} %get-tuple-element.21.a) | copy-start | bytes 798724
  53.7 12.4 %all-to-all-start.1 = ((f32[8,32,128]{2,1,0:T(8,128)}), f32[8,32,128]{2,1,0:T(8,128)S(1)}, u32[]{:S(2)}, u32[]{:S(2)}) async-start(f32[8,32,128]{2,1,0:T(8,128)} %get-tuple-element.31), calls=%async_computation.1 | async-start | bytes 262144 | tf_op jit(solution)/shard_map/all_to_all | solution.py:276
  57.1 1.3 %collective-permute-start.7 = (f32[40,128]{1,0:T(8,128)S(1)}, f32[40,128]{1,0:T(8,128)S(1)}, u32[]{:S(2)}, u32[]{:S(2)}) collective-permute-start(f32[40,128]{1,0:T(8,128)S(1)} %get-tuple-element.32.refs_0_), channel_id=1, source_target_pairs={{0,1},{1,0},{2,3},{3,2},{4,5},{5,4},{6,7},{7,6},{8,9},{9,8},{10,11... | collective-permute-start | bytes 61448 | tf_op jit(solution)/shard_map/ppermute | solution.py:272
  58.4 3.8 %collective-permute-start.8 = (f32[40,128]{1,0:T(8,128)S(1)}, f32[40,128]{1,0:T(8,128)S(1)}, u32[]{:S(2)}, u32[]{:S(2)}) collective-permute-start(f32[40,128]{1,0:T(8,128)S(1)} %core_sum.1.refs_0_), channel_id=1, source_target_pairs={{0,2},{2,0},{4,6},{6,4},{1,3},{3,1},{5,7},{7,5},{8,10},{10,8},{12,... | collective-permute-start | bytes 61448 | tf_op jit(solution)/shard_map/ppermute | solution.py:281
  66.1 7.4 %collective-permute-start.10 = (f32[256,128]{1,0:T(8,128)S(1)}, f32[256,128]{1,0:T(8,128)S(1)}, u32[]{:S(2)}, u32[]{:S(2)}) collective-permute-start(f32[256,128]{1,0:T(8,128)S(1)} %bitcast.3), channel_id=1, source_target_pairs={{0,16},{8,24},{16,0},{24,8},{1,17},{9,25},{17,1},{25,9},{2,18},{10... | collective-permute-start | bytes 393224 | tf_op jit(solution)/shard_map/ppermute | solution.py:272
  67.7 6.1 %collective-permute-start.11 = (f32[256,128]{1,0:T(8,128)S(1)}, f32[256,128]{1,0:T(8,128)S(1)}, u32[]{:S(2)}, u32[]{:S(2)}) collective-permute-start(f32[256,128]{1,0:T(8,128)S(1)} %bitcast.4), channel_id=1, source_target_pairs={{0,24},{8,0},{16,8},{24,16},{1,25},{9,1},{17,9},{25,17},{2,26},{10... | collective-permute-start | bytes 393224 | tf_op jit(solution)/shard_map/ppermute | solution.py:272
  69.6 6.2 %collective-permute-start.9 = (f32[256,128]{1,0:T(8,128)S(1)}, f32[256,128]{1,0:T(8,128)S(1)}, u32[]{:S(2)}, u32[]{:S(2)}) collective-permute-start(f32[256,128]{1,0:T(8,128)S(1)} %bitcast.5), channel_id=1, source_target_pairs={{0,8},{8,16},{16,24},{24,0},{1,9},{9,17},{17,25},{25,1},{2,10},{10... | collective-permute-start | bytes 393224 | tf_op jit(solution)/shard_map/ppermute | solution.py:272
  69.7 1.6 %collective-permute-start.13 = (f32[128,128]{1,0:T(8,128)S(1)}, f32[128,128]{1,0:T(8,128)S(1)}, u32[]{:S(2)}, u32[]{:S(2)}) collective-permute-start(f32[128,128]{1,0:T(8,128)S(1)} %src_y_sum.1.src_own), channel_id=1, source_target_pairs={{0,1},{1,0},{2,3},{3,2},{4,5},{5,4},{6,7},{7,6},{8,9},{9,8},{10,11... | collective-permute-start | bytes 196616 | tf_op jit(solution)/shard_map/ppermute | solution.py:272
  69.7 3.8 %collective-permute-start.12 = (f32[40,128]{1,0:T(8,128)S(1)}, f32[40,128]{1,0:T(8,128)S(1)}, u32[]{:S(2)}, u32[]{:S(2)}) collective-permute-start(f32[40,128]{1,0:T(8,128)S(1)} %near_sum.1.t0), channel_id=1, source_target_pairs={{0,6},{2,4},{4,2},{6,0},{1,7},{3,5},{5,3},{7,1},{8,14},{10,12},{12... | collective-permute-start | bytes 61448 | tf_op jit(solution)/shard_map/ppermute | solution.py:281

commit v5 on v4

--- a/solution.py
+++ b/solution.py
@@ -44,16 +44,14 @@
     return jnp.concatenate(split(x), axis=axis)
 
 
-def main_kernel(zs, hour_ref, counts_hbm, src_hbm, dst_hbm, core_hbm,
-                m0, m1, m2, m3, src_own, src_send,
+def main_kernel(hour_ref, counts_hbm, src_hbm, dst_hbm, core_hbm,
+                a0, a1, a2, a3, own, send,
                 counts, src, dst, core, fit_rows, fit_cols, dst_cols, dst_rows, hi_all, lo_all, dst_sum, turned,
-                core_hours, projected, rowsums, message, sems):
+                core_hours, projected, src_all, sems):
     hours, rows, cols = counts.shape
     rank, p1, q1 = core.shape
     steps = hours // GROUP
-    block = turned.shape[1]
     x, c = lax.axis_index("x"), lax.axis_index("core")
-    outs = (m0, m1, m2, m3)
     small = [pltpu.make_async_copy(a, b, sems.at[i])
              for i, (a, b) in enumerate(((core_hbm, core), (src_hbm, src), (dst_hbm, dst)))]
     parts = [pl.ds(s * GROUP, GROUP) for s in range(steps)]
@@ -113,58 +111,30 @@
             both = both[:p1] + both[p1:]
             projected[k] = both[:, :q1] + both[:, q1:]
     turned[...] = dst_sum[...].T.reshape(turned.shape)
-    places = [lax.rem(x + s, X) for s in range(X)]
-    sends = [pltpu.make_async_copy(turned.at[place], out.at[pl.ds(0, block)], sems.at[3 + steps + i])
-             for i, (place, out) in enumerate(zip(places, outs))]
-    for copy in sends:
+    src_all[...] = src_sum.reshape(src_all.shape)
+    first = 3 + steps
+    moves = [(turned.at[lax.rem(x + s, X)], out) for s, out in enumerate((a0, a1, a2, a3))]
+    half = hours // CORES
+    for mine, out in ((c, own), (1 - c, send)):
+        moves.append((projected.at[pl.ds(mine * half, half)], out.at[pl.ds(0, half)]))
+        moves.append((src_all.at[pl.ds(mine, 1)], out.at[pl.ds(half, 1)]))
+    copies = [pltpu.make_async_copy(a, b, sems.at[first + i]) for i, (a, b) in enumerate(moves)]
+    for copy in copies:
         copy.start()
-    half = rows // CORES
-
-    @pl.when(c == 0)
-    def _():
-        src_own[...] = src_sum[:half]
-        src_send[...] = src_sum[half:]
-
-    @pl.when(c == 1)
-    def _():
-        src_own[...] = src_sum[half:]
-        src_send[...] = src_sum[:half]
-
-    for k in range(hours):
-        here = projected[k]
-        for r in range(rank):
-            product = (here * core[r]).reshape(p1 // 8, 8, q1)
-            at = k * rank + r
-            rowsums[at:at + 1, :] = jnp.sum(jnp.sum(product, axis=0), axis=0, keepdims=True)
-        for z in range(zs):
-            for b in range(X):
-                start = (z * X + b) * 4
-                row = z * 4 * hours + 4 * k
-                message[b, row:row + 4, :] = here[start:start + 4]
-    sums = jnp.sum(rowsums[...].T, axis=0, keepdims=True)
-    spare = jnp.zeros((8 - sums.shape[1] // 128, 128), F32)
-    tail = jnp.concatenate([sums[:, i:i + 128] for i in range(0, sums.shape[1], 128)] + [spare], axis=0)
-    size = message.shape[1]
-    for b in range(X):
-        message[b, size - 8:, :] = tail
-    more = [pltpu.make_async_copy(message.at[place], out.at[pl.ds(block, size)], sems.at[3 + steps + X + i])
-            for i, (place, out) in enumerate(zip(places, outs))]
-    for copy in more:
-        copy.start()
-    for copy in sends + more:
+    for copy in copies:
         copy.wait()
 
 
-def main_call(hour, counts, src, dst, core, zs):
+def main_call(hour, counts, src, dst, core):
     hours, rows, cols = counts.shape
     rank, p1, q1 = core.shape
     block = cols // X
-    size = hours * p1 // X + 8
+    half = hours // CORES + 1
     return pl.pallas_call(
-        functools.partial(main_kernel, zs),
-        out_shape=[struct(block + size, q1)] * X + [struct(rows // CORES, p1)] * 2,
+        main_kernel,
+        out_shape=[struct(block, q1)] * X + [struct(half, p1, q1)] * 2,
         in_specs=[SMEM] + [HBM] * 4,
-        out_specs=[HBM] * X + [VMEM] * 2,
+        out_specs=[HBM] * (X + 2),
         scratch_shapes=[
             pltpu.VMEM(counts.shape, jnp.int32),
             pltpu.VMEM(src.shape, F32),
@@ -180,9 +150,8 @@
             pltpu.VMEM((X, block, q1), F32),
             pltpu.VMEM((hours, p1, q1), F32),
             pltpu.VMEM((hours, p1, q1), F32),
-            pltpu.VMEM((hours * rank, q1), F32),
-            pltpu.VMEM((X, size, q1), F32),
-            pltpu.SemaphoreType.DMA((3 + hours // GROUP + 2 * X,)),
+            pltpu.VMEM((CORES, rows // CORES, p1), F32),
+            pltpu.SemaphoreType.DMA((3 + hours // GROUP + X + 4,)),
         ],
         compiler_params=params(60),
         cost_estimate=cost(2 * 9 * counts.size * q1, 14 << 20),
@@ -190,15 +159,51 @@
     )(hour, counts, src, dst, core)
 
 
+def share_kernel(zs, own, came, core, m0, m1, m2, m3, src_half, rowsums, message):
+    half = own.shape[0] - 1
+    rank, p1, q1 = core.shape
+    x = lax.axis_index("x")
+    src_half[...] = own[half] + came[half]
+    for k in range(half):
+        here = own[k] + came[k]
+        for r in range(rank):
+            product = (here * core[r]).reshape(p1 // 8, 8, q1)
+            at = k * rank + r
+            rowsums[at:at + 1, :] = jnp.sum(jnp.sum(product, axis=0), axis=0, keepdims=True)
+        for z in range(zs):
+            for b in range(X):
+                start = (z * X + b) * 4
+                row = (z * half + k) * 4
+                message[b, row:row + 4, :] = here[start:start + 4]
+    sums = jnp.sum(rowsums[...].T, axis=0, keepdims=True)
+    tail = jnp.concatenate([sums, jnp.zeros((7, q1), F32)], axis=0)
+    size = message.shape[1]
+    for s, out in enumerate((m0, m1, m2, m3)):
+        out[:size, :] = message[lax.rem(x + s, X)]
+        out[size:, :] = tail
+
+
+def share_call(own, came, core, zs):
+    half = own.shape[0] - 1
+    rank, p1, q1 = core.shape
+    size = half * p1 // X
+    return pl.pallas_call(
+        functools.partial(share_kernel, zs),
+        out_shape=[struct(size + 8, q1)] * X + [struct(p1, q1)],
+        in_specs=[VMEM] * 3,
+        out_specs=[VMEM] * (X + 1),
+        scratch_shapes=[pltpu.VMEM((half * rank, q1), F32), pltpu.VMEM((X, size, q1), F32)],
+        compiler_params=params(8),
+        cost_estimate=cost(1 << 34, 4 << 20),
+        name="hour_terms",
+    )(own, came, core)
+
+
 def small_call(kernel, name, outs, args, flops=1 << 20):
     return pl.pallas_call(
         kernel, out_shape=outs, in_specs=[VMEM] * len(args), out_specs=jax.tree.map(lambda _: VMEM, outs),
         compiler_params=params(4), cost_estimate=cost(flops, 1 << 20), name=name,
     )(*args)
-
-
-def hold_kernel(a, out):
-    out[...] = a[...]
 
 
 def sum_kernel(*refs):
@@ -213,15 +218,16 @@
     return small_call(sum_kernel, name, struct(*parts[0].shape), parts)
 
 
-def x_kernel(m0, m1, m2, m3, out):
+def x_kernel(a0, a1, a2, a3, m0, m1, m2, m3, out):
     zs, rows, _ = out.shape
-    share = (rows - 8) // 2
-    block = share * zs
+    share = a0.shape[0] // zs
+    each = rows - share - 8
+    a = (a0[...] + a2[...]) + (a1[...] + a3[...])
     m = (m0[...] + m2[...]) + (m1[...] + m3[...])
     for z in range(zs):
-        out[z, :share, :] = m[z * share:(z + 1) * share]
-        out[z, share:2 * share, :] = m[block + z * share:block + (z + 1) * share]
-        out[z, 2 * share:, :] = m[2 * block:]
+        out[z, :share, :] = a[z * share:(z + 1) * share]
+        out[z, share:share + each, :] = m[z * each:(z + 1) * each]
+        out[z, share + each:, :] = m[zs * each:]
 
 
 def z_kernel(w, copies, tail):
@@ -232,22 +238,23 @@
     tail[...] = total[share:]
 
 
-def end_kernel(scales, hour_ref, b0, b1, b2, b3, t0, t1, src_own, src_other,
-               src_out, dst_out, hour_out, core_out):
+def end_kernel(scales, hour_ref, b0, b1, b2, b3, own, other, src_own, src_other,
+               src_out, dst_out, hour_out, core_out, both):
     x, c = lax.axis_index("x"), lax.axis_index("core")
     src_scale, dst_scale, hour_scale, core_scale = scales
     for s, block in enumerate((b0, b1, b2, b3)):
         dst_out[lax.rem(x - s + X, X)] = block[...] * dst_scale
     src_out[c] = src_own[...] * src_scale
     src_out[1 - c] = src_other[...] * src_scale
+    both[c] = own[...]
+    both[1 - c] = other[...]
     hours, rank = hour_ref.shape
-    share = 4 * hours
-    total = t0[...] + t1[...]
-    each = 128 // rank
+    half = hours // CORES
+    tiles = []
     for k in range(hours):
-        row = share + k // each
-        hour_out[k:k + 1, :] = total[row:row + 1, k % each * rank:(k % each + 1) * rank] * hour_scale
-    tiles = [total[4 * k:4 * k + 4] * core_scale for k in range(hours)]
+        at, i = k // half, k % half
+        hour_out[k:k + 1, :] = both[at, 4 * half:4 * half + 1, i * rank:(i + 1) * rank] * hour_scale
+        tiles.append(both[at, 4 * i:4 * i + 4, :] * core_scale)
     for r in range(rank):
         out = hour_ref[0, r] * tiles[0]
         for k in range(1, hours):
@@ -255,7 +262,7 @@
         core_out[r] = out
 
 
-def end_call(scales, hour, blocks, tails, src_own, src_other):
+def end_call(scales, hour, blocks, own, other, src_own, src_other):
     block, q1 = blocks[0].shape
     hours, rank = hour.shape
     return pl.pallas_call(
@@ -263,8 +270,9 @@
         in_specs=[SMEM] + [VMEM] * 8,
         out_specs=[VMEM] * 4,
         out_shape=[struct(CORES, *src_own.shape), struct(X, block, q1), struct(hours, rank), struct(rank, 4, q1)],
+        scratch_shapes=[pltpu.VMEM((CORES, *own.shape), F32)],
         compiler_params=params(8), cost_estimate=cost(1 << 20, 1 << 20), name="outputs",
-    )(hour, *blocks, *tails, src_own, src_other)
+    )(hour, *blocks, own, other, src_own, src_other)
 
 
 def shifted(x, axis, s):
@@ -288,24 +296,25 @@
 def shards(scales, counts, src_factor, dst_factor, hour_factor, core):
     zs = lax.axis_size("z")
     q1 = dst_factor.shape[1]
-    hours = counts.shape[0]
-    *m, src_own, src_send = main_call(hour_factor, counts, src_factor, dst_factor, core, zs)
-    kept = small_call(hold_kernel, "kept", struct(*m[0].shape), [m[0]])
-    m = [kept] + [shifted(m[s], "x", s) for s in (1, 2, 3)]
-    src_half = summed("src_core_sum", src_own, shifted(src_send, "core", 1))
+    a0, a1, a2, a3, own, send = main_call(hour_factor, counts, src_factor, dst_factor, core)
+    a = [a0] + [shifted(v, "x", s) for s, v in ((1, a1), (2, a2), (3, a3))]
+    m0, m1, m2, m3, src_half = share_call(own, shifted(send, "core", 1), core, zs)
+    m = [m0] + [shifted(v, "x", s) for s, v in ((1, m1), (2, m2), (3, m3))]
+    share = a0.shape[0] // zs
+    each = (m0.shape[0] - 8) // zs
+    w = small_call(x_kernel, "x_sums", struct(zs, share + each + 8, q1), [*a, *m])
     src_half = summed("src_y_sum", *around(src_half, "y"))
     src_other = shifted(src_half, "core", 1)
-    m = lax.optimization_barrier((*m, src_half))[:X]
-    share = dst_factor.shape[0] // X // zs
-    w = small_call(x_kernel, "x_sums", struct(zs, 2 * share + 8, q1), m)
-    copies, tail = small_call(z_kernel, "z_sums", [struct(zs, share, q1), struct(share + 8, q1)], [swapped(w, "z")])
-    tail = summed("core_sum", tail, shifted(tail, "core", 1))
+    w = lax.optimization_barrier((swapped(w, "z"), src_half))[0]
+    copies, tail = small_call(z_kernel, "z_sums", [struct(zs, share, q1), struct(each + 8, q1)], [w])
     tail = summed("near_sum", tail, paired(tail, "y", lambda i, n: i ^ 1))
     block = swapped(copies, "z").reshape(zs * share, q1)
     block = lax.optimization_barrier((block, tail))[0]
-    tails = [tail, paired(tail, "y", lambda i, n: n - 1 - i)]
+    tail = summed("far_sum", tail, paired(tail, "y", lambda i, n: n - 1 - i))
+    other = shifted(tail, "core", 1)
     blocks = around(block, "x")
-    grad_src, grad_dst, grad_hour, grad_core = end_call(scales, hour_factor, blocks, tails, src_half, src_other)
+    grad_src, grad_dst, grad_hour, grad_core = end_call(
+        scales, hour_factor, blocks, tail, other, src_half, src_other)
     return (grad_src.reshape(src_factor.shape), grad_dst.reshape(dst_factor.shape), grad_hour, grad_core)
 
 

time: 78 us -> 77.4 us (level)
  the two profiles are of different devices: /device:TPU:8 before, /device:TPU:3 now
where the time goes in v5:
time: 77.4 us; the launch traced here: 77 us
  starting transfers between devices  39.4 us (51%)
  waiting for transfers between devices  19 us (25%)
  Pallas kernels  17 us (22%)
  local copies, waits for them, and re-layouts  0.99 us (1%)
    ppermute x15, starting transfers between devices, shifted(): return lax.ppermute(x, axis, [(i, (i + s) % n) for i in range(n)])  25 us
    all_to_all x2, starting transfers between devices, swapped(): return lax.all_to_all(x, axis, split_axis=0, concat_axis=0, tiled=True)  14.2 us
    pallas_call x1, Pallas kernels, main_call(): pl.pallas_call(main_kernel, out_shape=[struct(block, q1)] * X + [struct(h...  13.3 us
    ppermute x15, waiting for transfers between devices, shifted(): return lax.ppermute(x, axis, [(i, (i + s) % n) for i in range(n)])  6.85 us
    all_to_all x2, waiting for transfers between devices, swapped(): return lax.all_to_all(x, axis, split_axis=0, concat_axis=0, tiled=True)  6.09 us
    ppermute x2, waiting for transfers between devices, paired(): return lax.ppermute(x, axis, [(i, flip(i, n)) for i in range(n)])  6.01 us
  transfers between devices with their start and end apart: 19, of which 11 were waited for; matrix products, arithmetic and copies ran while one was open for 0% of the time, Pallas kernels for 1%

profile of v5, /device:TPU:3, one launch (start us, length us, event | category | flops | bytes accessed | tf_op | source)
XLA Modules:
  0.0 77.0 jit_solution(977238542907831915)
XLA Ops:
  0.6 13.3 %all_terms.1 = (f32[256,128]{1,0:T(8,128)}, f32[256,128]{1,0:T(8,128)}, f32[256,128]{1,0:T(8,128)}, f32[256,128]{1,0:T(8,128)}, f32[5,128,128]{2,1,0:T(8,128)}, /*index=5*/f32[5,128,128]{2,1,0:T(8,128)}) custom-call(f32[8,32]{1,0:T(8,128)} %hour_ref.3, s32[8,256,1024]{2,1,0:T(8,128)} %counts_hbm.1, f32[256,128]{1,0:T(8,128)} %src_hbm.1, ...), custom_call_target="tpu_custom_call" | custom-call | flops 4831838208 | bytes 14680064 | tf_op jit(solution)/shard_map/all_terms/pallas_call | solution.py:133
  13.9 0.8 collective-permute-start.3
  14.7 1.2 %collective-permute-start = (f32[256,128]{1,0:T(8,128)}, f32[256,128]{1,0:T(8,128)S(1)}, u32[]{:S(2)}, u32[]{:S(2)}) collective-permute-start(f32[256,128]{1,0:T(8,128)} %get-tuple-element.24), channel_id=1, source_target_pairs={{0,8},{8,16},{16,24},{24,0},{1,9},{9,17},{17,25},{25,1},{2,10},{10... | collective-permute-start | bytes 393224 | tf_op jit(solution)/shard_map/ppermute | solution.py:280
  15.9 2.6 %collective-permute-start.1 = (f32[256,128]{1,0:T(8,128)}, f32[256,128]{1,0:T(8,128)S(1)}, u32[]{:S(2)}, u32[]{:S(2)}) collective-permute-start(f32[256,128]{1,0:T(8,128)} %get-tuple-element.25), channel_id=1, source_target_pairs={{0,16},{8,24},{16,0},{24,8},{1,17},{9,25},{17,1},{25,9},{2,18},{10... | collective-permute-start | bytes 393224 | tf_op jit(solution)/shard_map/ppermute | solution.py:280
  18.6 1.0 %copy-done.3 = f32[5,128,128]{2,1,0:T(8,128)S(1)} copy-done((f32[5,128,128]{2,1,0:T(8,128)S(1)}, f32[5,128,128]{2,1,0:T(8,128)}, u32[]{:S(2)}) %copy-start.3) | copy-done | bytes 327704
  19.6 0.8 hour_terms.1
  20.4 1.4 %collective-permute-start.4 = (f32[136,128]{1,0:T(8,128)S(1)}, f32[136,128]{1,0:T(8,128)S(1)}, u32[]{:S(2)}, u32[]{:S(2)}) collective-permute-start(f32[136,128]{1,0:T(8,128)S(1)} %get-tuple-element.30), channel_id=1, source_target_pairs={{0,8},{8,16},{16,24},{24,0},{1,9},{9,17},{17,25},{25,1},{2,10},{10... | collective-permute-start | bytes 208904 | tf_op jit(solution)/shard_map/ppermute | solution.py:280
  21.8 1.6 %collective-permute-start.5 = (f32[136,128]{1,0:T(8,128)S(1)}, f32[136,128]{1,0:T(8,128)S(1)}, u32[]{:S(2)}, u32[]{:S(2)}) collective-permute-start(f32[136,128]{1,0:T(8,128)S(1)} %get-tuple-element.31), channel_id=1, source_target_pairs={{0,16},{8,24},{16,0},{24,8},{1,17},{9,25},{17,1},{25,9},{2,18},{10... | collective-permute-start | bytes 208904 | tf_op jit(solution)/shard_map/ppermute | solution.py:280
  23.4 2.4 %collective-permute-start.6 = (f32[136,128]{1,0:T(8,128)S(1)}, f32[136,128]{1,0:T(8,128)S(1)}, u32[]{:S(2)}, u32[]{:S(2)}) collective-permute-start(f32[136,128]{1,0:T(8,128)S(1)} %get-tuple-element.32), channel_id=1, source_target_pairs={{0,24},{8,0},{16,8},{24,16},{1,25},{9,1},{17,9},{25,17},{2,26},{10... | collective-permute-start | bytes 208904 | tf_op jit(solution)/shard_map/ppermute | solution.py:280
  27.2 0.7 x_sums.1
  27.9 8.5 %all-to-all-start = ((f32[8,56,128]{2,1,0:T(8,128)}), f32[8,56,128]{2,1,0:T(8,128)S(1)}, u32[]{:S(2)}, u32[]{:S(2)}) async-start(f32[8,56,128]{2,1,0:T(8,128)} %x_sums.1), calls=%async_computation | async-start | bytes 458752 | tf_op jit(solution)/shard_map/all_to_all | solution.py:284
  36.4 2.7 %collective-permute-start.9 = (f32[128,128]{1,0:T(8,128)S(1)}, f32[128,128]{1,0:T(8,128)S(1)}, u32[]{:S(2)}, u32[]{:S(2)}) collective-permute-start(f32[128,128]{1,0:T(8,128)S(1)} %get-tuple-element.33.refs_0_), channel_id=1, source_target_pairs={{0,6},{2,0},{4,2},{6,4},{1,7},{3,1},{5,3},{7,5},{8,14},{10,8},{12,... | collective-permute-start | bytes 196616 | tf_op jit(solution)/shard_map/ppermute | solution.py:280
  40.5 3.4 %collective-permute-done.8.refs_2_ = f32[128,128]{1,0:T(8,128)S(1)} collective-permute-done((f32[128,128]{1,0:T(8,128)S(1)}, f32[128,128]{1,0:T(8,128)S(1)}, u32[]{:S(2)}, u32[]{:S(2)}) %collective-permute-start.8) | collective-permute-done | bytes 65568 | tf_op jit(solution)/shard_map/ppermute | solution.py:280
  43.9 0.9 %collective-permute-done.7.refs_1_ = f32[128,128]{1,0:T(8,128)S(1)} collective-permute-done((f32[128,128]{1,0:T(8,128)S(1)}, f32[128,128]{1,0:T(8,128)S(1)}, u32[]{:S(2)}, u32[]{:S(2)}) %collective-permute-start.7) | collective-permute-done | bytes 65568 | tf_op jit(solution)/shard_map/ppermute | solution.py:280
  46.2 5.7 %all-to-all-start.1 = ((f32[8,32,128]{2,1,0:T(8,128)}), f32[8,32,128]{2,1,0:T(8,128)S(1)}, u32[]{:S(2)}, u32[]{:S(2)}) async-start(f32[8,32,128]{2,1,0:T(8,128)} %get-tuple-element.35), calls=%async_computation.1 | async-start | bytes 262144 | tf_op jit(solution)/shard_map/all_to_all | solution.py:284
  51.9 2.5 %collective-permute-done.10.refs_1_ = f32[24,128]{1,0:T(8,128)S(1)} collective-permute-done((f32[24,128]{1,0:T(8,128)S(1)}, f32[24,128]{1,0:T(8,128)S(1)}, u32[]{:S(2)}, u32[]{:S(2)}) %collective-permute-start.10) | collective-permute-done | bytes 12320 | tf_op jit(solution)/shard_map/ppermute | solution.py:289
  54.4 5.4 %all-to-all-done.1 = f32[8,32,128]{2,1,0:T(8,128)S(1)} async-done(((f32[8,32,128]{2,1,0:T(8,128)}), f32[8,32,128]{2,1,0:T(8,128)S(1)}, u32[]{:S(2)}, u32[]{:S(2)}) %all-to-all-start.1) | async-done | bytes 131104 | tf_op jit(solution)/shard_map/all_to_all | solution.py:284
  60.3 1.3 %collective-permute-start.12 = (f32[256,128]{1,0:T(8,128)S(1)}, f32[256,128]{1,0:T(8,128)S(1)}, u32[]{:S(2)}, u32[]{:S(2)}) collective-permute-start(f32[256,128]{1,0:T(8,128)S(1)} %bitcast.4), channel_id=1, source_target_pairs={{0,16},{8,24},{16,0},{24,8},{1,17},{9,25},{17,1},{25,9},{2,18},{10... | collective-permute-start | bytes 393224 | tf_op jit(solution)/shard_map/ppermute | solution.py:280
  61.6 1.5 %collective-permute-start.11 = (f32[256,128]{1,0:T(8,128)S(1)}, f32[256,128]{1,0:T(8,128)S(1)}, u32[]{:S(2)}, u32[]{:S(2)}) collective-permute-start(f32[256,128]{1,0:T(8,128)S(1)} %bitcast.5), channel_id=1, source_target_pairs={{0,8},{8,16},{16,24},{24,0},{1,9},{9,17},{17,25},{25,1},{2,10},{10... | collective-permute-start | bytes 393224 | tf_op jit(solution)/shard_map/ppermute | solution.py:280
  63.1 6.6 %collective-permute-start.16 = (f32[128,128]{1,0:T(8,128)S(1)}, f32[128,128]{1,0:T(8,128)S(1)}, u32[]{:S(2)}, u32[]{:S(2)}) collective-permute-start(f32[128,128]{1,0:T(8,128)S(1)} %src_y_sum.1.src_own), channel_id=1, source_target_pairs={{0,1},{1,0},{2,3},{3,2},{4,5},{5,4},{6,7},{7,6},{8,9},{9,8},{10,11... | collective-permute-start | bytes 196616 | tf_op jit(solution)/shard_map/ppermute | solution.py:280
  70.0 3.5 %collective-permute-done.14.refs_1_ = f32[24,128]{1,0:T(8,128)S(1)} collective-permute-done((f32[24,128]{1,0:T(8,128)S(1)}, f32[24,128]{1,0:T(8,128)S(1)}, u32[]{:S(2)}, u32[]{:S(2)}) %collective-permute-start.14) | collective-permute-done | bytes 12320 | tf_op jit(solution)/shard_map/ppermute | solution.py:289
  73.5 1.2 %collective-permute-start.15 = (f32[24,128]{1,0:T(8,128)S(1)}, f32[24,128]{1,0:T(8,128)S(1)}, u32[]{:S(2)}, u32[]{:S(2)}) collective-permute-start(f32[24,128]{1,0:T(8,128)S(1)} %far_sum.1.own), channel_id=1, source_target_pairs={{0,1},{1,0},{2,3},{3,2},{4,5},{5,4},{6,7},{7,6},{8,9},{9,8},{10,11... | collective-permute-start | bytes 36872 | tf_op jit(solution)/shard_map/ppermute | solution.py:280
  74.7 0.8 %collective-permute-done.15.other = f32[24,128]{1,0:T(8,128)S(1)} collective-permute-done((f32[24,128]{1,0:T(8,128)S(1)}, f32[24,128]{1,0:T(8,128)S(1)}, u32[]{:S(2)}, u32[]{:S(2)}) %collective-permute-start.15) | collective-permute-done | bytes 12320 | tf_op jit(solution)/shard_map/ppermute | solution.py:280
  75.5 1.5 %outputs.1 = (f32[2,128,128]{2,1,0:T(8,128)}, f32[4,256,128]{2,1,0:T(8,128)}, f32[8,32]{1,0:T(8,128)}, f32[32,4,128]{2,1,0:T(4,128)}) custom-call(f32[8,32]{1,0:T(8,128)S(1)} %copy-done.1, f32[256,128]{1,0:T(8,128)S(1)} %bitcast.6, f32[256,128]{1,0:T(8,128)S(1)} %collective-permute-done.11.b1, f32[256,128]{1,0:T(8,128)S(1)} %collective-permute-done.12.b2, ...), custom_call_target="tpu_custom_call" | custom-call | flops 1048576 | bytes 1048576 | tf_op jit(solution)/shard_map/outputs/pallas_call | solution.py:268
  (30 shorter events, 5.1 us)
Async XLA Ops:
  0.6 18.0 %copy-start.2 = (f32[32,128,128]{2,1,0:T(8,128)S(1)}, f32[32,128,128]{2,1,0:T(8,128)}, u32[]{:S(2)}) copy-start(f32[32,128,128]{2,1,0:T(8,128)} %core.1) | copy-start | bytes 6291460
  13.9 4.7 %collective-permute-start.3 = (f32[5,128,128]{2,1,0:T(8,128)}, f32[5,128,128]{2,1,0:T(8,128)S(1)}, u32[]{:S(2)}, u32[]{:S(2)}) collective-permute-start(f32[5,128,128]{2,1,0:T(8,128)} %get-tuple-element.28), channel_id=1, source_target_pairs={{0,1},{1,0},{2,3},{3,2},{4,5},{5,4},{6,7},{7,6},{8,9},{9,8},{10,11... | collective-permute-start | bytes 983048 | tf_op jit(solution)/shard_map/ppermute | solution.py:280
  14.7 8.7 %collective-permute-start = (f32[256,128]{1,0:T(8,128)}, f32[256,128]{1,0:T(8,128)S(1)}, u32[]{:S(2)}, u32[]{:S(2)}) collective-permute-start(f32[256,128]{1,0:T(8,128)} %get-tuple-element.24), channel_id=1, source_target_pairs={{0,8},{8,16},{16,24},{24,0},{1,9},{9,17},{17,25},{25,1},{2,10},{10... | collective-permute-start | bytes 393224 | tf_op jit(solution)/shard_map/ppermute | solution.py:280
  15.9 9.8 %collective-permute-start.1 = (f32[256,128]{1,0:T(8,128)}, f32[256,128]{1,0:T(8,128)S(1)}, u32[]{:S(2)}, u32[]{:S(2)}) collective-permute-start(f32[256,128]{1,0:T(8,128)} %get-tuple-element.25), channel_id=1, source_target_pairs={{0,16},{8,24},{16,0},{24,8},{1,17},{9,25},{17,1},{25,9},{2,18},{10... | collective-permute-start | bytes 393224 | tf_op jit(solution)/shard_map/ppermute | solution.py:280
  18.5 7.4 %collective-permute-start.2 = (f32[256,128]{1,0:T(8,128)}, f32[256,128]{1,0:T(8,128)S(1)}, u32[]{:S(2)}, u32[]{:S(2)}) collective-permute-start(f32[256,128]{1,0:T(8,128)} %get-tuple-element.26), channel_id=1, source_target_pairs={{0,24},{8,0},{16,8},{24,16},{1,25},{9,1},{17,9},{25,17},{2,26},{10... | collective-permute-start | bytes 393224 | tf_op jit(solution)/shard_map/ppermute | solution.py:280
  18.6 1.0 %copy-start.3 = (f32[5,128,128]{2,1,0:T(8,128)S(1)}, f32[5,128,128]{2,1,0:T(8,128)}, u32[]{:S(2)}) copy-start(f32[5,128,128]{2,1,0:T(8,128)} %get-tuple-element.27.own) | copy-start | bytes 983044
  19.6 7.6 %copy-start = (f32[256,128]{1,0:T(8,128)S(1)}, f32[256,128]{1,0:T(8,128)}, u32[]{:S(2)}) copy-start(f32[256,128]{1,0:T(8,128)} %get-tuple-element.23.a0) | copy-start | bytes 393220
  19.6 55.9 %copy-start.1 = (f32[8,32]{1,0:T(8,128)S(1)}, f32[8,32]{1,0:T(8,128)}, u32[]{:S(2)}) copy-start(f32[8,32]{1,0:T(8,128)} %hour_ref.3) | copy-start | bytes 3076
  20.4 5.5 %collective-permute-start.4 = (f32[136,128]{1,0:T(8,128)S(1)}, f32[136,128]{1,0:T(8,128)S(1)}, u32[]{:S(2)}, u32[]{:S(2)}) collective-permute-start(f32[136,128]{1,0:T(8,128)S(1)} %get-tuple-element.30), channel_id=1, source_target_pairs={{0,8},{8,16},{16,24},{24,0},{1,9},{9,17},{17,25},{25,1},{2,10},{10... | collective-permute-start | bytes 208904 | tf_op jit(solution)/shard_map/ppermute | solution.py:280
  21.8 4.7 %collective-permute-start.5 = (f32[136,128]{1,0:T(8,128)S(1)}, f32[136,128]{1,0:T(8,128)S(1)}, u32[]{:S(2)}, u32[]{:S(2)}) collective-permute-start(f32[136,128]{1,0:T(8,128)S(1)} %get-tuple-element.31), channel_id=1, source_target_pairs={{0,16},{8,24},{16,0},{24,8},{1,17},{9,25},{17,1},{25,9},{2,18},{10... | collective-permute-start | bytes 208904 | tf_op jit(solution)/shard_map/ppermute | solution.py:280
  23.4 3.8 %collective-permute-start.6 = (f32[136,128]{1,0:T(8,128)S(1)}, f32[136,128]{1,0:T(8,128)S(1)}, u32[]{:S(2)}, u32[]{:S(2)}) collective-permute-start(f32[136,128]{1,0:T(8,128)S(1)} %get-tuple-element.32), channel_id=1, source_target_pairs={{0,24},{8,0},{16,8},{24,16},{1,25},{9,1},{17,9},{25,17},{2,26},{10... | collective-permute-start | bytes 208904 | tf_op jit(solution)/shard_map/ppermute | solution.py:280
  27.9 17.6 %all-to-all-start = ((f32[8,56,128]{2,1,0:T(8,128)}), f32[8,56,128]{2,1,0:T(8,128)S(1)}, u32[]{:S(2)}, u32[]{:S(2)}) async-start(f32[8,56,128]{2,1,0:T(8,128)} %x_sums.1), calls=%async_computation | async-start | bytes 458752 | tf_op jit(solution)/shard_map/all_to_all | solution.py:284
  36.4 4.1 %collective-permute-start.9 = (f32[128,128]{1,0:T(8,128)S(1)}, f32[128,128]{1,0:T(8,128)S(1)}, u32[]{:S(2)}, u32[]{:S(2)}) collective-permute-start(f32[128,128]{1,0:T(8,128)S(1)} %get-tuple-element.33.refs_0_), channel_id=1, source_target_pairs={{0,6},{2,0},{4,2},{6,4},{1,7},{3,1},{5,3},{7,5},{8,14},{10,8},{12,... | collective-permute-start | bytes 196616 | tf_op jit(solution)/shard_map/ppermute | solution.py:280
  39.2 4.7 %collective-permute-start.8 = (f32[128,128]{1,0:T(8,128)S(1)}, f32[128,128]{1,0:T(8,128)S(1)}, u32[]{:S(2)}, u32[]{:S(2)}) collective-permute-start(f32[128,128]{1,0:T(8,128)S(1)} %get-tuple-element.33.refs_0_), channel_id=1, source_target_pairs={{0,4},{2,6},{4,0},{6,2},{1,5},{3,7},{5,1},{7,3},{8,12},{10,14},{12... | collective-permute-start | bytes 196616 | tf_op jit(solution)/shard_map/ppermute | solution.py:280
  39.5 5.3 %collective-permute-start.7 = (f32[128,128]{1,0:T(8,128)S(1)}, f32[128,128]{1,0:T(8,128)S(1)}, u32[]{:S(2)}, u32[]{:S(2)}) collective-permute-start(f32[128,128]{1,0:T(8,128)S(1)} %get-tuple-element.33.refs_0_), channel_id=1, source_target_pairs={{0,2},{2,4},{4,6},{6,0},{1,3},{3,5},{5,7},{7,1},{8,10},{10,12},{12... | collective-permute-start | bytes 196616 | tf_op jit(solution)/shard_map/ppermute | solution.py:280
  46.2 13.6 %all-to-all-start.1 = ((f32[8,32,128]{2,1,0:T(8,128)}), f32[8,32,128]{2,1,0:T(8,128)S(1)}, u32[]{:S(2)}, u32[]{:S(2)}) async-start(f32[8,32,128]{2,1,0:T(8,128)} %get-tuple-element.35), calls=%async_computation.1 | async-start | bytes 262144 | tf_op jit(solution)/shard_map/all_to_all | solution.py:284
  51.8 2.5 %collective-permute-start.10 = (f32[24,128]{1,0:T(8,128)S(1)}, f32[24,128]{1,0:T(8,128)S(1)}, u32[]{:S(2)}, u32[]{:S(2)}) collective-permute-start(f32[24,128]{1,0:T(8,128)S(1)} %get-tuple-element.36.refs_0_), channel_id=1, source_target_pairs={{0,2},{2,0},{4,6},{6,4},{1,3},{3,1},{5,7},{7,5},{8,10},{10,8},{12,... | collective-permute-start | bytes 36872 | tf_op jit(solution)/shard_map/ppermute | solution.py:289
  59.8 15.7 %collective-permute-start.13 = (f32[256,128]{1,0:T(8,128)S(1)}, f32[256,128]{1,0:T(8,128)S(1)}, u32[]{:S(2)}, u32[]{:S(2)}) collective-permute-start(f32[256,128]{1,0:T(8,128)S(1)} %bitcast.3), channel_id=1, source_target_pairs={{0,24},{8,0},{16,8},{24,16},{1,25},{9,1},{17,9},{25,17},{2,26},{10... | collective-permute-start | bytes 393224 | tf_op jit(solution)/shard_map/ppermute | solution.py:280
  60.3 15.2 %collective-permute-start.12 = (f32[256,128]{1,0:T(8,128)S(1)}, f32[256,128]{1,0:T(8,128)S(1)}, u32[]{:S(2)}, u32[]{:S(2)}) collective-permute-start(f32[256,128]{1,0:T(8,128)S(1)} %bitcast.4), channel_id=1, source_target_pairs={{0,16},{8,24},{16,0},{24,8},{1,17},{9,25},{17,1},{25,9},{2,18},{10... | collective-permute-start | bytes 393224 | tf_op jit(solution)/shard_map/ppermute | solution.py:280
  61.6 13.9 %collective-permute-start.11 = (f32[256,128]{1,0:T(8,128)S(1)}, f32[256,128]{1,0:T(8,128)S(1)}, u32[]{:S(2)}, u32[]{:S(2)}) collective-permute-start(f32[256,128]{1,0:T(8,128)S(1)} %bitcast.5), channel_id=1, source_target_pairs={{0,8},{8,16},{16,24},{24,0},{1,9},{9,17},{17,25},{25,1},{2,10},{10... | collective-permute-start | bytes 393224 | tf_op jit(solution)/shard_map/ppermute | solution.py:280
  63.1 11.5 %collective-permute-start.16 = (f32[128,128]{1,0:T(8,128)S(1)}, f32[128,128]{1,0:T(8,128)S(1)}, u32[]{:S(2)}, u32[]{:S(2)}) collective-permute-start(f32[128,128]{1,0:T(8,128)S(1)} %src_y_sum.1.src_own), channel_id=1, source_target_pairs={{0,1},{1,0},{2,3},{3,2},{4,5},{5,4},{6,7},{7,6},{8,9},{9,8},{10,11... | collective-permute-start | bytes 196616 | tf_op jit(solution)/shard_map/ppermute | solution.py:280
  69.7 3.8 %collective-permute-start.14 = (f32[24,128]{1,0:T(8,128)S(1)}, f32[24,128]{1,0:T(8,128)S(1)}, u32[]{:S(2)}, u32[]{:S(2)}) collective-permute-start(f32[24,128]{1,0:T(8,128)S(1)} %near_sum.1.refs_0_), channel_id=1, source_target_pairs={{0,6},{2,4},{4,2},{6,0},{1,7},{3,5},{5,3},{7,1},{8,14},{10,12},{12... | collective-permute-start | bytes 36872 | tf_op jit(solution)/shard_map/ppermute | solution.py:289
  73.5 2.0 %collective-permute-start.15 = (f32[24,128]{1,0:T(8,128)S(1)}, f32[24,128]{1,0:T(8,128)S(1)}, u32[]{:S(2)}, u32[]{:S(2)}) collective-permute-start(f32[24,128]{1,0:T(8,128)S(1)} %far_sum.1.own), channel_id=1, source_target_pairs={{0,1},{1,0},{2,3},{3,2},{4,5},{5,4},{6,7},{7,6},{8,9},{9,8},{10,11... | collective-permute-start | bytes 36872 | tf_op jit(solution)/shard_map/ppermute | solution.py:280

commit v6 on v5

--- a/solution.py
+++ b/solution.py
@@ -57,7 +57,7 @@
     parts = [pl.ds(s * GROUP, GROUP) for s in range(steps)]
     large = [pltpu.make_async_copy(counts_hbm.at[part], counts.at[part], sems.at[3 + s])
              for s, part in enumerate(parts)]
-    for copy in small + large:
+    for copy in small[::-1] + large:
         copy.start()
     small[2].wait()
     dst_rows[...] = halves(dst[...], 1)
@@ -230,12 +230,15 @@
         out[z, share + each:, :] = m[zs * each:]
 
 
-def z_kernel(w, copies, tail):
+def tail_kernel(share, w, tail):
+    tail[...] = jnp.sum(w[:, share:, :], axis=0)
+
+
+def z_kernel(w, copies):
     share = copies.shape[1]
-    total = jnp.sum(w[...], axis=0)
+    total = jnp.sum(w[:, :share, :], axis=0)
     for z in range(copies.shape[0]):
-        copies[z] = total[:share]
-    tail[...] = total[share:]
+        copies[z] = total
 
 
 def end_kernel(scales, hour_ref, b0, b1, b2, b3, own, other, src_own, src_other,
@@ -289,6 +292,14 @@
     return lax.ppermute(x, axis, [(i, flip(i, n)) for i in range(n)])
 
 
+def near(i, n):
+    return i ^ 1
+
+
+def far(i, n):
+    return n - 1 - i
+
+
 def around(x, axis):
     return [x] + [shifted(x, axis, s) for s in range(1, lax.axis_size(axis))]
 
@@ -302,15 +313,19 @@
     m = [m0] + [shifted(v, "x", s) for s, v in ((1, m1), (2, m2), (3, m3))]
     share = a0.shape[0] // zs
     each = (m0.shape[0] - 8) // zs
+    src_half = summed("src_near_sum", src_half, paired(src_half, "y", near))
     w = small_call(x_kernel, "x_sums", struct(zs, share + each + 8, q1), [*a, *m])
-    src_half = summed("src_y_sum", *around(src_half, "y"))
+    w = swapped(w, "z")
+    src_half = summed("src_far_sum", src_half, paired(src_half, "y", far))
+    w, src_half = lax.optimization_barrier((w, src_half))
     src_other = shifted(src_half, "core", 1)
-    w = lax.optimization_barrier((swapped(w, "z"), src_half))[0]
-    copies, tail = small_call(z_kernel, "z_sums", [struct(zs, share, q1), struct(each + 8, q1)], [w])
-    tail = summed("near_sum", tail, paired(tail, "y", lambda i, n: i ^ 1))
+    tail = small_call(functools.partial(tail_kernel, share), "tail_sums", struct(each + 8, q1), [w])
+    came = paired(tail, "y", near)
+    copies = small_call(z_kernel, "z_sums", struct(zs, share, q1), [w], 1 << 34)
     block = swapped(copies, "z").reshape(zs * share, q1)
-    block = lax.optimization_barrier((block, tail))[0]
-    tail = summed("far_sum", tail, paired(tail, "y", lambda i, n: n - 1 - i))
+    tail = summed("near_sum", tail, came)
+    tail = summed("far_sum", tail, paired(tail, "y", far))
+    block, tail = lax.optimization_barrier((block, tail))
     other = shifted(tail, "core", 1)
     blocks = around(block, "x")
     grad_src, grad_dst, grad_hour, grad_core = end_call(

time: 77.4 us -> 77.4 us (level)
  the two profiles are of different devices: /device:TPU:3 before, /device:TPU:8 now
where the time goes in v6:
time: 77.4 us; the launch traced here: 75.8 us
  starting transfers between devices  33.4 us (43%)
  waiting for transfers between devices  23.5 us (30%)
  Pallas kernels  17.2 us (22%)
  local copies, waits for them, and re-layouts  0.99 us (1%)
    all_to_all x2, starting transfers between devices, swapped(): return lax.all_to_all(x, axis, split_axis=0, concat_axis=0, tiled=True)  14.1 us
    pallas_call x1, Pallas kernels, main_call(): pl.pallas_call(main_kernel, out_shape=[struct(block, q1)] * X + [struct(h...  13.5 us
    ppermute x12, starting transfers between devices, shifted(): return lax.ppermute(x, axis, [(i, (i + s) % n) for i in range(n)])  13.5 us
    ppermute x4, waiting for transfers between devices, paired(): return lax.ppermute(x, axis, [(i, flip(i, n)) for i in range(n)])  10.2 us
    ppermute x12, waiting for transfers between devices, shifted(): return lax.ppermute(x, axis, [(i, (i + s) % n) for i in range(n)])  10.1 us
    ppermute x4, starting transfers between devices, paired(): return lax.ppermute(x, axis, [(i, flip(i, n)) for i in range(n)])  5.88 us
    all_to_all x2, waiting for transfers between devices, swapped(): return lax.all_to_all(x, axis, split_axis=0, concat_axis=0, tiled=True)  3.18 us
  transfers between devices with their start and end apart: 18, of which 14 were waited for; matrix products, arithmetic and copies ran while one was open for 0% of the time, Pallas kernels for 1%

profile of v6, /device:TPU:8, one launch (start us, length us, event | category | flops | bytes accessed | tf_op | source)
XLA Modules:
  0.0 75.8 jit_solution(13868227832865871246)
XLA Ops:
  0.6 13.5 %all_terms.1 = (f32[256,128]{1,0:T(8,128)}, f32[256,128]{1,0:T(8,128)}, f32[256,128]{1,0:T(8,128)}, f32[256,128]{1,0:T(8,128)}, f32[5,128,128]{2,1,0:T(8,128)}, /*index=5*/f32[5,128,128]{2,1,0:T(8,128)}) custom-call(f32[8,32]{1,0:T(8,128)} %hour_ref.3, s32[8,256,1024]{2,1,0:T(8,128)} %counts_hbm.1, f32[256,128]{1,0:T(8,128)} %src_hbm.1, ...), custom_call_target="tpu_custom_call" | custom-call | flops 4831838208 | bytes 14680064 | tf_op jit(solution)/shard_map/all_terms/pallas_call | solution.py:133
  14.3 1.6 %collective-permute-start = (f32[256,128]{1,0:T(8,128)}, f32[256,128]{1,0:T(8,128)S(1)}, u32[]{:S(2)}, u32[]{:S(2)}) collective-permute-start(f32[256,128]{1,0:T(8,128)} %get-tuple-element.24), channel_id=1, source_target_pairs={{0,8},{8,16},{16,24},{24,0},{1,9},{9,17},{17,25},{25,1},{2,10},{10... | collective-permute-start | bytes 393224 | tf_op jit(solution)/shard_map/ppermute | solution.py:283
  15.8 2.7 %collective-permute-start.1 = (f32[256,128]{1,0:T(8,128)}, f32[256,128]{1,0:T(8,128)S(1)}, u32[]{:S(2)}, u32[]{:S(2)}) collective-permute-start(f32[256,128]{1,0:T(8,128)} %get-tuple-element.25), channel_id=1, source_target_pairs={{0,16},{8,24},{16,0},{24,8},{1,17},{9,25},{17,1},{25,9},{2,18},{10... | collective-permute-start | bytes 393224 | tf_op jit(solution)/shard_map/ppermute | solution.py:283
  18.6 1.4 %collective-permute-start.2 = (f32[256,128]{1,0:T(8,128)}, f32[256,128]{1,0:T(8,128)S(1)}, u32[]{:S(2)}, u32[]{:S(2)}) collective-permute-start(f32[256,128]{1,0:T(8,128)} %get-tuple-element.26), channel_id=1, source_target_pairs={{0,24},{8,0},{16,8},{24,16},{1,25},{9,1},{17,9},{25,17},{2,26},{10... | collective-permute-start | bytes 393224 | tf_op jit(solution)/shard_map/ppermute | solution.py:283
  20.0 1.0 %copy-done.3 = f32[5,128,128]{2,1,0:T(8,128)S(1)} copy-done((f32[5,128,128]{2,1,0:T(8,128)S(1)}, f32[5,128,128]{2,1,0:T(8,128)}, u32[]{:S(2)}) %copy-start.3) | copy-done | bytes 327704
  22.4 0.9 %collective-permute-start.5 = (f32[136,128]{1,0:T(8,128)S(1)}, f32[136,128]{1,0:T(8,128)S(1)}, u32[]{:S(2)}, u32[]{:S(2)}) collective-permute-start(f32[136,128]{1,0:T(8,128)S(1)} %get-tuple-element.31), channel_id=1, source_target_pairs={{0,16},{8,24},{16,0},{24,8},{1,17},{9,25},{17,1},{25,9},{2,18},{10... | collective-permute-start | bytes 208904 | tf_op jit(solution)/shard_map/ppermute | solution.py:283
  23.3 2.1 %collective-permute-start.6 = (f32[136,128]{1,0:T(8,128)S(1)}, f32[136,128]{1,0:T(8,128)S(1)}, u32[]{:S(2)}, u32[]{:S(2)}) collective-permute-start(f32[136,128]{1,0:T(8,128)S(1)} %get-tuple-element.32), channel_id=1, source_target_pairs={{0,24},{8,0},{16,8},{24,16},{1,25},{9,1},{17,9},{25,17},{2,26},{10... | collective-permute-start | bytes 208904 | tf_op jit(solution)/shard_map/ppermute | solution.py:283
  25.9 2.9 %collective-permute-done.4.m1 = f32[136,128]{1,0:T(8,128)S(1)} collective-permute-done((f32[136,128]{1,0:T(8,128)S(1)}, f32[136,128]{1,0:T(8,128)S(1)}, u32[]{:S(2)}, u32[]{:S(2)}) %collective-permute-start.4) | collective-permute-done | bytes 69664 | tf_op jit(solution)/shard_map/ppermute | solution.py:283
  29.7 8.5 %all-to-all-start = ((f32[8,56,128]{2,1,0:T(8,128)}), f32[8,56,128]{2,1,0:T(8,128)S(1)}, u32[]{:S(2)}, u32[]{:S(2)}) async-start(f32[8,56,128]{2,1,0:T(8,128)} %x_sums.1), calls=%async_computation | async-start | bytes 458752 | tf_op jit(solution)/shard_map/all_to_all | solution.py:287
  38.6 3.8 %collective-permute-done.7.refs_1_ = f32[128,128]{1,0:T(8,128)S(1)} collective-permute-done((f32[128,128]{1,0:T(8,128)S(1)}, f32[128,128]{1,0:T(8,128)S(1)}, u32[]{:S(2)}, u32[]{:S(2)}) %collective-permute-start.7) | collective-permute-done | bytes 65568 | tf_op jit(solution)/shard_map/ppermute | solution.py:292
  42.4 1.7 %collective-permute-start.8 = (f32[128,128]{1,0:T(8,128)S(1)}, f32[128,128]{1,0:T(8,128)S(1)}, u32[]{:S(2)}, u32[]{:S(2)}) collective-permute-start(f32[128,128]{1,0:T(8,128)S(1)} %src_near_sum.1.refs_0_), channel_id=1, source_target_pairs={{0,6},{2,4},{4,2},{6,0},{1,7},{3,5},{5,3},{7,1},{8,14},{10,12},{12... | collective-permute-start | bytes 196616 | tf_op jit(solution)/shard_map/ppermute | solution.py:292
  44.1 2.7 %collective-permute-done.8.refs_1_ = f32[128,128]{1,0:T(8,128)S(1)} collective-permute-done((f32[128,128]{1,0:T(8,128)S(1)}, f32[128,128]{1,0:T(8,128)S(1)}, u32[]{:S(2)}, u32[]{:S(2)}) %collective-permute-start.8) | collective-permute-done | bytes 65568 | tf_op jit(solution)/shard_map/ppermute | solution.py:292
  46.8 1.6 %all-to-all-done.w = f32[8,56,128]{2,1,0:T(8,128)S(1)} async-done(((f32[8,56,128]{2,1,0:T(8,128)}), f32[8,56,128]{2,1,0:T(8,128)S(1)}, u32[]{:S(2)}, u32[]{:S(2)}) %all-to-all-start) | async-done | bytes 229408 | tf_op jit(solution)/shard_map/all_to_all | solution.py:287
  49.1 5.6 %all-to-all-start.1 = ((f32[8,32,128]{2,1,0:T(8,128)}), f32[8,32,128]{2,1,0:T(8,128)S(1)}, u32[]{:S(2)}, u32[]{:S(2)}) async-start(f32[8,32,128]{2,1,0:T(8,128)} %z_sums.1), calls=%async_computation.1 | async-start | bytes 262144 | tf_op jit(solution)/shard_map/all_to_all | solution.py:287
  54.7 1.7 %collective-permute-start.9 = (f32[24,128]{1,0:T(8,128)S(1)}, f32[24,128]{1,0:T(8,128)S(1)}, u32[]{:S(2)}, u32[]{:S(2)}) collective-permute-start(f32[24,128]{1,0:T(8,128)S(1)} %tail_sums.1.refs_0_), channel_id=1, source_target_pairs={{0,2},{2,0},{4,6},{6,4},{1,3},{3,1},{5,7},{7,5},{8,10},{10,8},{12,... | collective-permute-start | bytes 36872 | tf_op jit(solution)/shard_map/ppermute | solution.py:292
  56.4 2.0 %collective-permute-done.9.refs_1_ = f32[24,128]{1,0:T(8,128)S(1)} collective-permute-done((f32[24,128]{1,0:T(8,128)S(1)}, f32[24,128]{1,0:T(8,128)S(1)}, u32[]{:S(2)}, u32[]{:S(2)}) %collective-permute-start.9) | collective-permute-done | bytes 12320 | tf_op jit(solution)/shard_map/ppermute | solution.py:292
  58.5 2.0 %collective-permute-start.10 = (f32[24,128]{1,0:T(8,128)S(1)}, f32[24,128]{1,0:T(8,128)S(1)}, u32[]{:S(2)}, u32[]{:S(2)}) collective-permute-start(f32[24,128]{1,0:T(8,128)S(1)} %near_sum.1.refs_0_), channel_id=1, source_target_pairs={{0,6},{2,4},{4,2},{6,0},{1,7},{3,5},{5,3},{7,1},{8,14},{10,12},{12... | collective-permute-start | bytes 36872 | tf_op jit(solution)/shard_map/ppermute | solution.py:292
  60.5 1.7 %collective-permute-done.10.refs_1_ = f32[24,128]{1,0:T(8,128)S(1)} collective-permute-done((f32[24,128]{1,0:T(8,128)S(1)}, f32[24,128]{1,0:T(8,128)S(1)}, u32[]{:S(2)}, u32[]{:S(2)}) %collective-permute-start.10) | collective-permute-done | bytes 12320 | tf_op jit(solution)/shard_map/ppermute | solution.py:292
  62.2 1.6 %all-to-all-done.1 = f32[8,32,128]{2,1,0:T(8,128)S(1)} async-done(((f32[8,32,128]{2,1,0:T(8,128)}), f32[8,32,128]{2,1,0:T(8,128)S(1)}, u32[]{:S(2)}, u32[]{:S(2)}) %all-to-all-start.1) | async-done | bytes 131104 | tf_op jit(solution)/shard_map/all_to_all | solution.py:287
  63.8 2.7 %collective-permute-start.13 = (f32[256,128]{1,0:T(8,128)S(1)}, f32[256,128]{1,0:T(8,128)S(1)}, u32[]{:S(2)}, u32[]{:S(2)}) collective-permute-start(f32[256,128]{1,0:T(8,128)S(1)} %bitcast.3), channel_id=1, source_target_pairs={{0,24},{8,0},{16,8},{24,16},{1,25},{9,1},{17,9},{25,17},{2,26},{10... | collective-permute-start | bytes 393224 | tf_op jit(solution)/shard_map/ppermute | solution.py:283
  68.6 1.7 %collective-permute-done.13.b3 = f32[256,128]{1,0:T(8,128)S(1)} collective-permute-done((f32[256,128]{1,0:T(8,128)S(1)}, f32[256,128]{1,0:T(8,128)S(1)}, u32[]{:S(2)}, u32[]{:S(2)}) %collective-permute-start.13) | collective-permute-done | bytes 131104 | tf_op jit(solution)/shard_map/ppermute | solution.py:283
  70.4 2.6 %collective-permute-done.12.b2 = f32[256,128]{1,0:T(8,128)S(1)} collective-permute-done((f32[256,128]{1,0:T(8,128)S(1)}, f32[256,128]{1,0:T(8,128)S(1)}, u32[]{:S(2)}, u32[]{:S(2)}) %collective-permute-start.12) | collective-permute-done | bytes 131104 | tf_op jit(solution)/shard_map/ppermute | solution.py:283
  73.0 1.3 %collective-permute-done.11.b1 = f32[256,128]{1,0:T(8,128)S(1)} collective-permute-done((f32[256,128]{1,0:T(8,128)S(1)}, f32[256,128]{1,0:T(8,128)S(1)}, u32[]{:S(2)}, u32[]{:S(2)}) %collective-permute-start.11) | collective-permute-done | bytes 131104 | tf_op jit(solution)/shard_map/ppermute | solution.py:283
  74.3 1.5 %outputs.1 = (f32[2,128,128]{2,1,0:T(8,128)}, f32[4,256,128]{2,1,0:T(8,128)}, f32[8,32]{1,0:T(8,128)}, f32[32,4,128]{2,1,0:T(4,128)}) custom-call(f32[8,32]{1,0:T(8,128)S(1)} %copy-done.1, f32[256,128]{1,0:T(8,128)S(1)} %bitcast.6, f32[256,128]{1,0:T(8,128)S(1)} %collective-permute-done.11.b1, f32[256,128]{1,0:T(8,128)S(1)} %collective-permute-done.12.b2, ...), custom_call_target="tpu_custom_call" | custom-call | flops 1048576 | bytes 1048576 | tf_op jit(solution)/shard_map/outputs/pallas_call | solution.py:271
  (30 shorter events, 6.3 us)
Async XLA Ops:
  0.6 19.4 %copy-start.2 = (f32[32,128,128]{2,1,0:T(8,128)S(1)}, f32[32,128,128]{2,1,0:T(8,128)}, u32[]{:S(2)}) copy-start(f32[32,128,128]{2,1,0:T(8,128)} %core.1) | copy-start | bytes 6291460
  14.2 5.8 %collective-permute-start.3 = (f32[5,128,128]{2,1,0:T(8,128)}, f32[5,128,128]{2,1,0:T(8,128)S(1)}, u32[]{:S(2)}, u32[]{:S(2)}) collective-permute-start(f32[5,128,128]{2,1,0:T(8,128)} %get-tuple-element.28), channel_id=1, source_target_pairs={{0,1},{1,0},{2,3},{3,2},{4,5},{5,4},{6,7},{7,6},{8,9},{9,8},{10,11... | collective-permute-start | bytes 983048 | tf_op jit(solution)/shard_map/ppermute | solution.py:283
  14.3 9.0 %collective-permute-start = (f32[256,128]{1,0:T(8,128)}, f32[256,128]{1,0:T(8,128)S(1)}, u32[]{:S(2)}, u32[]{:S(2)}) collective-permute-start(f32[256,128]{1,0:T(8,128)} %get-tuple-element.24), channel_id=1, source_target_pairs={{0,8},{8,16},{16,24},{24,0},{1,9},{9,17},{17,25},{25,1},{2,10},{10... | collective-permute-start | bytes 393224 | tf_op jit(solution)/shard_map/ppermute | solution.py:283
  15.8 10.0 %collective-permute-start.1 = (f32[256,128]{1,0:T(8,128)}, f32[256,128]{1,0:T(8,128)S(1)}, u32[]{:S(2)}, u32[]{:S(2)}) collective-permute-start(f32[256,128]{1,0:T(8,128)} %get-tuple-element.25), channel_id=1, source_target_pairs={{0,16},{8,24},{16,0},{24,8},{1,17},{9,25},{17,1},{25,9},{2,18},{10... | collective-permute-start | bytes 393224 | tf_op jit(solution)/shard_map/ppermute | solution.py:283
  18.6 7.3 %collective-permute-start.2 = (f32[256,128]{1,0:T(8,128)}, f32[256,128]{1,0:T(8,128)S(1)}, u32[]{:S(2)}, u32[]{:S(2)}) collective-permute-start(f32[256,128]{1,0:T(8,128)} %get-tuple-element.26), channel_id=1, source_target_pairs={{0,24},{8,0},{16,8},{24,16},{1,25},{9,1},{17,9},{25,17},{2,26},{10... | collective-permute-start | bytes 393224 | tf_op jit(solution)/shard_map/ppermute | solution.py:283
  20.0 1.0 %copy-start.3 = (f32[5,128,128]{2,1,0:T(8,128)S(1)}, f32[5,128,128]{2,1,0:T(8,128)}, u32[]{:S(2)}) copy-start(f32[5,128,128]{2,1,0:T(8,128)} %get-tuple-element.27.own) | copy-start | bytes 983044
  21.0 8.0 %copy-start = (f32[256,128]{1,0:T(8,128)S(1)}, f32[256,128]{1,0:T(8,128)}, u32[]{:S(2)}) copy-start(f32[256,128]{1,0:T(8,128)} %get-tuple-element.23.a0) | copy-start | bytes 393220
  21.7 7.0 %collective-permute-start.4 = (f32[136,128]{1,0:T(8,128)S(1)}, f32[136,128]{1,0:T(8,128)S(1)}, u32[]{:S(2)}, u32[]{:S(2)}) collective-permute-start(f32[136,128]{1,0:T(8,128)S(1)} %get-tuple-element.30), channel_id=1, source_target_pairs={{0,8},{8,16},{16,24},{24,0},{1,9},{9,17},{17,25},{25,1},{2,10},{10... | collective-permute-start | bytes 208904 | tf_op jit(solution)/shard_map/ppermute | solution.py:283
  22.4 6.3 %collective-permute-start.5 = (f32[136,128]{1,0:T(8,128)S(1)}, f32[136,128]{1,0:T(8,128)S(1)}, u32[]{:S(2)}, u32[]{:S(2)}) collective-permute-start(f32[136,128]{1,0:T(8,128)S(1)} %get-tuple-element.31), channel_id=1, source_target_pairs={{0,16},{8,24},{16,0},{24,8},{1,17},{9,25},{17,1},{25,9},{2,18},{10... | collective-permute-start | bytes 208904 | tf_op jit(solution)/shard_map/ppermute | solution.py:283
  23.3 5.7 %collective-permute-start.6 = (f32[136,128]{1,0:T(8,128)S(1)}, f32[136,128]{1,0:T(8,128)S(1)}, u32[]{:S(2)}, u32[]{:S(2)}) collective-permute-start(f32[136,128]{1,0:T(8,128)S(1)} %get-tuple-element.32), channel_id=1, source_target_pairs={{0,24},{8,0},{16,8},{24,16},{1,25},{9,1},{17,9},{25,17},{2,26},{10... | collective-permute-start | bytes 208904 | tf_op jit(solution)/shard_map/ppermute | solution.py:283
  29.7 18.7 %all-to-all-start = ((f32[8,56,128]{2,1,0:T(8,128)}), f32[8,56,128]{2,1,0:T(8,128)S(1)}, u32[]{:S(2)}, u32[]{:S(2)}) async-start(f32[8,56,128]{2,1,0:T(8,128)} %x_sums.1), calls=%async_computation | async-start | bytes 458752 | tf_op jit(solution)/shard_map/all_to_all | solution.py:287
  38.1 4.3 %collective-permute-start.7 = (f32[128,128]{1,0:T(8,128)S(1)}, f32[128,128]{1,0:T(8,128)S(1)}, u32[]{:S(2)}, u32[]{:S(2)}) collective-permute-start(f32[128,128]{1,0:T(8,128)S(1)} %get-tuple-element.33.refs_0_), channel_id=1, source_target_pairs={{0,2},{2,0},{4,6},{6,4},{1,3},{3,1},{5,7},{7,5},{8,10},{10,8},{12,... | collective-permute-start | bytes 196616 | tf_op jit(solution)/shard_map/ppermute | solution.py:292
  42.4 4.4 %collective-permute-start.8 = (f32[128,128]{1,0:T(8,128)S(1)}, f32[128,128]{1,0:T(8,128)S(1)}, u32[]{:S(2)}, u32[]{:S(2)}) collective-permute-start(f32[128,128]{1,0:T(8,128)S(1)} %src_near_sum.1.refs_0_), channel_id=1, source_target_pairs={{0,6},{2,4},{4,2},{6,0},{1,7},{3,5},{5,3},{7,1},{8,14},{10,12},{12... | collective-permute-start | bytes 196616 | tf_op jit(solution)/shard_map/ppermute | solution.py:292
  46.8 27.5 %copy-start.1 = (f32[8,32]{1,0:T(8,128)S(1)}, f32[8,32]{1,0:T(8,128)}, u32[]{:S(2)}) copy-start(f32[8,32]{1,0:T(8,128)} %hour_ref.3) | copy-start | bytes 3076
  49.1 14.7 %all-to-all-start.1 = ((f32[8,32,128]{2,1,0:T(8,128)}), f32[8,32,128]{2,1,0:T(8,128)S(1)}, u32[]{:S(2)}, u32[]{:S(2)}) async-start(f32[8,32,128]{2,1,0:T(8,128)} %z_sums.1), calls=%async_computation.1 | async-start | bytes 262144 | tf_op jit(solution)/shard_map/all_to_all | solution.py:287
  54.7 3.8 %collective-permute-start.9 = (f32[24,128]{1,0:T(8,128)S(1)}, f32[24,128]{1,0:T(8,128)S(1)}, u32[]{:S(2)}, u32[]{:S(2)}) collective-permute-start(f32[24,128]{1,0:T(8,128)S(1)} %tail_sums.1.refs_0_), channel_id=1, source_target_pairs={{0,2},{2,0},{4,6},{6,4},{1,3},{3,1},{5,7},{7,5},{8,10},{10,8},{12,... | collective-permute-start | bytes 36872 | tf_op jit(solution)/shard_map/ppermute | solution.py:292
  58.5 3.7 %collective-permute-start.10 = (f32[24,128]{1,0:T(8,128)S(1)}, f32[24,128]{1,0:T(8,128)S(1)}, u32[]{:S(2)}, u32[]{:S(2)}) collective-permute-start(f32[24,128]{1,0:T(8,128)S(1)} %near_sum.1.refs_0_), channel_id=1, source_target_pairs={{0,6},{2,4},{4,2},{6,0},{1,7},{3,5},{5,3},{7,1},{8,14},{10,12},{12... | collective-permute-start | bytes 36872 | tf_op jit(solution)/shard_map/ppermute | solution.py:292
  63.8 6.6 %collective-permute-start.13 = (f32[256,128]{1,0:T(8,128)S(1)}, f32[256,128]{1,0:T(8,128)S(1)}, u32[]{:S(2)}, u32[]{:S(2)}) collective-permute-start(f32[256,128]{1,0:T(8,128)S(1)} %bitcast.3), channel_id=1, source_target_pairs={{0,24},{8,0},{16,8},{24,16},{1,25},{9,1},{17,9},{25,17},{2,26},{10... | collective-permute-start | bytes 393224 | tf_op jit(solution)/shard_map/ppermute | solution.py:283
  66.4 6.6 %collective-permute-start.12 = (f32[256,128]{1,0:T(8,128)S(1)}, f32[256,128]{1,0:T(8,128)S(1)}, u32[]{:S(2)}, u32[]{:S(2)}) collective-permute-start(f32[256,128]{1,0:T(8,128)S(1)} %bitcast.4), channel_id=1, source_target_pairs={{0,16},{8,24},{16,0},{24,8},{1,17},{9,25},{17,1},{25,9},{2,18},{10... | collective-permute-start | bytes 393224 | tf_op jit(solution)/shard_map/ppermute | solution.py:283
  67.2 7.1 %collective-permute-start.11 = (f32[256,128]{1,0:T(8,128)S(1)}, f32[256,128]{1,0:T(8,128)S(1)}, u32[]{:S(2)}, u32[]{:S(2)}) collective-permute-start(f32[256,128]{1,0:T(8,128)S(1)} %bitcast.5), channel_id=1, source_target_pairs={{0,8},{8,16},{16,24},{24,0},{1,9},{9,17},{17,25},{25,1},{2,10},{10... | collective-permute-start | bytes 393224 | tf_op jit(solution)/shard_map/ppermute | solution.py:283
  67.3 1.3 %collective-permute-start.15 = (f32[128,128]{1,0:T(8,128)S(1)}, f32[128,128]{1,0:T(8,128)S(1)}, u32[]{:S(2)}, u32[]{:S(2)}) collective-permute-start(f32[128,128]{1,0:T(8,128)S(1)} %src_far_sum.1.src_own), channel_id=1, source_target_pairs={{0,1},{1,0},{2,3},{3,2},{4,5},{5,4},{6,7},{7,6},{8,9},{9,8},{10,11... | collective-permute-start | bytes 196616 | tf_op jit(solution)/shard_map/ppermute | solution.py:283
  67.3 1.3 %collective-permute-start.14 = (f32[24,128]{1,0:T(8,128)S(1)}, f32[24,128]{1,0:T(8,128)S(1)}, u32[]{:S(2)}, u32[]{:S(2)}) collective-permute-start(f32[24,128]{1,0:T(8,128)S(1)} %far_sum.1.own), channel_id=1, source_target_pairs={{0,1},{1,0},{2,3},{3,2},{4,5},{5,4},{6,7},{7,6},{8,9},{9,8},{10,11... | collective-permute-start | bytes 36872 | tf_op jit(solution)/shard_map/ppermute | solution.py:283

commit v7 on v6

--- a/solution.py
+++ b/solution.py
@@ -234,6 +234,12 @@
     tail[...] = jnp.sum(w[:, share:, :], axis=0)
 
 
+def pair_kernel(own, other, out):
+    c = lax.axis_index("core")
+    out[c] = own[...]
+    out[1 - c] = other[...]
+
+
 def z_kernel(w, copies):
     share = copies.shape[1]
     total = jnp.sum(w[:, :share, :], axis=0)
@@ -241,7 +247,7 @@
         copies[z] = total
 
 
-def end_kernel(scales, hour_ref, b0, b1, b2, b3, own, other, src_own, src_other,
+def end_kernel(scales, hour_ref, b0, b1, b2, b3, tails, more, src_own, src_other,
                src_out, dst_out, hour_out, core_out, both):
     x, c = lax.axis_index("x"), lax.axis_index("core")
     src_scale, dst_scale, hour_scale, core_scale = scales
@@ -249,8 +255,7 @@
         dst_out[lax.rem(x - s + X, X)] = block[...] * dst_scale
     src_out[c] = src_own[...] * src_scale
     src_out[1 - c] = src_other[...] * src_scale
-    both[c] = own[...]
-    both[1 - c] = other[...]
+    both[...] = tails[...] + more[...]
     hours, rank = hour_ref.shape
     half = hours // CORES
     tiles = []
@@ -265,7 +270,7 @@
         core_out[r] = out
 
 
-def end_call(scales, hour, blocks, own, other, src_own, src_other):
+def end_call(scales, hour, blocks, tails, more, src_own, src_other):
     block, q1 = blocks[0].shape
     hours, rank = hour.shape
     return pl.pallas_call(
@@ -273,9 +278,9 @@
         in_specs=[SMEM] + [VMEM] * 8,
         out_specs=[VMEM] * 4,
         out_shape=[struct(CORES, *src_own.shape), struct(X, block, q1), struct(hours, rank), struct(rank, 4, q1)],
-        scratch_shapes=[pltpu.VMEM((CORES, *own.shape), F32)],
+        scratch_shapes=[pltpu.VMEM(tails.shape, F32)],
         compiler_params=params(8), cost_estimate=cost(1 << 20, 1 << 20), name="outputs",
-    )(hour, *blocks, own, other, src_own, src_other)
+    )(hour, *blocks, tails, more, src_own, src_other)
 
 
 def shifted(x, axis, s):
@@ -313,23 +318,24 @@
     m = [m0] + [shifted(v, "x", s) for s, v in ((1, m1), (2, m2), (3, m3))]
     share = a0.shape[0] // zs
     each = (m0.shape[0] - 8) // zs
+    src_half, *a = lax.optimization_barrier((src_half, *a))
     src_half = summed("src_near_sum", src_half, paired(src_half, "y", near))
+    m, src_half = lax.optimization_barrier((m, src_half))
     w = small_call(x_kernel, "x_sums", struct(zs, share + each + 8, q1), [*a, *m])
     w = swapped(w, "z")
     src_half = summed("src_far_sum", src_half, paired(src_half, "y", far))
     w, src_half = lax.optimization_barrier((w, src_half))
     src_other = shifted(src_half, "core", 1)
     tail = small_call(functools.partial(tail_kernel, share), "tail_sums", struct(each + 8, q1), [w])
-    came = paired(tail, "y", near)
-    copies = small_call(z_kernel, "z_sums", struct(zs, share, q1), [w], 1 << 34)
+    copies = small_call(z_kernel, "z_sums", struct(zs, share, q1), [w])
+    tails = small_call(pair_kernel, "both_tails", struct(CORES, *tail.shape), [tail, shifted(tail, "core", 1)])
+    tails = summed("near_sum", tails, paired(tails, "y", near))
     block = swapped(copies, "z").reshape(zs * share, q1)
-    tail = summed("near_sum", tail, came)
-    tail = summed("far_sum", tail, paired(tail, "y", far))
-    block, tail = lax.optimization_barrier((block, tail))
-    other = shifted(tail, "core", 1)
+    block, tails = lax.optimization_barrier((block, tails))
+    more = paired(tails, "y", far)
     blocks = around(block, "x")
     grad_src, grad_dst, grad_hour, grad_core = end_call(
-        scales, hour_factor, blocks, tail, other, src_half, src_other)
+        scales, hour_factor, blocks, tails, more, src_half, src_other)
     return (grad_src.reshape(src_factor.shape), grad_dst.reshape(dst_factor.shape), grad_hour, grad_core)
 
 

time: 77.4 us -> 74.6 us (0.964)
  starting transfers between devices: 33.4 us -> 31.4 us
    ppermute x12, waiting for transfers between devices: 10.1 us -> 3.13 us  [shifted(): return lax.ppermute(x, axis, [(i, (i + s) % n) for i in range(n)])]
    all_to_all x2, waiting for transfers between devices: 3.18 us -> 9.71 us  [swapped(): return lax.all_to_all(x, axis, split_axis=0, concat_axis=0, tiled=True)]
    all_to_all x2, starting transfers between devices: 14.1 us -> 11.8 us  [swapped(): return lax.all_to_all(x, axis, split_axis=0, concat_axis=0, tiled=True)]
  transfers between devices with their start and end apart: 18 -> 18, of which waited for: 14 -> 10; matrix products, arithmetic and copies ran while one was open for 0% -> 0% of each run, Pallas kernels for 1% -> 1%
where the time goes in v7:
time: 74.6 us; the launch traced here: 73.8 us
  starting transfers between devices  31.4 us (42%)
  waiting for transfers between devices  23.4 us (31%)
  Pallas kernels  17.2 us (23%)
  local copies, waits for them, and re-layouts  0.99 us (1%)
    ppermute x12, starting transfers between devices, shifted(): return lax.ppermute(x, axis, [(i, (i + s) % n) for i in range(n)])  14 us
    pallas_call x1, Pallas kernels, main_call(): pl.pallas_call(main_kernel, out_shape=[struct(block, q1)] * X + [struct(h...  13.5 us
    all_to_all x2, starting transfers between devices, swapped(): return lax.all_to_all(x, axis, split_axis=0, concat_axis=0, tiled=True)  11.8 us
    ppermute x4, waiting for transfers between devices, paired(): return lax.ppermute(x, axis, [(i, flip(i, n)) for i in range(n)])  10.6 us
    all_to_all x2, waiting for transfers between devices, swapped(): return lax.all_to_all(x, axis, split_axis=0, concat_axis=0, tiled=True)  9.71 us
    ppermute x4, starting transfers between devices, paired(): return lax.ppermute(x, axis, [(i, flip(i, n)) for i in range(n)])  5.68 us
    ppermute x12, waiting for transfers between devices, shifted(): return lax.ppermute(x, axis, [(i, (i + s) % n) for i in range(n)])  3.13 us
    pallas_call x1, Pallas kernels, end_call(): pl.pallas_call(functools.partial(end_kernel, scales), in_specs=[SMEM] + [...  1.5 us
  transfers between devices with their start and end apart: 18, of which 10 were waited for; matrix products, arithmetic and copies ran while one was open for 0% of the time, Pallas kernels for 1%

profile of v7, /device:TPU:8, one launch (start us, length us, event | category | flops | bytes accessed | tf_op | source)
XLA Modules:
  0.0 73.8 jit_solution(8100800936235376701)
XLA Ops:
  0.6 13.5 %all_terms.1 = (f32[256,128]{1,0:T(8,128)}, f32[256,128]{1,0:T(8,128)}, f32[256,128]{1,0:T(8,128)}, f32[256,128]{1,0:T(8,128)}, f32[5,128,128]{2,1,0:T(8,128)}, /*index=5*/f32[5,128,128]{2,1,0:T(8,128)}) custom-call(f32[8,32]{1,0:T(8,128)} %hour_ref.3, s32[8,256,1024]{2,1,0:T(8,128)} %counts_hbm.1, f32[256,128]{1,0:T(8,128)} %src_hbm.1, ...), custom_call_target="tpu_custom_call" | custom-call | flops 4831838208 | bytes 14680064 | tf_op jit(solution)/shard_map/all_terms/pallas_call | solution.py:133
  14.3 1.6 %collective-permute-start.1 = (f32[256,128]{1,0:T(8,128)}, f32[256,128]{1,0:T(8,128)S(1)}, u32[]{:S(2)}, u32[]{:S(2)}) collective-permute-start(f32[256,128]{1,0:T(8,128)} %get-tuple-element.37), channel_id=1, source_target_pairs={{0,8},{8,16},{16,24},{24,0},{1,9},{9,17},{17,25},{25,1},{2,10},{10... | collective-permute-start | bytes 393224 | tf_op jit(solution)/shard_map/ppermute | solution.py:288
  15.8 2.7 %collective-permute-start.2 = (f32[256,128]{1,0:T(8,128)}, f32[256,128]{1,0:T(8,128)S(1)}, u32[]{:S(2)}, u32[]{:S(2)}) collective-permute-start(f32[256,128]{1,0:T(8,128)} %get-tuple-element.38), channel_id=1, source_target_pairs={{0,16},{8,24},{16,0},{24,8},{1,17},{9,25},{17,1},{25,9},{2,18},{10... | collective-permute-start | bytes 393224 | tf_op jit(solution)/shard_map/ppermute | solution.py:288
  18.6 1.4 %collective-permute-start.3 = (f32[256,128]{1,0:T(8,128)}, f32[256,128]{1,0:T(8,128)S(1)}, u32[]{:S(2)}, u32[]{:S(2)}) collective-permute-start(f32[256,128]{1,0:T(8,128)} %get-tuple-element.39), channel_id=1, source_target_pairs={{0,24},{8,0},{16,8},{24,16},{1,25},{9,1},{17,9},{25,17},{2,26},{10... | collective-permute-start | bytes 393224 | tf_op jit(solution)/shard_map/ppermute | solution.py:288
  20.0 1.0 %copy-done.3 = f32[5,128,128]{2,1,0:T(8,128)S(1)} copy-done((f32[5,128,128]{2,1,0:T(8,128)S(1)}, f32[5,128,128]{2,1,0:T(8,128)}, u32[]{:S(2)}) %copy-start.3) | copy-done | bytes 327704
  22.4 0.9 %collective-permute-start.5 = (f32[136,128]{1,0:T(8,128)S(1)}, f32[136,128]{1,0:T(8,128)S(1)}, u32[]{:S(2)}, u32[]{:S(2)}) collective-permute-start(f32[136,128]{1,0:T(8,128)S(1)} %get-tuple-element.46), channel_id=1, source_target_pairs={{0,16},{8,24},{16,0},{24,8},{1,17},{9,25},{17,1},{25,9},{2,18},{10... | collective-permute-start | bytes 208904 | tf_op jit(solution)/shard_map/ppermute | solution.py:288
  23.3 2.1 %collective-permute-start.6 = (f32[136,128]{1,0:T(8,128)S(1)}, f32[136,128]{1,0:T(8,128)S(1)}, u32[]{:S(2)}, u32[]{:S(2)}) collective-permute-start(f32[136,128]{1,0:T(8,128)S(1)} %get-tuple-element.47), channel_id=1, source_target_pairs={{0,24},{8,0},{16,8},{24,16},{1,25},{9,1},{17,9},{25,17},{2,26},{10... | collective-permute-start | bytes 208904 | tf_op jit(solution)/shard_map/ppermute | solution.py:288
  25.9 2.1 %collective-permute-start.7 = (f32[128,128]{1,0:T(8,128)S(1)}, f32[128,128]{1,0:T(8,128)S(1)}, u32[]{:S(2)}, u32[]{:S(2)}) collective-permute-start(f32[128,128]{1,0:T(8,128)S(1)} %get-tuple-element.48.refs_0_), channel_id=1, source_target_pairs={{0,2},{2,0},{4,6},{6,4},{1,3},{3,1},{5,7},{7,5},{8,10},{10,8},{12,... | collective-permute-start | bytes 196616 | tf_op jit(solution)/shard_map/ppermute | solution.py:297
  28.0 2.2 %collective-permute-done.7.refs_1_ = f32[128,128]{1,0:T(8,128)S(1)} collective-permute-done((f32[128,128]{1,0:T(8,128)S(1)}, f32[128,128]{1,0:T(8,128)S(1)}, u32[]{:S(2)}, u32[]{:S(2)}) %collective-permute-start.7) | collective-permute-done | bytes 65568 | tf_op jit(solution)/shard_map/ppermute | solution.py:297
  31.0 8.4 %all-to-all-start = ((f32[8,56,128]{2,1,0:T(8,128)}), f32[8,56,128]{2,1,0:T(8,128)S(1)}, u32[]{:S(2)}, u32[]{:S(2)}) async-start(f32[8,56,128]{2,1,0:T(8,128)} %x_sums.1), calls=%async_computation | async-start | bytes 458752 | tf_op jit(solution)/shard_map/all_to_all | solution.py:292
  39.4 1.6 %collective-permute-start.8 = (f32[128,128]{1,0:T(8,128)S(1)}, f32[128,128]{1,0:T(8,128)S(1)}, u32[]{:S(2)}, u32[]{:S(2)}) collective-permute-start(f32[128,128]{1,0:T(8,128)S(1)} %src_near_sum.1.refs_0_), channel_id=1, source_target_pairs={{0,6},{2,4},{4,2},{6,0},{1,7},{3,5},{5,3},{7,1},{8,14},{10,12},{12... | collective-permute-start | bytes 196616 | tf_op jit(solution)/shard_map/ppermute | solution.py:297
  41.0 2.7 %collective-permute-done.8.refs_1_ = f32[128,128]{1,0:T(8,128)S(1)} collective-permute-done((f32[128,128]{1,0:T(8,128)S(1)}, f32[128,128]{1,0:T(8,128)S(1)}, u32[]{:S(2)}, u32[]{:S(2)}) %collective-permute-start.8) | collective-permute-done | bytes 65568 | tf_op jit(solution)/shard_map/ppermute | solution.py:297
  43.7 5.9 %all-to-all-done.w = f32[8,56,128]{2,1,0:T(8,128)S(1)} async-done(((f32[8,56,128]{2,1,0:T(8,128)}), f32[8,56,128]{2,1,0:T(8,128)S(1)}, u32[]{:S(2)}, u32[]{:S(2)}) %all-to-all-start) | async-done | bytes 229408 | tf_op jit(solution)/shard_map/all_to_all | solution.py:292
  50.2 3.4 %all-to-all-start.1 = ((f32[8,32,128]{2,1,0:T(8,128)}), f32[8,32,128]{2,1,0:T(8,128)S(1)}, u32[]{:S(2)}, u32[]{:S(2)}) async-start(f32[8,32,128]{2,1,0:T(8,128)} %z_sums.1), calls=%async_computation.1 | async-start | bytes 262144 | tf_op jit(solution)/shard_map/all_to_all | solution.py:292
  53.7 1.2 %collective-permute-done.9.other = f32[24,128]{1,0:T(8,128)S(1)} collective-permute-done((f32[24,128]{1,0:T(8,128)S(1)}, f32[24,128]{1,0:T(8,128)S(1)}, u32[]{:S(2)}, u32[]{:S(2)}) %collective-permute-start.9) | collective-permute-done | bytes 12320 | tf_op jit(solution)/shard_map/ppermute | solution.py:288
  55.3 3.4 %collective-permute-done.10.refs_1_ = f32[2,24,128]{2,1,0:T(8,128)S(1)} collective-permute-done((f32[2,24,128]{2,1,0:T(8,128)S(1)}, f32[2,24,128]{2,1,0:T(8,128)S(1)}, u32[]{:S(2)}, u32[]{:S(2)}) %collective-permute-start.10) | collective-permute-done | bytes 24608 | tf_op jit(solution)/shard_map/ppermute | solution.py:297
  58.7 3.9 %all-to-all-done.1 = f32[8,32,128]{2,1,0:T(8,128)S(1)} async-done(((f32[8,32,128]{2,1,0:T(8,128)}), f32[8,32,128]{2,1,0:T(8,128)S(1)}, u32[]{:S(2)}, u32[]{:S(2)}) %all-to-all-start.1) | async-done | bytes 131104 | tf_op jit(solution)/shard_map/all_to_all | solution.py:292
  62.6 1.8 %collective-permute-start.13 = (f32[256,128]{1,0:T(8,128)S(1)}, f32[256,128]{1,0:T(8,128)S(1)}, u32[]{:S(2)}, u32[]{:S(2)}) collective-permute-start(f32[256,128]{1,0:T(8,128)S(1)} %bitcast.3), channel_id=1, source_target_pairs={{0,24},{8,0},{16,8},{24,16},{1,25},{9,1},{17,9},{25,17},{2,26},{10... | collective-permute-start | bytes 393224 | tf_op jit(solution)/shard_map/ppermute | solution.py:288
  64.4 1.2 %collective-permute-start.12 = (f32[256,128]{1,0:T(8,128)S(1)}, f32[256,128]{1,0:T(8,128)S(1)}, u32[]{:S(2)}, u32[]{:S(2)}) collective-permute-start(f32[256,128]{1,0:T(8,128)S(1)} %bitcast.4), channel_id=1, source_target_pairs={{0,16},{8,24},{16,0},{24,8},{1,17},{9,25},{17,1},{25,9},{2,18},{10... | collective-permute-start | bytes 393224 | tf_op jit(solution)/shard_map/ppermute | solution.py:288
  65.6 1.4 %collective-permute-start.11 = (f32[256,128]{1,0:T(8,128)S(1)}, f32[256,128]{1,0:T(8,128)S(1)}, u32[]{:S(2)}, u32[]{:S(2)}) collective-permute-start(f32[256,128]{1,0:T(8,128)S(1)} %bitcast.5), channel_id=1, source_target_pairs={{0,8},{8,16},{16,24},{24,0},{1,9},{9,17},{17,25},{25,1},{2,10},{10... | collective-permute-start | bytes 393224 | tf_op jit(solution)/shard_map/ppermute | solution.py:288
  67.0 1.6 %collective-permute-start.14 = (f32[2,24,128]{2,1,0:T(8,128)S(1)}, f32[2,24,128]{2,1,0:T(8,128)S(1)}, u32[]{:S(2)}, u32[]{:S(2)}) collective-permute-start(f32[2,24,128]{2,1,0:T(8,128)S(1)} %near_sum.1.tails), channel_id=1, source_target_pairs={{0,6},{2,4},{4,2},{6,0},{1,7},{3,5},{5,3},{7,1},{8,14},{10,12},{12... | collective-permute-start | bytes 73736 | tf_op jit(solution)/shard_map/ppermute | solution.py:297
  68.5 2.3 %collective-permute-done.14.more = f32[2,24,128]{2,1,0:T(8,128)S(1)} collective-permute-done((f32[2,24,128]{2,1,0:T(8,128)S(1)}, f32[2,24,128]{2,1,0:T(8,128)S(1)}, u32[]{:S(2)}, u32[]{:S(2)}) %collective-permute-start.14) | collective-permute-done | bytes 24608 | tf_op jit(solution)/shard_map/ppermute | solution.py:297
  70.9 1.3 %collective-permute-done.11.b1 = f32[256,128]{1,0:T(8,128)S(1)} collective-permute-done((f32[256,128]{1,0:T(8,128)S(1)}, f32[256,128]{1,0:T(8,128)S(1)}, u32[]{:S(2)}, u32[]{:S(2)}) %collective-permute-start.11) | collective-permute-done | bytes 131104 | tf_op jit(solution)/shard_map/ppermute | solution.py:288
  72.3 1.5 %outputs.1 = (f32[2,128,128]{2,1,0:T(8,128)}, f32[4,256,128]{2,1,0:T(8,128)}, f32[8,32]{1,0:T(8,128)}, f32[32,4,128]{2,1,0:T(4,128)}) custom-call(f32[8,32]{1,0:T(8,128)S(1)} %copy-done.1, f32[256,128]{1,0:T(8,128)S(1)} %bitcast.6, f32[256,128]{1,0:T(8,128)S(1)} %collective-permute-done.11.b1, f32[256,128]{1,0:T(8,128)S(1)} %collective-permute-done.12.b2, ...), custom_call_target="tpu_custom_call" | custom-call | flops 1048576 | bytes 1048576 | tf_op jit(solution)/shard_map/outputs/pallas_call | solution.py:276
  (30 shorter events, 4.1 us)
Async XLA Ops:
  0.6 19.4 %copy-start.2 = (f32[32,128,128]{2,1,0:T(8,128)S(1)}, f32[32,128,128]{2,1,0:T(8,128)}, u32[]{:S(2)}) copy-start(f32[32,128,128]{2,1,0:T(8,128)} %core.1) | copy-start | bytes 6291460
  14.2 5.8 %collective-permute-start = (f32[5,128,128]{2,1,0:T(8,128)}, f32[5,128,128]{2,1,0:T(8,128)S(1)}, u32[]{:S(2)}, u32[]{:S(2)}) collective-permute-start(f32[5,128,128]{2,1,0:T(8,128)} %get-tuple-element.34), channel_id=1, source_target_pairs={{0,1},{1,0},{2,3},{3,2},{4,5},{5,4},{6,7},{7,6},{8,9},{9,8},{10,11... | collective-permute-start | bytes 983048 | tf_op jit(solution)/shard_map/ppermute | solution.py:288
  14.3 9.0 %collective-permute-start.1 = (f32[256,128]{1,0:T(8,128)}, f32[256,128]{1,0:T(8,128)S(1)}, u32[]{:S(2)}, u32[]{:S(2)}) collective-permute-start(f32[256,128]{1,0:T(8,128)} %get-tuple-element.37), channel_id=1, source_target_pairs={{0,8},{8,16},{16,24},{24,0},{1,9},{9,17},{17,25},{25,1},{2,10},{10... | collective-permute-start | bytes 393224 | tf_op jit(solution)/shard_map/ppermute | solution.py:288
  15.8 10.0 %collective-permute-start.2 = (f32[256,128]{1,0:T(8,128)}, f32[256,128]{1,0:T(8,128)S(1)}, u32[]{:S(2)}, u32[]{:S(2)}) collective-permute-start(f32[256,128]{1,0:T(8,128)} %get-tuple-element.38), channel_id=1, source_target_pairs={{0,16},{8,24},{16,0},{24,8},{1,17},{9,25},{17,1},{25,9},{2,18},{10... | collective-permute-start | bytes 393224 | tf_op jit(solution)/shard_map/ppermute | solution.py:288
  18.6 7.3 %collective-permute-start.3 = (f32[256,128]{1,0:T(8,128)}, f32[256,128]{1,0:T(8,128)S(1)}, u32[]{:S(2)}, u32[]{:S(2)}) collective-permute-start(f32[256,128]{1,0:T(8,128)} %get-tuple-element.39), channel_id=1, source_target_pairs={{0,24},{8,0},{16,8},{24,16},{1,25},{9,1},{17,9},{25,17},{2,26},{10... | collective-permute-start | bytes 393224 | tf_op jit(solution)/shard_map/ppermute | solution.py:288
  20.0 1.0 %copy-start.3 = (f32[5,128,128]{2,1,0:T(8,128)S(1)}, f32[5,128,128]{2,1,0:T(8,128)}, u32[]{:S(2)}) copy-start(f32[5,128,128]{2,1,0:T(8,128)} %get-tuple-element.33.own) | copy-start | bytes 983044
  21.0 9.3 %copy-start = (f32[256,128]{1,0:T(8,128)S(1)}, f32[256,128]{1,0:T(8,128)}, u32[]{:S(2)}) copy-start(f32[256,128]{1,0:T(8,128)} %get-tuple-element.40.a0) | copy-start | bytes 393220
  21.0 51.3 %copy-start.1 = (f32[8,32]{1,0:T(8,128)S(1)}, f32[8,32]{1,0:T(8,128)}, u32[]{:S(2)}) copy-start(f32[8,32]{1,0:T(8,128)} %hour_ref.3) | copy-start | bytes 3076
  21.7 8.5 %collective-permute-start.4 = (f32[136,128]{1,0:T(8,128)S(1)}, f32[136,128]{1,0:T(8,128)S(1)}, u32[]{:S(2)}, u32[]{:S(2)}) collective-permute-start(f32[136,128]{1,0:T(8,128)S(1)} %get-tuple-element.45), channel_id=1, source_target_pairs={{0,8},{8,16},{16,24},{24,0},{1,9},{9,17},{17,25},{25,1},{2,10},{10... | collective-permute-start | bytes 208904 | tf_op jit(solution)/shard_map/ppermute | solution.py:288
  22.4 7.8 %collective-permute-start.5 = (f32[136,128]{1,0:T(8,128)S(1)}, f32[136,128]{1,0:T(8,128)S(1)}, u32[]{:S(2)}, u32[]{:S(2)}) collective-permute-start(f32[136,128]{1,0:T(8,128)S(1)} %get-tuple-element.46), channel_id=1, source_target_pairs={{0,16},{8,24},{16,0},{24,8},{1,17},{9,25},{17,1},{25,9},{2,18},{10... | collective-permute-start | bytes 208904 | tf_op jit(solution)/shard_map/ppermute | solution.py:288
  23.3 6.9 %collective-permute-start.6 = (f32[136,128]{1,0:T(8,128)S(1)}, f32[136,128]{1,0:T(8,128)S(1)}, u32[]{:S(2)}, u32[]{:S(2)}) collective-permute-start(f32[136,128]{1,0:T(8,128)S(1)} %get-tuple-element.47), channel_id=1, source_target_pairs={{0,24},{8,0},{16,8},{24,16},{1,25},{9,1},{17,9},{25,17},{2,26},{10... | collective-permute-start | bytes 208904 | tf_op jit(solution)/shard_map/ppermute | solution.py:288
  25.9 4.3 %collective-permute-start.7 = (f32[128,128]{1,0:T(8,128)S(1)}, f32[128,128]{1,0:T(8,128)S(1)}, u32[]{:S(2)}, u32[]{:S(2)}) collective-permute-start(f32[128,128]{1,0:T(8,128)S(1)} %get-tuple-element.48.refs_0_), channel_id=1, source_target_pairs={{0,2},{2,0},{4,6},{6,4},{1,3},{3,1},{5,7},{7,5},{8,10},{10,8},{12,... | collective-permute-start | bytes 196616 | tf_op jit(solution)/shard_map/ppermute | solution.py:297
  31.0 18.5 %all-to-all-start = ((f32[8,56,128]{2,1,0:T(8,128)}), f32[8,56,128]{2,1,0:T(8,128)S(1)}, u32[]{:S(2)}, u32[]{:S(2)}) async-start(f32[8,56,128]{2,1,0:T(8,128)} %x_sums.1), calls=%async_computation | async-start | bytes 458752 | tf_op jit(solution)/shard_map/all_to_all | solution.py:292
  39.4 4.3 %collective-permute-start.8 = (f32[128,128]{1,0:T(8,128)S(1)}, f32[128,128]{1,0:T(8,128)S(1)}, u32[]{:S(2)}, u32[]{:S(2)}) collective-permute-start(f32[128,128]{1,0:T(8,128)S(1)} %src_near_sum.1.refs_0_), channel_id=1, source_target_pairs={{0,6},{2,4},{4,2},{6,0},{1,7},{3,5},{5,3},{7,1},{8,14},{10,12},{12... | collective-permute-start | bytes 196616 | tf_op jit(solution)/shard_map/ppermute | solution.py:297
  50.2 12.4 %all-to-all-start.1 = ((f32[8,32,128]{2,1,0:T(8,128)}), f32[8,32,128]{2,1,0:T(8,128)S(1)}, u32[]{:S(2)}, u32[]{:S(2)}) async-start(f32[8,32,128]{2,1,0:T(8,128)} %z_sums.1), calls=%async_computation.1 | async-start | bytes 262144 | tf_op jit(solution)/shard_map/all_to_all | solution.py:292
  53.6 1.3 %collective-permute-start.9 = (f32[24,128]{1,0:T(8,128)S(1)}, f32[24,128]{1,0:T(8,128)S(1)}, u32[]{:S(2)}, u32[]{:S(2)}) collective-permute-start(f32[24,128]{1,0:T(8,128)S(1)} %tail_sums.1.own), channel_id=1, source_target_pairs={{0,1},{1,0},{2,3},{3,2},{4,5},{5,4},{6,7},{7,6},{8,9},{9,8},{10,11... | collective-permute-start | bytes 36872 | tf_op jit(solution)/shard_map/ppermute | solution.py:288
  54.9 3.8 %collective-permute-start.10 = (f32[2,24,128]{2,1,0:T(8,128)S(1)}, f32[2,24,128]{2,1,0:T(8,128)S(1)}, u32[]{:S(2)}, u32[]{:S(2)}) collective-permute-start(f32[2,24,128]{2,1,0:T(8,128)S(1)} %both_tails.1.refs_0_), channel_id=1, source_target_pairs={{0,2},{2,0},{4,6},{6,4},{1,3},{3,1},{5,7},{7,5},{8,10},{10,8},{12,... | collective-permute-start | bytes 73736 | tf_op jit(solution)/shard_map/ppermute | solution.py:297
  62.6 8.2 %collective-permute-start.13 = (f32[256,128]{1,0:T(8,128)S(1)}, f32[256,128]{1,0:T(8,128)S(1)}, u32[]{:S(2)}, u32[]{:S(2)}) collective-permute-start(f32[256,128]{1,0:T(8,128)S(1)} %bitcast.3), channel_id=1, source_target_pairs={{0,24},{8,0},{16,8},{24,16},{1,25},{9,1},{17,9},{25,17},{2,26},{10... | collective-permute-start | bytes 393224 | tf_op jit(solution)/shard_map/ppermute | solution.py:288
  64.4 6.5 %collective-permute-start.12 = (f32[256,128]{1,0:T(8,128)S(1)}, f32[256,128]{1,0:T(8,128)S(1)}, u32[]{:S(2)}, u32[]{:S(2)}) collective-permute-start(f32[256,128]{1,0:T(8,128)S(1)} %bitcast.4), channel_id=1, source_target_pairs={{0,16},{8,24},{16,0},{24,8},{1,17},{9,25},{17,1},{25,9},{2,18},{10... | collective-permute-start | bytes 393224 | tf_op jit(solution)/shard_map/ppermute | solution.py:288
  65.6 6.7 %collective-permute-start.11 = (f32[256,128]{1,0:T(8,128)S(1)}, f32[256,128]{1,0:T(8,128)S(1)}, u32[]{:S(2)}, u32[]{:S(2)}) collective-permute-start(f32[256,128]{1,0:T(8,128)S(1)} %bitcast.5), channel_id=1, source_target_pairs={{0,8},{8,16},{16,24},{24,0},{1,9},{9,17},{17,25},{25,1},{2,10},{10... | collective-permute-start | bytes 393224 | tf_op jit(solution)/shard_map/ppermute | solution.py:288
  67.0 1.6 %collective-permute-start.15 = (f32[128,128]{1,0:T(8,128)S(1)}, f32[128,128]{1,0:T(8,128)S(1)}, u32[]{:S(2)}, u32[]{:S(2)}) collective-permute-start(f32[128,128]{1,0:T(8,128)S(1)} %src_far_sum.1.src_own), channel_id=1, source_target_pairs={{0,1},{1,0},{2,3},{3,2},{4,5},{5,4},{6,7},{7,6},{8,9},{9,8},{10,11... | collective-permute-start | bytes 196616 | tf_op jit(solution)/shard_map/ppermute | solution.py:288
  67.0 3.8 %collective-permute-start.14 = (f32[2,24,128]{2,1,0:T(8,128)S(1)}, f32[2,24,128]{2,1,0:T(8,128)S(1)}, u32[]{:S(2)}, u32[]{:S(2)}) collective-permute-start(f32[2,24,128]{2,1,0:T(8,128)S(1)} %near_sum.1.tails), channel_id=1, source_target_pairs={{0,6},{2,4},{4,2},{6,0},{1,7},{3,5},{5,3},{7,1},{8,14},{10,12},{12... | collective-permute-start | bytes 73736 | tf_op jit(solution)/shard_map/ppermute | solution.py:297

commit v8 on v7

--- a/solution.py
+++ b/solution.py
@@ -240,21 +240,26 @@
     out[1 - c] = other[...]
 
 
-def z_kernel(w, copies):
+def scaled_sum_kernel(scale, a, b, out):
+    out[...] = (a[...] + b[...]) * scale
+
+
+def z_kernel(scale, w, copies):
     share = copies.shape[1]
-    total = jnp.sum(w[:, :share, :], axis=0)
+    total = jnp.sum(w[:, :share, :], axis=0) * scale
     for z in range(copies.shape[0]):
         copies[z] = total
 
 
 def end_kernel(scales, hour_ref, b0, b1, b2, b3, tails, more, src_own, src_other,
-               src_out, dst_out, hour_out, core_out, both):
+               src_out, dst_out, hour_out, core_out, both, sems):
     x, c = lax.axis_index("x"), lax.axis_index("core")
-    src_scale, dst_scale, hour_scale, core_scale = scales
-    for s, block in enumerate((b0, b1, b2, b3)):
-        dst_out[lax.rem(x - s + X, X)] = block[...] * dst_scale
-    src_out[c] = src_own[...] * src_scale
-    src_out[1 - c] = src_other[...] * src_scale
+    hour_scale, core_scale = scales
+    moves = [(block, dst_out.at[lax.rem(x - s + X, X)]) for s, block in enumerate((b0, b1, b2, b3))]
+    moves += [(src_own, src_out.at[c]), (src_other, src_out.at[1 - c])]
+    copies = [pltpu.make_async_copy(a, b, sems.at[i]) for i, (a, b) in enumerate(moves)]
+    for copy in copies:
+        copy.start()
     both[...] = tails[...] + more[...]
     hours, rank = hour_ref.shape
     half = hours // CORES
@@ -268,6 +273,8 @@
         for k in range(1, hours):
             out = out + hour_ref[k, r] * tiles[k]
         core_out[r] = out
+    for copy in copies:
+        copy.wait()
 
 
 def end_call(scales, hour, blocks, tails, more, src_own, src_other):
@@ -276,9 +283,9 @@
     return pl.pallas_call(
         functools.partial(end_kernel, scales),
         in_specs=[SMEM] + [VMEM] * 8,
-        out_specs=[VMEM] * 4,
+        out_specs=[HBM] * 2 + [VMEM] * 2,
         out_shape=[struct(CORES, *src_own.shape), struct(X, block, q1), struct(hours, rank), struct(rank, 4, q1)],
-        scratch_shapes=[pltpu.VMEM(tails.shape, F32)],
+        scratch_shapes=[pltpu.VMEM(tails.shape, F32), pltpu.SemaphoreType.DMA((X + CORES,))],
         compiler_params=params(8), cost_estimate=cost(1 << 20, 1 << 20), name="outputs",
     )(hour, *blocks, tails, more, src_own, src_other)
 
@@ -323,19 +330,21 @@
     m, src_half = lax.optimization_barrier((m, src_half))
     w = small_call(x_kernel, "x_sums", struct(zs, share + each + 8, q1), [*a, *m])
     w = swapped(w, "z")
-    src_half = summed("src_far_sum", src_half, paired(src_half, "y", far))
+    src_half = small_call(functools.partial(scaled_sum_kernel, scales[0]), "src_far_sum",
+                          struct(*src_half.shape), [src_half, paired(src_half, "y", far)])
     w, src_half = lax.optimization_barrier((w, src_half))
     src_other = shifted(src_half, "core", 1)
     tail = small_call(functools.partial(tail_kernel, share), "tail_sums", struct(each + 8, q1), [w])
-    copies = small_call(z_kernel, "z_sums", struct(zs, share, q1), [w])
-    tails = small_call(pair_kernel, "both_tails", struct(CORES, *tail.shape), [tail, shifted(tail, "core", 1)])
+    copies = small_call(functools.partial(z_kernel, scales[1]), "z_sums", struct(zs, share, q1), [w])
+    copies, other = lax.optimization_barrier((copies, shifted(tail, "core", 1)))
+    tails = small_call(pair_kernel, "both_tails", struct(CORES, *tail.shape), [tail, other])
     tails = summed("near_sum", tails, paired(tails, "y", near))
     block = swapped(copies, "z").reshape(zs * share, q1)
     block, tails = lax.optimization_barrier((block, tails))
     more = paired(tails, "y", far)
     blocks = around(block, "x")
     grad_src, grad_dst, grad_hour, grad_core = end_call(
-        scales, hour_factor, blocks, tails, more, src_half, src_other)
+        scales[2:], hour_factor, blocks, tails, more, src_half, src_other)
     return (grad_src.reshape(src_factor.shape), grad_dst.reshape(dst_factor.shape), grad_hour, grad_core)
 
 

time: 74.6 us -> 76.6 us (1.027)
  waiting for transfers between devices: 23.4 us -> 25 us
    all_to_all x2, waiting for transfers between devices: 9.71 us -> 11.5 us  [swapped(): return lax.all_to_all(x, axis, split_axis=0, concat_axis=0, tiled=True)]
  transfers between devices with their start and end apart: 18 -> 18, of which waited for: 10 -> 10; matrix products, arithmetic and copies ran while one was open for 0% -> 0% of each run, Pallas kernels for 1% -> 2%
where the time goes in v8:
time: 76.6 us; the launch traced here: 76.2 us
  starting transfers between devices  31.5 us (41%)
  waiting for transfers between devices  25 us (33%)
  Pallas kernels  17.8 us (23%)
  local copies, waits for them, and re-layouts  0.99 us (1%)
  between operations  0.9 us (1%)
    ppermute x12, starting transfers between devices, shifted(): return lax.ppermute(x, axis, [(i, (i + s) % n) for i in range(n)])  13.9 us
    pallas_call x1, Pallas kernels, main_call(): pl.pallas_call(main_kernel, out_shape=[struct(block, q1)] * X + [struct(h...  13.5 us
    all_to_all x2, starting transfers between devices, swapped(): return lax.all_to_all(x, axis, split_axis=0, concat_axis=0, tiled=True)  11.8 us
    all_to_all x2, waiting for transfers between devices, swapped(): return lax.all_to_all(x, axis, split_axis=0, concat_axis=0, tiled=True)  11.5 us
    ppermute x4, waiting for transfers between devices, paired(): return lax.ppermute(x, axis, [(i, flip(i, n)) for i in range(n)])  10.6 us
    ppermute x4, starting transfers between devices, paired(): return lax.ppermute(x, axis, [(i, flip(i, n)) for i in range(n)])  5.77 us
    ppermute x12, waiting for transfers between devices, shifted(): return lax.ppermute(x, axis, [(i, (i + s) % n) for i in range(n)])  2.95 us
    pallas_call x1, Pallas kernels, end_call(): pl.pallas_call(functools.partial(end_kernel, scales), in_specs=[SMEM] + [...  2.13 us
  transfers between devices with their start and end apart: 18, of which 10 were waited for; matrix products, arithmetic and copies ran while one was open for 0% of the time, Pallas kernels for 2%

profile of v8, /device:TPU:8, one launch (start us, length us, event | category | flops | bytes accessed | tf_op | source)
XLA Modules:
  0.0 76.2 jit_solution(11358355448033982671)
XLA Ops:
  0.6 13.5 %all_terms.1 = (f32[256,128]{1,0:T(8,128)}, f32[256,128]{1,0:T(8,128)}, f32[256,128]{1,0:T(8,128)}, f32[256,128]{1,0:T(8,128)}, f32[5,128,128]{2,1,0:T(8,128)}, /*index=5*/f32[5,128,128]{2,1,0:T(8,128)}) custom-call(f32[8,32]{1,0:T(8,128)} %hour_ref.3, s32[8,256,1024]{2,1,0:T(8,128)} %counts_hbm.1, f32[256,128]{1,0:T(8,128)} %src_hbm.1, ...), custom_call_target="tpu_custom_call" | custom-call | flops 4831838208 | bytes 14680064 | tf_op jit(solution)/shard_map/all_terms/pallas_call | solution.py:133
  14.3 1.6 %collective-permute-start.1 = (f32[256,128]{1,0:T(8,128)}, f32[256,128]{1,0:T(8,128)S(1)}, u32[]{:S(2)}, u32[]{:S(2)}) collective-permute-start(f32[256,128]{1,0:T(8,128)} %get-tuple-element.39), channel_id=1, source_target_pairs={{0,8},{8,16},{16,24},{24,0},{1,9},{9,17},{17,25},{25,1},{2,10},{10... | collective-permute-start | bytes 393224 | tf_op jit(solution)/shard_map/ppermute | solution.py:295
  15.8 2.7 %collective-permute-start.2 = (f32[256,128]{1,0:T(8,128)}, f32[256,128]{1,0:T(8,128)S(1)}, u32[]{:S(2)}, u32[]{:S(2)}) collective-permute-start(f32[256,128]{1,0:T(8,128)} %get-tuple-element.40), channel_id=1, source_target_pairs={{0,16},{8,24},{16,0},{24,8},{1,17},{9,25},{17,1},{25,9},{2,18},{10... | collective-permute-start | bytes 393224 | tf_op jit(solution)/shard_map/ppermute | solution.py:295
  18.6 1.4 %collective-permute-start.3 = (f32[256,128]{1,0:T(8,128)}, f32[256,128]{1,0:T(8,128)S(1)}, u32[]{:S(2)}, u32[]{:S(2)}) collective-permute-start(f32[256,128]{1,0:T(8,128)} %get-tuple-element.41), channel_id=1, source_target_pairs={{0,24},{8,0},{16,8},{24,16},{1,25},{9,1},{17,9},{25,17},{2,26},{10... | collective-permute-start | bytes 393224 | tf_op jit(solution)/shard_map/ppermute | solution.py:295
  20.0 1.0 %copy-done.3 = f32[5,128,128]{2,1,0:T(8,128)S(1)} copy-done((f32[5,128,128]{2,1,0:T(8,128)S(1)}, f32[5,128,128]{2,1,0:T(8,128)}, u32[]{:S(2)}) %copy-start.3) | copy-done | bytes 327704
  21.0 0.8 hour_terms.1
  22.4 0.9 %collective-permute-start.5 = (f32[136,128]{1,0:T(8,128)S(1)}, f32[136,128]{1,0:T(8,128)S(1)}, u32[]{:S(2)}, u32[]{:S(2)}) collective-permute-start(f32[136,128]{1,0:T(8,128)S(1)} %get-tuple-element.48), channel_id=1, source_target_pairs={{0,16},{8,24},{16,0},{24,8},{1,17},{9,25},{17,1},{25,9},{2,18},{10... | collective-permute-start | bytes 208904 | tf_op jit(solution)/shard_map/ppermute | solution.py:295
  23.3 2.1 %collective-permute-start.6 = (f32[136,128]{1,0:T(8,128)S(1)}, f32[136,128]{1,0:T(8,128)S(1)}, u32[]{:S(2)}, u32[]{:S(2)}) collective-permute-start(f32[136,128]{1,0:T(8,128)S(1)} %get-tuple-element.49), channel_id=1, source_target_pairs={{0,24},{8,0},{16,8},{24,16},{1,25},{9,1},{17,9},{25,17},{2,26},{10... | collective-permute-start | bytes 208904 | tf_op jit(solution)/shard_map/ppermute | solution.py:295
  25.9 2.1 %collective-permute-start.7 = (f32[128,128]{1,0:T(8,128)S(1)}, f32[128,128]{1,0:T(8,128)S(1)}, u32[]{:S(2)}, u32[]{:S(2)}) collective-permute-start(f32[128,128]{1,0:T(8,128)S(1)} %get-tuple-element.50.refs_0_), channel_id=1, source_target_pairs={{0,2},{2,0},{4,6},{6,4},{1,3},{3,1},{5,7},{7,5},{8,10},{10,8},{12,... | collective-permute-start | bytes 196616 | tf_op jit(solution)/shard_map/ppermute | solution.py:304
  28.0 2.2 %collective-permute-done.7.refs_1_ = f32[128,128]{1,0:T(8,128)S(1)} collective-permute-done((f32[128,128]{1,0:T(8,128)S(1)}, f32[128,128]{1,0:T(8,128)S(1)}, u32[]{:S(2)}, u32[]{:S(2)}) %collective-permute-start.7) | collective-permute-done | bytes 65568 | tf_op jit(solution)/shard_map/ppermute | solution.py:304
  31.0 8.4 %all-to-all-start = ((f32[8,56,128]{2,1,0:T(8,128)}), f32[8,56,128]{2,1,0:T(8,128)S(1)}, u32[]{:S(2)}, u32[]{:S(2)}) async-start(f32[8,56,128]{2,1,0:T(8,128)} %x_sums.1), calls=%async_computation | async-start | bytes 458752 | tf_op jit(solution)/shard_map/all_to_all | solution.py:299
  39.4 1.6 %collective-permute-start.8 = (f32[128,128]{1,0:T(8,128)S(1)}, f32[128,128]{1,0:T(8,128)S(1)}, u32[]{:S(2)}, u32[]{:S(2)}) collective-permute-start(f32[128,128]{1,0:T(8,128)S(1)} %src_near_sum.1.a), channel_id=1, source_target_pairs={{0,6},{2,4},{4,2},{6,0},{1,7},{3,5},{5,3},{7,1},{8,14},{10,12},{12... | collective-permute-start | bytes 196616 | tf_op jit(solution)/shard_map/ppermute | solution.py:304
  41.0 2.7 %collective-permute-done.8.b = f32[128,128]{1,0:T(8,128)S(1)} collective-permute-done((f32[128,128]{1,0:T(8,128)S(1)}, f32[128,128]{1,0:T(8,128)S(1)}, u32[]{:S(2)}, u32[]{:S(2)}) %collective-permute-start.8) | collective-permute-done | bytes 65568 | tf_op jit(solution)/shard_map/ppermute | solution.py:304
  43.7 5.9 %all-to-all-done.w = f32[8,56,128]{2,1,0:T(8,128)S(1)} async-done(((f32[8,56,128]{2,1,0:T(8,128)}), f32[8,56,128]{2,1,0:T(8,128)S(1)}, u32[]{:S(2)}, u32[]{:S(2)}) %all-to-all-start) | async-done | bytes 229408 | tf_op jit(solution)/shard_map/all_to_all | solution.py:299
  50.8 3.4 %all-to-all-start.1 = ((f32[8,32,128]{2,1,0:T(8,128)}), f32[8,32,128]{2,1,0:T(8,128)S(1)}, u32[]{:S(2)}, u32[]{:S(2)}) async-start(f32[8,32,128]{2,1,0:T(8,128)} %z_sums.1), calls=%async_computation.1 | async-start | bytes 262144 | tf_op jit(solution)/shard_map/all_to_all | solution.py:299
  54.7 3.4 %collective-permute-done.10.refs_1_ = f32[2,24,128]{2,1,0:T(8,128)S(1)} collective-permute-done((f32[2,24,128]{2,1,0:T(8,128)S(1)}, f32[2,24,128]{2,1,0:T(8,128)S(1)}, u32[]{:S(2)}, u32[]{:S(2)}) %collective-permute-start.10) | collective-permute-done | bytes 24608 | tf_op jit(solution)/shard_map/ppermute | solution.py:304
  58.1 5.6 %all-to-all-done.1 = f32[8,32,128]{2,1,0:T(8,128)S(1)} async-done(((f32[8,32,128]{2,1,0:T(8,128)}), f32[8,32,128]{2,1,0:T(8,128)S(1)}, u32[]{:S(2)}, u32[]{:S(2)}) %all-to-all-start.1) | async-done | bytes 131104 | tf_op jit(solution)/shard_map/all_to_all | solution.py:299
  63.8 1.8 %collective-permute-start.13 = (f32[256,128]{1,0:T(8,128)S(1)}, f32[256,128]{1,0:T(8,128)S(1)}, u32[]{:S(2)}, u32[]{:S(2)}) collective-permute-start(f32[256,128]{1,0:T(8,128)S(1)} %bitcast.3), channel_id=1, source_target_pairs={{0,24},{8,0},{16,8},{24,16},{1,25},{9,1},{17,9},{25,17},{2,26},{10... | collective-permute-start | bytes 393224 | tf_op jit(solution)/shard_map/ppermute | solution.py:295
  65.6 1.2 %collective-permute-start.12 = (f32[256,128]{1,0:T(8,128)S(1)}, f32[256,128]{1,0:T(8,128)S(1)}, u32[]{:S(2)}, u32[]{:S(2)}) collective-permute-start(f32[256,128]{1,0:T(8,128)S(1)} %bitcast.4), channel_id=1, source_target_pairs={{0,16},{8,24},{16,0},{24,8},{1,17},{9,25},{17,1},{25,9},{2,18},{10... | collective-permute-start | bytes 393224 | tf_op jit(solution)/shard_map/ppermute | solution.py:295
  66.8 1.4 %collective-permute-start.11 = (f32[256,128]{1,0:T(8,128)S(1)}, f32[256,128]{1,0:T(8,128)S(1)}, u32[]{:S(2)}, u32[]{:S(2)}) collective-permute-start(f32[256,128]{1,0:T(8,128)S(1)} %bitcast.5), channel_id=1, source_target_pairs={{0,8},{8,16},{16,24},{24,0},{1,9},{9,17},{17,25},{25,1},{2,10},{10... | collective-permute-start | bytes 393224 | tf_op jit(solution)/shard_map/ppermute | solution.py:295
  68.2 1.6 %collective-permute-start.14 = (f32[2,24,128]{2,1,0:T(8,128)S(1)}, f32[2,24,128]{2,1,0:T(8,128)S(1)}, u32[]{:S(2)}, u32[]{:S(2)}) collective-permute-start(f32[2,24,128]{2,1,0:T(8,128)S(1)} %near_sum.1.tails), channel_id=1, source_target_pairs={{0,6},{2,4},{4,2},{6,0},{1,7},{3,5},{5,3},{7,1},{8,14},{10,12},{12... | collective-permute-start | bytes 73736 | tf_op jit(solution)/shard_map/ppermute | solution.py:304
  69.7 2.3 %collective-permute-done.14.more = f32[2,24,128]{2,1,0:T(8,128)S(1)} collective-permute-done((f32[2,24,128]{2,1,0:T(8,128)S(1)}, f32[2,24,128]{2,1,0:T(8,128)S(1)}, u32[]{:S(2)}, u32[]{:S(2)}) %collective-permute-start.14) | collective-permute-done | bytes 24608 | tf_op jit(solution)/shard_map/ppermute | solution.py:304
  72.6 1.3 %collective-permute-done.11.b1 = f32[256,128]{1,0:T(8,128)S(1)} collective-permute-done((f32[256,128]{1,0:T(8,128)S(1)}, f32[256,128]{1,0:T(8,128)S(1)}, u32[]{:S(2)}, u32[]{:S(2)}) %collective-permute-start.11) | collective-permute-done | bytes 131104 | tf_op jit(solution)/shard_map/ppermute | solution.py:295
  73.9 2.1 %outputs.1 = (f32[2,128,128]{2,1,0:T(8,128)}, f32[4,256,128]{2,1,0:T(8,128)}, f32[8,32]{1,0:T(8,128)}, f32[32,4,128]{2,1,0:T(4,128)}) custom-call(f32[8,32]{1,0:T(8,128)S(1)} %copy-done.1, f32[256,128]{1,0:T(8,128)S(1)} %bitcast.6, f32[256,128]{1,0:T(8,128)S(1)} %collective-permute-done.11.b1, f32[256,128]{1,0:T(8,128)S(1)} %collective-permute-done.12.b2, ...), custom_call_target="tpu_custom_call" | custom-call | flops 1048576 | bytes 1048576 | tf_op jit(solution)/shard_map/outputs/pallas_call | solution.py:283
  (30 shorter events, 4.5 us)
Async XLA Ops:
  0.6 19.4 %copy-start.2 = (f32[32,128,128]{2,1,0:T(8,128)S(1)}, f32[32,128,128]{2,1,0:T(8,128)}, u32[]{:S(2)}) copy-start(f32[32,128,128]{2,1,0:T(8,128)} %core.1) | copy-start | bytes 6291460
  14.2 5.8 %collective-permute-start = (f32[5,128,128]{2,1,0:T(8,128)}, f32[5,128,128]{2,1,0:T(8,128)S(1)}, u32[]{:S(2)}, u32[]{:S(2)}) collective-permute-start(f32[5,128,128]{2,1,0:T(8,128)} %get-tuple-element.36), channel_id=1, source_target_pairs={{0,1},{1,0},{2,3},{3,2},{4,5},{5,4},{6,7},{7,6},{8,9},{9,8},{10,11... | collective-permute-start | bytes 983048 | tf_op jit(solution)/shard_map/ppermute | solution.py:295
  14.3 9.0 %collective-permute-start.1 = (f32[256,128]{1,0:T(8,128)}, f32[256,128]{1,0:T(8,128)S(1)}, u32[]{:S(2)}, u32[]{:S(2)}) collective-permute-start(f32[256,128]{1,0:T(8,128)} %get-tuple-element.39), channel_id=1, source_target_pairs={{0,8},{8,16},{16,24},{24,0},{1,9},{9,17},{17,25},{25,1},{2,10},{10... | collective-permute-start | bytes 393224 | tf_op jit(solution)/shard_map/ppermute | solution.py:295
  15.8 10.0 %collective-permute-start.2 = (f32[256,128]{1,0:T(8,128)}, f32[256,128]{1,0:T(8,128)S(1)}, u32[]{:S(2)}, u32[]{:S(2)}) collective-permute-start(f32[256,128]{1,0:T(8,128)} %get-tuple-element.40), channel_id=1, source_target_pairs={{0,16},{8,24},{16,0},{24,8},{1,17},{9,25},{17,1},{25,9},{2,18},{10... | collective-permute-start | bytes 393224 | tf_op jit(solution)/shard_map/ppermute | solution.py:295
  18.6 7.3 %collective-permute-start.3 = (f32[256,128]{1,0:T(8,128)}, f32[256,128]{1,0:T(8,128)S(1)}, u32[]{:S(2)}, u32[]{:S(2)}) collective-permute-start(f32[256,128]{1,0:T(8,128)} %get-tuple-element.41), channel_id=1, source_target_pairs={{0,24},{8,0},{16,8},{24,16},{1,25},{9,1},{17,9},{25,17},{2,26},{10... | collective-permute-start | bytes 393224 | tf_op jit(solution)/shard_map/ppermute | solution.py:295
  20.0 1.0 %copy-start.3 = (f32[5,128,128]{2,1,0:T(8,128)S(1)}, f32[5,128,128]{2,1,0:T(8,128)}, u32[]{:S(2)}) copy-start(f32[5,128,128]{2,1,0:T(8,128)} %get-tuple-element.35.own) | copy-start | bytes 983044
  21.0 9.3 %copy-start = (f32[256,128]{1,0:T(8,128)S(1)}, f32[256,128]{1,0:T(8,128)}, u32[]{:S(2)}) copy-start(f32[256,128]{1,0:T(8,128)} %get-tuple-element.42.a0) | copy-start | bytes 393220
  21.0 53.0 %copy-start.1 = (f32[8,32]{1,0:T(8,128)S(1)}, f32[8,32]{1,0:T(8,128)}, u32[]{:S(2)}) copy-start(f32[8,32]{1,0:T(8,128)} %hour_ref.3) | copy-start | bytes 3076
  21.7 8.5 %collective-permute-start.4 = (f32[136,128]{1,0:T(8,128)S(1)}, f32[136,128]{1,0:T(8,128)S(1)}, u32[]{:S(2)}, u32[]{:S(2)}) collective-permute-start(f32[136,128]{1,0:T(8,128)S(1)} %get-tuple-element.47), channel_id=1, source_target_pairs={{0,8},{8,16},{16,24},{24,0},{1,9},{9,17},{17,25},{25,1},{2,10},{10... | collective-permute-start | bytes 208904 | tf_op jit(solution)/shard_map/ppermute | solution.py:295
  22.4 7.8 %collective-permute-start.5 = (f32[136,128]{1,0:T(8,128)S(1)}, f32[136,128]{1,0:T(8,128)S(1)}, u32[]{:S(2)}, u32[]{:S(2)}) collective-permute-start(f32[136,128]{1,0:T(8,128)S(1)} %get-tuple-element.48), channel_id=1, source_target_pairs={{0,16},{8,24},{16,0},{24,8},{1,17},{9,25},{17,1},{25,9},{2,18},{10... | collective-permute-start | bytes 208904 | tf_op jit(solution)/shard_map/ppermute | solution.py:295
  23.3 6.9 %collective-permute-start.6 = (f32[136,128]{1,0:T(8,128)S(1)}, f32[136,128]{1,0:T(8,128)S(1)}, u32[]{:S(2)}, u32[]{:S(2)}) collective-permute-start(f32[136,128]{1,0:T(8,128)S(1)} %get-tuple-element.49), channel_id=1, source_target_pairs={{0,24},{8,0},{16,8},{24,16},{1,25},{9,1},{17,9},{25,17},{2,26},{10... | collective-permute-start | bytes 208904 | tf_op jit(solution)/shard_map/ppermute | solution.py:295
  25.9 4.3 %collective-permute-start.7 = (f32[128,128]{1,0:T(8,128)S(1)}, f32[128,128]{1,0:T(8,128)S(1)}, u32[]{:S(2)}, u32[]{:S(2)}) collective-permute-start(f32[128,128]{1,0:T(8,128)S(1)} %get-tuple-element.50.refs_0_), channel_id=1, source_target_pairs={{0,2},{2,0},{4,6},{6,4},{1,3},{3,1},{5,7},{7,5},{8,10},{10,8},{12,... | collective-permute-start | bytes 196616 | tf_op jit(solution)/shard_map/ppermute | solution.py:304
  31.0 18.5 %all-to-all-start = ((f32[8,56,128]{2,1,0:T(8,128)}), f32[8,56,128]{2,1,0:T(8,128)S(1)}, u32[]{:S(2)}, u32[]{:S(2)}) async-start(f32[8,56,128]{2,1,0:T(8,128)} %x_sums.1), calls=%async_computation | async-start | bytes 458752 | tf_op jit(solution)/shard_map/all_to_all | solution.py:299
  39.4 4.3 %collective-permute-start.8 = (f32[128,128]{1,0:T(8,128)S(1)}, f32[128,128]{1,0:T(8,128)S(1)}, u32[]{:S(2)}, u32[]{:S(2)}) collective-permute-start(f32[128,128]{1,0:T(8,128)S(1)} %src_near_sum.1.a), channel_id=1, source_target_pairs={{0,6},{2,4},{4,2},{6,0},{1,7},{3,5},{5,3},{7,1},{8,14},{10,12},{12... | collective-permute-start | bytes 196616 | tf_op jit(solution)/shard_map/ppermute | solution.py:304
  49.5 1.3 %collective-permute-start.9 = (f32[24,128]{1,0:T(8,128)S(1)}, f32[24,128]{1,0:T(8,128)S(1)}, u32[]{:S(2)}, u32[]{:S(2)}) collective-permute-start(f32[24,128]{1,0:T(8,128)S(1)} %tail_sums.1.own), channel_id=1, source_target_pairs={{0,1},{1,0},{2,3},{3,2},{4,5},{5,4},{6,7},{7,6},{8,9},{9,8},{10,11... | collective-permute-start | bytes 36872 | tf_op jit(solution)/shard_map/ppermute | solution.py:295
  50.8 13.0 %all-to-all-start.1 = ((f32[8,32,128]{2,1,0:T(8,128)}), f32[8,32,128]{2,1,0:T(8,128)S(1)}, u32[]{:S(2)}, u32[]{:S(2)}) async-start(f32[8,32,128]{2,1,0:T(8,128)} %z_sums.1), calls=%async_computation.1 | async-start | bytes 262144 | tf_op jit(solution)/shard_map/all_to_all | solution.py:299
  54.2 3.9 %collective-permute-start.10 = (f32[2,24,128]{2,1,0:T(8,128)S(1)}, f32[2,24,128]{2,1,0:T(8,128)S(1)}, u32[]{:S(2)}, u32[]{:S(2)}) collective-permute-start(f32[2,24,128]{2,1,0:T(8,128)S(1)} %both_tails.1.refs_0_), channel_id=1, source_target_pairs={{0,2},{2,0},{4,6},{6,4},{1,3},{3,1},{5,7},{7,5},{8,10},{10,8},{12,... | collective-permute-start | bytes 73736 | tf_op jit(solution)/shard_map/ppermute | solution.py:304
  63.8 8.2 %collective-permute-start.13 = (f32[256,128]{1,0:T(8,128)S(1)}, f32[256,128]{1,0:T(8,128)S(1)}, u32[]{:S(2)}, u32[]{:S(2)}) collective-permute-start(f32[256,128]{1,0:T(8,128)S(1)} %bitcast.3), channel_id=1, source_target_pairs={{0,24},{8,0},{16,8},{24,16},{1,25},{9,1},{17,9},{25,17},{2,26},{10... | collective-permute-start | bytes 393224 | tf_op jit(solution)/shard_map/ppermute | solution.py:295
  65.6 7.0 %collective-permute-start.12 = (f32[256,128]{1,0:T(8,128)S(1)}, f32[256,128]{1,0:T(8,128)S(1)}, u32[]{:S(2)}, u32[]{:S(2)}) collective-permute-start(f32[256,128]{1,0:T(8,128)S(1)} %bitcast.4), channel_id=1, source_target_pairs={{0,16},{8,24},{16,0},{24,8},{1,17},{9,25},{17,1},{25,9},{2,18},{10... | collective-permute-start | bytes 393224 | tf_op jit(solution)/shard_map/ppermute | solution.py:295
  66.8 7.2 %collective-permute-start.11 = (f32[256,128]{1,0:T(8,128)S(1)}, f32[256,128]{1,0:T(8,128)S(1)}, u32[]{:S(2)}, u32[]{:S(2)}) collective-permute-start(f32[256,128]{1,0:T(8,128)S(1)} %bitcast.5), channel_id=1, source_target_pairs={{0,8},{8,16},{16,24},{24,0},{1,9},{9,17},{17,25},{25,1},{2,10},{10... | collective-permute-start | bytes 393224 | tf_op jit(solution)/shard_map/ppermute | solution.py:295
  68.2 1.6 %collective-permute-start.15 = (f32[128,128]{1,0:T(8,128)S(1)}, f32[128,128]{1,0:T(8,128)S(1)}, u32[]{:S(2)}, u32[]{:S(2)}) collective-permute-start(f32[128,128]{1,0:T(8,128)S(1)} %src_far_sum.1.src_own), channel_id=1, source_target_pairs={{0,1},{1,0},{2,3},{3,2},{4,5},{5,4},{6,7},{7,6},{8,9},{9,8},{10,11... | collective-permute-start | bytes 196616 | tf_op jit(solution)/shard_map/ppermute | solution.py:295
  68.2 3.8 %collective-permute-start.14 = (f32[2,24,128]{2,1,0:T(8,128)S(1)}, f32[2,24,128]{2,1,0:T(8,128)S(1)}, u32[]{:S(2)}, u32[]{:S(2)}) collective-permute-start(f32[2,24,128]{2,1,0:T(8,128)S(1)} %near_sum.1.tails), channel_id=1, source_target_pairs={{0,6},{2,4},{4,2},{6,0},{1,7},{3,5},{5,3},{7,1},{8,14},{10,12},{12... | collective-permute-start | bytes 73736 | tf_op jit(solution)/shard_map/ppermute | solution.py:304

commit v9 on v7

--- a/solution.py
+++ b/solution.py
@@ -318,14 +318,14 @@
     m = [m0] + [shifted(v, "x", s) for s, v in ((1, m1), (2, m2), (3, m3))]
     share = a0.shape[0] // zs
     each = (m0.shape[0] - 8) // zs
-    src_half, *a = lax.optimization_barrier((src_half, *a))
+    src_half, a[1], a[2] = lax.optimization_barrier((src_half, a[1], a[2]))
     src_half = summed("src_near_sum", src_half, paired(src_half, "y", near))
     m, src_half = lax.optimization_barrier((m, src_half))
     w = small_call(x_kernel, "x_sums", struct(zs, share + each + 8, q1), [*a, *m])
     w = swapped(w, "z")
     src_half = summed("src_far_sum", src_half, paired(src_half, "y", far))
-    w, src_half = lax.optimization_barrier((w, src_half))
     src_other = shifted(src_half, "core", 1)
+    w, src_half, src_other = lax.optimization_barrier((w, src_half, src_other))
     tail = small_call(functools.partial(tail_kernel, share), "tail_sums", struct(each + 8, q1), [w])
     copies = small_call(z_kernel, "z_sums", struct(zs, share, q1), [w])
     tails = small_call(pair_kernel, "both_tails", struct(CORES, *tail.shape), [tail, shifted(tail, "core", 1)])

time: 74.6 us -> 74.6 us (level)
  starting transfers between devices: 31.4 us -> 30.5 us
    ppermute x12, waiting for transfers between devices: 3.13 us -> 4.85 us  [shifted(): return lax.ppermute(x, axis, [(i, (i + s) % n) for i in range(n)])]
    all_to_all x2, waiting for transfers between devices: 9.71 us -> 8.39 us  [swapped(): return lax.all_to_all(x, axis, split_axis=0, concat_axis=0, tiled=True)]
    ppermute x12, starting transfers between devices: 14 us -> 13.2 us  [shifted(): return lax.ppermute(x, axis, [(i, (i + s) % n) for i in range(n)])]
  transfers between devices with their start and end apart: 18 -> 18, of which waited for: 10 -> 11; matrix products, arithmetic and copies ran while one was open for 0% -> 0% of each run, Pallas kernels for 1% -> 1%
where the time goes in v9:
time: 74.6 us; the launch traced here: 73.4 us
  starting transfers between devices  30.5 us (41%)
  waiting for transfers between devices  24 us (32%)
  Pallas kernels  17.2 us (23%)
  local copies, waits for them, and re-layouts  0.99 us (1%)
  between operations  0.76 us (1%)
    pallas_call x1, Pallas kernels, main_call(): pl.pallas_call(main_kernel, out_shape=[struct(block, q1)] * X + [struct(h...  13.5 us
    ppermute x12, starting transfers between devices, shifted(): return lax.ppermute(x, axis, [(i, (i + s) % n) for i in range(n)])  13.2 us
    all_to_all x2, starting transfers between devices, swapped(): return lax.all_to_all(x, axis, split_axis=0, concat_axis=0, tiled=True)  11.8 us
    ppermute x4, waiting for transfers between devices, paired(): return lax.ppermute(x, axis, [(i, flip(i, n)) for i in range(n)])  10.7 us
    all_to_all x2, waiting for transfers between devices, swapped(): return lax.all_to_all(x, axis, split_axis=0, concat_axis=0, tiled=True)  8.39 us
    ppermute x4, starting transfers between devices, paired(): return lax.ppermute(x, axis, [(i, flip(i, n)) for i in range(n)])  5.46 us
    ppermute x12, waiting for transfers between devices, shifted(): return lax.ppermute(x, axis, [(i, (i + s) % n) for i in range(n)])  4.85 us
    pallas_call x1, Pallas kernels, end_call(): pl.pallas_call(functools.partial(end_kernel, scales), in_specs=[SMEM] + [...  1.5 us
  transfers between devices with their start and end apart: 18, of which 11 were waited for; matrix products, arithmetic and copies ran while one was open for 0% of the time, Pallas kernels for 1%

profile of v9, /device:TPU:8, one launch (start us, length us, event | category | flops | bytes accessed | tf_op | source)
XLA Modules:
  0.0 73.4 jit_solution(2707600298248887835)
XLA Ops:
  0.6 13.5 %all_terms.1 = (f32[256,128]{1,0:T(8,128)}, f32[256,128]{1,0:T(8,128)}, f32[256,128]{1,0:T(8,128)}, f32[256,128]{1,0:T(8,128)}, f32[5,128,128]{2,1,0:T(8,128)}, /*index=5*/f32[5,128,128]{2,1,0:T(8,128)}) custom-call(f32[8,32]{1,0:T(8,128)} %hour_ref.3, s32[8,256,1024]{2,1,0:T(8,128)} %counts_hbm.1, f32[256,128]{1,0:T(8,128)} %src_hbm.1, ...), custom_call_target="tpu_custom_call" | custom-call | flops 4831838208 | bytes 14680064 | tf_op jit(solution)/shard_map/all_terms/pallas_call | solution.py:133
  14.3 1.6 %collective-permute-start.1 = (f32[256,128]{1,0:T(8,128)}, f32[256,128]{1,0:T(8,128)S(1)}, u32[]{:S(2)}, u32[]{:S(2)}) collective-permute-start(f32[256,128]{1,0:T(8,128)} %get-tuple-element.36), channel_id=1, source_target_pairs={{0,8},{8,16},{16,24},{24,0},{1,9},{9,17},{17,25},{25,1},{2,10},{10... | collective-permute-start | bytes 393224 | tf_op jit(solution)/shard_map/ppermute | solution.py:288
  15.8 2.7 %collective-permute-start.2 = (f32[256,128]{1,0:T(8,128)}, f32[256,128]{1,0:T(8,128)S(1)}, u32[]{:S(2)}, u32[]{:S(2)}) collective-permute-start(f32[256,128]{1,0:T(8,128)} %get-tuple-element.37), channel_id=1, source_target_pairs={{0,16},{8,24},{16,0},{24,8},{1,17},{9,25},{17,1},{25,9},{2,18},{10... | collective-permute-start | bytes 393224 | tf_op jit(solution)/shard_map/ppermute | solution.py:288
  18.6 1.4 %collective-permute-start.3 = (f32[256,128]{1,0:T(8,128)}, f32[256,128]{1,0:T(8,128)S(1)}, u32[]{:S(2)}, u32[]{:S(2)}) collective-permute-start(f32[256,128]{1,0:T(8,128)} %get-tuple-element.40), channel_id=1, source_target_pairs={{0,24},{8,0},{16,8},{24,16},{1,25},{9,1},{17,9},{25,17},{2,26},{10... | collective-permute-start | bytes 393224 | tf_op jit(solution)/shard_map/ppermute | solution.py:288
  20.0 1.0 %copy-done.3 = f32[5,128,128]{2,1,0:T(8,128)S(1)} copy-done((f32[5,128,128]{2,1,0:T(8,128)S(1)}, f32[5,128,128]{2,1,0:T(8,128)}, u32[]{:S(2)}) %copy-start.3) | copy-done | bytes 327704
  23.3 2.1 %collective-permute-start.6 = (f32[136,128]{1,0:T(8,128)S(1)}, f32[136,128]{1,0:T(8,128)S(1)}, u32[]{:S(2)}, u32[]{:S(2)}) collective-permute-start(f32[136,128]{1,0:T(8,128)S(1)} %get-tuple-element.44), channel_id=1, source_target_pairs={{0,24},{8,0},{16,8},{24,16},{1,25},{9,1},{17,9},{25,17},{2,26},{10... | collective-permute-start | bytes 208904 | tf_op jit(solution)/shard_map/ppermute | solution.py:288
  25.9 1.4 %collective-permute-start.7 = (f32[128,128]{1,0:T(8,128)S(1)}, f32[128,128]{1,0:T(8,128)S(1)}, u32[]{:S(2)}, u32[]{:S(2)}) collective-permute-start(f32[128,128]{1,0:T(8,128)S(1)} %get-tuple-element.45.refs_0_), channel_id=1, source_target_pairs={{0,2},{2,0},{4,6},{6,4},{1,3},{3,1},{5,7},{7,5},{8,10},{10,8},{12,... | collective-permute-start | bytes 196616 | tf_op jit(solution)/shard_map/ppermute | solution.py:297
  27.2 2.9 %collective-permute-done.7.refs_1_ = f32[128,128]{1,0:T(8,128)S(1)} collective-permute-done((f32[128,128]{1,0:T(8,128)S(1)}, f32[128,128]{1,0:T(8,128)S(1)}, u32[]{:S(2)}, u32[]{:S(2)}) %collective-permute-start.7) | collective-permute-done | bytes 65568 | tf_op jit(solution)/shard_map/ppermute | solution.py:297
  30.9 8.5 %all-to-all-start = ((f32[8,56,128]{2,1,0:T(8,128)}), f32[8,56,128]{2,1,0:T(8,128)S(1)}, u32[]{:S(2)}, u32[]{:S(2)}) async-start(f32[8,56,128]{2,1,0:T(8,128)} %x_sums.1), calls=%async_computation | async-start | bytes 458752 | tf_op jit(solution)/shard_map/all_to_all | solution.py:292
  39.4 1.6 %collective-permute-start.8 = (f32[128,128]{1,0:T(8,128)S(1)}, f32[128,128]{1,0:T(8,128)S(1)}, u32[]{:S(2)}, u32[]{:S(2)}) collective-permute-start(f32[128,128]{1,0:T(8,128)S(1)} %src_near_sum.1.refs_0_), channel_id=1, source_target_pairs={{0,6},{2,4},{4,2},{6,0},{1,7},{3,5},{5,3},{7,1},{8,14},{10,12},{12... | collective-permute-start | bytes 196616 | tf_op jit(solution)/shard_map/ppermute | solution.py:297
  41.0 2.7 %collective-permute-done.8.refs_1_ = f32[128,128]{1,0:T(8,128)S(1)} collective-permute-done((f32[128,128]{1,0:T(8,128)S(1)}, f32[128,128]{1,0:T(8,128)S(1)}, u32[]{:S(2)}, u32[]{:S(2)}) %collective-permute-start.8) | collective-permute-done | bytes 65568 | tf_op jit(solution)/shard_map/ppermute | solution.py:297
  43.8 1.2 %collective-permute-done.9.src_other = f32[128,128]{1,0:T(8,128)S(1)} collective-permute-done((f32[128,128]{1,0:T(8,128)S(1)}, f32[128,128]{1,0:T(8,128)S(1)}, u32[]{:S(2)}, u32[]{:S(2)}) %collective-permute-start.9) | collective-permute-done | bytes 65568 | tf_op jit(solution)/shard_map/ppermute | solution.py:288
  45.0 4.5 %all-to-all-done.w = f32[8,56,128]{2,1,0:T(8,128)S(1)} async-done(((f32[8,56,128]{2,1,0:T(8,128)}), f32[8,56,128]{2,1,0:T(8,128)S(1)}, u32[]{:S(2)}, u32[]{:S(2)}) %all-to-all-start) | async-done | bytes 229408 | tf_op jit(solution)/shard_map/all_to_all | solution.py:292
  50.2 3.4 %all-to-all-start.1 = ((f32[8,32,128]{2,1,0:T(8,128)}), f32[8,32,128]{2,1,0:T(8,128)S(1)}, u32[]{:S(2)}, u32[]{:S(2)}) async-start(f32[8,32,128]{2,1,0:T(8,128)} %z_sums.1), calls=%async_computation.1 | async-start | bytes 262144 | tf_op jit(solution)/shard_map/all_to_all | solution.py:292
  53.7 1.2 %collective-permute-done.10.other = f32[24,128]{1,0:T(8,128)S(1)} collective-permute-done((f32[24,128]{1,0:T(8,128)S(1)}, f32[24,128]{1,0:T(8,128)S(1)}, u32[]{:S(2)}, u32[]{:S(2)}) %collective-permute-start.10) | collective-permute-done | bytes 12320 | tf_op jit(solution)/shard_map/ppermute | solution.py:288
  54.9 1.0 %collective-permute-start.11 = (f32[2,24,128]{2,1,0:T(8,128)S(1)}, f32[2,24,128]{2,1,0:T(8,128)S(1)}, u32[]{:S(2)}, u32[]{:S(2)}) collective-permute-start(f32[2,24,128]{2,1,0:T(8,128)S(1)} %both_tails.1.refs_0_), channel_id=1, source_target_pairs={{0,2},{2,0},{4,6},{6,4},{1,3},{3,1},{5,7},{7,5},{8,10},{10,8},{12,... | collective-permute-start | bytes 73736 | tf_op jit(solution)/shard_map/ppermute | solution.py:297
  55.8 2.9 %collective-permute-done.11.refs_1_ = f32[2,24,128]{2,1,0:T(8,128)S(1)} collective-permute-done((f32[2,24,128]{2,1,0:T(8,128)S(1)}, f32[2,24,128]{2,1,0:T(8,128)S(1)}, u32[]{:S(2)}, u32[]{:S(2)}) %collective-permute-start.11) | collective-permute-done | bytes 24608 | tf_op jit(solution)/shard_map/ppermute | solution.py:297
  58.7 3.9 %all-to-all-done.1 = f32[8,32,128]{2,1,0:T(8,128)S(1)} async-done(((f32[8,32,128]{2,1,0:T(8,128)}), f32[8,32,128]{2,1,0:T(8,128)S(1)}, u32[]{:S(2)}, u32[]{:S(2)}) %all-to-all-start.1) | async-done | bytes 131104 | tf_op jit(solution)/shard_map/all_to_all | solution.py:292
  62.6 1.4 %collective-permute-start.14 = (f32[256,128]{1,0:T(8,128)S(1)}, f32[256,128]{1,0:T(8,128)S(1)}, u32[]{:S(2)}, u32[]{:S(2)}) collective-permute-start(f32[256,128]{1,0:T(8,128)S(1)} %bitcast.3), channel_id=1, source_target_pairs={{0,24},{8,0},{16,8},{24,16},{1,25},{9,1},{17,9},{25,17},{2,26},{10... | collective-permute-start | bytes 393224 | tf_op jit(solution)/shard_map/ppermute | solution.py:288
  64.8 1.3 %collective-permute-start.12 = (f32[256,128]{1,0:T(8,128)S(1)}, f32[256,128]{1,0:T(8,128)S(1)}, u32[]{:S(2)}, u32[]{:S(2)}) collective-permute-start(f32[256,128]{1,0:T(8,128)S(1)} %bitcast.5), channel_id=1, source_target_pairs={{0,8},{8,16},{16,24},{24,0},{1,9},{9,17},{17,25},{25,1},{2,10},{10... | collective-permute-start | bytes 393224 | tf_op jit(solution)/shard_map/ppermute | solution.py:288
  66.1 1.6 %collective-permute-start.15 = (f32[2,24,128]{2,1,0:T(8,128)S(1)}, f32[2,24,128]{2,1,0:T(8,128)S(1)}, u32[]{:S(2)}, u32[]{:S(2)}) collective-permute-start(f32[2,24,128]{2,1,0:T(8,128)S(1)} %near_sum.1.tails), channel_id=1, source_target_pairs={{0,6},{2,4},{4,2},{6,0},{1,7},{3,5},{5,3},{7,1},{8,14},{10,12},{12... | collective-permute-start | bytes 73736 | tf_op jit(solution)/shard_map/ppermute | solution.py:297
  67.7 2.3 %collective-permute-done.15.more = f32[2,24,128]{2,1,0:T(8,128)S(1)} collective-permute-done((f32[2,24,128]{2,1,0:T(8,128)S(1)}, f32[2,24,128]{2,1,0:T(8,128)S(1)}, u32[]{:S(2)}, u32[]{:S(2)}) %collective-permute-start.15) | collective-permute-done | bytes 24608 | tf_op jit(solution)/shard_map/ppermute | solution.py:297
  70.6 1.3 %collective-permute-done.12.b1 = f32[256,128]{1,0:T(8,128)S(1)} collective-permute-done((f32[256,128]{1,0:T(8,128)S(1)}, f32[256,128]{1,0:T(8,128)S(1)}, u32[]{:S(2)}, u32[]{:S(2)}) %collective-permute-start.12) | collective-permute-done | bytes 131104 | tf_op jit(solution)/shard_map/ppermute | solution.py:288
  71.9 1.5 %outputs.1 = (f32[2,128,128]{2,1,0:T(8,128)}, f32[4,256,128]{2,1,0:T(8,128)}, f32[8,32]{1,0:T(8,128)}, f32[32,4,128]{2,1,0:T(4,128)}) custom-call(f32[8,32]{1,0:T(8,128)S(1)} %copy-done.1, f32[256,128]{1,0:T(8,128)S(1)} %bitcast.6, f32[256,128]{1,0:T(8,128)S(1)} %collective-permute-done.12.b1, f32[256,128]{1,0:T(8,128)S(1)} %collective-permute-done.13.b2, ...), custom_call_target="tpu_custom_call" | custom-call | flops 1048576 | bytes 1048576 | tf_op jit(solution)/shard_map/outputs/pallas_call | solution.py:276
  (30 shorter events, 6.0 us)
Async XLA Ops:
  0.6 19.4 %copy-start.2 = (f32[32,128,128]{2,1,0:T(8,128)S(1)}, f32[32,128,128]{2,1,0:T(8,128)}, u32[]{:S(2)}) copy-start(f32[32,128,128]{2,1,0:T(8,128)} %core.1) | copy-start | bytes 6291460
  14.2 5.8 %collective-permute-start = (f32[5,128,128]{2,1,0:T(8,128)}, f32[5,128,128]{2,1,0:T(8,128)S(1)}, u32[]{:S(2)}, u32[]{:S(2)}) collective-permute-start(f32[5,128,128]{2,1,0:T(8,128)} %get-tuple-element.34), channel_id=1, source_target_pairs={{0,1},{1,0},{2,3},{3,2},{4,5},{5,4},{6,7},{7,6},{8,9},{9,8},{10,11... | collective-permute-start | bytes 983048 | tf_op jit(solution)/shard_map/ppermute | solution.py:288
  14.3 9.0 %collective-permute-start.1 = (f32[256,128]{1,0:T(8,128)}, f32[256,128]{1,0:T(8,128)S(1)}, u32[]{:S(2)}, u32[]{:S(2)}) collective-permute-start(f32[256,128]{1,0:T(8,128)} %get-tuple-element.36), channel_id=1, source_target_pairs={{0,8},{8,16},{16,24},{24,0},{1,9},{9,17},{17,25},{25,1},{2,10},{10... | collective-permute-start | bytes 393224 | tf_op jit(solution)/shard_map/ppermute | solution.py:288
  15.8 10.0 %collective-permute-start.2 = (f32[256,128]{1,0:T(8,128)}, f32[256,128]{1,0:T(8,128)S(1)}, u32[]{:S(2)}, u32[]{:S(2)}) collective-permute-start(f32[256,128]{1,0:T(8,128)} %get-tuple-element.37), channel_id=1, source_target_pairs={{0,16},{8,24},{16,0},{24,8},{1,17},{9,25},{17,1},{25,9},{2,18},{10... | collective-permute-start | bytes 393224 | tf_op jit(solution)/shard_map/ppermute | solution.py:288
  18.6 11.6 %collective-permute-start.3 = (f32[256,128]{1,0:T(8,128)}, f32[256,128]{1,0:T(8,128)S(1)}, u32[]{:S(2)}, u32[]{:S(2)}) collective-permute-start(f32[256,128]{1,0:T(8,128)} %get-tuple-element.40), channel_id=1, source_target_pairs={{0,24},{8,0},{16,8},{24,16},{1,25},{9,1},{17,9},{25,17},{2,26},{10... | collective-permute-start | bytes 393224 | tf_op jit(solution)/shard_map/ppermute | solution.py:288
  20.0 1.0 %copy-start.3 = (f32[5,128,128]{2,1,0:T(8,128)S(1)}, f32[5,128,128]{2,1,0:T(8,128)}, u32[]{:S(2)}) copy-start(f32[5,128,128]{2,1,0:T(8,128)} %get-tuple-element.33.own) | copy-start | bytes 983044
  21.0 9.2 %copy-start = (f32[256,128]{1,0:T(8,128)S(1)}, f32[256,128]{1,0:T(8,128)}, u32[]{:S(2)}) copy-start(f32[256,128]{1,0:T(8,128)} %get-tuple-element.32.a0) | copy-start | bytes 393220
  21.0 50.9 %copy-start.1 = (f32[8,32]{1,0:T(8,128)S(1)}, f32[8,32]{1,0:T(8,128)}, u32[]{:S(2)}) copy-start(f32[8,32]{1,0:T(8,128)} %hour_ref.3) | copy-start | bytes 3076
  21.7 8.4 %collective-permute-start.4 = (f32[136,128]{1,0:T(8,128)S(1)}, f32[136,128]{1,0:T(8,128)S(1)}, u32[]{:S(2)}, u32[]{:S(2)}) collective-permute-start(f32[136,128]{1,0:T(8,128)S(1)} %get-tuple-element.42), channel_id=1, source_target_pairs={{0,8},{8,16},{16,24},{24,0},{1,9},{9,17},{17,25},{25,1},{2,10},{10... | collective-permute-start | bytes 208904 | tf_op jit(solution)/shard_map/ppermute | solution.py:288
  22.4 7.7 %collective-permute-start.5 = (f32[136,128]{1,0:T(8,128)S(1)}, f32[136,128]{1,0:T(8,128)S(1)}, u32[]{:S(2)}, u32[]{:S(2)}) collective-permute-start(f32[136,128]{1,0:T(8,128)S(1)} %get-tuple-element.43), channel_id=1, source_target_pairs={{0,16},{8,24},{16,0},{24,8},{1,17},{9,25},{17,1},{25,9},{2,18},{10... | collective-permute-start | bytes 208904 | tf_op jit(solution)/shard_map/ppermute | solution.py:288
  23.3 6.9 %collective-permute-start.6 = (f32[136,128]{1,0:T(8,128)S(1)}, f32[136,128]{1,0:T(8,128)S(1)}, u32[]{:S(2)}, u32[]{:S(2)}) collective-permute-start(f32[136,128]{1,0:T(8,128)S(1)} %get-tuple-element.44), channel_id=1, source_target_pairs={{0,24},{8,0},{16,8},{24,16},{1,25},{9,1},{17,9},{25,17},{2,26},{10... | collective-permute-start | bytes 208904 | tf_op jit(solution)/shard_map/ppermute | solution.py:288
  25.9 4.3 %collective-permute-start.7 = (f32[128,128]{1,0:T(8,128)S(1)}, f32[128,128]{1,0:T(8,128)S(1)}, u32[]{:S(2)}, u32[]{:S(2)}) collective-permute-start(f32[128,128]{1,0:T(8,128)S(1)} %get-tuple-element.45.refs_0_), channel_id=1, source_target_pairs={{0,2},{2,0},{4,6},{6,4},{1,3},{3,1},{5,7},{7,5},{8,10},{10,8},{12,... | collective-permute-start | bytes 196616 | tf_op jit(solution)/shard_map/ppermute | solution.py:297
  30.9 18.6 %all-to-all-start = ((f32[8,56,128]{2,1,0:T(8,128)}), f32[8,56,128]{2,1,0:T(8,128)S(1)}, u32[]{:S(2)}, u32[]{:S(2)}) async-start(f32[8,56,128]{2,1,0:T(8,128)} %x_sums.1), calls=%async_computation | async-start | bytes 458752 | tf_op jit(solution)/shard_map/all_to_all | solution.py:292
  39.4 4.3 %collective-permute-start.8 = (f32[128,128]{1,0:T(8,128)S(1)}, f32[128,128]{1,0:T(8,128)S(1)}, u32[]{:S(2)}, u32[]{:S(2)}) collective-permute-start(f32[128,128]{1,0:T(8,128)S(1)} %src_near_sum.1.refs_0_), channel_id=1, source_target_pairs={{0,6},{2,4},{4,2},{6,0},{1,7},{3,5},{5,3},{7,1},{8,14},{10,12},{12... | collective-permute-start | bytes 196616 | tf_op jit(solution)/shard_map/ppermute | solution.py:297
  43.7 1.3 %collective-permute-start.9 = (f32[128,128]{1,0:T(8,128)S(1)}, f32[128,128]{1,0:T(8,128)S(1)}, u32[]{:S(2)}, u32[]{:S(2)}) collective-permute-start(f32[128,128]{1,0:T(8,128)S(1)} %src_far_sum.1.src_own), channel_id=1, source_target_pairs={{0,1},{1,0},{2,3},{3,2},{4,5},{5,4},{6,7},{7,6},{8,9},{9,8},{10,11... | collective-permute-start | bytes 196616 | tf_op jit(solution)/shard_map/ppermute | solution.py:288
  50.2 12.4 %all-to-all-start.1 = ((f32[8,32,128]{2,1,0:T(8,128)}), f32[8,32,128]{2,1,0:T(8,128)S(1)}, u32[]{:S(2)}, u32[]{:S(2)}) async-start(f32[8,32,128]{2,1,0:T(8,128)} %z_sums.1), calls=%async_computation.1 | async-start | bytes 262144 | tf_op jit(solution)/shard_map/all_to_all | solution.py:292
  53.6 1.3 %collective-permute-start.10 = (f32[24,128]{1,0:T(8,128)S(1)}, f32[24,128]{1,0:T(8,128)S(1)}, u32[]{:S(2)}, u32[]{:S(2)}) collective-permute-start(f32[24,128]{1,0:T(8,128)S(1)} %tail_sums.1.own), channel_id=1, source_target_pairs={{0,1},{1,0},{2,3},{3,2},{4,5},{5,4},{6,7},{7,6},{8,9},{9,8},{10,11... | collective-permute-start | bytes 36872 | tf_op jit(solution)/shard_map/ppermute | solution.py:288
  54.9 3.8 %collective-permute-start.11 = (f32[2,24,128]{2,1,0:T(8,128)S(1)}, f32[2,24,128]{2,1,0:T(8,128)S(1)}, u32[]{:S(2)}, u32[]{:S(2)}) collective-permute-start(f32[2,24,128]{2,1,0:T(8,128)S(1)} %both_tails.1.refs_0_), channel_id=1, source_target_pairs={{0,2},{2,0},{4,6},{6,4},{1,3},{3,1},{5,7},{7,5},{8,10},{10,8},{12,... | collective-permute-start | bytes 73736 | tf_op jit(solution)/shard_map/ppermute | solution.py:297
  62.6 7.4 %collective-permute-start.14 = (f32[256,128]{1,0:T(8,128)S(1)}, f32[256,128]{1,0:T(8,128)S(1)}, u32[]{:S(2)}, u32[]{:S(2)}) collective-permute-start(f32[256,128]{1,0:T(8,128)S(1)} %bitcast.3), channel_id=1, source_target_pairs={{0,24},{8,0},{16,8},{24,16},{1,25},{9,1},{17,9},{25,17},{2,26},{10... | collective-permute-start | bytes 393224 | tf_op jit(solution)/shard_map/ppermute | solution.py:288
  64.0 6.6 %collective-permute-start.13 = (f32[256,128]{1,0:T(8,128)S(1)}, f32[256,128]{1,0:T(8,128)S(1)}, u32[]{:S(2)}, u32[]{:S(2)}) collective-permute-start(f32[256,128]{1,0:T(8,128)S(1)} %bitcast.4), channel_id=1, source_target_pairs={{0,16},{8,24},{16,0},{24,8},{1,17},{9,25},{17,1},{25,9},{2,18},{10... | collective-permute-start | bytes 393224 | tf_op jit(solution)/shard_map/ppermute | solution.py:288
  64.8 7.1 %collective-permute-start.12 = (f32[256,128]{1,0:T(8,128)S(1)}, f32[256,128]{1,0:T(8,128)S(1)}, u32[]{:S(2)}, u32[]{:S(2)}) collective-permute-start(f32[256,128]{1,0:T(8,128)S(1)} %bitcast.5), channel_id=1, source_target_pairs={{0,8},{8,16},{16,24},{24,0},{1,9},{9,17},{17,25},{25,1},{2,10},{10... | collective-permute-start | bytes 393224 | tf_op jit(solution)/shard_map/ppermute | solution.py:288
  66.1 3.8 %collective-permute-start.15 = (f32[2,24,128]{2,1,0:T(8,128)S(1)}, f32[2,24,128]{2,1,0:T(8,128)S(1)}, u32[]{:S(2)}, u32[]{:S(2)}) collective-permute-start(f32[2,24,128]{2,1,0:T(8,128)S(1)} %near_sum.1.tails), channel_id=1, source_target_pairs={{0,6},{2,4},{4,2},{6,0},{1,7},{3,5},{5,3},{7,1},{8,14},{10,12},{12... | collective-permute-start | bytes 73736 | tf_op jit(solution)/shard_map/ppermute | solution.py:297

commit v10 on v9

--- a/solution.py
+++ b/solution.py
@@ -230,14 +230,24 @@
         out[z, share + each:, :] = m[zs * each:]
 
 
-def tail_kernel(share, w, tail):
-    tail[...] = jnp.sum(w[:, share:, :], axis=0)
-
-
-def pair_kernel(own, other, out):
+def tail_kernel(share, w, src_half, out):
+    tail = w.shape[1] - share
+    out[:tail, :] = jnp.sum(w[:, share:, :], axis=0)
+    out[tail:, :] = src_half[...]
+
+
+def pair_kernel(own, other, tails, src_both):
     c = lax.axis_index("core")
-    out[c] = own[...]
-    out[1 - c] = other[...]
+    tail = tails.shape[1]
+    for at, part in ((c, own), (1 - c, other)):
+        tails[at] = part[:tail, :]
+        src_both[at] = part[tail:, :]
+
+
+def join_kernel(own, came, src_both, out):
+    tail = own.shape[1]
+    out[:, :tail, :] = own[...] + came[...]
+    out[:, tail:, :] = src_both[...]
 
 
 def z_kernel(w, copies):
@@ -247,15 +257,15 @@
         copies[z] = total
 
 
-def end_kernel(scales, hour_ref, b0, b1, b2, b3, tails, more, src_own, src_other,
+def end_kernel(scales, hour_ref, b0, b1, b2, b3, joined, more,
                src_out, dst_out, hour_out, core_out, both):
-    x, c = lax.axis_index("x"), lax.axis_index("core")
+    x = lax.axis_index("x")
     src_scale, dst_scale, hour_scale, core_scale = scales
     for s, block in enumerate((b0, b1, b2, b3)):
         dst_out[lax.rem(x - s + X, X)] = block[...] * dst_scale
-    src_out[c] = src_own[...] * src_scale
-    src_out[1 - c] = src_other[...] * src_scale
-    both[...] = tails[...] + more[...]
+    tail = both.shape[1]
+    src_out[...] = (joined[:, tail:, :] + more[:, tail:, :]) * src_scale
+    both[...] = joined[:, :tail, :] + more[:, :tail, :]
     hours, rank = hour_ref.shape
     half = hours // CORES
     tiles = []
@@ -270,17 +280,19 @@
         core_out[r] = out
 
 
-def end_call(scales, hour, blocks, tails, more, src_own, src_other):
+def end_call(scales, hour, blocks, joined, more):
     block, q1 = blocks[0].shape
     hours, rank = hour.shape
+    tail = 4 * hours // CORES + 8
     return pl.pallas_call(
         functools.partial(end_kernel, scales),
-        in_specs=[SMEM] + [VMEM] * 8,
+        in_specs=[SMEM] + [VMEM] * 6,
         out_specs=[VMEM] * 4,
-        out_shape=[struct(CORES, *src_own.shape), struct(X, block, q1), struct(hours, rank), struct(rank, 4, q1)],
-        scratch_shapes=[pltpu.VMEM(tails.shape, F32)],
+        out_shape=[struct(CORES, joined.shape[1] - tail, q1), struct(X, block, q1),
+                   struct(hours, rank), struct(rank, 4, q1)],
+        scratch_shapes=[pltpu.VMEM((CORES, tail, q1), F32)],
         compiler_params=params(8), cost_estimate=cost(1 << 20, 1 << 20), name="outputs",
-    )(hour, *blocks, tails, more, src_own, src_other)
+    )(hour, *blocks, joined, more)
 
 
 def shifted(x, axis, s):
@@ -323,19 +335,21 @@
     m, src_half = lax.optimization_barrier((m, src_half))
     w = small_call(x_kernel, "x_sums", struct(zs, share + each + 8, q1), [*a, *m])
     w = swapped(w, "z")
-    src_half = summed("src_far_sum", src_half, paired(src_half, "y", far))
-    src_other = shifted(src_half, "core", 1)
-    w, src_half, src_other = lax.optimization_barrier((w, src_half, src_other))
-    tail = small_call(functools.partial(tail_kernel, share), "tail_sums", struct(each + 8, q1), [w])
+    tail = each + 8
+    own = small_call(functools.partial(tail_kernel, share), "tail_sums",
+                     struct(tail + src_half.shape[0], q1), [w, src_half])
     copies = small_call(z_kernel, "z_sums", struct(zs, share, q1), [w])
-    tails = small_call(pair_kernel, "both_tails", struct(CORES, *tail.shape), [tail, shifted(tail, "core", 1)])
-    tails = summed("near_sum", tails, paired(tails, "y", near))
+    tails, src_both = small_call(pair_kernel, "both_tails",
+                                 [struct(CORES, tail, q1), struct(CORES, *src_half.shape)],
+                                 [own, shifted(own, "core", 1)])
+    joined = small_call(join_kernel, "near_sum", struct(CORES, *own.shape),
+                        [tails, paired(tails, "y", near), src_both])
     block = swapped(copies, "z").reshape(zs * share, q1)
-    block, tails = lax.optimization_barrier((block, tails))
-    more = paired(tails, "y", far)
+    block, joined = lax.optimization_barrier((block, joined))
+    more = paired(joined, "y", far)
     blocks = around(block, "x")
     grad_src, grad_dst, grad_hour, grad_core = end_call(
-        scales, hour_factor, blocks, tails, more, src_half, src_other)
+        scales, hour_factor, blocks, joined, more)
     return (grad_src.reshape(src_factor.shape), grad_dst.reshape(dst_factor.shape), grad_hour, grad_core)
 
 

time: 74.6 us -> 74.4 us (level); the launches traced: 73.4 us -> 74.1 us
  blocking collectives: 0 us -> 18.4 us
  starting transfers between devices: 30.5 us -> 19.9 us
  waiting for transfers between devices: 24 us -> 17.5 us
    all_to_all x0 -> x1, blocking collectives: none -> 18.4 us  [swapped(): return lax.all_to_all(x, axis, split_axis=0, concat_axis=0, tiled=True)]
    all_to_all x2 -> x1, starting transfers between devices: 11.8 us -> 3.37 us  [swapped(): return lax.all_to_all(x, axis, split_axis=0, concat_axis=0, tiled=True)]
    all_to_all x2 -> x1, waiting for transfers between devices: 8.39 us -> 3.65 us  [swapped(): return lax.all_to_all(x, axis, split_axis=0, concat_axis=0, tiled=True)]
    ppermute x4 -> x3, waiting for transfers between devices: 10.7 us -> 6.3 us  [paired(): return lax.ppermute(x, axis, [(i, flip(i, n)) for i in range(n)])]
    ppermute x12 -> x11, waiting for transfers between devices: 4.85 us -> 7.53 us  [shifted(): return lax.ppermute(x, axis, [(i, (i + s) % n) for i in range(n)])]
    ppermute x4 -> x3, starting transfers between devices: 5.46 us -> 3.46 us  [paired(): return lax.ppermute(x, axis, [(i, flip(i, n)) for i in range(n)])]
    ppermute x12 -> x11, starting transfers between devices: 13.2 us -> 13.1 us  [shifted(): return lax.ppermute(x, axis, [(i, (i + s) % n) for i in range(n)])]
  transfers between devices with their start and end apart: 18 -> 15, of which waited for: 11 -> 8; matrix products, arithmetic and copies ran while one was open for 0% -> 0% of each run, Pallas kernels for 1% -> 1%
where the time goes in v10:
time: 74.4 us; the launch traced here: 74.1 us
  starting transfers between devices  19.9 us (27%)
  blocking collectives  18.4 us (25%)
  waiting for transfers between devices  17.5 us (24%)
  Pallas kernels  16.5 us (22%)
  local copies, waits for them, and re-layouts  0.99 us (1%)
  between operations  0.75 us (1%)
    all_to_all x1, blocking collectives, swapped(): return lax.all_to_all(x, axis, split_axis=0, concat_axis=0, tiled=True)  18.4 us
    pallas_call x1, Pallas kernels, main_call(): pl.pallas_call(main_kernel, out_shape=[struct(block, q1)] * X + [struct(h...  13.5 us
    ppermute x11, starting transfers between devices, shifted(): return lax.ppermute(x, axis, [(i, (i + s) % n) for i in range(n)])  13.1 us
    ppermute x11, waiting for transfers between devices, shifted(): return lax.ppermute(x, axis, [(i, (i + s) % n) for i in range(n)])  7.53 us
    ppermute x3, waiting for transfers between devices, paired(): return lax.ppermute(x, axis, [(i, flip(i, n)) for i in range(n)])  6.3 us
    all_to_all x1, waiting for transfers between devices, swapped(): return lax.all_to_all(x, axis, split_axis=0, concat_axis=0, tiled=True)  3.65 us
    ppermute x3, starting transfers between devices, paired(): return lax.ppermute(x, axis, [(i, flip(i, n)) for i in range(n)])  3.46 us
    all_to_all x1, starting transfers between devices, swapped(): return lax.all_to_all(x, axis, split_axis=0, concat_axis=0, tiled=True)  3.37 us
  transfers between devices with their start and end apart: 15, of which 8 were waited for; matrix products, arithmetic and copies ran while one was open for 0% of the time, Pallas kernels for 1%

profile of v10, /device:TPU:8, one launch (start us, length us, event | category | flops | bytes accessed | tf_op | source)
XLA Modules:
  0.0 74.1 jit_solution(17603290552054824465)
XLA Ops:
  0.6 13.5 %all_terms.1 = (f32[256,128]{1,0:T(8,128)}, f32[256,128]{1,0:T(8,128)}, f32[256,128]{1,0:T(8,128)}, f32[256,128]{1,0:T(8,128)}, f32[5,128,128]{2,1,0:T(8,128)}, /*index=5*/f32[5,128,128]{2,1,0:T(8,128)}) custom-call(f32[8,32]{1,0:T(8,128)} %hour_ref.3, s32[8,256,1024]{2,1,0:T(8,128)} %counts_hbm.1, f32[256,128]{1,0:T(8,128)} %src_hbm.1, ...), custom_call_target="tpu_custom_call" | custom-call | flops 4831838208 | bytes 14680064 | tf_op jit(solution)/shard_map/all_terms/pallas_call | solution.py:133
  14.2 1.6 %collective-permute-start.1 = (f32[256,128]{1,0:T(8,128)}, f32[256,128]{1,0:T(8,128)S(1)}, u32[]{:S(2)}, u32[]{:S(2)}) collective-permute-start(f32[256,128]{1,0:T(8,128)} %get-tuple-element.35), channel_id=1, source_target_pairs={{0,8},{8,16},{16,24},{24,0},{1,9},{9,17},{17,25},{25,1},{2,10},{10... | collective-permute-start | bytes 393224 | tf_op jit(solution)/shard_map/ppermute | solution.py:300
  15.8 2.7 %collective-permute-start.2 = (f32[256,128]{1,0:T(8,128)}, f32[256,128]{1,0:T(8,128)S(1)}, u32[]{:S(2)}, u32[]{:S(2)}) collective-permute-start(f32[256,128]{1,0:T(8,128)} %get-tuple-element.36), channel_id=1, source_target_pairs={{0,16},{8,24},{16,0},{24,8},{1,17},{9,25},{17,1},{25,9},{2,18},{10... | collective-permute-start | bytes 393224 | tf_op jit(solution)/shard_map/ppermute | solution.py:300
  18.6 1.4 %collective-permute-start.3 = (f32[256,128]{1,0:T(8,128)}, f32[256,128]{1,0:T(8,128)S(1)}, u32[]{:S(2)}, u32[]{:S(2)}) collective-permute-start(f32[256,128]{1,0:T(8,128)} %get-tuple-element.39), channel_id=1, source_target_pairs={{0,24},{8,0},{16,8},{24,16},{1,25},{9,1},{17,9},{25,17},{2,26},{10... | collective-permute-start | bytes 393224 | tf_op jit(solution)/shard_map/ppermute | solution.py:300
  20.0 1.0 %copy-done.3 = f32[5,128,128]{2,1,0:T(8,128)S(1)} copy-done((f32[5,128,128]{2,1,0:T(8,128)S(1)}, f32[5,128,128]{2,1,0:T(8,128)}, u32[]{:S(2)}) %copy-start.3) | copy-done | bytes 327704
  21.0 0.8 %hour_terms.1 = (f32[136,128]{1,0:T(8,128)S(1)}, f32[136,128]{1,0:T(8,128)S(1)}, f32[136,128]{1,0:T(8,128)S(1)}, f32[136,128]{1,0:T(8,128)S(1)}, f32[128,128]{1,0:T(8,128)S(1)}) custom-call(f32[5,128,128]{2,1,0:T(8,128)S(1)} %copy-done.3, f32[5,128,128]{2,1,0:T(8,128)S(1)} %collective-permute-done.came, f32[32,128,128]{2,1,0:T(8,128)S(1)} %copy-done.2), custom_call_target="tpu_custom_call" | custom-call | flops 17179869184 | bytes 4194304 | tf_op jit(solution)/shard_map/hour_terms/pallas_call | solution.py:190
  22.4 0.9 %collective-permute-start.5 = (f32[136,128]{1,0:T(8,128)S(1)}, f32[136,128]{1,0:T(8,128)S(1)}, u32[]{:S(2)}, u32[]{:S(2)}) collective-permute-start(f32[136,128]{1,0:T(8,128)S(1)} %get-tuple-element.42), channel_id=1, source_target_pairs={{0,16},{8,24},{16,0},{24,8},{1,17},{9,25},{17,1},{25,9},{2,18},{10... | collective-permute-start | bytes 208904 | tf_op jit(solution)/shard_map/ppermute | solution.py:300
  23.3 2.1 %collective-permute-start.6 = (f32[136,128]{1,0:T(8,128)S(1)}, f32[136,128]{1,0:T(8,128)S(1)}, u32[]{:S(2)}, u32[]{:S(2)}) collective-permute-start(f32[136,128]{1,0:T(8,128)S(1)} %get-tuple-element.43), channel_id=1, source_target_pairs={{0,24},{8,0},{16,8},{24,16},{1,25},{9,1},{17,9},{25,17},{2,26},{10... | collective-permute-start | bytes 208904 | tf_op jit(solution)/shard_map/ppermute | solution.py:300
  25.9 1.4 %collective-permute-start.7 = (f32[128,128]{1,0:T(8,128)S(1)}, f32[128,128]{1,0:T(8,128)S(1)}, u32[]{:S(2)}, u32[]{:S(2)}) collective-permute-start(f32[128,128]{1,0:T(8,128)S(1)} %get-tuple-element.44.refs_0_), channel_id=1, source_target_pairs={{0,2},{2,0},{4,6},{6,4},{1,3},{3,1},{5,7},{7,5},{8,10},{10,8},{12,... | collective-permute-start | bytes 196616 | tf_op jit(solution)/shard_map/ppermute | solution.py:309
  27.2 2.9 %collective-permute-done.7.refs_1_ = f32[128,128]{1,0:T(8,128)S(1)} collective-permute-done((f32[128,128]{1,0:T(8,128)S(1)}, f32[128,128]{1,0:T(8,128)S(1)}, u32[]{:S(2)}, u32[]{:S(2)}) %collective-permute-start.7) | collective-permute-done | bytes 65568 | tf_op jit(solution)/shard_map/ppermute | solution.py:309
  30.2 18.4 %all_to_all.10.w = f32[8,56,128]{2,1,0:T(8,128)S(1)} all-to-all(f32[8,56,128]{2,1,0:T(8,128)S(1)} %x_sums.1), channel_id=1, replica_groups=mesh['z'=8,'x'=4,'y'=4,'core'=2] {'z'}, dimensions={0} | all-to-all | bytes 458752 | tf_op jit(solution)/shard_map/all_to_all | solution.py:304
  48.6 0.7 z_sums.1
  49.3 3.4 %all-to-all-start.1 = ((f32[8,32,128]{2,1,0:T(8,128)}), f32[8,32,128]{2,1,0:T(8,128)S(1)}, u32[]{:S(2)}, u32[]{:S(2)}) async-start(f32[8,32,128]{2,1,0:T(8,128)} %z_sums.1), calls=%async_computation.1 | async-start | bytes 262144 | tf_op jit(solution)/shard_map/all_to_all | solution.py:304
  52.8 1.3 %collective-permute-done.8.other = f32[152,128]{1,0:T(8,128)S(1)} collective-permute-done((f32[152,128]{1,0:T(8,128)S(1)}, f32[152,128]{1,0:T(8,128)S(1)}, u32[]{:S(2)}, u32[]{:S(2)}) %collective-permute-start.8) | collective-permute-done | bytes 77856 | tf_op jit(solution)/shard_map/ppermute | solution.py:300
  54.6 3.4 %collective-permute-done.9.came = f32[2,24,128]{2,1,0:T(8,128)S(1)} collective-permute-done((f32[2,24,128]{2,1,0:T(8,128)S(1)}, f32[2,24,128]{2,1,0:T(8,128)S(1)}, u32[]{:S(2)}, u32[]{:S(2)}) %collective-permute-start.9) | collective-permute-done | bytes 24608 | tf_op jit(solution)/shard_map/ppermute | solution.py:309
  58.0 3.7 %all-to-all-done.1 = f32[8,32,128]{2,1,0:T(8,128)S(1)} async-done(((f32[8,32,128]{2,1,0:T(8,128)}), f32[8,32,128]{2,1,0:T(8,128)S(1)}, u32[]{:S(2)}, u32[]{:S(2)}) %all-to-all-start.1) | async-done | bytes 131104 | tf_op jit(solution)/shard_map/all_to_all | solution.py:304
  61.7 1.6 %collective-permute-start.13 = (f32[2,152,128]{2,1,0:T(8,128)S(1)}, f32[2,152,128]{2,1,0:T(8,128)S(1)}, u32[]{:S(2)}, u32[]{:S(2)}) collective-permute-start(f32[2,152,128]{2,1,0:T(8,128)S(1)} %near_sum.1.joined), channel_id=1, source_target_pairs={{0,6},{2,4},{4,2},{6,0},{1,7},{3,5},{5,3},{7,1},{8,14},{10,12},{12... | collective-permute-start | bytes 466952 | tf_op jit(solution)/shard_map/ppermute | solution.py:309
  63.2 1.4 %collective-permute-start.12 = (f32[256,128]{1,0:T(8,128)S(1)}, f32[256,128]{1,0:T(8,128)S(1)}, u32[]{:S(2)}, u32[]{:S(2)}) collective-permute-start(f32[256,128]{1,0:T(8,128)S(1)} %bitcast.3), channel_id=1, source_target_pairs={{0,24},{8,0},{16,8},{24,16},{1,25},{9,1},{17,9},{25,17},{2,26},{10... | collective-permute-start | bytes 393224 | tf_op jit(solution)/shard_map/ppermute | solution.py:300
  64.7 0.8 %collective-permute-start.11 = (f32[256,128]{1,0:T(8,128)S(1)}, f32[256,128]{1,0:T(8,128)S(1)}, u32[]{:S(2)}, u32[]{:S(2)}) collective-permute-start(f32[256,128]{1,0:T(8,128)S(1)} %bitcast.4), channel_id=1, source_target_pairs={{0,16},{8,24},{16,0},{24,8},{1,17},{9,25},{17,1},{25,9},{2,18},{10... | collective-permute-start | bytes 393224 | tf_op jit(solution)/shard_map/ppermute | solution.py:300
  65.5 1.3 %collective-permute-start.10 = (f32[256,128]{1,0:T(8,128)S(1)}, f32[256,128]{1,0:T(8,128)S(1)}, u32[]{:S(2)}, u32[]{:S(2)}) collective-permute-start(f32[256,128]{1,0:T(8,128)S(1)} %bitcast.5), channel_id=1, source_target_pairs={{0,8},{8,16},{16,24},{24,0},{1,9},{9,17},{17,25},{25,1},{2,10},{10... | collective-permute-start | bytes 393224 | tf_op jit(solution)/shard_map/ppermute | solution.py:300
  66.8 1.4 %collective-permute-done.12.b3 = f32[256,128]{1,0:T(8,128)S(1)} collective-permute-done((f32[256,128]{1,0:T(8,128)S(1)}, f32[256,128]{1,0:T(8,128)S(1)}, u32[]{:S(2)}, u32[]{:S(2)}) %collective-permute-start.12) | collective-permute-done | bytes 131104 | tf_op jit(solution)/shard_map/ppermute | solution.py:300
  68.2 3.0 %collective-permute-done.11.b2 = f32[256,128]{1,0:T(8,128)S(1)} collective-permute-done((f32[256,128]{1,0:T(8,128)S(1)}, f32[256,128]{1,0:T(8,128)S(1)}, u32[]{:S(2)}, u32[]{:S(2)}) %collective-permute-start.11) | collective-permute-done | bytes 131104 | tf_op jit(solution)/shard_map/ppermute | solution.py:300
  71.2 1.3 %collective-permute-done.10.b1 = f32[256,128]{1,0:T(8,128)S(1)} collective-permute-done((f32[256,128]{1,0:T(8,128)S(1)}, f32[256,128]{1,0:T(8,128)S(1)}, u32[]{:S(2)}, u32[]{:S(2)}) %collective-permute-start.10) | collective-permute-done | bytes 131104 | tf_op jit(solution)/shard_map/ppermute | solution.py:300
  72.6 1.5 %outputs.1 = (f32[2,128,128]{2,1,0:T(8,128)}, f32[4,256,128]{2,1,0:T(8,128)}, f32[8,32]{1,0:T(8,128)}, f32[32,4,128]{2,1,0:T(4,128)}) custom-call(f32[8,32]{1,0:T(8,128)S(1)} %copy-done.1, f32[256,128]{1,0:T(8,128)S(1)} %bitcast.6, f32[256,128]{1,0:T(8,128)S(1)} %collective-permute-done.10.b1, f32[256,128]{1,0:T(8,128)S(1)} %collective-permute-done.11.b2, ...), custom_call_target="tpu_custom_call" | custom-call | flops 1048576 | bytes 1048576 | tf_op jit(solution)/shard_map/outputs/pallas_call | solution.py:287
  (24 shorter events, 2.0 us)
Async XLA Ops:
  0.6 19.4 %copy-start.2 = (f32[32,128,128]{2,1,0:T(8,128)S(1)}, f32[32,128,128]{2,1,0:T(8,128)}, u32[]{:S(2)}) copy-start(f32[32,128,128]{2,1,0:T(8,128)} %core.1) | copy-start | bytes 6291460
  14.1 5.8 %collective-permute-start = (f32[5,128,128]{2,1,0:T(8,128)}, f32[5,128,128]{2,1,0:T(8,128)S(1)}, u32[]{:S(2)}, u32[]{:S(2)}) collective-permute-start(f32[5,128,128]{2,1,0:T(8,128)} %get-tuple-element.33), channel_id=1, source_target_pairs={{0,1},{1,0},{2,3},{3,2},{4,5},{5,4},{6,7},{7,6},{8,9},{9,8},{10,11... | collective-permute-start | bytes 983048 | tf_op jit(solution)/shard_map/ppermute | solution.py:300
  14.2 9.0 %collective-permute-start.1 = (f32[256,128]{1,0:T(8,128)}, f32[256,128]{1,0:T(8,128)S(1)}, u32[]{:S(2)}, u32[]{:S(2)}) collective-permute-start(f32[256,128]{1,0:T(8,128)} %get-tuple-element.35), channel_id=1, source_target_pairs={{0,8},{8,16},{16,24},{24,0},{1,9},{9,17},{17,25},{25,1},{2,10},{10... | collective-permute-start | bytes 393224 | tf_op jit(solution)/shard_map/ppermute | solution.py:300
  15.8 10.0 %collective-permute-start.2 = (f32[256,128]{1,0:T(8,128)}, f32[256,128]{1,0:T(8,128)S(1)}, u32[]{:S(2)}, u32[]{:S(2)}) collective-permute-start(f32[256,128]{1,0:T(8,128)} %get-tuple-element.36), channel_id=1, source_target_pairs={{0,16},{8,24},{16,0},{24,8},{1,17},{9,25},{17,1},{25,9},{2,18},{10... | collective-permute-start | bytes 393224 | tf_op jit(solution)/shard_map/ppermute | solution.py:300
  18.6 11.6 %collective-permute-start.3 = (f32[256,128]{1,0:T(8,128)}, f32[256,128]{1,0:T(8,128)S(1)}, u32[]{:S(2)}, u32[]{:S(2)}) collective-permute-start(f32[256,128]{1,0:T(8,128)} %get-tuple-element.39), channel_id=1, source_target_pairs={{0,24},{8,0},{16,8},{24,16},{1,25},{9,1},{17,9},{25,17},{2,26},{10... | collective-permute-start | bytes 393224 | tf_op jit(solution)/shard_map/ppermute | solution.py:300
  20.0 1.0 %copy-start.3 = (f32[5,128,128]{2,1,0:T(8,128)S(1)}, f32[5,128,128]{2,1,0:T(8,128)}, u32[]{:S(2)}) copy-start(f32[5,128,128]{2,1,0:T(8,128)} %get-tuple-element.32.own) | copy-start | bytes 983044
  21.0 9.2 %copy-start = (f32[256,128]{1,0:T(8,128)S(1)}, f32[256,128]{1,0:T(8,128)}, u32[]{:S(2)}) copy-start(f32[256,128]{1,0:T(8,128)} %get-tuple-element.31.a0) | copy-start | bytes 393220
  21.0 51.6 %copy-start.1 = (f32[8,32]{1,0:T(8,128)S(1)}, f32[8,32]{1,0:T(8,128)}, u32[]{:S(2)}) copy-start(f32[8,32]{1,0:T(8,128)} %hour_ref.3) | copy-start | bytes 3076
  21.7 8.4 %collective-permute-start.4 = (f32[136,128]{1,0:T(8,128)S(1)}, f32[136,128]{1,0:T(8,128)S(1)}, u32[]{:S(2)}, u32[]{:S(2)}) collective-permute-start(f32[136,128]{1,0:T(8,128)S(1)} %get-tuple-element.41), channel_id=1, source_target_pairs={{0,8},{8,16},{16,24},{24,0},{1,9},{9,17},{17,25},{25,1},{2,10},{10... | collective-permute-start | bytes 208904 | tf_op jit(solution)/shard_map/ppermute | solution.py:300
  22.4 7.7 %collective-permute-start.5 = (f32[136,128]{1,0:T(8,128)S(1)}, f32[136,128]{1,0:T(8,128)S(1)}, u32[]{:S(2)}, u32[]{:S(2)}) collective-permute-start(f32[136,128]{1,0:T(8,128)S(1)} %get-tuple-element.42), channel_id=1, source_target_pairs={{0,16},{8,24},{16,0},{24,8},{1,17},{9,25},{17,1},{25,9},{2,18},{10... | collective-permute-start | bytes 208904 | tf_op jit(solution)/shard_map/ppermute | solution.py:300
  23.3 6.9 %collective-permute-start.6 = (f32[136,128]{1,0:T(8,128)S(1)}, f32[136,128]{1,0:T(8,128)S(1)}, u32[]{:S(2)}, u32[]{:S(2)}) collective-permute-start(f32[136,128]{1,0:T(8,128)S(1)} %get-tuple-element.43), channel_id=1, source_target_pairs={{0,24},{8,0},{16,8},{24,16},{1,25},{9,1},{17,9},{25,17},{2,26},{10... | collective-permute-start | bytes 208904 | tf_op jit(solution)/shard_map/ppermute | solution.py:300
  25.9 4.3 %collective-permute-start.7 = (f32[128,128]{1,0:T(8,128)S(1)}, f32[128,128]{1,0:T(8,128)S(1)}, u32[]{:S(2)}, u32[]{:S(2)}) collective-permute-start(f32[128,128]{1,0:T(8,128)S(1)} %get-tuple-element.44.refs_0_), channel_id=1, source_target_pairs={{0,2},{2,0},{4,6},{6,4},{1,3},{3,1},{5,7},{7,5},{8,10},{10,8},{12,... | collective-permute-start | bytes 196616 | tf_op jit(solution)/shard_map/ppermute | solution.py:309
  49.3 12.4 %all-to-all-start.1 = ((f32[8,32,128]{2,1,0:T(8,128)}), f32[8,32,128]{2,1,0:T(8,128)S(1)}, u32[]{:S(2)}, u32[]{:S(2)}) async-start(f32[8,32,128]{2,1,0:T(8,128)} %z_sums.1), calls=%async_computation.1 | async-start | bytes 262144 | tf_op jit(solution)/shard_map/all_to_all | solution.py:304
  52.7 1.4 %collective-permute-start.8 = (f32[152,128]{1,0:T(8,128)S(1)}, f32[152,128]{1,0:T(8,128)S(1)}, u32[]{:S(2)}, u32[]{:S(2)}) collective-permute-start(f32[152,128]{1,0:T(8,128)S(1)} %tail_sums.1.own), channel_id=1, source_target_pairs={{0,1},{1,0},{2,3},{3,2},{4,5},{5,4},{6,7},{7,6},{8,9},{9,8},{10,11... | collective-permute-start | bytes 233480 | tf_op jit(solution)/shard_map/ppermute | solution.py:300
  54.1 3.9 %collective-permute-start.9 = (f32[2,24,128]{2,1,0:T(8,128)S(1)}, f32[2,24,128]{2,1,0:T(8,128)S(1)}, u32[]{:S(2)}, u32[]{:S(2)}) collective-permute-start(f32[2,24,128]{2,1,0:T(8,128)S(1)} %get-tuple-element.50.own), channel_id=1, source_target_pairs={{0,2},{2,0},{4,6},{6,4},{1,3},{3,1},{5,7},{7,5},{8,10},{10,8},{12,... | collective-permute-start | bytes 73736 | tf_op jit(solution)/shard_map/ppermute | solution.py:309
  61.7 10.9 %collective-permute-start.13 = (f32[2,152,128]{2,1,0:T(8,128)S(1)}, f32[2,152,128]{2,1,0:T(8,128)S(1)}, u32[]{:S(2)}, u32[]{:S(2)}) collective-permute-start(f32[2,152,128]{2,1,0:T(8,128)S(1)} %near_sum.1.joined), channel_id=1, source_target_pairs={{0,6},{2,4},{4,2},{6,0},{1,7},{3,5},{5,3},{7,1},{8,14},{10,12},{12... | collective-permute-start | bytes 466952 | tf_op jit(solution)/shard_map/ppermute | solution.py:309
  63.2 5.0 %collective-permute-start.12 = (f32[256,128]{1,0:T(8,128)S(1)}, f32[256,128]{1,0:T(8,128)S(1)}, u32[]{:S(2)}, u32[]{:S(2)}) collective-permute-start(f32[256,128]{1,0:T(8,128)S(1)} %bitcast.3), channel_id=1, source_target_pairs={{0,24},{8,0},{16,8},{24,16},{1,25},{9,1},{17,9},{25,17},{2,26},{10... | collective-permute-start | bytes 393224 | tf_op jit(solution)/shard_map/ppermute | solution.py:300
  64.7 6.6 %collective-permute-start.11 = (f32[256,128]{1,0:T(8,128)S(1)}, f32[256,128]{1,0:T(8,128)S(1)}, u32[]{:S(2)}, u32[]{:S(2)}) collective-permute-start(f32[256,128]{1,0:T(8,128)S(1)} %bitcast.4), channel_id=1, source_target_pairs={{0,16},{8,24},{16,0},{24,8},{1,17},{9,25},{17,1},{25,9},{2,18},{10... | collective-permute-start | bytes 393224 | tf_op jit(solution)/shard_map/ppermute | solution.py:300
  65.5 7.1 %collective-permute-start.10 = (f32[256,128]{1,0:T(8,128)S(1)}, f32[256,128]{1,0:T(8,128)S(1)}, u32[]{:S(2)}, u32[]{:S(2)}) collective-permute-start(f32[256,128]{1,0:T(8,128)S(1)} %bitcast.5), channel_id=1, source_target_pairs={{0,8},{8,16},{16,24},{24,0},{1,9},{9,17},{17,25},{25,1},{2,10},{10... | collective-permute-start | bytes 393224 | tf_op jit(solution)/shard_map/ppermute | solution.py:300

commit v11 on v10

--- a/solution.py
+++ b/solution.py
@@ -236,20 +236,6 @@
     out[tail:, :] = src_half[...]
 
 
-def pair_kernel(own, other, tails, src_both):
-    c = lax.axis_index("core")
-    tail = tails.shape[1]
-    for at, part in ((c, own), (1 - c, other)):
-        tails[at] = part[:tail, :]
-        src_both[at] = part[tail:, :]
-
-
-def join_kernel(own, came, src_both, out):
-    tail = own.shape[1]
-    out[:, :tail, :] = own[...] + came[...]
-    out[:, tail:, :] = src_both[...]
-
-
 def z_kernel(w, copies):
     share = copies.shape[1]
     total = jnp.sum(w[:, :share, :], axis=0)
@@ -257,15 +243,17 @@
         copies[z] = total
 
 
-def end_kernel(scales, hour_ref, b0, b1, b2, b3, joined, more,
+def end_kernel(scales, hour_ref, b0, b1, b2, b3, own, distant, sibling, diagonal,
                src_out, dst_out, hour_out, core_out, both):
-    x = lax.axis_index("x")
+    x, c = lax.axis_index("x"), lax.axis_index("core")
     src_scale, dst_scale, hour_scale, core_scale = scales
     for s, block in enumerate((b0, b1, b2, b3)):
         dst_out[lax.rem(x - s + X, X)] = block[...] * dst_scale
     tail = both.shape[1]
-    src_out[...] = (joined[:, tail:, :] + more[:, tail:, :]) * src_scale
-    both[...] = joined[:, :tail, :] + more[:, :tail, :]
+    for at, p, q in ((c, own, distant), (1 - c, sibling, diagonal)):
+        total = p[...] + q[...]
+        both[at] = total[:tail]
+        src_out[at] = total[tail:] * src_scale
     hours, rank = hour_ref.shape
     half = hours // CORES
     tiles = []
@@ -280,19 +268,19 @@
         core_out[r] = out
 
 
-def end_call(scales, hour, blocks, joined, more):
+def end_call(scales, hour, blocks, sums):
     block, q1 = blocks[0].shape
     hours, rank = hour.shape
     tail = 4 * hours // CORES + 8
     return pl.pallas_call(
         functools.partial(end_kernel, scales),
-        in_specs=[SMEM] + [VMEM] * 6,
+        in_specs=[SMEM] + [VMEM] * 8,
         out_specs=[VMEM] * 4,
-        out_shape=[struct(CORES, joined.shape[1] - tail, q1), struct(X, block, q1),
+        out_shape=[struct(CORES, sums[0].shape[0] - tail, q1), struct(X, block, q1),
                    struct(hours, rank), struct(rank, 4, q1)],
         scratch_shapes=[pltpu.VMEM((CORES, tail, q1), F32)],
         compiler_params=params(8), cost_estimate=cost(1 << 20, 1 << 20), name="outputs",
-    )(hour, *blocks, joined, more)
+    )(hour, *blocks, *sums)
 
 
 def shifted(x, axis, s):
@@ -330,26 +318,20 @@
     m = [m0] + [shifted(v, "x", s) for s, v in ((1, m1), (2, m2), (3, m3))]
     share = a0.shape[0] // zs
     each = (m0.shape[0] - 8) // zs
-    src_half, a[1], a[2] = lax.optimization_barrier((src_half, a[1], a[2]))
-    src_half = summed("src_near_sum", src_half, paired(src_half, "y", near))
-    m, src_half = lax.optimization_barrier((m, src_half))
     w = small_call(x_kernel, "x_sums", struct(zs, share + each + 8, q1), [*a, *m])
     w = swapped(w, "z")
     tail = each + 8
     own = small_call(functools.partial(tail_kernel, share), "tail_sums",
                      struct(tail + src_half.shape[0], q1), [w, src_half])
     copies = small_call(z_kernel, "z_sums", struct(zs, share, q1), [w])
-    tails, src_both = small_call(pair_kernel, "both_tails",
-                                 [struct(CORES, tail, q1), struct(CORES, *src_half.shape)],
-                                 [own, shifted(own, "core", 1)])
-    joined = small_call(join_kernel, "near_sum", struct(CORES, *own.shape),
-                        [tails, paired(tails, "y", near), src_both])
+    own = summed("near_sum", own, paired(own, "y", near))
     block = swapped(copies, "z").reshape(zs * share, q1)
-    block, joined = lax.optimization_barrier((block, joined))
-    more = paired(joined, "y", far)
+    block, own = lax.optimization_barrier((block, own))
+    mine = [own, paired(own, "y", far)]
+    others = [shifted(own, "core", 1), paired(own, ("y", "core"), far)]
     blocks = around(block, "x")
     grad_src, grad_dst, grad_hour, grad_core = end_call(
-        scales, hour_factor, blocks, joined, more)
+        scales, hour_factor, blocks, mine + others)
     return (grad_src.reshape(src_factor.shape), grad_dst.reshape(dst_factor.shape), grad_hour, grad_core)
 
 

time: 74.4 us -> 76.4 us (1.027)
  waiting for transfers between devices: 17.5 us -> 19.8 us
  starting transfers between devices: 19.9 us -> 18.8 us
    ppermute x3, starting transfers between devices: 3.46 us -> 1.4 us  [paired(): return lax.ppermute(x, axis, [(i, flip(i, n)) for i in range(n)])]
    ppermute x3, waiting for transfers between devices: 6.3 us -> 7.53 us  [paired(): return lax.ppermute(x, axis, [(i, flip(i, n)) for i in range(n)])]
    ppermute x11, starting transfers between devices: 13.1 us -> 14 us  [shifted(): return lax.ppermute(x, axis, [(i, (i + s) % n) for i in range(n)])]
    all_to_all x1, waiting for transfers between devices: 3.65 us -> 4.47 us  [swapped(): return lax.all_to_all(x, axis, split_axis=0, concat_axis=0, tiled=True)]
  transfers between devices with their start and end apart: 15 -> 15, of which waited for: 8 -> 9; matrix products, arithmetic and copies ran while one was open for 0% -> 0% of each run, Pallas kernels for 1% -> 1%
where the time goes in v11:
time: 76.4 us; the launch traced here: 75.3 us
  waiting for transfers between devices  19.8 us (26%)
  starting transfers between devices  18.8 us (25%)
  blocking collectives  18.5 us (24%)
  Pallas kernels  16.5 us (22%)
  local copies, waits for them, and re-layouts  0.99 us (1%)
    all_to_all x1, blocking collectives, swapped(): return lax.all_to_all(x, axis, split_axis=0, concat_axis=0, tiled=True)  18.5 us
    ppermute x11, starting transfers between devices, shifted(): return lax.ppermute(x, axis, [(i, (i + s) % n) for i in range(n)])  14 us
    pallas_call x1, Pallas kernels, main_call(): pl.pallas_call(main_kernel, out_shape=[struct(block, q1)] * X + [struct(h...  13.5 us
    ppermute x11, waiting for transfers between devices, shifted(): return lax.ppermute(x, axis, [(i, (i + s) % n) for i in range(n)])  7.83 us
    ppermute x3, waiting for transfers between devices, paired(): return lax.ppermute(x, axis, [(i, flip(i, n)) for i in range(n)])  7.53 us
    all_to_all x1, waiting for transfers between devices, swapped(): return lax.all_to_all(x, axis, split_axis=0, concat_axis=0, tiled=True)  4.47 us
    all_to_all x1, starting transfers between devices, swapped(): return lax.all_to_all(x, axis, split_axis=0, concat_axis=0, tiled=True)  3.37 us
  transfers between devices with their start and end apart: 15, of which 9 were waited for; matrix products, arithmetic and copies ran while one was open for 0% of the time, Pallas kernels for 1%

profile of v11, /device:TPU:8, one launch (start us, length us, event | category | flops | bytes accessed | tf_op | source)
XLA Modules:
  0.0 75.3 jit_solution(5764325556945684251)
XLA Ops:
  0.6 13.5 %all_terms.1 = (f32[256,128]{1,0:T(8,128)}, f32[256,128]{1,0:T(8,128)}, f32[256,128]{1,0:T(8,128)}, f32[256,128]{1,0:T(8,128)}, f32[5,128,128]{2,1,0:T(8,128)}, /*index=5*/f32[5,128,128]{2,1,0:T(8,128)}) custom-call(f32[8,32]{1,0:T(8,128)} %hour_ref.3, s32[8,256,1024]{2,1,0:T(8,128)} %counts_hbm.1, f32[256,128]{1,0:T(8,128)} %src_hbm.1, ...), custom_call_target="tpu_custom_call" | custom-call | flops 4831838208 | bytes 14680064 | tf_op jit(solution)/shard_map/all_terms/pallas_call | solution.py:133
  14.3 1.6 %collective-permute-start = (f32[256,128]{1,0:T(8,128)}, f32[256,128]{1,0:T(8,128)S(1)}, u32[]{:S(2)}, u32[]{:S(2)}) collective-permute-start(f32[256,128]{1,0:T(8,128)} %get-tuple-element.22), channel_id=1, source_target_pairs={{0,8},{8,16},{16,24},{24,0},{1,9},{9,17},{17,25},{25,1},{2,10},{10... | collective-permute-start | bytes 393224 | tf_op jit(solution)/shard_map/ppermute | solution.py:288
  15.8 2.7 %collective-permute-start.1 = (f32[256,128]{1,0:T(8,128)}, f32[256,128]{1,0:T(8,128)S(1)}, u32[]{:S(2)}, u32[]{:S(2)}) collective-permute-start(f32[256,128]{1,0:T(8,128)} %get-tuple-element.23), channel_id=1, source_target_pairs={{0,16},{8,24},{16,0},{24,8},{1,17},{9,25},{17,1},{25,9},{2,18},{10... | collective-permute-start | bytes 393224 | tf_op jit(solution)/shard_map/ppermute | solution.py:288
  18.6 1.4 %collective-permute-start.2 = (f32[256,128]{1,0:T(8,128)}, f32[256,128]{1,0:T(8,128)S(1)}, u32[]{:S(2)}, u32[]{:S(2)}) collective-permute-start(f32[256,128]{1,0:T(8,128)} %get-tuple-element.24), channel_id=1, source_target_pairs={{0,24},{8,0},{16,8},{24,16},{1,25},{9,1},{17,9},{25,17},{2,26},{10... | collective-permute-start | bytes 393224 | tf_op jit(solution)/shard_map/ppermute | solution.py:288
  20.0 1.0 %copy-done.3 = f32[5,128,128]{2,1,0:T(8,128)S(1)} copy-done((f32[5,128,128]{2,1,0:T(8,128)S(1)}, f32[5,128,128]{2,1,0:T(8,128)}, u32[]{:S(2)}) %copy-start.3) | copy-done | bytes 327704
  21.0 0.8 hour_terms.1
  21.7 0.7 collective-permute-start.4
  22.4 0.9 %collective-permute-start.5 = (f32[136,128]{1,0:T(8,128)S(1)}, f32[136,128]{1,0:T(8,128)S(1)}, u32[]{:S(2)}, u32[]{:S(2)}) collective-permute-start(f32[136,128]{1,0:T(8,128)S(1)} %get-tuple-element.29), channel_id=1, source_target_pairs={{0,16},{8,24},{16,0},{24,8},{1,17},{9,25},{17,1},{25,9},{2,18},{10... | collective-permute-start | bytes 208904 | tf_op jit(solution)/shard_map/ppermute | solution.py:288
  23.3 2.1 %collective-permute-start.6 = (f32[136,128]{1,0:T(8,128)S(1)}, f32[136,128]{1,0:T(8,128)S(1)}, u32[]{:S(2)}, u32[]{:S(2)}) collective-permute-start(f32[136,128]{1,0:T(8,128)S(1)} %get-tuple-element.30), channel_id=1, source_target_pairs={{0,24},{8,0},{16,8},{24,16},{1,25},{9,1},{17,9},{25,17},{2,26},{10... | collective-permute-start | bytes 208904 | tf_op jit(solution)/shard_map/ppermute | solution.py:288
  25.9 2.9 %collective-permute-done.4.m1 = f32[136,128]{1,0:T(8,128)S(1)} collective-permute-done((f32[136,128]{1,0:T(8,128)S(1)}, f32[136,128]{1,0:T(8,128)S(1)}, u32[]{:S(2)}, u32[]{:S(2)}) %collective-permute-start.4) | collective-permute-done | bytes 69664 | tf_op jit(solution)/shard_map/ppermute | solution.py:288
  29.0 18.5 %all_to_all.10.w = f32[8,56,128]{2,1,0:T(8,128)S(1)} all-to-all(f32[8,56,128]{2,1,0:T(8,128)S(1)} %x_sums.1), channel_id=1, replica_groups=mesh['z'=8,'x'=4,'y'=4,'core'=2] {'z'}, dimensions={0} | all-to-all | bytes 458752 | tf_op jit(solution)/shard_map/all_to_all | solution.py:292
  47.5 0.7 z_sums.1
  48.2 3.4 %all-to-all-start.1 = ((f32[8,32,128]{2,1,0:T(8,128)}), f32[8,32,128]{2,1,0:T(8,128)S(1)}, u32[]{:S(2)}, u32[]{:S(2)}) async-start(f32[8,32,128]{2,1,0:T(8,128)} %z_sums.1), calls=%async_computation.1 | async-start | bytes 262144 | tf_op jit(solution)/shard_map/all_to_all | solution.py:292
  51.6 0.5 collective-permute-start.7
  52.1 3.9 %collective-permute-done.7.refs_1_ = f32[152,128]{1,0:T(8,128)S(1)} collective-permute-done((f32[152,128]{1,0:T(8,128)S(1)}, f32[152,128]{1,0:T(8,128)S(1)}, u32[]{:S(2)}, u32[]{:S(2)}) %collective-permute-start.7) | collective-permute-done | bytes 77856 | tf_op jit(solution)/shard_map/ppermute | solution.py:297
  56.1 4.5 %all-to-all-done.1 = f32[8,32,128]{2,1,0:T(8,128)S(1)} async-done(((f32[8,32,128]{2,1,0:T(8,128)}), f32[8,32,128]{2,1,0:T(8,128)S(1)}, u32[]{:S(2)}, u32[]{:S(2)}) %all-to-all-start.1) | async-done | bytes 131104 | tf_op jit(solution)/shard_map/all_to_all | solution.py:292
  60.6 2.6 %collective-permute-start.10 = (f32[256,128]{1,0:T(8,128)S(1)}, f32[256,128]{1,0:T(8,128)S(1)}, u32[]{:S(2)}, u32[]{:S(2)}) collective-permute-start(f32[256,128]{1,0:T(8,128)S(1)} %bitcast.3), channel_id=1, source_target_pairs={{0,24},{8,0},{16,8},{24,16},{1,25},{9,1},{17,9},{25,17},{2,26},{10... | collective-permute-start | bytes 393224 | tf_op jit(solution)/shard_map/ppermute | solution.py:288
  63.1 0.8 %collective-permute-start.9 = (f32[256,128]{1,0:T(8,128)S(1)}, f32[256,128]{1,0:T(8,128)S(1)}, u32[]{:S(2)}, u32[]{:S(2)}) collective-permute-start(f32[256,128]{1,0:T(8,128)S(1)} %bitcast.4), channel_id=1, source_target_pairs={{0,16},{8,24},{16,0},{24,8},{1,17},{9,25},{17,1},{25,9},{2,18},{10... | collective-permute-start | bytes 393224 | tf_op jit(solution)/shard_map/ppermute | solution.py:288
  64.2 0.9 %collective-permute-start.12 = (f32[152,128]{1,0:T(8,128)S(1)}, f32[152,128]{1,0:T(8,128)S(1)}, u32[]{:S(2)}, u32[]{:S(2)}) collective-permute-start(f32[152,128]{1,0:T(8,128)S(1)} %near_sum.1.own), channel_id=1, source_target_pairs={{0,1},{1,0},{2,3},{3,2},{4,5},{5,4},{6,7},{7,6},{8,9},{9,8},{10,11... | collective-permute-start | bytes 233480 | tf_op jit(solution)/shard_map/ppermute | solution.py:288
  65.1 0.9 %collective-permute-start.11 = (f32[152,128]{1,0:T(8,128)S(1)}, f32[152,128]{1,0:T(8,128)S(1)}, u32[]{:S(2)}, u32[]{:S(2)}) collective-permute-start(f32[152,128]{1,0:T(8,128)S(1)} %near_sum.1.own), channel_id=1, source_target_pairs={{0,6},{2,4},{4,2},{6,0},{1,7},{3,5},{5,3},{7,1},{8,14},{10,12},{12... | collective-permute-start | bytes 233480 | tf_op jit(solution)/shard_map/ppermute | solution.py:297
  66.0 3.6 %collective-permute-done.11.distant = f32[152,128]{1,0:T(8,128)S(1)} collective-permute-done((f32[152,128]{1,0:T(8,128)S(1)}, f32[152,128]{1,0:T(8,128)S(1)}, u32[]{:S(2)}, u32[]{:S(2)}) %collective-permute-start.11) | collective-permute-done | bytes 77856 | tf_op jit(solution)/shard_map/ppermute | solution.py:297
  69.6 1.2 %collective-permute-done.9.b2 = f32[256,128]{1,0:T(8,128)S(1)} collective-permute-done((f32[256,128]{1,0:T(8,128)S(1)}, f32[256,128]{1,0:T(8,128)S(1)}, u32[]{:S(2)}, u32[]{:S(2)}) %collective-permute-start.9) | collective-permute-done | bytes 131104 | tf_op jit(solution)/shard_map/ppermute | solution.py:288
  70.7 3.0 %collective-permute-done.8.b1 = f32[256,128]{1,0:T(8,128)S(1)} collective-permute-done((f32[256,128]{1,0:T(8,128)S(1)}, f32[256,128]{1,0:T(8,128)S(1)}, u32[]{:S(2)}, u32[]{:S(2)}) %collective-permute-start.8) | collective-permute-done | bytes 131104 | tf_op jit(solution)/shard_map/ppermute | solution.py:288
  73.8 1.5 %outputs.1 = (f32[2,128,128]{2,1,0:T(8,128)}, f32[4,256,128]{2,1,0:T(8,128)}, f32[8,32]{1,0:T(8,128)}, f32[32,4,128]{2,1,0:T(4,128)}) custom-call(f32[8,32]{1,0:T(8,128)S(1)} %copy-done.1, f32[256,128]{1,0:T(8,128)S(1)} %bitcast.6, f32[256,128]{1,0:T(8,128)S(1)} %collective-permute-done.8.b1, f32[256,128]{1,0:T(8,128)S(1)} %collective-permute-done.9.b2, ...), custom_call_target="tpu_custom_call" | custom-call | flops 1048576 | bytes 1048576 | tf_op jit(solution)/shard_map/outputs/pallas_call | solution.py:275
  (22 shorter events, 1.3 us)
Async XLA Ops:
  0.6 19.4 %copy-start.2 = (f32[32,128,128]{2,1,0:T(8,128)S(1)}, f32[32,128,128]{2,1,0:T(8,128)}, u32[]{:S(2)}) copy-start(f32[32,128,128]{2,1,0:T(8,128)} %core.1) | copy-start | bytes 6291460
  14.2 5.8 %collective-permute-start.3 = (f32[5,128,128]{2,1,0:T(8,128)}, f32[5,128,128]{2,1,0:T(8,128)S(1)}, u32[]{:S(2)}, u32[]{:S(2)}) collective-permute-start(f32[5,128,128]{2,1,0:T(8,128)} %get-tuple-element.26), channel_id=1, source_target_pairs={{0,1},{1,0},{2,3},{3,2},{4,5},{5,4},{6,7},{7,6},{8,9},{9,8},{10,11... | collective-permute-start | bytes 983048 | tf_op jit(solution)/shard_map/ppermute | solution.py:288
  14.3 9.0 %collective-permute-start = (f32[256,128]{1,0:T(8,128)}, f32[256,128]{1,0:T(8,128)S(1)}, u32[]{:S(2)}, u32[]{:S(2)}) collective-permute-start(f32[256,128]{1,0:T(8,128)} %get-tuple-element.22), channel_id=1, source_target_pairs={{0,8},{8,16},{16,24},{24,0},{1,9},{9,17},{17,25},{25,1},{2,10},{10... | collective-permute-start | bytes 393224 | tf_op jit(solution)/shard_map/ppermute | solution.py:288
  15.8 10.0 %collective-permute-start.1 = (f32[256,128]{1,0:T(8,128)}, f32[256,128]{1,0:T(8,128)S(1)}, u32[]{:S(2)}, u32[]{:S(2)}) collective-permute-start(f32[256,128]{1,0:T(8,128)} %get-tuple-element.23), channel_id=1, source_target_pairs={{0,16},{8,24},{16,0},{24,8},{1,17},{9,25},{17,1},{25,9},{2,18},{10... | collective-permute-start | bytes 393224 | tf_op jit(solution)/shard_map/ppermute | solution.py:288
  18.6 7.3 %collective-permute-start.2 = (f32[256,128]{1,0:T(8,128)}, f32[256,128]{1,0:T(8,128)S(1)}, u32[]{:S(2)}, u32[]{:S(2)}) collective-permute-start(f32[256,128]{1,0:T(8,128)} %get-tuple-element.24), channel_id=1, source_target_pairs={{0,24},{8,0},{16,8},{24,16},{1,25},{9,1},{17,9},{25,17},{2,26},{10... | collective-permute-start | bytes 393224 | tf_op jit(solution)/shard_map/ppermute | solution.py:288
  20.0 1.0 %copy-start.3 = (f32[5,128,128]{2,1,0:T(8,128)S(1)}, f32[5,128,128]{2,1,0:T(8,128)}, u32[]{:S(2)}) copy-start(f32[5,128,128]{2,1,0:T(8,128)} %get-tuple-element.25.own) | copy-start | bytes 983044
  21.0 8.0 %copy-start = (f32[256,128]{1,0:T(8,128)S(1)}, f32[256,128]{1,0:T(8,128)}, u32[]{:S(2)}) copy-start(f32[256,128]{1,0:T(8,128)} %get-tuple-element.21.a0) | copy-start | bytes 393220
  21.0 52.8 %copy-start.1 = (f32[8,32]{1,0:T(8,128)S(1)}, f32[8,32]{1,0:T(8,128)}, u32[]{:S(2)}) copy-start(f32[8,32]{1,0:T(8,128)} %hour_ref.3) | copy-start | bytes 3076
  21.7 7.0 %collective-permute-start.4 = (f32[136,128]{1,0:T(8,128)S(1)}, f32[136,128]{1,0:T(8,128)S(1)}, u32[]{:S(2)}, u32[]{:S(2)}) collective-permute-start(f32[136,128]{1,0:T(8,128)S(1)} %get-tuple-element.28), channel_id=1, source_target_pairs={{0,8},{8,16},{16,24},{24,0},{1,9},{9,17},{17,25},{25,1},{2,10},{10... | collective-permute-start | bytes 208904 | tf_op jit(solution)/shard_map/ppermute | solution.py:288
  22.4 6.3 %collective-permute-start.5 = (f32[136,128]{1,0:T(8,128)S(1)}, f32[136,128]{1,0:T(8,128)S(1)}, u32[]{:S(2)}, u32[]{:S(2)}) collective-permute-start(f32[136,128]{1,0:T(8,128)S(1)} %get-tuple-element.29), channel_id=1, source_target_pairs={{0,16},{8,24},{16,0},{24,8},{1,17},{9,25},{17,1},{25,9},{2,18},{10... | collective-permute-start | bytes 208904 | tf_op jit(solution)/shard_map/ppermute | solution.py:288
  23.3 5.7 %collective-permute-start.6 = (f32[136,128]{1,0:T(8,128)S(1)}, f32[136,128]{1,0:T(8,128)S(1)}, u32[]{:S(2)}, u32[]{:S(2)}) collective-permute-start(f32[136,128]{1,0:T(8,128)S(1)} %get-tuple-element.30), channel_id=1, source_target_pairs={{0,24},{8,0},{16,8},{24,16},{1,25},{9,1},{17,9},{25,17},{2,26},{10... | collective-permute-start | bytes 208904 | tf_op jit(solution)/shard_map/ppermute | solution.py:288
  48.2 12.4 %all-to-all-start.1 = ((f32[8,32,128]{2,1,0:T(8,128)}), f32[8,32,128]{2,1,0:T(8,128)S(1)}, u32[]{:S(2)}, u32[]{:S(2)}) async-start(f32[8,32,128]{2,1,0:T(8,128)} %z_sums.1), calls=%async_computation.1 | async-start | bytes 262144 | tf_op jit(solution)/shard_map/all_to_all | solution.py:292
  51.6 4.5 %collective-permute-start.7 = (f32[152,128]{1,0:T(8,128)S(1)}, f32[152,128]{1,0:T(8,128)S(1)}, u32[]{:S(2)}, u32[]{:S(2)}) collective-permute-start(f32[152,128]{1,0:T(8,128)S(1)} %tail_sums.1.refs_0_), channel_id=1, source_target_pairs={{0,2},{2,0},{4,6},{6,4},{1,3},{3,1},{5,7},{7,5},{8,10},{10,8},{12,... | collective-permute-start | bytes 233480 | tf_op jit(solution)/shard_map/ppermute | solution.py:297
  60.6 4.5 %collective-permute-start.13 = (f32[152,128]{1,0:T(8,128)S(1)}, f32[152,128]{1,0:T(8,128)S(1)}, u32[]{:S(2)}, u32[]{:S(2)}) collective-permute-start(f32[152,128]{1,0:T(8,128)S(1)} %near_sum.1.own), channel_id=1, source_target_pairs={{0,7},{1,6},{2,5},{3,4},{4,3},{5,2},{6,1},{7,0},{8,15},{9,14},{10,... | collective-permute-start | bytes 233480 | tf_op jit(solution)/shard_map/ppermute | solution.py:297
  60.6 9.0 %collective-permute-start.10 = (f32[256,128]{1,0:T(8,128)S(1)}, f32[256,128]{1,0:T(8,128)S(1)}, u32[]{:S(2)}, u32[]{:S(2)}) collective-permute-start(f32[256,128]{1,0:T(8,128)S(1)} %bitcast.3), channel_id=1, source_target_pairs={{0,24},{8,0},{16,8},{24,16},{1,25},{9,1},{17,9},{25,17},{2,26},{10... | collective-permute-start | bytes 393224 | tf_op jit(solution)/shard_map/ppermute | solution.py:288
  63.1 7.6 %collective-permute-start.9 = (f32[256,128]{1,0:T(8,128)S(1)}, f32[256,128]{1,0:T(8,128)S(1)}, u32[]{:S(2)}, u32[]{:S(2)}) collective-permute-start(f32[256,128]{1,0:T(8,128)S(1)} %bitcast.4), channel_id=1, source_target_pairs={{0,16},{8,24},{16,0},{24,8},{1,17},{9,25},{17,1},{25,9},{2,18},{10... | collective-permute-start | bytes 393224 | tf_op jit(solution)/shard_map/ppermute | solution.py:288
  63.9 9.9 %collective-permute-start.8 = (f32[256,128]{1,0:T(8,128)S(1)}, f32[256,128]{1,0:T(8,128)S(1)}, u32[]{:S(2)}, u32[]{:S(2)}) collective-permute-start(f32[256,128]{1,0:T(8,128)S(1)} %bitcast.5), channel_id=1, source_target_pairs={{0,8},{8,16},{16,24},{24,0},{1,9},{9,17},{17,25},{25,1},{2,10},{10... | collective-permute-start | bytes 393224 | tf_op jit(solution)/shard_map/ppermute | solution.py:288
  64.2 1.8 %collective-permute-start.12 = (f32[152,128]{1,0:T(8,128)S(1)}, f32[152,128]{1,0:T(8,128)S(1)}, u32[]{:S(2)}, u32[]{:S(2)}) collective-permute-start(f32[152,128]{1,0:T(8,128)S(1)} %near_sum.1.own), channel_id=1, source_target_pairs={{0,1},{1,0},{2,3},{3,2},{4,5},{5,4},{6,7},{7,6},{8,9},{9,8},{10,11... | collective-permute-start | bytes 233480 | tf_op jit(solution)/shard_map/ppermute | solution.py:288
  65.1 4.5 %collective-permute-start.11 = (f32[152,128]{1,0:T(8,128)S(1)}, f32[152,128]{1,0:T(8,128)S(1)}, u32[]{:S(2)}, u32[]{:S(2)}) collective-permute-start(f32[152,128]{1,0:T(8,128)S(1)} %near_sum.1.own), channel_id=1, source_target_pairs={{0,6},{2,4},{4,2},{6,0},{1,7},{3,5},{5,3},{7,1},{8,14},{10,12},{12... | collective-permute-start | bytes 233480 | tf_op jit(solution)/shard_map/ppermute | solution.py:297

commit v12 on v11

--- a/solution.py
+++ b/solution.py
@@ -236,6 +236,12 @@
     out[tail:, :] = src_half[...]
 
 
+def pair_kernel(own, other, out):
+    c = lax.axis_index("core")
+    out[c] = own[...]
+    out[1 - c] = other[...]
+
+
 def z_kernel(w, copies):
     share = copies.shape[1]
     total = jnp.sum(w[:, :share, :], axis=0)
@@ -243,17 +249,15 @@
         copies[z] = total
 
 
-def end_kernel(scales, hour_ref, b0, b1, b2, b3, own, distant, sibling, diagonal,
+def end_kernel(scales, hour_ref, b0, b1, b2, b3, joined, more,
                src_out, dst_out, hour_out, core_out, both):
-    x, c = lax.axis_index("x"), lax.axis_index("core")
+    x = lax.axis_index("x")
     src_scale, dst_scale, hour_scale, core_scale = scales
     for s, block in enumerate((b0, b1, b2, b3)):
         dst_out[lax.rem(x - s + X, X)] = block[...] * dst_scale
     tail = both.shape[1]
-    for at, p, q in ((c, own, distant), (1 - c, sibling, diagonal)):
-        total = p[...] + q[...]
-        both[at] = total[:tail]
-        src_out[at] = total[tail:] * src_scale
+    src_out[...] = (joined[:, tail:, :] + more[:, tail:, :]) * src_scale
+    both[...] = joined[:, :tail, :] + more[:, :tail, :]
     hours, rank = hour_ref.shape
     half = hours // CORES
     tiles = []
@@ -274,9 +278,9 @@
     tail = 4 * hours // CORES + 8
     return pl.pallas_call(
         functools.partial(end_kernel, scales),
-        in_specs=[SMEM] + [VMEM] * 8,
+        in_specs=[SMEM] + [VMEM] * 6,
         out_specs=[VMEM] * 4,
-        out_shape=[struct(CORES, sums[0].shape[0] - tail, q1), struct(X, block, q1),
+        out_shape=[struct(CORES, sums[0].shape[1] - tail, q1), struct(X, block, q1),
                    struct(hours, rank), struct(rank, 4, q1)],
         scratch_shapes=[pltpu.VMEM((CORES, tail, q1), F32)],
         compiler_params=params(8), cost_estimate=cost(1 << 20, 1 << 20), name="outputs",
@@ -325,13 +329,13 @@
                      struct(tail + src_half.shape[0], q1), [w, src_half])
     copies = small_call(z_kernel, "z_sums", struct(zs, share, q1), [w])
     own = summed("near_sum", own, paired(own, "y", near))
+    both = small_call(pair_kernel, "both_tails", struct(CORES, *own.shape), [own, shifted(own, "core", 1)])
     block = swapped(copies, "z").reshape(zs * share, q1)
-    block, own = lax.optimization_barrier((block, own))
-    mine = [own, paired(own, "y", far)]
-    others = [shifted(own, "core", 1), paired(own, ("y", "core"), far)]
+    block, both = lax.optimization_barrier((block, both))
+    more = paired(both, "y", far)
     blocks = around(block, "x")
     grad_src, grad_dst, grad_hour, grad_core = end_call(
-        scales, hour_factor, blocks, mine + others)
+        scales, hour_factor, blocks, [both, more])
     return (grad_src.reshape(src_factor.shape), grad_dst.reshape(dst_factor.shape), grad_hour, grad_core)
 
 

time: 76.4 us -> 74.4 us (0.974)
  waiting for transfers between devices: 19.8 us -> 18.6 us
    ppermute x11, waiting for transfers between devices: 7.83 us -> 11.6 us  [shifted(): return lax.ppermute(x, axis, [(i, (i + s) % n) for i in range(n)])]
    ppermute x3 -> x2, waiting for transfers between devices: 7.53 us -> 3.95 us  [paired(): return lax.ppermute(x, axis, [(i, flip(i, n)) for i in range(n)])]
    all_to_all x1, waiting for transfers between devices: 4.47 us -> 3.08 us  [swapped(): return lax.all_to_all(x, axis, split_axis=0, concat_axis=0, tiled=True)]
    ppermute x11, starting transfers between devices: 14 us -> 13.2 us  [shifted(): return lax.ppermute(x, axis, [(i, (i + s) % n) for i in range(n)])]
    ppermute x3 -> x2, starting transfers between devices: 1.4 us -> 2.11 us  [paired(): return lax.ppermute(x, axis, [(i, flip(i, n)) for i in range(n)])]
  transfers between devices with their start and end apart: 15 -> 14, of which waited for: 9 -> 9; matrix products, arithmetic and copies ran while one was open for 0% -> 0% of each run, Pallas kernels for 1% -> 1%
where the time goes in v12:
time: 74.4 us; the launch traced here: 74.1 us
  starting transfers between devices  18.7 us (25%)
  waiting for transfers between devices  18.6 us (25%)
  blocking collectives  18.5 us (25%)
  Pallas kernels  16.5 us (22%)
  local copies, waits for them, and re-layouts  0.99 us (1%)
    all_to_all x1, blocking collectives, swapped(): return lax.all_to_all(x, axis, split_axis=0, concat_axis=0, tiled=True)  18.5 us
    pallas_call x1, Pallas kernels, main_call(): pl.pallas_call(main_kernel, out_shape=[struct(block, q1)] * X + [struct(h...  13.5 us
    ppermute x11, starting transfers between devices, shifted(): return lax.ppermute(x, axis, [(i, (i + s) % n) for i in range(n)])  13.2 us
    ppermute x11, waiting for transfers between devices, shifted(): return lax.ppermute(x, axis, [(i, (i + s) % n) for i in range(n)])  11.6 us
    ppermute x2, waiting for transfers between devices, paired(): return lax.ppermute(x, axis, [(i, flip(i, n)) for i in range(n)])  3.95 us
    all_to_all x1, starting transfers between devices, swapped(): return lax.all_to_all(x, axis, split_axis=0, concat_axis=0, tiled=True)  3.37 us
    all_to_all x1, waiting for transfers between devices, swapped(): return lax.all_to_all(x, axis, split_axis=0, concat_axis=0, tiled=True)  3.08 us
    ppermute x2, starting transfers between devices, paired(): return lax.ppermute(x, axis, [(i, flip(i, n)) for i in range(n)])  2.11 us
  transfers between devices with their start and end apart: 14, of which 9 were waited for; matrix products, arithmetic and copies ran while one was open for 0% of the time, Pallas kernels for 1%

profile of v12, /device:TPU:8, one launch (start us, length us, event | category | flops | bytes accessed | tf_op | source)
XLA Modules:
  0.0 74.1 jit_solution(3875492690643858643)
XLA Ops:
  0.6 13.5 %all_terms.1 = (f32[256,128]{1,0:T(8,128)}, f32[256,128]{1,0:T(8,128)}, f32[256,128]{1,0:T(8,128)}, f32[256,128]{1,0:T(8,128)}, f32[5,128,128]{2,1,0:T(8,128)}, /*index=5*/f32[5,128,128]{2,1,0:T(8,128)}) custom-call(f32[8,32]{1,0:T(8,128)} %hour_ref.3, s32[8,256,1024]{2,1,0:T(8,128)} %counts_hbm.1, f32[256,128]{1,0:T(8,128)} %src_hbm.1, ...), custom_call_target="tpu_custom_call" | custom-call | flops 4831838208 | bytes 14680064 | tf_op jit(solution)/shard_map/all_terms/pallas_call | solution.py:133
  14.2 1.6 %collective-permute-start = (f32[256,128]{1,0:T(8,128)}, f32[256,128]{1,0:T(8,128)S(1)}, u32[]{:S(2)}, u32[]{:S(2)}) collective-permute-start(f32[256,128]{1,0:T(8,128)} %get-tuple-element.22), channel_id=1, source_target_pairs={{0,8},{8,16},{16,24},{24,0},{1,9},{9,17},{17,25},{25,1},{2,10},{10... | collective-permute-start | bytes 393224 | tf_op jit(solution)/shard_map/ppermute | solution.py:292
  15.8 2.7 %collective-permute-start.1 = (f32[256,128]{1,0:T(8,128)}, f32[256,128]{1,0:T(8,128)S(1)}, u32[]{:S(2)}, u32[]{:S(2)}) collective-permute-start(f32[256,128]{1,0:T(8,128)} %get-tuple-element.23), channel_id=1, source_target_pairs={{0,16},{8,24},{16,0},{24,8},{1,17},{9,25},{17,1},{25,9},{2,18},{10... | collective-permute-start | bytes 393224 | tf_op jit(solution)/shard_map/ppermute | solution.py:292
  18.6 1.4 %collective-permute-start.2 = (f32[256,128]{1,0:T(8,128)}, f32[256,128]{1,0:T(8,128)S(1)}, u32[]{:S(2)}, u32[]{:S(2)}) collective-permute-start(f32[256,128]{1,0:T(8,128)} %get-tuple-element.24), channel_id=1, source_target_pairs={{0,24},{8,0},{16,8},{24,16},{1,25},{9,1},{17,9},{25,17},{2,26},{10... | collective-permute-start | bytes 393224 | tf_op jit(solution)/shard_map/ppermute | solution.py:292
  20.0 1.0 %copy-done.3 = f32[5,128,128]{2,1,0:T(8,128)S(1)} copy-done((f32[5,128,128]{2,1,0:T(8,128)S(1)}, f32[5,128,128]{2,1,0:T(8,128)}, u32[]{:S(2)}) %copy-start.3) | copy-done | bytes 327704
  21.0 0.8 %hour_terms.1 = (f32[136,128]{1,0:T(8,128)S(1)}, f32[136,128]{1,0:T(8,128)S(1)}, f32[136,128]{1,0:T(8,128)S(1)}, f32[136,128]{1,0:T(8,128)S(1)}, f32[128,128]{1,0:T(8,128)S(1)}) custom-call(f32[5,128,128]{2,1,0:T(8,128)S(1)} %copy-done.3, f32[5,128,128]{2,1,0:T(8,128)S(1)} %collective-permute-done.3.came, f32[32,128,128]{2,1,0:T(8,128)S(1)} %copy-done.2), custom_call_target="tpu_custom_call" | custom-call | flops 17179869184 | bytes 4194304 | tf_op jit(solution)/shard_map/hour_terms/pallas_call | solution.py:190
  21.7 0.7 collective-permute-start.4
  22.4 0.9 %collective-permute-start.5 = (f32[136,128]{1,0:T(8,128)S(1)}, f32[136,128]{1,0:T(8,128)S(1)}, u32[]{:S(2)}, u32[]{:S(2)}) collective-permute-start(f32[136,128]{1,0:T(8,128)S(1)} %get-tuple-element.29), channel_id=1, source_target_pairs={{0,16},{8,24},{16,0},{24,8},{1,17},{9,25},{17,1},{25,9},{2,18},{10... | collective-permute-start | bytes 208904 | tf_op jit(solution)/shard_map/ppermute | solution.py:292
  23.3 2.1 %collective-permute-start.6 = (f32[136,128]{1,0:T(8,128)S(1)}, f32[136,128]{1,0:T(8,128)S(1)}, u32[]{:S(2)}, u32[]{:S(2)}) collective-permute-start(f32[136,128]{1,0:T(8,128)S(1)} %get-tuple-element.30), channel_id=1, source_target_pairs={{0,24},{8,0},{16,8},{24,16},{1,25},{9,1},{17,9},{25,17},{2,26},{10... | collective-permute-start | bytes 208904 | tf_op jit(solution)/shard_map/ppermute | solution.py:292
  25.9 2.9 %collective-permute-done.4.m1 = f32[136,128]{1,0:T(8,128)S(1)} collective-permute-done((f32[136,128]{1,0:T(8,128)S(1)}, f32[136,128]{1,0:T(8,128)S(1)}, u32[]{:S(2)}, u32[]{:S(2)}) %collective-permute-start.4) | collective-permute-done | bytes 69664 | tf_op jit(solution)/shard_map/ppermute | solution.py:292
  29.0 18.5 %all_to_all.10.w = f32[8,56,128]{2,1,0:T(8,128)S(1)} all-to-all(f32[8,56,128]{2,1,0:T(8,128)S(1)} %x_sums.1), channel_id=1, replica_groups=mesh['z'=8,'x'=4,'y'=4,'core'=2] {'z'}, dimensions={0} | all-to-all | bytes 458752 | tf_op jit(solution)/shard_map/all_to_all | solution.py:296
  47.5 0.7 z_sums.1
  48.2 3.4 %all-to-all-start.1 = ((f32[8,32,128]{2,1,0:T(8,128)}), f32[8,32,128]{2,1,0:T(8,128)S(1)}, u32[]{:S(2)}, u32[]{:S(2)}) async-start(f32[8,32,128]{2,1,0:T(8,128)} %z_sums.1), calls=%async_computation.1 | async-start | bytes 262144 | tf_op jit(solution)/shard_map/all_to_all | solution.py:296
  51.6 0.5 collective-permute-start.7
  52.1 3.9 %collective-permute-done.7.refs_1_ = f32[152,128]{1,0:T(8,128)S(1)} collective-permute-done((f32[152,128]{1,0:T(8,128)S(1)}, f32[152,128]{1,0:T(8,128)S(1)}, u32[]{:S(2)}, u32[]{:S(2)}) %collective-permute-start.7) | collective-permute-done | bytes 77856 | tf_op jit(solution)/shard_map/ppermute | solution.py:301
  56.2 1.3 %collective-permute-done.8.other = f32[152,128]{1,0:T(8,128)S(1)} collective-permute-done((f32[152,128]{1,0:T(8,128)S(1)}, f32[152,128]{1,0:T(8,128)S(1)}, u32[]{:S(2)}, u32[]{:S(2)}) %collective-permute-start.8) | collective-permute-done | bytes 77856 | tf_op jit(solution)/shard_map/ppermute | solution.py:292
  57.5 3.1 %all-to-all-done.1 = f32[8,32,128]{2,1,0:T(8,128)S(1)} async-done(((f32[8,32,128]{2,1,0:T(8,128)}), f32[8,32,128]{2,1,0:T(8,128)S(1)}, u32[]{:S(2)}, u32[]{:S(2)}) %all-to-all-start.1) | async-done | bytes 131104 | tf_op jit(solution)/shard_map/all_to_all | solution.py:296
  60.5 1.6 %collective-permute-start.12 = (f32[2,152,128]{2,1,0:T(8,128)S(1)}, f32[2,152,128]{2,1,0:T(8,128)S(1)}, u32[]{:S(2)}, u32[]{:S(2)}) collective-permute-start(f32[2,152,128]{2,1,0:T(8,128)S(1)} %both_tails.1.joined), channel_id=1, source_target_pairs={{0,6},{2,4},{4,2},{6,0},{1,7},{3,5},{5,3},{7,1},{8,14},{10,12},{12... | collective-permute-start | bytes 466952 | tf_op jit(solution)/shard_map/ppermute | solution.py:301
  62.1 2.5 %collective-permute-start.11 = (f32[256,128]{1,0:T(8,128)S(1)}, f32[256,128]{1,0:T(8,128)S(1)}, u32[]{:S(2)}, u32[]{:S(2)}) collective-permute-start(f32[256,128]{1,0:T(8,128)S(1)} %bitcast.3), channel_id=1, source_target_pairs={{0,24},{8,0},{16,8},{24,16},{1,25},{9,1},{17,9},{25,17},{2,26},{10... | collective-permute-start | bytes 393224 | tf_op jit(solution)/shard_map/ppermute | solution.py:292
  64.7 0.8 %collective-permute-start.10 = (f32[256,128]{1,0:T(8,128)S(1)}, f32[256,128]{1,0:T(8,128)S(1)}, u32[]{:S(2)}, u32[]{:S(2)}) collective-permute-start(f32[256,128]{1,0:T(8,128)S(1)} %bitcast.4), channel_id=1, source_target_pairs={{0,16},{8,24},{16,0},{24,8},{1,17},{9,25},{17,1},{25,9},{2,18},{10... | collective-permute-start | bytes 393224 | tf_op jit(solution)/shard_map/ppermute | solution.py:292
  65.8 2.8 %collective-permute-done.11.b3 = f32[256,128]{1,0:T(8,128)S(1)} collective-permute-done((f32[256,128]{1,0:T(8,128)S(1)}, f32[256,128]{1,0:T(8,128)S(1)}, u32[]{:S(2)}, u32[]{:S(2)}) %collective-permute-start.11) | collective-permute-done | bytes 131104 | tf_op jit(solution)/shard_map/ppermute | solution.py:292
  68.6 2.6 %collective-permute-done.10.b2 = f32[256,128]{1,0:T(8,128)S(1)} collective-permute-done((f32[256,128]{1,0:T(8,128)S(1)}, f32[256,128]{1,0:T(8,128)S(1)}, u32[]{:S(2)}, u32[]{:S(2)}) %collective-permute-start.10) | collective-permute-done | bytes 131104 | tf_op jit(solution)/shard_map/ppermute | solution.py:292
  71.2 1.3 %collective-permute-done.9.b1 = f32[256,128]{1,0:T(8,128)S(1)} collective-permute-done((f32[256,128]{1,0:T(8,128)S(1)}, f32[256,128]{1,0:T(8,128)S(1)}, u32[]{:S(2)}, u32[]{:S(2)}) %collective-permute-start.9) | collective-permute-done | bytes 131104 | tf_op jit(solution)/shard_map/ppermute | solution.py:292
  72.6 1.5 %outputs.1 = (f32[2,128,128]{2,1,0:T(8,128)}, f32[4,256,128]{2,1,0:T(8,128)}, f32[8,32]{1,0:T(8,128)}, f32[32,4,128]{2,1,0:T(4,128)}) custom-call(f32[8,32]{1,0:T(8,128)S(1)} %copy-done.1, f32[256,128]{1,0:T(8,128)S(1)} %bitcast.6, f32[256,128]{1,0:T(8,128)S(1)} %collective-permute-done.9.b1, f32[256,128]{1,0:T(8,128)S(1)} %collective-permute-done.10.b2, ...), custom_call_target="tpu_custom_call" | custom-call | flops 1048576 | bytes 1048576 | tf_op jit(solution)/shard_map/outputs/pallas_call | solution.py:279
  (21 shorter events, 1.3 us)
Async XLA Ops:
  0.6 19.4 %copy-start.2 = (f32[32,128,128]{2,1,0:T(8,128)S(1)}, f32[32,128,128]{2,1,0:T(8,128)}, u32[]{:S(2)}) copy-start(f32[32,128,128]{2,1,0:T(8,128)} %core.1) | copy-start | bytes 6291460
  14.1 5.8 %collective-permute-start.3 = (f32[5,128,128]{2,1,0:T(8,128)}, f32[5,128,128]{2,1,0:T(8,128)S(1)}, u32[]{:S(2)}, u32[]{:S(2)}) collective-permute-start(f32[5,128,128]{2,1,0:T(8,128)} %get-tuple-element.26), channel_id=1, source_target_pairs={{0,1},{1,0},{2,3},{3,2},{4,5},{5,4},{6,7},{7,6},{8,9},{9,8},{10,11... | collective-permute-start | bytes 983048 | tf_op jit(solution)/shard_map/ppermute | solution.py:292
  14.2 9.0 %collective-permute-start = (f32[256,128]{1,0:T(8,128)}, f32[256,128]{1,0:T(8,128)S(1)}, u32[]{:S(2)}, u32[]{:S(2)}) collective-permute-start(f32[256,128]{1,0:T(8,128)} %get-tuple-element.22), channel_id=1, source_target_pairs={{0,8},{8,16},{16,24},{24,0},{1,9},{9,17},{17,25},{25,1},{2,10},{10... | collective-permute-start | bytes 393224 | tf_op jit(solution)/shard_map/ppermute | solution.py:292
  15.8 10.0 %collective-permute-start.1 = (f32[256,128]{1,0:T(8,128)}, f32[256,128]{1,0:T(8,128)S(1)}, u32[]{:S(2)}, u32[]{:S(2)}) collective-permute-start(f32[256,128]{1,0:T(8,128)} %get-tuple-element.23), channel_id=1, source_target_pairs={{0,16},{8,24},{16,0},{24,8},{1,17},{9,25},{17,1},{25,9},{2,18},{10... | collective-permute-start | bytes 393224 | tf_op jit(solution)/shard_map/ppermute | solution.py:292
  18.6 7.3 %collective-permute-start.2 = (f32[256,128]{1,0:T(8,128)}, f32[256,128]{1,0:T(8,128)S(1)}, u32[]{:S(2)}, u32[]{:S(2)}) collective-permute-start(f32[256,128]{1,0:T(8,128)} %get-tuple-element.24), channel_id=1, source_target_pairs={{0,24},{8,0},{16,8},{24,16},{1,25},{9,1},{17,9},{25,17},{2,26},{10... | collective-permute-start | bytes 393224 | tf_op jit(solution)/shard_map/ppermute | solution.py:292
  20.0 1.0 %copy-start.3 = (f32[5,128,128]{2,1,0:T(8,128)S(1)}, f32[5,128,128]{2,1,0:T(8,128)}, u32[]{:S(2)}) copy-start(f32[5,128,128]{2,1,0:T(8,128)} %get-tuple-element.25.own) | copy-start | bytes 983044
  21.0 8.0 %copy-start = (f32[256,128]{1,0:T(8,128)S(1)}, f32[256,128]{1,0:T(8,128)}, u32[]{:S(2)}) copy-start(f32[256,128]{1,0:T(8,128)} %get-tuple-element.21.a0) | copy-start | bytes 393220
  21.0 51.6 %copy-start.1 = (f32[8,32]{1,0:T(8,128)S(1)}, f32[8,32]{1,0:T(8,128)}, u32[]{:S(2)}) copy-start(f32[8,32]{1,0:T(8,128)} %hour_ref.3) | copy-start | bytes 3076
  21.7 7.0 %collective-permute-start.4 = (f32[136,128]{1,0:T(8,128)S(1)}, f32[136,128]{1,0:T(8,128)S(1)}, u32[]{:S(2)}, u32[]{:S(2)}) collective-permute-start(f32[136,128]{1,0:T(8,128)S(1)} %get-tuple-element.28), channel_id=1, source_target_pairs={{0,8},{8,16},{16,24},{24,0},{1,9},{9,17},{17,25},{25,1},{2,10},{10... | collective-permute-start | bytes 208904 | tf_op jit(solution)/shard_map/ppermute | solution.py:292
  22.4 6.3 %collective-permute-start.5 = (f32[136,128]{1,0:T(8,128)S(1)}, f32[136,128]{1,0:T(8,128)S(1)}, u32[]{:S(2)}, u32[]{:S(2)}) collective-permute-start(f32[136,128]{1,0:T(8,128)S(1)} %get-tuple-element.29), channel_id=1, source_target_pairs={{0,16},{8,24},{16,0},{24,8},{1,17},{9,25},{17,1},{25,9},{2,18},{10... | collective-permute-start | bytes 208904 | tf_op jit(solution)/shard_map/ppermute | solution.py:292
  23.3 5.7 %collective-permute-start.6 = (f32[136,128]{1,0:T(8,128)S(1)}, f32[136,128]{1,0:T(8,128)S(1)}, u32[]{:S(2)}, u32[]{:S(2)}) collective-permute-start(f32[136,128]{1,0:T(8,128)S(1)} %get-tuple-element.30), channel_id=1, source_target_pairs={{0,24},{8,0},{16,8},{24,16},{1,25},{9,1},{17,9},{25,17},{2,26},{10... | collective-permute-start | bytes 208904 | tf_op jit(solution)/shard_map/ppermute | solution.py:292
  48.2 12.4 %all-to-all-start.1 = ((f32[8,32,128]{2,1,0:T(8,128)}), f32[8,32,128]{2,1,0:T(8,128)S(1)}, u32[]{:S(2)}, u32[]{:S(2)}) async-start(f32[8,32,128]{2,1,0:T(8,128)} %z_sums.1), calls=%async_computation.1 | async-start | bytes 262144 | tf_op jit(solution)/shard_map/all_to_all | solution.py:296
  51.6 4.5 %collective-permute-start.7 = (f32[152,128]{1,0:T(8,128)S(1)}, f32[152,128]{1,0:T(8,128)S(1)}, u32[]{:S(2)}, u32[]{:S(2)}) collective-permute-start(f32[152,128]{1,0:T(8,128)S(1)} %tail_sums.1.refs_0_), channel_id=1, source_target_pairs={{0,2},{2,0},{4,6},{6,4},{1,3},{3,1},{5,7},{7,5},{8,10},{10,8},{12,... | collective-permute-start | bytes 233480 | tf_op jit(solution)/shard_map/ppermute | solution.py:301
  56.1 1.4 %collective-permute-start.8 = (f32[152,128]{1,0:T(8,128)S(1)}, f32[152,128]{1,0:T(8,128)S(1)}, u32[]{:S(2)}, u32[]{:S(2)}) collective-permute-start(f32[152,128]{1,0:T(8,128)S(1)} %near_sum.1.own), channel_id=1, source_target_pairs={{0,1},{1,0},{2,3},{3,2},{4,5},{5,4},{6,7},{7,6},{8,9},{9,8},{10,11... | collective-permute-start | bytes 233480 | tf_op jit(solution)/shard_map/ppermute | solution.py:292
  60.5 12.0 %collective-permute-start.12 = (f32[2,152,128]{2,1,0:T(8,128)S(1)}, f32[2,152,128]{2,1,0:T(8,128)S(1)}, u32[]{:S(2)}, u32[]{:S(2)}) collective-permute-start(f32[2,152,128]{2,1,0:T(8,128)S(1)} %both_tails.1.joined), channel_id=1, source_target_pairs={{0,6},{2,4},{4,2},{6,0},{1,7},{3,5},{5,3},{7,1},{8,14},{10,12},{12... | collective-permute-start | bytes 466952 | tf_op jit(solution)/shard_map/ppermute | solution.py:301
  62.1 6.5 %collective-permute-start.11 = (f32[256,128]{1,0:T(8,128)S(1)}, f32[256,128]{1,0:T(8,128)S(1)}, u32[]{:S(2)}, u32[]{:S(2)}) collective-permute-start(f32[256,128]{1,0:T(8,128)S(1)} %bitcast.3), channel_id=1, source_target_pairs={{0,24},{8,0},{16,8},{24,16},{1,25},{9,1},{17,9},{25,17},{2,26},{10... | collective-permute-start | bytes 393224 | tf_op jit(solution)/shard_map/ppermute | solution.py:292
  64.7 6.6 %collective-permute-start.10 = (f32[256,128]{1,0:T(8,128)S(1)}, f32[256,128]{1,0:T(8,128)S(1)}, u32[]{:S(2)}, u32[]{:S(2)}) collective-permute-start(f32[256,128]{1,0:T(8,128)S(1)} %bitcast.4), channel_id=1, source_target_pairs={{0,16},{8,24},{16,0},{24,8},{1,17},{9,25},{17,1},{25,9},{2,18},{10... | collective-permute-start | bytes 393224 | tf_op jit(solution)/shard_map/ppermute | solution.py:292
  65.5 7.1 %collective-permute-start.9 = (f32[256,128]{1,0:T(8,128)S(1)}, f32[256,128]{1,0:T(8,128)S(1)}, u32[]{:S(2)}, u32[]{:S(2)}) collective-permute-start(f32[256,128]{1,0:T(8,128)S(1)} %bitcast.5), channel_id=1, source_target_pairs={{0,8},{8,16},{16,24},{24,0},{1,9},{9,17},{17,25},{25,1},{2,10},{10... | collective-permute-start | bytes 393224 | tf_op jit(solution)/shard_map/ppermute | solution.py:292
